TPU v7x, 32 devices: a whole 2x2x4 slice. The times are simulated.
32 devices in a mesh: dp: 8 (over y, x, core), tensor: 4 (over z).
Axes of the slice: x: 2, y: 2, z: 4, core: 2. Of those that a mesh axis runs over, the one named last changes fastest.
Arguments:
- tokens: bfloat16 [8192, 1024], P(('dp', 'tensor')), may hold values from -6 to 6
- segments: int32 [8, 1024], P('dp'), may hold values from 0 to 3, never falling along the last dimension, each value on 1 to 512 neighbouring positions
- routes: int32 [8192, 2], P('dp'), may hold values from 0 to 15, all different within a row; in each aligned block of 1024 rows (0 to 1023, 1024 to 2047, ...) at most 160 rows name the same one
- w_qkv: bfloat16 [1024, 3, 1024], P('dp', None, 'tensor'), may hold values from -0.21875 to 0.21875
- w_attn_out: bfloat16 [1024, 1024], P('tensor', 'dp'), may hold values from -1 to 1
- bias_table: bfloat16 [32, 16], P('dp', 'tensor'), may hold values from -4 to 4
- gain_attn: bfloat16 [1024], P('dp'), may hold values from 0.5 to 1.5
- gain_moe: bfloat16 [1024], P('dp'), may hold values from 0.5 to 1.5
- router: bfloat16 [1024, 16], P('dp'), may hold values from -0.125 to 0.125
- w_in: bfloat16 [16, 2, 2816, 1024], P('dp', None, 'tensor'), may hold values from -0.1875 to 0.1875
- w_out: bfloat16 [16, 2816, 1024], P('dp', 'tensor'), may hold values from -0.1875 to 0.1875
- cotangent: bfloat16 [8192, 1024], P(('dp', 'tensor')), may hold values from -6 to 6
Outputs:
- layer_out: bfloat16 [8192, 1024], P(('dp', 'tensor'))
- grad_tokens: bfloat16 [8192, 1024], P(('dp', 'tensor'))
- grad_w_qkv: float32 [1024, 3, 1024], P('dp', None, 'tensor')
- grad_w_attn_out: float32 [1024, 1024], P('tensor', 'dp')
- grad_bias_table: float32 [32, 16], P('dp', 'tensor')
- grad_gain_attn: float32 [1024], P('dp')
- grad_gain_moe: float32 [1024], P('dp')
- grad_router: float32 [1024, 16], P('dp')
- grad_w_in: float32 [16, 2, 2816, 1024], P('dp', None, 'tensor')
- grad_w_out: float32 [16, 2816, 1024], P('dp', 'tensor')
Inputs may be any that keep to these rules, and one draw needn't show every extreme that they name: `routes`: the two experts of a token differ. Among the tokens of one sequence (aligned blocks of 1024 rows) no expert is named more than 160 times, a bound that some block reaches in some sequence of every draw. `segments`: document numbers never fall along a sequence; each document has 1 to 512 tokens, and one has exactly 512.
All inputs are finite; a program needn't handle non-finite values.
Results may differ from a plain program's by a relative error of at most 0.025.
Values may be sent and summed in bfloat16 or wider, within the bound.
A program may use at most 320 MiB of HBM per device.

v0:
```python
import math

import jax
import jax.numpy as jnp
import numpy as np
from jax import lax
from jax.sharding import PartitionSpec as P

HD = 64
TOP = 2
NB = 32
NEAR = 128


EPS = 1e-06
NEG = -1e30


def distance_buckets():
    half_buckets = NB // 2
    thresholds = [bucket_level for bucket_level in range(1, half_buckets)]
    thresholds = thresholds + [
        int(
            math.ceil(
                half_buckets
                * (NEAR / half_buckets) ** ((bucket_level - half_buckets) / half_buckets)
            )
        )
        for bucket_level in range(half_buckets, NB)
    ]
    distance = np.arange(NEAR + 1)
    return (distance[:, None] >= np.array(thresholds)[None, :]).sum(axis=1)


def rms_scale(values):
    return lax.rsqrt(jnp.mean(values * values, axis=-1, keepdims=True) + EPS)


def norm_backward(grad_normed, values, scale_inv, gain):
    normed_unit = values * scale_inv
    grad_unit = grad_normed * gain
    grad_values = scale_inv * (
        grad_unit - normed_unit * jnp.mean(grad_unit * normed_unit, axis=-1, keepdims=True)
    )
    return (grad_values, jnp.sum(grad_normed * normed_unit, axis=0))


def gelu_tanh(values):
    return jax.nn.gelu(values, approximate=True)


def route_slots(route_ids, experts, capacity):
    flat_routes = route_ids.reshape(-1)
    onehot = (flat_routes[:, None] == jnp.arange(experts, dtype=jnp.int32)[None, :]).astype(
        jnp.int32
    )
    ranks = jnp.cumsum(onehot, axis=0) - 1
    rank_own = jnp.sum(ranks * onehot, axis=1)
    return (flat_routes * capacity + rank_own).reshape(-1, TOP)


def bias_block(offsets, far_value, block_start, row_count, seq_len):
    heads_local = offsets.shape[0]
    window = row_count + NEAR
    pattern = (
        jnp.zeros((heads_local, window + 1), jnp.float32).at[:, : NEAR + 1].set(offsets[:, ::-1])
    )
    tiled = jnp.tile(pattern, (1, row_count))[:, : row_count * window].reshape(
        heads_local, row_count, window
    )
    canvas = jnp.zeros((heads_local, row_count, seq_len + NEAR), jnp.float32)
    zero_index = jnp.zeros((), jnp.int32)
    canvas = lax.dynamic_update_slice(canvas, tiled, (zero_index, zero_index, block_start))
    return canvas[:, :, NEAR:] + far_value[:, None, None]


def diagonal_sums(grad_scores, block_start):
    heads_local, row_count, _ = grad_scores.shape
    window = row_count + NEAR
    padded = jnp.pad(grad_scores, ((0, 0), (0, 0), (NEAR, 0)))
    sliced = lax.dynamic_slice_in_dim(padded, block_start, window, 2)
    flattened = jnp.pad(sliced.reshape(heads_local, row_count * window), ((0, 0), (0, row_count)))
    skewed = flattened.reshape(heads_local, row_count, window + 1)
    return jnp.sum(skewed[:, :, : NEAR + 1], axis=1)[:, ::-1]


def block_scores(query_block, keys_all, offsets, far_value, segment_row, block_start, scale):
    block_rows = query_block.shape[1]
    seq_len = keys_all.shape[1]
    raw_scores = (
        jnp.einsum("hqd,hkd->hqk", query_block, keys_all, preferred_element_type=jnp.float32)
        * scale
    )
    raw_scores = raw_scores + bias_block(offsets, far_value, block_start, block_rows, seq_len)
    row_index = block_start + jnp.arange(block_rows, dtype=jnp.int32)
    key_index = jnp.arange(seq_len, dtype=jnp.int32)
    row_segments = lax.dynamic_slice_in_dim(segment_row, block_start, block_rows, 0)
    allowed = (row_index[:, None] >= key_index[None, :]) & (
        row_segments[:, None] == segment_row[None, :]
    )
    return (jnp.where(allowed[None], raw_scores, NEG), allowed)


def on_device(
    tokens,
    segments,
    routes,
    w_qkv,
    w_attn_out,
    bias_table,
    gain_attn,
    gain_moe,
    router,
    w_in,
    w_out,
    cotangent,
):
    own_rows, model_width = tokens.shape
    seq_len = own_rows * lax.axis_size("tensor")
    own_start = lax.axis_index("tensor") * own_rows
    head_cols = w_qkv.shape[2]
    heads_local = head_cols // HD
    experts = router.shape[1]
    capacity = 5 * seq_len * TOP // (4 * experts)
    block_rows = min(512, seq_len)
    block_count = seq_len // block_rows
    scale = HD ** (-0.5)
    highest = lax.Precision.HIGHEST
    segment_row = segments[0]
    qkv_full, attn_out_full, table_full, gain_one, gain_two, router_full = (
        lax.all_gather(w_qkv, "dp", axis=0, tiled=True),
        lax.all_gather(w_attn_out, "dp", axis=1, tiled=True),
        lax.all_gather(bias_table, "dp", axis=0, tiled=True),
        lax.all_gather(gain_attn, "dp", axis=0, tiled=True),
        lax.all_gather(gain_moe, "dp", axis=0, tiled=True),
        lax.all_gather(router, "dp", axis=0, tiled=True),
    )
    w_in_full, w_out_full = (
        lax.all_gather(w_in, "dp", axis=0, tiled=True),
        lax.all_gather(w_out, "dp", axis=0, tiled=True),
    )
    in_local, out_local = (w_in_full, w_out_full)
    tokens_float = tokens.astype(jnp.float32)
    gain_one_float = gain_one.astype(jnp.float32)
    scale_one = rms_scale(tokens_float)
    hidden_one = (tokens_float * scale_one * gain_one_float).astype(jnp.bfloat16)
    gathered_one = lax.all_gather(hidden_one, "tensor", axis=0, tiled=True)
    qkv_matrix = qkv_full.reshape(model_width, 3 * head_cols)
    projected = jnp.dot(gathered_one, qkv_matrix, preferred_element_type=jnp.float32).astype(
        jnp.bfloat16
    )
    split_heads = jnp.transpose(projected.reshape(seq_len, 3, heads_local, HD), (1, 2, 0, 3))
    queries, keys_all, values_all = (split_heads[0], split_heads[1], split_heads[2])
    table_float = table_full.astype(jnp.float32)
    selector = jnp.asarray(distance_buckets()[:, None] == np.arange(NB)[None, :], jnp.float32)
    far_value = table_float[NB - 1]
    offsets = jnp.transpose(jnp.dot(selector, table_float, precision=highest) - far_value[None, :])

    def forward_block(block_index):
        block_start = block_index * block_rows
        query_block = lax.dynamic_slice_in_dim(queries, block_start, block_rows, 1)
        scores, allowed = block_scores(
            query_block, keys_all, offsets, far_value, segment_row, block_start, scale
        )
        top_score = jnp.max(scores, axis=-1, keepdims=True)
        log_total = top_score + jnp.log(
            jnp.sum(jnp.exp(scores - top_score), axis=-1, keepdims=True)
        )
        probs_low = jnp.exp(scores - log_total).astype(jnp.bfloat16)
        attended_block = jnp.einsum(
            "hqk,hkd->hqd", probs_low, values_all, preferred_element_type=jnp.float32
        )
        return (attended_block, log_total[..., 0])

    attended_blocks, total_blocks = lax.map(forward_block, jnp.arange(block_count, dtype=jnp.int32))
    attended_low = (
        jnp.transpose(attended_blocks, (0, 2, 1, 3))
        .reshape(seq_len, head_cols)
        .astype(jnp.bfloat16)
    )
    log_totals = jnp.transpose(total_blocks, (1, 0, 2)).reshape(heads_local, seq_len)
    picked = attended_low
    branch = lax.psum_scatter(
        jnp.dot(picked, attn_out_full, preferred_element_type=jnp.float32),
        "tensor",
        scatter_dimension=0,
        tiled=True,
    )
    residual = tokens_float + branch
    gain_two_float = gain_two.astype(jnp.float32)
    scale_two = rms_scale(residual)
    hidden_two = (residual * scale_two * gain_two_float).astype(jnp.bfloat16)
    gathered_two = lax.all_gather(hidden_two, "tensor", axis=0, tiled=True)
    expert_ids = jnp.arange(experts, dtype=jnp.int32)

    def gate_values(logit_values, route_rows):
        expert_probs = jax.nn.softmax(logit_values, axis=-1)
        picked = jnp.sum(
            jnp.where(
                route_rows[:, :, None] == expert_ids[None, None, :], expert_probs[:, None, :], 0.0
            ),
            axis=-1,
        )
        return picked / jnp.sum(picked, axis=1, keepdims=True)

    gates = gate_values(
        jnp.dot(gathered_two, router_full, preferred_element_type=jnp.float32), routes
    )
    slot_ids = route_slots(routes, experts, capacity)
    slot_flat = slot_ids.reshape(-1)
    token_ids = jnp.repeat(jnp.arange(seq_len, dtype=jnp.int32), TOP)
    sources = jnp.full((experts * capacity,), seq_len, jnp.int32).at[slot_flat].set(token_ids)
    slot_gates = jnp.zeros((experts * capacity,), jnp.float32).at[slot_flat].set(gates.reshape(-1))
    local_sources = sources.reshape(experts, capacity).reshape(-1)
    local_gates = slot_gates.reshape(experts, capacity).reshape(-1)
    inside = (slot_ids >= 0) & (slot_ids < experts * capacity)
    safe_slots = jnp.clip(slot_ids, 0, experts * capacity - 1)
    inside_float = inside.astype(jnp.float32)
    gates_on = gates * inside_float
    padded_two = jnp.concatenate([gathered_two, jnp.zeros((1, model_width), jnp.bfloat16)], axis=0)
    dispatched = padded_two[local_sources].reshape(experts, capacity, model_width)
    gate_up = jnp.einsum("ecd,egfd->ecgf", dispatched, in_local, preferred_element_type=jnp.float32)
    gate_part = gate_up[:, :, 0]
    up_part = gate_up[:, :, 1]
    gelu_value, gelu_pull = jax.vjp(gelu_tanh, gate_part)
    activated = (gelu_value * up_part).astype(jnp.bfloat16)
    expert_out = jnp.einsum(
        "ecf,efd->ecd", activated, out_local, preferred_element_type=jnp.float32
    ).reshape(experts * capacity, model_width)
    mixture = lax.psum_scatter(
        (
            gates_on[:, 0:1] * expert_out[safe_slots[:, 0]]
            + gates_on[:, 1:2] * expert_out[safe_slots[:, 1]]
        ).astype(jnp.bfloat16),
        "tensor",
        scatter_dimension=0,
        tiled=True,
    ).astype(jnp.float32)
    layer_out = (residual + mixture).astype(jnp.bfloat16)
    grad_gathered = lax.all_gather(cotangent, "tensor", axis=0, tiled=True)
    padded_grad = jnp.concatenate(
        [grad_gathered, jnp.zeros((1, model_width), jnp.bfloat16)], axis=0
    )
    grad_expert = (
        (local_gates[:, None] * padded_grad[local_sources])
        .astype(jnp.bfloat16)
        .reshape(experts, capacity, model_width)
    )
    grad_float = grad_gathered.astype(jnp.float32)
    grad_gate_part = (
        jnp.stack(
            [
                jnp.sum(grad_float * expert_out[safe_slots[:, 0]], axis=1),
                jnp.sum(grad_float * expert_out[safe_slots[:, 1]], axis=1),
            ],
            axis=1,
        )
        * inside_float
    )
    grad_act = jnp.einsum(
        "ecd,efd->ecf", grad_expert, out_local, preferred_element_type=jnp.float32
    )
    grad_w_out = jnp.einsum(
        "ecf,ecd->efd", activated, grad_expert, preferred_element_type=jnp.float32
    )
    grad_gelu_in = gelu_pull(grad_act * up_part)[0]
    grad_gate_up = jnp.stack([grad_gelu_in, grad_act * gelu_value], axis=2).astype(jnp.bfloat16)
    grad_dispatched = jnp.einsum(
        "ecgf,egfd->ecd", grad_gate_up, in_local, preferred_element_type=jnp.float32
    ).reshape(experts * capacity, model_width)
    grad_w_in = jnp.einsum(
        "ecd,ecgf->egfd", dispatched, grad_gate_up, preferred_element_type=jnp.float32
    )
    grad_hidden_part = (
        inside_float[:, 0:1] * grad_dispatched[safe_slots[:, 0]]
        + inside_float[:, 1:2] * grad_dispatched[safe_slots[:, 1]]
    )
    grad_own, grad_gate_own = (
        lax.psum_scatter(grad_hidden_part, "tensor", scatter_dimension=0, tiled=True),
        lax.psum_scatter(grad_gate_part, "tensor", scatter_dimension=0, tiled=True),
    )
    own_routes = lax.dynamic_slice_in_dim(routes, own_start, own_rows, 0)
    own_logits = jnp.dot(hidden_two, router_full, preferred_element_type=jnp.float32)

    def own_gates(logit_values):
        return gate_values(logit_values, own_routes)

    _, gate_pull = jax.vjp(own_gates, own_logits)
    grad_logits = gate_pull(grad_gate_own)[0]
    router_float = router_full.astype(jnp.float32)
    grad_hidden_two = grad_own + jnp.dot(grad_logits, router_float.T, precision=highest)
    grad_router_part = jnp.dot(hidden_two.astype(jnp.float32).T, grad_logits, precision=highest)
    grad_from_norm, grad_gain_two = norm_backward(
        grad_hidden_two, residual, scale_two, gain_two_float
    )
    grad_residual = cotangent.astype(jnp.float32) + grad_from_norm
    grad_branch_all = lax.all_gather(
        grad_residual.astype(jnp.bfloat16), "tensor", axis=0, tiled=True
    )
    grad_attended = lax.dot_general(
        grad_branch_all, attn_out_full, (((1,), (1,)), ((), ())), preferred_element_type=jnp.float32
    ).astype(jnp.bfloat16)
    grad_w_attn_out = lax.dot_general(
        attended_low, grad_branch_all, (((0,), (0,)), ((), ())), preferred_element_type=jnp.float32
    )
    grad_heads = jnp.transpose(grad_attended.reshape(seq_len, heads_local, HD), (1, 0, 2))

    def backward_block(carry, block_index):
        grad_keys, grad_values, grad_table = carry
        block_start = block_index * block_rows
        query_block = lax.dynamic_slice_in_dim(queries, block_start, block_rows, 1)
        scores, allowed = block_scores(
            query_block, keys_all, offsets, far_value, segment_row, block_start, scale
        )
        total_block = lax.dynamic_slice_in_dim(log_totals, block_start, block_rows, 1)
        probs_full = jnp.exp(scores - total_block[:, :, None])
        probs_low = probs_full.astype(jnp.bfloat16)
        grad_block = lax.dynamic_slice_in_dim(grad_heads, block_start, block_rows, 1)
        grad_probs = jnp.einsum(
            "hqd,hkd->hqk", grad_block, values_all, preferred_element_type=jnp.float32
        )
        delta = jnp.sum(grad_probs * probs_full, axis=-1, keepdims=True)
        grad_low = jnp.where(allowed[None], probs_full * (grad_probs - delta), 0.0).astype(
            jnp.bfloat16
        )
        grad_query = (
            jnp.einsum("hqk,hkd->hqd", grad_low, keys_all, preferred_element_type=jnp.float32)
            * scale
        )
        grad_keys = (
            grad_keys
            + jnp.einsum("hqk,hqd->hkd", grad_low, query_block, preferred_element_type=jnp.float32)
            * scale
        )
        grad_values = grad_values + jnp.einsum(
            "hqk,hqd->hkd", probs_low, grad_block, preferred_element_type=jnp.float32
        )
        grad_rounded = grad_low.astype(jnp.float32)
        diagonal = diagonal_sums(grad_rounded, block_start)
        near_part = jnp.dot(diagonal, selector, precision=highest)
        far_part = jnp.sum(grad_rounded, axis=(1, 2)) - jnp.sum(diagonal, axis=1)
        near_part = near_part.at[:, NB - 1].add(far_part)
        return ((grad_keys, grad_values, grad_table + near_part.T), grad_query)

    zero_heads = jnp.zeros((heads_local, seq_len, HD), jnp.float32)
    init_carry = (zero_heads, zero_heads, jnp.zeros((NB, heads_local), jnp.float32))
    final_carry, query_blocks = lax.scan(
        backward_block, init_carry, jnp.arange(block_count, dtype=jnp.int32)
    )
    grad_keys, grad_values, grad_table = final_carry
    grad_queries = jnp.transpose(query_blocks, (1, 0, 2, 3)).reshape(heads_local, seq_len, HD)
    grad_projected = (
        jnp.transpose(jnp.stack([grad_queries, grad_keys, grad_values]), (2, 0, 1, 3))
        .reshape(seq_len, 3 * head_cols)
        .astype(jnp.bfloat16)
    )
    grad_w_qkv = lax.dot_general(
        gathered_one, grad_projected, (((0,), (0,)), ((), ())), preferred_element_type=jnp.float32
    ).reshape(model_width, 3, head_cols)
    picked = grad_projected
    grad_hidden_one = lax.psum_scatter(
        lax.dot_general(
            picked, qkv_matrix, (((1,), (1,)), ((), ())), preferred_element_type=jnp.float32
        ),
        "tensor",
        scatter_dimension=0,
        tiled=True,
    )
    grad_from_first, grad_gain_one = norm_backward(
        grad_hidden_one, tokens_float, scale_one, gain_one_float
    )
    grad_tokens = (grad_residual + grad_from_first).astype(jnp.bfloat16)
    gain_sum_one, gain_sum_two, router_sum = lax.psum(
        (grad_gain_one, grad_gain_two, grad_router_part), "tensor"
    )
    (
        reduced_qkv,
        reduced_attn_out,
        reduced_table,
        reduced_gain_one,
        reduced_gain_two,
        reduced_router,
        reduced_w_in,
        reduced_w_out,
    ) = (
        lax.psum_scatter(grad_w_qkv, "dp", scatter_dimension=0, tiled=True),
        lax.psum_scatter(grad_w_attn_out, "dp", scatter_dimension=1, tiled=True),
        lax.psum_scatter(grad_table, "dp", scatter_dimension=0, tiled=True),
        lax.psum_scatter(gain_sum_one, "dp", scatter_dimension=0, tiled=True),
        lax.psum_scatter(gain_sum_two, "dp", scatter_dimension=0, tiled=True),
        lax.psum_scatter(router_sum, "dp", scatter_dimension=0, tiled=True),
        lax.psum_scatter(grad_w_in, "dp", scatter_dimension=0, tiled=True),
        lax.psum_scatter(grad_w_out, "dp", scatter_dimension=0, tiled=True),
    )
    return (
        layer_out,
        grad_tokens,
        reduced_qkv,
        reduced_attn_out,
        reduced_table,
        reduced_gain_one,
        reduced_gain_two,
        reduced_router,
        reduced_w_in,
        reduced_w_out,
    )


def solution(mesh):
    return jax.shard_map(
        on_device,
        mesh=mesh,
        in_specs=(
            P(("dp", "tensor"), None),
            P("dp", None),
            P("dp", None),
            P("dp", None, "tensor"),
            P("tensor", "dp"),
            P("dp", "tensor"),
            P("dp"),
            P("dp"),
            P("dp", None),
            P("dp", None, "tensor", None),
            P("dp", "tensor", None),
            P(("dp", "tensor"), None),
        ),
        out_specs=(
            P(("dp", "tensor"), None),
            P(("dp", "tensor"), None),
            P("dp", None, "tensor"),
            P("tensor", "dp"),
            P("dp", "tensor"),
            P("dp"),
            P("dp"),
            P("dp", None),
            P("dp", None, "tensor", None),
            P("dp", "tensor", None),
        ),
        check_vma=False,
    )
```

profile of v0, /device:TPU:0, one launch (start us, length us, event | category | flops | bytes accessed | tf_op | source)
XLA Modules:
  0.0 2134.9 jit_solution(6209545852603585853)
XLA Ops:
  9.0 10.3 all-gather
  23.3 8.8 all-gather.1
  32.4 10.1 all_gather.40
  43.6 44.3 %all-gather.11.cloned.1.call-done = bf16[1024,1024]{1,0:T(8,128)(2,1)} async-done(((bf16[256,1024]{1,0:T(8,128)(2,1)}), bf16[1024,1024]{1,0:T(8,128)(2,1)}) %all-gather.11.cloned.1.call-update) | async-done | bytes 2097168 | tf_op jit(solution)/shard_map/all_gather | solution.py:147
  87.9 3.9 convolution_convert_fusion
  92.0 54.3 %while.39 = (s32[]{:T(128)}, bf16[2,4,512,64]{2,3,1,0:T(8,128)(2,1)S(1)}, f32[2,4,512]{2,1,0:T(4,128)S(1)}, s32[2]{0:T(128)S(1)}, s32[1024]{0:T(1024)S(1)}, /*in...) while((s32[]{:T(128)}, ...), condition=%wide.region_5.6_spmd, body=%wide.region_1.5_spmd.sunk | while | flops 557317120 | bytes 87958400 | solution.py:175
  95.9 3.2 tile.48
  99.0 10.9 tile.49
  122.7 3.2 tile.48
  125.8 10.9 tile.49
  151.3 8.7 all-gather.2
  160.0 66.3 %reduce-scatter.13.cloned.1.call-done = f32[256,1024]{1,0:T(8,128)} async-done(((f32[1024,1024]{1,0:T(8,128)}), f32[256,1024]{1,0:T(8,128)}) %reduce-scatter.13.cloned.1.call-update) | async-done | bytes 1048592 | tf_op jit(solution)/shard_map/reduce_scatter | solution.py:183
  231.9 4.5 reduce-window.6
  238.8 8.1 scatter_custom_fusion
  246.8 8.8 all_gather.43
  255.7 18.3 all-gather.21.cloned.1.call-done
  275.8 8.8 gather_fusion.3
  284.6 35.7 %all-gather.15.cloned.1.call-done = bf16[1024,1024]{1,0:T(8,128)(2,1)} async-done(((bf16[256,1024]{1,0:T(8,128)(2,1)}), bf16[1024,1024]{1,0:T(8,128)(2,1)}) %all-gather.15.cloned.1.call-update) | async-done | bytes 2097168 | tf_op jit(solution)/shard_map/all_gather | solution.py:193
  322.1 8.9 gather_fusion
  334.0 201.7 %all-gather.17.cloned.1.call-done = bf16[16,2,704,1024]{3,2,1,0:T(8,128)(2,1)} async-done(((bf16[2,2,704,1024]{3,2,1,0:T(8,128)(2,1)}), bf16[16,2,704,1024]{3,2,1,0:T(8,128)(2,1)}) %all-gather.17.cloned.1.call-update) | async-done | bytes 46137360 | tf_op jit(solution)/shard_map/all_gather | solution.py:139
  535.7 27.1 %fusion.109 = f32[16,160,2,704]{3,1,2,0:T(8,128)} fusion(bf16[16,160,1024,1]{2,1,3,0:T(8,128)(2,1)} %bitcast.255, bf16[16,2,704,1024]{3,2,1,0:T(8,128)(2,1)} %all-gather.17.cloned.1.call-done), kind=kOutput, calls=%fused_computation.197 | convolution fusion | flops 7381975040 | bytes 65798144 | tf_op jit(solution)/shard_map/ecd,egfd->ecgf/dot_general | solution.py:222
  562.8 8.2 multiply_convert_fusion.1
  570.9 83.3 %all-gather.19.cloned.1.call-done = bf16[16,704,1024]{2,1,0:T(8,128)(2,1)} async-done(((bf16[2,704,1024]{2,1,0:T(8,128)(2,1)}), bf16[16,704,1024]{2,1,0:T(8,128)(2,1)}) %all-gather.19.cloned.1.call-update) | async-done | bytes 23068688 | tf_op jit(solution)/shard_map/all_gather | solution.py:140
  654.2 17.1 fusion.110
  671.3 10.4 gather_fusion.2
  681.7 10.8 gather_fusion.1
  692.5 4.5 fusion.62
  698.2 8.1 scatter_custom_fusion.1
  706.3 20.0 fusion.65
  726.3 22.5 %fusion.46 = f32[16,160,1024,1]{2,1,0,3:T(8,128)} fusion(bf16[16,2,704,1024]{3,2,1,0:T(8,128)(2,1)} %all-gather.17.cloned.1.call-done, bf16[16,160,1,704]{3,1,0,2:T(8,128)(2,1)} %get-tuple-element.851, bf16[16,160,1,704]{3,1,0,2:T(8,128)(2,1)S(1)} %get-tuple-element.850), kind=kOutput, calls=%fused_computation.70 | convolution fusion | flops 7385579520 | bytes 63832064 | tf_op jit(solution)/shard_map/ecgf,egfd->ecd/dot_general | solution.py:268
  748.9 10.3 gather_fusion.5
  759.2 10.4 gather_fusion.4
  770.7 6.1 multiply_add_fusion
  777.3 15.1 reduce-scatter.31.cloned.1.call-done
  793.5 76.9 %reduce-scatter.17.cloned.1.call-done = f32[256,1024]{1,0:T(8,128)} async-done(((f32[1024,1024]{1,0:T(8,128)}), f32[256,1024]{1,0:T(8,128)}) %reduce-scatter.17.cloned.1.call-update) | async-done | bytes 1048592 | tf_op jit(solution)/shard_map/reduce_scatter | solution.py:279
  876.1 45.9 %all-gather.23.cloned.1.call-done = bf16[1024,1024]{1,0:T(8,128)(2,1)} async-done(((bf16[256,1024]{1,0:T(8,128)(2,1)}), bf16[1024,1024]{1,0:T(8,128)(2,1)}) %all-gather.23.cloned.1.call-update) | async-done | bytes 2097168 | tf_op jit(solution)/shard_map/all_gather | solution.py:297
  922.0 3.2 convolution_convert_fusion.1
  926.1 170.6 %while.40 = (s32[]{:T(128)}, f32[4,1024,64]{1,2,0:T(8,128)S(1)}, f32[4,1024,64]{1,2,0:T(8,128)}, f32[32,4]{0,1:T(4,128)S(1)}, bf16[2,4,512,64]{2,3,1,0:T(8,128)(...) while((s32[]{:T(128)}, f32[4,1024,64]{1,2,0:T(8,128)S(1)}, ...), condition=%wide.region_37.38_spmd.clone.clone, body=%wide.region_31.37_spmd.sunk.clone.clone.sunk | while | flops 1643454208 | bytes 231117264 | solution.py:347
  949.3 3.2 tile.51
  952.4 10.9 tile.52
  969.5 3.4 copy-done.1
  974.8 13.4 fusion.198
  990.8 3.4 copy.157
  1000.6 13.1 reshape.591
  1020.2 3.2 tile.51
  1023.4 10.9 tile.52
  1040.5 3.4 copy-done.1
  1043.9 3.1 fusion.200
  1047.0 13.5 fusion.198
  1063.3 3.4 copy.157
  1073.1 13.1 reshape.591
  1101.3 5.4 fusion.111
  1108.0 5.6 add_convert_fusion
  1115.5 5.6 fusion.66
  1121.1 20.4 fusion.58
  1141.7 36.6 %fusion.56 = f32[16,2,704,1024]{3,2,1,0:T(8,128)} fusion(bf16[16,160,1024,1]{2,1,3,0:T(8,128)(2,1)} %bitcast.256, bf16[16,160,1,704]{3,1,0,2:T(8,128)(2,1)} %get-tuple-element.851, bf16[16,160,1,704]{3,1,0,2:T(8,128)(2,1)} %copy-done.23), kind=kOutput, calls=%fused_computation.86 | convolution fusion | flops 7385579520 | bytes 104726528 | tf_op jit(solution)/shard_map/ecd,ecgf->egfd/dot_general | solution.py:271
  1184.1 24.0 %all-reduce.9 = (f32[32,4]{1,0:T(8,128)S(1)}, f32[1024]{0:T(1024)S(1)}, f32[1024]{0:T(1024)S(1)}) all-reduce(f32[32,4]{1,0:T(8,128)S(1)} %copy.129, f32[1024]{0:T(1024)S(1)} %get-tuple-element.770, f32[1024]{0:T(1024)S(1)} %copy-done.60), channel_id=9, replica_groups=mesh['dp'=8,'tensor'=4] {'dp'}, use_global_device_ids=true, to_apply=%region_42.43.clone | all-reduce | flops 2176 | bytes 17408
  1208.3 9.8 reduce-scatter.29.cloned.1.call-done
  1218.1 12.8 all-reduce.10
  1231.4 32.8 %reduce-scatter.15.cloned.1.call-done = bf16[256,1024]{1,0:T(8,128)(2,1)} async-done(((bf16[1024,1024]{1,0:T(8,128)(2,1)}), bf16[256,1024]{1,0:T(8,128)(2,1)}) %reduce-scatter.15.cloned.1.call-update) | async-done | bytes 524304 | tf_op jit(solution)/shard_map/reduce_scatter | solution.py:230
  1267.1 36.4 %reduce-scatter.23.cloned.1.call-done = f32[256,128]{1,0:T(8,128)} async-done(((f32[256,1024]{1,0:T(8,128)}), f32[256,128]{1,0:T(8,128)}) %reduce-scatter.23.cloned.1.call-update) | async-done | bytes 131088 | tf_op jit(solution)/shard_map/reduce_scatter | solution.py:387
  1303.6 50.4 %reduce-scatter.21.cloned.1.call-done = f32[128,3,256]{2,0,1:T(8,128)} async-done(((f32[1024,3,256]{2,0,1:T(8,128)}), f32[128,3,256]{2,0,1:T(8,128)}) %reduce-scatter.21.cloned.1.call-update) | async-done | bytes 393232 | tf_op jit(solution)/shard_map/reduce_scatter | solution.py:386
  1354.0 268.4 %reduce-scatter.27.cloned.1.call-done = f32[2,704,1024]{2,1,0:T(8,128)} async-done(((f32[16,704,1024]{2,1,0:T(8,128)}), f32[2,704,1024]{2,1,0:T(8,128)}) %reduce-scatter.27.cloned.1.call-update) | async-done | bytes 5767184 | tf_op jit(solution)/shard_map/reduce_scatter | solution.py:393
  1622.4 505.7 %reduce-scatter.25.cloned.1.call-done = f32[2,2,704,1024]{3,2,1,0:T(8,128)} async-done(((f32[16,2,704,1024]{3,2,1,0:T(8,128)}), f32[2,2,704,1024]{3,2,1,0:T(8,128)}) %reduce-scatter.25.cloned.1.call-update) | async-done | bytes 11534352 | tf_op jit(solution)/shard_map/reduce_scatter | solution.py:392
  (362 shorter events, 120.7 us)
Async XLA Ops:
  7.2 36.4 %all-gather.13.cloned.1.call-start = ((), (), s32[]{:S(2)}) async-start(), calls=%async_computation.11 | async-start | bytes 1769472 | tf_op jit(solution)/shard_map/all_gather | solution.py:131
  9.0 78.9 %all-gather.11.cloned.1.call-start = ((), (), s32[]{:S(2)}) async-start(), calls=%async_computation.10 | async-start | bytes 2621440 | tf_op jit(solution)/shard_map/all_gather | solution.py:147
  23.2 203.0 %reduce-scatter.13.cloned.1.call-start = ((), (), s32[]{:S(2)}) async-start(), calls=%async_computation.12 | async-start | bytes 5242880 | tf_op jit(solution)/shard_map/reduce_scatter | solution.py:183
  42.5 104.4 %copy-start.26 = (bf16[256,1024]{1,0:T(8,128)(2,1)}, bf16[256,1024]{1,0:T(8,128)(2,1)S(1)}, u32[]{:S(2)}) copy-start(bf16[256,1024]{1,0:T(8,128)(2,1)S(1)} %all_gather.40) | copy-start | bytes 1572868
  146.2 4.3 copy-start.2
  147.8 78.5 %copy-start.12 = (bf16[256,1024]{1,0:T(8,128)(2,1)S(1)}, bf16[256,1024]{1,0:T(8,128)(2,1)}, u32[]{:S(2)}) copy-start(bf16[256,1024]{1,0:T(8,128)(2,1)} %param.23) | copy-start | bytes 1572868
  150.6 123.4 %all-gather.21.cloned.1.call-start = ((), (), s32[]{:S(2)}) async-start(), calls=%async_computation.17 | async-start | bytes 2621440 | tf_op jit(solution)/shard_map/all_gather | solution.py:240
  151.2 169.1 %all-gather.15.cloned.1.call-start = ((), (), s32[]{:S(2)}) async-start(), calls=%async_computation.13 | async-start | bytes 2621440 | tf_op jit(solution)/shard_map/all_gather | solution.py:193
  160.0 70.3 %copy-start.41 = (f32[8,1,128]{2,1,0:T(1,128)}, f32[8,1,128]{2,1,0:T(1,128)S(1)}, u32[]{:S(2)}) copy-start(f32[8,1,128]{2,1,0:T(1,128)S(1)} %convert_element_type.158) | copy-start | bytes 12292
  229.7 306.0 %all-gather.17.cloned.1.call-start = ((), (), s32[]{:S(2)}) async-start(), calls=%async_computation.14 | async-start | bytes 51904512 | tf_op jit(solution)/shard_map/all_gather | solution.py:139
  230.3 16.6 copy-start.65
  230.3 424.0 %all-gather.19.cloned.1.call-start = ((), (), s32[]{:S(2)}) async-start(), calls=%async_computation.15 | async-start | bytes 25952256 | tf_op jit(solution)/shard_map/all_gather | solution.py:140
  231.0 561.3 %reduce-scatter.31.cloned.1.call-start = ((), (), s32[]{:S(2)}) async-start(), calls=%async_computation.26 | async-start | bytes 655360
  681.7 10.8 copy-start.18
  706.3 20.0 copy-start.36
  726.3 22.6 %copy-start.23 = (bf16[16,160,1,704]{3,1,0,2:T(8,128)(2,1)}, bf16[16,160,1,704]{3,1,0,2:T(8,128)(2,1)S(1)}, u32[]{:S(2)}) copy-start(bf16[16,160,1,704]{3,1,0,2:T(8,128)(2,1)S(1)} %get-tuple-element.850) | copy-start | bytes 10813444
  770.6 99.8 %reduce-scatter.17.cloned.1.call-start = ((), (), s32[]{:S(2)}) async-start(), calls=%async_computation.18 | async-start | bytes 5242880 | tf_op jit(solution)/shard_map/reduce_scatter | solution.py:279
  770.7 6.2 copy-start.16
  770.7 99.7 %copy-start.42 = (f32[8,1,128]{2,1,0:T(1,128)S(1)}, f32[8,1,128]{2,1,0:T(1,128)}, u32[]{:S(2)}) copy-start(f32[8,1,128]{2,1,0:T(1,128)} %copy-done.41) | copy-start | bytes 12292
  770.7 99.7 %copy-start.56 = (f32[256]{0:T(256)S(1)}, f32[256]{0:T(256)}, u32[]{:S(2)}) copy-start(f32[256]{0:T(256)} %copy-done.55) | copy-start | bytes 3076
  776.8 93.7 %copy-start.10 = (f32[256,1024]{1,0:T(8,128)S(1)}, f32[256,1024]{1,0:T(8,128)}, u32[]{:S(2)}) copy-start(f32[256,1024]{1,0:T(8,128)} %copy-done.9) | copy-start | bytes 3145732
  776.8 97.5 %copy-start.21 = (bf16[256,1024]{1,0:T(8,128)(2,1)S(1)}, bf16[256,1024]{1,0:T(8,128)(2,1)}, u32[]{:S(2)}) copy-start(bf16[256,1024]{1,0:T(8,128)(2,1)} %param.34) | copy-start | bytes 1572868
  776.8 145.2 %all-gather.23.cloned.1.call-start = ((), (), s32[]{:S(2)}) async-start(), calls=%async_computation.19 | async-start | bytes 2621440 | tf_op jit(solution)/shard_map/all_gather | solution.py:297
  777.1 93.2 %copy-start.32 = (f32[256,16]{0,1:T(8,128)}, f32[256,16]{0,1:T(8,128)S(1)}, u32[]{:S(2)}) copy-start(f32[256,16]{0,1:T(8,128)S(1)} %get-tuple-element.868) | copy-start | bytes 49156
  777.1 93.2 %copy-start.50 = (f32[256]{0:T(256)}, f32[256]{0:T(256)S(1)}, u32[]{:S(2)}) copy-start(f32[256]{0:T(256)S(1)} %get-tuple-element.867) | copy-start | bytes 3076
  777.2 93.2 %copy-start.53 = (f32[256]{0:T(256)}, f32[256]{0:T(256)S(1)}, u32[]{:S(2)}) copy-start(f32[256]{0:T(256)S(1)} %fusion.87) | copy-start | bytes 3076
  793.4 77.0 %copy-start.38 = (f32[256,16]{0,1:T(8,128)}, f32[256,16]{0,1:T(8,128)S(1)}, u32[]{:S(2)}) copy-start(f32[256,16]{0,1:T(8,128)S(1)} %select_reduce_fusion.4) | copy-start | bytes 49156
  793.5 76.9 %copy-start.63 = (f32[256]{0:T(256)}, f32[256]{0:T(256)S(1)}, u32[]{:S(2)}) copy-start(f32[256]{0:T(256)S(1)} %neg.13) | copy-start | bytes 3076
  873.2 52.8 %copy-start.3 = (bf16[4,1024,64]{1,2,0:T(8,128)(2,1)S(1)}, bf16[4,1024,64]{1,2,0:T(8,128)(2,1)}, u32[]{:S(2)}) copy-start(bf16[4,1024,64]{1,2,0:T(8,128)(2,1)} %copy-done.2) | copy-start | bytes 1572868
  873.2 52.8 %copy-start.5 = (bf16[4,1024,64]{1,2,0:T(8,128)(2,1)S(1)}, bf16[4,1024,64]{1,2,0:T(8,128)(2,1)}, u32[]{:S(2)}) copy-start(bf16[4,1024,64]{1,2,0:T(8,128)(2,1)} %copy-done.4) | copy-start | bytes 1572868
  873.2 52.8 %copy-start.7 = (bf16[4,1024,64]{1,2,0:T(8,128)(2,1)S(1)}, bf16[4,1024,64]{1,2,0:T(8,128)(2,1)}, u32[]{:S(2)}) copy-start(bf16[4,1024,64]{1,2,0:T(8,128)(2,1)} %copy-done.6) | copy-start | bytes 1572868
  873.2 52.8 %copy-start.24 = (f32[129,32]{1,0:T(8,128)S(1)}, f32[129,32]{1,0:T(8,128)}, u32[]{:S(2)}) copy-start(f32[129,32]{1,0:T(8,128)} %constant.321.clone) | copy-start | bytes 49540
  873.2 52.8 %copy-start.31 = (s32[1,1024]{1,0:T(1,128)S(1)}, s32[1,1024]{1,0:T(1,128)}, u32[]{:S(2)}) copy-start(s32[1,1024]{1,0:T(1,128)} %param.24) | copy-start | bytes 12292
  873.2 52.8 %copy-start.35 = (f32[4,129]{1,0:T(4,128)S(1)}, f32[4,129]{1,0:T(4,128)}, u32[]{:S(2)}) copy-start(f32[4,129]{1,0:T(4,128)} %copy-done.34) | copy-start | bytes 6196
  873.2 52.8 %copy-start.45 = (f32[2,4,512]{2,1,0:T(4,128)S(1)}, f32[2,4,512]{2,1,0:T(4,128)}, u32[]{:S(2)}) copy-start(f32[2,4,512]{2,1,0:T(4,128)} %copy-done.44) | copy-start | bytes 49156
  873.3 52.8 %copy-start.49 = (f32[1,4]{1,0:T(1,128)S(1)}, f32[1,4]{1,0:T(1,128)}, u32[]{:S(2)}) copy-start(f32[1,4]{1,0:T(1,128)} %copy-done.48) | copy-start | bytes 52
  875.4 307.0 %reduce-scatter.19.cloned.1.call-start = ((), (), s32[]{:S(2)}) async-start(), calls=%async_computation.20 | async-start | bytes 5242880 | tf_op jit(solution)/shard_map/reduce_scatter | solution.py:361
  966.5 6.4 copy-start.8
  999.6 14.1 copy-start.28
  1037.4 6.4 copy-start.8
  1072.2 14.1 copy-start.28
  1101.3 5.5 copy-start.52
  1101.3 5.5 copy-start.17
  1101.3 5.5 copy-start.33
  1101.3 5.6 copy-start.39
  1101.3 5.6 copy-start.51
  1101.3 5.6 copy-start.54
  1101.3 5.6 copy-start.64
  1106.8 111.3 %reduce-scatter.29.cloned.1.call-start = ((), (), s32[]{:S(2)}) async-start(), calls=%async_computation.25 | async-start | bytes 73728 | tf_op jit(solution)/shard_map/reduce_scatter | solution.py:391
  1107.9 156.4 %reduce-scatter.15.cloned.1.call-start = ((), (), s32[]{:S(2)}) async-start(), calls=%async_computation.16 | async-start | bytes 2621440 | tf_op jit(solution)/shard_map/reduce_scatter | solution.py:230
  1107.9 5.7 copy-start.20
  1107.9 5.7 copy-start.25
  1113.6 189.9 %reduce-scatter.23.cloned.1.call-start = ((), (), s32[]{:S(2)}) async-start(), calls=%async_computation.22 | async-start | bytes 1179648 | tf_op jit(solution)/shard_map/reduce_scatter | solution.py:387
  1115.4 238.6 %reduce-scatter.21.cloned.1.call-start = ((), (), s32[]{:S(2)}) async-start(), calls=%async_computation.21 | async-start | bytes 3538944 | tf_op jit(solution)/shard_map/reduce_scatter | solution.py:386
  1115.5 5.7 copy-start.37
  1121.1 501.3 %reduce-scatter.27.cloned.1.call-start = ((), (), s32[]{:S(2)}) async-start(), calls=%async_computation.24 | async-start | bytes 51904512 | tf_op jit(solution)/shard_map/reduce_scatter | solution.py:393
  1141.6 986.5 %reduce-scatter.25.cloned.1.call-start = ((), (), s32[]{:S(2)}) async-start(), calls=%async_computation.23 | async-start | bytes 103809024 | tf_op jit(solution)/shard_map/reduce_scatter | solution.py:392
  1178.3 5.8 copy-start.60
  1178.3 85.9 %copy-start.11 = (f32[256,1024]{1,0:T(8,128)S(1)}, f32[256,1024]{1,0:T(8,128)}, u32[]{:S(2)}) copy-start(f32[256,1024]{1,0:T(8,128)} %copy-done.9) | copy-start | bytes 3145732
  1178.3 85.9 %copy-start.15 = (f32[256,1024]{1,0:T(8,128)S(1)}, f32[256,1024]{1,0:T(8,128)}, u32[]{:S(2)}) copy-start(f32[256,1024]{1,0:T(8,128)} %copy-done.14) | copy-start | bytes 3145732
  1178.3 85.9 %copy-start.22 = (bf16[256,1024]{1,0:T(8,128)(2,1)S(1)}, bf16[256,1024]{1,0:T(8,128)(2,1)}, u32[]{:S(2)}) copy-start(bf16[256,1024]{1,0:T(8,128)(2,1)} %param.34) | copy-start | bytes 1572868
  1178.3 85.9 %copy-start.43 = (f32[8,1,128]{2,1,0:T(1,128)S(1)}, f32[8,1,128]{2,1,0:T(1,128)}, u32[]{:S(2)}) copy-start(f32[8,1,128]{2,1,0:T(1,128)} %copy-done.41) | copy-start | bytes 12292
  1178.4 85.9 %copy-start.57 = (f32[256]{0:T(256)S(1)}, f32[256]{0:T(256)}, u32[]{:S(2)}) copy-start(f32[256]{0:T(256)} %copy-done.55) | copy-start | bytes 3076
  1178.4 85.9 %copy-start.62 = (f32[256]{0:T(256)S(1)}, f32[256]{0:T(256)}, u32[]{:S(2)}) copy-start(f32[256]{0:T(256)} %copy-done.61) | copy-start | bytes 3076
  (30 other events, 82.9 us)
Sparse Core Ops, SparseCore 0:
  10.5 29.1 all-gather.12
  41.8 46.0 all-gather.10
  150.7 75.4 reduce-scatter.12
  227.8 46.2 all-gather.20
  275.5 44.7 all-gather.14
  322.3 213.3 all-gather.16
  537.7 116.4 all-gather.18
  770.7 21.5 reduce-scatter.30
  795.3 74.9 reduce-scatter.16
  875.5 46.4 all-gather.22
  1106.9 75.4 reduce-scatter.18
  1186.1 31.9 reduce-scatter.28
  1220.3 43.8 reduce-scatter.14
  1268.2 35.3 reduce-scatter.22
  1307.7 46.2 reduce-scatter.20
  1358.0 264.3 reduce-scatter.26
  1626.9 501.1 reduce-scatter.24
where the time goes:
time: 2140 us; the launch traced here: 2130 us
  waiting for transfers between devices  1490 us (70%)
  matrix products  226 us (11%)
  local copies, waits for them, and re-layouts  221 us (10%)
  blocking collectives  83.6 us (4%)
  other arithmetic  62.3 us (3%)
  loops' own time  30.7 us (1%)
    reduce_scatter x1, waiting for transfers between devices, on_device(): lax.psum_scatter(grad_w_in, 'dp', scatter_dimension=0, tiled=True)  506 us
    reduce_scatter x1, waiting for transfers between devices, on_device(): lax.psum_scatter(grad_w_out, 'dp', scatter_dimension=0, tiled=True)  268 us
    all_gather x1, waiting for transfers between devices, on_device(): lax.all_gather(w_in, 'dp', axis=0, tiled=True)  202 us
    all_gather x1, waiting for transfers between devices, on_device(): lax.all_gather(w_out, 'dp', axis=0, tiled=True)  83.3 us
    reduce_scatter x1, waiting for transfers between devices, on_device(): lax.psum_scatter(grad_hidden_part, 'tensor', scatter_dimension=0, tiled=T...  76.9 us
    reduce_scatter x1, waiting for transfers between devices, on_device(): lax.psum_scatter(jnp.dot(picked, attn_out_full, preferred_element_type=jn...  66.3 us
    another operation x8, local copies, waits for them, and re-layouts, bias_block(): jnp.tile(pattern, (1, row_count))[:, :row_count * window]  56.1 us
    reduce_scatter x1, waiting for transfers between devices, on_device(): lax.psum_scatter(grad_w_qkv, 'dp', scatter_dimension=0, tiled=True)  50.4 us
  transfers between devices with their start and end apart: 17, of which 16 were waited for; matrix products, arithmetic and copies ran while one was open for 8% of the time, Pallas kernels for 0%

commit v1 on v0

v1 whole, which is shorter than its diff:
```python
import functools
import math

import jax
import jax.numpy as jnp
import numpy as np
from jax import lax
from jax.experimental import pallas as pl
from jax.experimental.pallas import tpu as pltpu
from jax.sharding import PartitionSpec as P

HD = 64
TOP = 2
NB = 32
NEAR = 128
BS = 256

EPS = 1e-06
NEG = -1e30
F32 = jnp.float32
BF16 = jnp.bfloat16
VMEM_LIMIT = 60 * 1024 * 1024


def distance_buckets():
    half_buckets = NB // 2
    thresholds = [bucket_level for bucket_level in range(1, half_buckets)]
    thresholds = thresholds + [
        int(
            math.ceil(
                half_buckets
                * (NEAR / half_buckets) ** ((bucket_level - half_buckets) / half_buckets)
            )
        )
        for bucket_level in range(half_buckets, NB)
    ]
    distance = np.arange(NEAR + 1)
    return (distance[:, None] >= np.array(thresholds)[None, :]).sum(axis=1)


def distance_selectors():
    buckets = distance_buckets()
    lanes = np.arange(2 * BS)
    signed = np.where(lanes < BS, lanes, lanes - 2 * BS)
    out = []
    for base in (0, BS):
        distance = np.clip(base - signed, 0, NEAR)
        out.append(buckets[distance][:, None] == np.arange(NB)[None, :])
    return np.concatenate(out, axis=0).astype(np.float32)


def skew_selectors():
    buckets = distance_buckets()
    lanes = np.arange(2 * BS)
    out = []
    for base in (0, BS):
        distance = np.clip(base + BS - 1 - lanes, 0, NEAR)
        out.append(buckets[distance][:, None] == np.arange(NB)[None, :])
    return np.concatenate(out, axis=0).astype(np.float32)


def nt(a, b):
    return lax.dot_general(a, b, (((1,), (1,)), ((), ())), preferred_element_type=F32)


def tn(a, b):
    return lax.dot_general(a, b, (((0,), (0,)), ((), ())), preferred_element_type=F32)


def nn(a, b):
    return lax.dot_general(a, b, (((1,), (0,)), ((), ())), preferred_element_type=F32)


def toeplitz(row):
    return pltpu.roll(jnp.broadcast_to(row, (BS, 2 * BS)), 0, 1, stride=1, stride_axis=0)[:, :BS]


def head_lanes(heads, width):
    lane = lax.broadcasted_iota(jnp.int32, (1, width), 1)
    return [(lane >= h * HD) & (lane < (h + 1) * HD) for h in range(heads)]


def own_head(value, lanes, heads):
    return value if heads == 1 else jnp.where(lanes, value, jnp.zeros((), value.dtype))


def build_bias(heads, pattern_ref, bias):
    for h in range(heads):
        for t in range(2):
            bias[h, t] = toeplitz(pattern_ref[2 * h + t : 2 * h + t + 1, :])


def block_mask(qb, kb, seg_col_ref, seg_row_ref):
    q_seg = seg_col_ref[pl.ds(pl.multiple_of(qb * BS, BS), BS), :]
    k_seg = seg_row_ref[:, pl.ds(pl.multiple_of(kb * BS, BS), BS)]
    row = lax.broadcasted_iota(jnp.int32, (BS, BS), 0) + (qb - kb) * BS
    col = lax.broadcasted_iota(jnp.int32, (BS, BS), 1)
    return (q_seg == k_seg) & (row >= col)


def attn_fwd_kernel(heads, blocks, lo_ref, qkv_ref, seg_col_ref, seg_row_ref, pattern_ref, far_ref, out_ref, lse_ref, bias):
    width = heads * HD
    lanes = head_lanes(heads, width)
    scale = HD**-0.5
    build_bias(heads, pattern_ref, bias)

    def q_step(qb, _):
        q_rows = pl.ds(pl.multiple_of(qb * BS, BS), BS)
        q_all = (qkv_ref[q_rows, 0:width] * scale).astype(BF16)
        q_heads = [own_head(q_all, lanes[h], heads) for h in range(heads)]

        def k_step(kb, carry):
            k_rows = pl.ds(pl.multiple_of(kb * BS, BS), BS)
            k = qkv_ref[k_rows, width : 2 * width]
            v = qkv_ref[k_rows, 2 * width : 3 * width]
            allowed = block_mask(qb, kb, seg_col_ref, seg_row_ref)
            near = jnp.minimum(qb - kb, 1)
            is_far = qb - kb >= 2
            new = []
            for h in range(heads):
                top, total, acc = carry[3 * h : 3 * h + 3]
                b = jnp.where(is_far, far_ref[h], bias[h, near])
                s = jnp.where(allowed, nt(q_heads[h], k) + b, NEG)
                top_new = jnp.maximum(top, jnp.max(s, axis=1, keepdims=True))
                alpha = jnp.exp(top - top_new)
                p = jnp.exp(s - top_new)
                total = alpha * total + jnp.sum(p, axis=1, keepdims=True)
                acc = alpha * acc + nn(p.astype(BF16), v)
                new += [top_new, total, acc]
            return tuple(new)

        init = []
        for h in range(heads):
            init += [jnp.full((BS, 1), NEG, F32), jnp.zeros((BS, 1), F32), jnp.zeros((BS, width), F32)]
        res = lax.fori_loop(lo_ref[qb], qb + 1, k_step, tuple(init))
        out = jnp.zeros((BS, width), F32)
        for h in range(heads):
            top, total, acc = res[3 * h : 3 * h + 3]
            value = acc / total
            out = value if heads == 1 else jnp.where(lanes[h], value, out)
            lse_ref[q_rows, h : h + 1] = top + jnp.log(total)
        out_ref[q_rows, :] = out.astype(BF16)
        return 0

    lax.fori_loop(0, blocks, q_step, 0)


def attn_bwd_kernel(
    heads,
    blocks,
    lo_ref,
    qkv_ref,
    out_ref,
    grad_ref,
    lse_ref,
    seg_col_ref,
    seg_row_ref,
    pattern_ref,
    far_ref,
    grad_qkv_ref,
    diag_ref,
    bias,
    dk,
    dv,
    sums,
):
    width = heads * HD
    lanes = head_lanes(heads, width)
    scale = HD**-0.5
    build_bias(heads, pattern_ref, bias)
    dk[...] = jnp.zeros_like(dk)
    dv[...] = jnp.zeros_like(dv)
    sums[...] = jnp.zeros_like(sums)

    def q_step(qb, _):
        q_rows = pl.ds(pl.multiple_of(qb * BS, BS), BS)
        q_all = (qkv_ref[q_rows, 0:width] * scale).astype(BF16)
        g_all = grad_ref[q_rows, :]
        both = g_all.astype(F32) * out_ref[q_rows, :].astype(F32)
        q_heads = [own_head(q_all, lanes[h], heads) for h in range(heads)]
        g_heads = [own_head(g_all, lanes[h], heads) for h in range(heads)]
        deltas = [jnp.sum(own_head(both, lanes[h], heads), axis=1, keepdims=True) for h in range(heads)]
        totals = [lse_ref[q_rows, h : h + 1] for h in range(heads)]

        def k_step(kb, dq):
            k_rows = pl.ds(pl.multiple_of(kb * BS, BS), BS)
            k = qkv_ref[k_rows, width : 2 * width]
            v = qkv_ref[k_rows, 2 * width : 3 * width]
            allowed = block_mask(qb, kb, seg_col_ref, seg_row_ref)
            near = jnp.minimum(qb - kb, 1)
            place = jnp.minimum(qb - kb, 2)
            is_far = qb - kb >= 2
            dk_add = jnp.zeros((BS, width), F32)
            dv_add = jnp.zeros((BS, width), F32)
            for h in range(heads):
                b = jnp.where(is_far, far_ref[h], bias[h, near])
                s = jnp.where(allowed, nt(q_heads[h], k) + b, NEG)
                p = jnp.exp(s - totals[h])
                gp = nt(g_heads[h], v)
                ds = (p * (gp - deltas[h])).astype(BF16)
                dv_add += tn(p.astype(BF16), g_heads[h])
                dk_add += tn(ds, q_heads[h])
                dq = dq + own_head(nn(ds, k), lanes[h], heads)
                sums[h, place] += ds.astype(F32)
            dk[k_rows, :] += dk_add
            dv[k_rows, :] += dv_add
            return dq

        dq = lax.fori_loop(lo_ref[qb], qb + 1, k_step, jnp.zeros((BS, width), F32))
        grad_qkv_ref[q_rows, 0:width] = (dq * scale).astype(BF16)
        return 0

    lax.fori_loop(0, blocks, q_step, 0)
    grad_qkv_ref[:, width : 2 * width] = dk[...].astype(BF16)
    grad_qkv_ref[:, 2 * width : 3 * width] = dv[...].astype(BF16)
    row = lax.broadcasted_iota(jnp.int32, (BS, BS), 0)
    col = lax.broadcasted_iota(jnp.int32, (BS, BS), 1)
    upside_down = jnp.where(row + col == BS - 1, 1.0, 0.0).astype(F32)
    for h in range(heads):
        for t in range(2):
            flipped = jnp.dot(upside_down, sums[h, t], precision=lax.Precision.HIGHEST, preferred_element_type=F32)
            wide = jnp.concatenate([flipped, jnp.zeros((BS, BS), F32)], axis=1)
            skewed = pltpu.roll(wide, 0, 1, stride=1, stride_axis=0)
            diag_ref[3 * h + t : 3 * h + t + 1, :] = jnp.sum(skewed, axis=0, keepdims=True)
        rest = jnp.sum(sums[h, 2], axis=0, keepdims=True)
        diag_ref[3 * h + 2 : 3 * h + 3, :] = jnp.concatenate([rest, jnp.zeros((1, BS), F32)], axis=1)


def vspec():
    return pl.BlockSpec(memory_space=pltpu.VMEM)


def sspec():
    return pl.BlockSpec(memory_space=pltpu.SMEM)


def attention_forward(projected, lo, seg_col, seg_row, patterns, far, heads):
    seq_len = projected.shape[0]
    blocks = seq_len // BS
    return pl.pallas_call(
        functools.partial(attn_fwd_kernel, heads, blocks),
        out_shape=(
            jax.ShapeDtypeStruct((seq_len, heads * HD), BF16),
            jax.ShapeDtypeStruct((seq_len, heads), F32),
        ),
        in_specs=[sspec(), vspec(), vspec(), vspec(), vspec(), sspec()],
        out_specs=(vspec(), vspec()),
        scratch_shapes=[pltpu.VMEM((heads, 2, BS, BS), F32)],
        compiler_params=pltpu.CompilerParams(vmem_limit_bytes=VMEM_LIMIT),
        name="attn_fwd",
    )(lo, projected, seg_col, seg_row, patterns, far)


def attention_backward(projected, attended, grad, lse, lo, seg_col, seg_row, patterns, far, heads):
    seq_len = projected.shape[0]
    blocks = seq_len // BS
    width = heads * HD
    return pl.pallas_call(
        functools.partial(attn_bwd_kernel, heads, blocks),
        out_shape=(
            jax.ShapeDtypeStruct((seq_len, 3 * width), BF16),
            jax.ShapeDtypeStruct((3 * heads, 2 * BS), F32),
        ),
        in_specs=[sspec(), vspec(), vspec(), vspec(), vspec(), vspec(), vspec(), vspec(), sspec()],
        out_specs=(vspec(), vspec()),
        scratch_shapes=[
            pltpu.VMEM((heads, 2, BS, BS), F32),
            pltpu.VMEM((seq_len, width), F32),
            pltpu.VMEM((seq_len, width), F32),
            pltpu.VMEM((heads, 3, BS, BS), F32),
        ],
        compiler_params=pltpu.CompilerParams(vmem_limit_bytes=VMEM_LIMIT),
        name="attn_bwd",
    )(lo, projected, attended, grad, lse, seg_col, seg_row, patterns, far)


def rms_scale(values):
    return lax.rsqrt(jnp.mean(values * values, axis=-1, keepdims=True) + EPS)


def norm_backward(grad_normed, values, scale_inv, gain):
    normed_unit = values * scale_inv
    grad_unit = grad_normed * gain
    grad_values = scale_inv * (
        grad_unit - normed_unit * jnp.mean(grad_unit * normed_unit, axis=-1, keepdims=True)
    )
    return (grad_values, jnp.sum(grad_normed * normed_unit, axis=0))


def gelu_tanh(values):
    return jax.nn.gelu(values, approximate=True)


def route_slots(route_ids, experts, capacity):
    flat_routes = route_ids.reshape(-1)
    onehot = (flat_routes[:, None] == jnp.arange(experts, dtype=jnp.int32)[None, :]).astype(
        jnp.int32
    )
    ranks = jnp.cumsum(onehot, axis=0) - 1
    rank_own = jnp.sum(ranks * onehot, axis=1)
    return (flat_routes * capacity + rank_own).reshape(-1, TOP)


def on_device(
    tokens,
    segments,
    routes,
    w_qkv,
    w_attn_out,
    bias_table,
    gain_attn,
    gain_moe,
    router,
    w_in,
    w_out,
    cotangent,
):
    own_rows, model_width = tokens.shape
    n_tensor = lax.axis_size("tensor")
    n_dp = lax.axis_size("dp")
    seq_len = own_rows * n_tensor
    own_start = lax.axis_index("tensor") * own_rows
    head_cols = w_qkv.shape[2]
    heads = head_cols // HD
    experts = router.shape[1]
    local_experts = w_in.shape[0]
    capacity = 5 * seq_len * TOP // (4 * experts)
    highest = lax.Precision.HIGHEST
    slots = experts * capacity

    depth = w_qkv.shape[0]
    bias_rows = bias_table.shape[0]
    extra = jnp.concatenate(
        [
            router,
            gain_attn[:, None],
            gain_moe[:, None],
            jnp.pad(bias_table, ((0, depth - bias_rows), (0, 0))),
        ],
        axis=1,
    )
    extra = jnp.pad(extra, ((0, 0), (0, 128 - extra.shape[1])))
    packed = lax.all_gather(
        jnp.concatenate([w_qkv.reshape(depth, 3 * head_cols), extra], axis=1),
        "dp",
        axis=0,
        tiled=True,
    )
    qkv_matrix = packed[:, : 3 * head_cols]
    extras = packed[:, 3 * head_cols :]
    router_full = extras[:, :experts]
    gain_one = extras[:, experts].astype(F32)
    gain_two = extras[:, experts + 1].astype(F32)
    table = (
        extras.reshape(n_dp, depth, 128)[:, :bias_rows, experts + 2 : experts + 2 + heads]
        .reshape(NB, heads)
        .astype(F32)
    )
    out_columns = lax.all_gather(w_attn_out, "tensor", axis=0, tiled=True)
    out_matrix = lax.all_gather(out_columns, "dp", axis=1, tiled=True)

    tokens_float = tokens.astype(F32)
    scale_one = rms_scale(tokens_float)
    hidden_one = (tokens_float * scale_one * gain_one).astype(BF16)
    gathered_one = lax.all_gather(hidden_one, "tensor", axis=0, tiled=True)
    projected = jnp.dot(gathered_one, qkv_matrix, preferred_element_type=F32).astype(BF16)
    selectors = jnp.asarray(distance_selectors())
    patterns = jnp.dot(selectors, table, precision=highest)
    patterns = jnp.transpose(patterns.reshape(2, 2 * BS, heads), (2, 0, 1)).reshape(
        2 * heads, 2 * BS
    )
    far = table[NB - 1]
    segment_row = segments
    segment_col = segments.reshape(seq_len, 1)
    starts = segments[0, ::BS]
    ends = segments[0, BS - 1 :: BS]
    lowest = jnp.sum((ends[None, :] < starts[:, None]).astype(jnp.int32), axis=1)
    attended, lse = attention_forward(
        projected, lowest, segment_col, segment_row, patterns, far, heads
    )
    attended_own = lax.all_to_all(
        attended.reshape(n_tensor, own_rows, head_cols), "tensor", 0, 0
    )
    attended_own = jnp.transpose(attended_own, (1, 0, 2)).reshape(own_rows, n_tensor * head_cols)
    branch = jnp.dot(attended_own, out_matrix, preferred_element_type=F32)
    residual = tokens_float + branch
    scale_two = rms_scale(residual)
    hidden_two = (residual * scale_two * gain_two).astype(BF16)
    gathered_two = lax.all_gather(hidden_two, "tensor", axis=0, tiled=True)

    expert_ids = jnp.arange(experts, dtype=jnp.int32)

    def gate_values(logit_values, route_rows):
        expert_probs = jax.nn.softmax(logit_values, axis=-1)
        picked = jnp.sum(
            jnp.where(
                route_rows[:, :, None] == expert_ids[None, None, :], expert_probs[:, None, :], 0.0
            ),
            axis=-1,
        )
        return picked / jnp.sum(picked, axis=1, keepdims=True)

    gates = gate_values(jnp.dot(gathered_two, router_full, preferred_element_type=F32), routes)
    slot_ids = route_slots(routes, experts, capacity)
    slot_flat = slot_ids.reshape(-1)
    token_ids = jnp.repeat(jnp.arange(seq_len, dtype=jnp.int32), TOP)
    sources = jnp.full((slots,), seq_len, jnp.int32).at[slot_flat].set(token_ids)
    slot_gates = jnp.zeros((slots,), F32).at[slot_flat].set(gates.reshape(-1))
    grad_gathered = lax.all_gather(cotangent, "tensor", axis=0, tiled=True)

    def exchange(rows):
        parts = rows.reshape(n_dp, local_experts, capacity, model_width)
        return [
            lax.all_to_all(parts[:, i], "dp", 0, 0).reshape(n_dp * capacity, model_width)
            for i in range(local_experts)
        ]

    def give_back(parts):
        back = [
            lax.all_to_all(part.reshape(n_dp, capacity, model_width), "dp", 0, 0) for part in parts
        ]
        return jnp.stack(back, axis=1).reshape(slots, model_width)

    zero_row = jnp.zeros((1, model_width), BF16)
    dispatched = exchange(jnp.concatenate([gathered_two, zero_row], axis=0)[sources])
    padded_grad = jnp.concatenate([grad_gathered, zero_row], axis=0)
    grad_expert = exchange((slot_gates[:, None] * padded_grad[sources]).astype(BF16))

    outs, backs, grads_in, grads_out = [], [], [], []
    for i in range(local_experts):
        rows, grad_rows = dispatched[i], grad_expert[i]
        gate_part = nt(rows, w_in[i, 0])
        up_part = nt(rows, w_in[i, 1])
        gelu_value, gelu_pull = jax.vjp(gelu_tanh, gate_part)
        activated = (gelu_value * up_part).astype(BF16)
        outs.append(nn(activated, w_out[i]).astype(BF16))
        grad_act = nt(grad_rows, w_out[i])
        grads_out.append(tn(activated, grad_rows))
        grad_gate = gelu_pull(grad_act * up_part)[0].astype(BF16)
        grad_up = (grad_act * gelu_value).astype(BF16)
        backs.append((nn(grad_gate, w_in[i, 0]) + nn(grad_up, w_in[i, 1])).astype(BF16))
        grads_in.append(jnp.stack([tn(grad_gate, rows), tn(grad_up, rows)]))
    grad_w_in = jnp.stack(grads_in)
    grad_w_out = jnp.stack(grads_out)
    expert_out = give_back(outs)
    grad_dispatched = give_back(backs)

    first, second = slot_ids[:, 0], slot_ids[:, 1]
    picked_first = expert_out[first].astype(F32)
    picked_second = expert_out[second].astype(F32)
    mixture = lax.psum_scatter(
        (gates[:, 0:1] * picked_first + gates[:, 1:2] * picked_second).astype(BF16),
        "tensor",
        scatter_dimension=0,
        tiled=True,
    ).astype(F32)
    layer_out = (residual + mixture).astype(BF16)
    grad_float = grad_gathered.astype(F32)
    grad_gate_part = jnp.stack(
        [
            jnp.sum(grad_float * picked_first, axis=1),
            jnp.sum(grad_float * picked_second, axis=1),
        ],
        axis=1,
    )
    grad_hidden_part = (
        grad_dispatched[first].astype(F32) + grad_dispatched[second].astype(F32)
    ).astype(BF16)
    grad_own = lax.psum_scatter(
        grad_hidden_part, "tensor", scatter_dimension=0, tiled=True
    ).astype(F32)
    grad_gate_own = lax.dynamic_slice_in_dim(
        lax.psum(grad_gate_part, "tensor"), own_start, own_rows, 0
    )
    own_routes = lax.dynamic_slice_in_dim(routes, own_start, own_rows, 0)
    own_logits = jnp.dot(hidden_two, router_full, preferred_element_type=F32)

    def own_gates(logit_values):
        return gate_values(logit_values, own_routes)

    _, gate_pull = jax.vjp(own_gates, own_logits)
    grad_logits = gate_pull(grad_gate_own)[0]
    router_float = router_full.astype(F32)
    grad_hidden_two = grad_own + jnp.dot(grad_logits, router_float.T, precision=highest)
    grad_router_part = jnp.dot(hidden_two.astype(F32).T, grad_logits, precision=highest)
    grad_from_norm, grad_gain_two = norm_backward(grad_hidden_two, residual, scale_two, gain_two)
    grad_residual = cotangent.astype(F32) + grad_from_norm

    grad_branch = grad_residual.astype(BF16)
    grad_attended_own = nt(grad_branch, out_matrix).astype(BF16)
    grad_attended = lax.all_to_all(
        jnp.transpose(grad_attended_own.reshape(own_rows, n_tensor, head_cols), (1, 0, 2)),
        "tensor",
        0,
        0,
    ).reshape(seq_len, head_cols)
    grad_branch_all = lax.all_gather(grad_branch, "tensor", axis=0, tiled=True)
    grad_w_attn_out = tn(attended, grad_branch_all)
    grad_projected, diag = attention_backward(
        projected,
        attended,
        grad_attended,
        lse,
        lowest,
        segment_col,
        segment_row,
        patterns,
        far,
        heads,
    )
    diag = diag.reshape(heads, 3, 2 * BS)
    near = jnp.transpose(diag[:, :2].reshape(heads, 4 * BS))
    grad_table = lax.dot_general(
        jnp.asarray(skew_selectors()), near, (((0,), (0,)), ((), ())), precision=highest
    )
    grad_table = grad_table.at[NB - 1].add(jnp.sum(diag[:, 2], axis=1))
    grad_w_qkv = tn(gathered_one, grad_projected).reshape(model_width, 3, head_cols)
    grad_hidden_one = lax.psum_scatter(
        nt(grad_projected, qkv_matrix).astype(BF16),
        "tensor",
        scatter_dimension=0,
        tiled=True,
    ).astype(F32)
    grad_from_first, grad_gain_one = norm_backward(
        grad_hidden_one, tokens_float, scale_one, gain_one
    )
    grad_tokens = (grad_residual + grad_from_first).astype(BF16)

    small = jnp.concatenate(
        [grad_router_part, grad_gain_one[:, None], grad_gain_two[:, None]], axis=1
    )
    small = lax.psum(small, "tensor")
    small = lax.psum_scatter(small, "dp", scatter_dimension=0, tiled=True)
    reduced_qkv = lax.psum_scatter(grad_w_qkv, "dp", scatter_dimension=0, tiled=True)
    reduced_attn_out = lax.psum_scatter(grad_w_attn_out, "dp", scatter_dimension=1, tiled=True)
    reduced_table = lax.psum_scatter(grad_table, "dp", scatter_dimension=0, tiled=True)
    return (
        layer_out,
        grad_tokens,
        reduced_qkv,
        reduced_attn_out,
        reduced_table,
        small[:, experts],
        small[:, experts + 1],
        small[:, :experts],
        grad_w_in,
        grad_w_out,
    )


def solution(mesh):
    return jax.shard_map(
        on_device,
        mesh=mesh,
        in_specs=(
            P(("dp", "tensor"), None),
            P("dp", None),
            P("dp", None),
            P("dp", None, "tensor"),
            P("tensor", "dp"),
            P("dp", "tensor"),
            P("dp"),
            P("dp"),
            P("dp", None),
            P("dp", None, "tensor", None),
            P("dp", "tensor", None),
            P(("dp", "tensor"), None),
        ),
        out_specs=(
            P(("dp", "tensor"), None),
            P(("dp", "tensor"), None),
            P("dp", None, "tensor"),
            P("tensor", "dp"),
            P("dp", "tensor"),
            P("dp"),
            P("dp"),
            P("dp", None),
            P("dp", None, "tensor", None),
            P("dp", "tensor", None),
        ),
        check_vma=False,
    )
```

time: 2140 us -> 874 us (0.41)
  waiting for transfers between devices: 1490 us -> 394 us
  local copies, waits for them, and re-layouts: 221 us -> 108 us
  matrix products: 226 us -> 118 us
  starting transfers between devices: 0.7 us -> 34.2 us
  loops' own time: 30.7 us -> 0 us
  Pallas kernels: 0 us -> 29 us
  blocking collectives: 83.6 us -> 108 us
    reduce_scatter x6 -> x3, waiting for transfers between devices: 884 us -> 52.9 us  [the longest x1 43.6 us: on_device(): lax.psum_scatter(nt(grad_projected, qkv_matrix).astype(BF16), 'tensor', s...]
    all_gather x4 -> x3, waiting for transfers between devices: 331 us -> 79.7 us  [the longest x1 45.2 us: on_device(): grad_branch_all = lax.all_gather(grad_branch, 'tensor', axis=0, tiled=True)]
    all_to_all x0 -> x8, waiting for transfers between devices: none -> 106 us  [the longest x4 70.7 us: give_back(): lax.all_to_all(part.reshape(n_dp, capacity, model_width), 'dp', 0, 0)]
    dot_general x30 -> x29, matrix products: 196 us -> 116 us  [the longest x8 46.4 us: nt(): lax.dot_general(a, b, (((1,), (1,)), ((), ())), preferred_element_type=F32)]
    reduce_scatter x1, waiting for transfers between devices: 76.9 us -> 0.02 us  [on_device(): lax.psum_scatter(grad_hidden_part, 'tensor', scatter_dimension=0, tiled=T...]
    another operation x16 -> x3, local copies, waits for them, and re-layouts: 60.2 us -> 6.99 us  [the longest x2 6.57 us: give_back(): return jnp.stack(back, axis=1).reshape(slots, model_width)]
    all_to_all x0 -> x2, blocking collectives: none -> 49.4 us  [the longest x1 35.8 us: exchange(): lax.all_to_all(parts[:, i], 'dp', 0, 0)]
    all_to_all x0 -> x8, starting transfers between devices: none -> 33 us  [the longest x4 16.4 us: give_back(): lax.all_to_all(part.reshape(n_dp, capacity, model_width), 'dp', 0, 0)]
  transfers between devices with their start and end apart: 17 -> 20, of which waited for: 16 -> 16; matrix products, arithmetic and copies ran while one was open for 8% -> 30% of each run, Pallas kernels for 0% -> 1%
where the time goes in v1:
time: 874 us; the launch traced here: 864 us
  waiting for transfers between devices  394 us (45%)
  matrix products  118 us (14%)
  local copies, waits for them, and re-layouts  108 us (12%)
  blocking collectives  108 us (12%)
  other arithmetic  56.2 us (6%)
  starting transfers between devices  34.2 us (4%)
  Pallas kernels  29 us (3%)
  between operations  16.2 us (2%)
    all_to_all x4, waiting for transfers between devices, give_back(): lax.all_to_all(part.reshape(n_dp, capacity, model_width), 'dp', 0, 0)  70.7 us
    reduce_scatter x1, waiting for transfers between devices, on_device(): lax.psum_scatter(grad_w_qkv, 'dp', scatter_dimension=0, tiled=True)  50.4 us
    dot_general x8, matrix products, nt(): lax.dot_general(a, b, (((1,), (1,)), ((), ())), preferred_element_type=F32)  46.4 us
    all_gather x1, waiting for transfers between devices, on_device(): grad_branch_all = lax.all_gather(grad_branch, 'tensor', axis=0, tiled=True)  45.2 us
    reduce_scatter x1, waiting for transfers between devices, on_device(): lax.psum_scatter(nt(grad_projected, qkv_matrix).astype(BF16), 'tensor', s...  43.6 us
    all_to_all x1, blocking collectives, exchange(): lax.all_to_all(parts[:, i], 'dp', 0, 0)  35.8 us
    all_gather x1, waiting for transfers between devices, on_device(): gathered_two = lax.all_gather(hidden_two, 'tensor', axis=0, tiled=True)  30.4 us
    dot_general x6, matrix products, nn(): lax.dot_general(a, b, (((1,), (0,)), ((), ())), preferred_element_type=F32)  29.6 us
  transfers between devices with their start and end apart: 20, of which 16 were waited for; matrix products, arithmetic and copies ran while one was open for 30% of the time, Pallas kernels for 1%

profile of v1, /device:TPU:0, one launch (start us, length us, event | category | flops | bytes accessed | tf_op | source)
XLA Modules:
  0.0 863.8 jit_solution(6333700523294985158)
XLA Ops:
  11.9 28.6 %all-gather.7.cloned.1.call-done = bf16[1024,896]{0,1:T(8,128)(2,1)} async-done(((bf16[128,896]{0,1:T(8,128)(2,1)}), bf16[1024,896]{0,1:T(8,128)(2,1)}) %all-gather.7.cloned.1.call-update) | async-done | bytes 1835024 | tf_op jit(solution)/shard_map/all_gather | solution.py:343
  43.5 15.6 %all_gather.23 = bf16[1024,128]{1,0:T(8,128)(2,1)} all-gather(bf16[256,128]{1,0:T(8,128)(2,1)S(1)} %copy-done.19), channel_id=1, replica_groups=mesh['dp'=8,'tensor'=4] {'tensor'}, dimensions={0}, use_global_device_ids=true | all-gather | bytes 327680 | tf_op jit(solution)/shard_map/all_gather | solution.py:359
  63.0 28.2 %all-gather.9.cloned.1.call-done = bf16[1024,1024]{1,0:T(8,128)(2,1)} async-done(((bf16[256,1024]{1,0:T(8,128)(2,1)}), bf16[1024,1024]{1,0:T(8,128)(2,1)}) %all-gather.9.cloned.1.call-update) | async-done | bytes 2097168 | tf_op jit(solution)/shard_map/all_gather | solution.py:365
  91.2 4.6 convolution_convert_fusion.3.qkv_ref
  95.8 12.2 %attn_fwd.1 = (bf16[1024,256]{1,0:T(8,128)(2,1)}, f32[1024,4]{1,0:T(8,128)}) custom-call(s32[4]{0:T(128)} %convert_reduce_fusion.1.lo_ref, bf16[1024,768]{1,0:T(8,128)(2,1)} %convolution_convert_fusion.3.qkv_ref, s32[1024,1]{1,0:T(8,128)} %copy.98.seg_col_ref, s32[1,1024]{1,0:T(1,128)} %seg_row_ref.3, f32[8,512]{1,0:T(8,128)} %reshape.275.pattern_ref, ...), custom_call_target="tpu_custom_call" | custom-call | tf_op jit(solution)/shard_map/attn_fwd/pallas_call | solution.py:240
  113.5 5.9 all-gather.11.cloned.1.call-done
  119.4 8.9 %all-to-all-done = bf16[4,256,256]{1,2,0:T(8,128)(2,1)S(1)} async-done(((bf16[4,256,256]{1,2,0:T(8,128)(2,1)}), bf16[4,256,256]{1,2,0:T(8,128)(2,1)S(1)}, u32[]{:S(2)}, u32[]{:S(2)}) %all-to-all-start) | async-done | bytes 524320 | tf_op jit(solution)/shard_map/all_to_all | solution.py:381
  134.1 4.6 reduce-window.6
  140.7 8.1 scatter_custom_fusion
  148.8 30.4 %all-gather.13.cloned.1.call-done = bf16[1024,1024]{1,0:T(8,128)(2,1)} async-done(((bf16[256,1024]{1,0:T(8,128)(2,1)}), bf16[1024,1024]{1,0:T(8,128)(2,1)}) %all-gather.13.cloned.1.call-update) | async-done | bytes 2097168 | tf_op jit(solution)/shard_map/all_gather | solution.py:389
  180.9 8.8 %gather_fusion = bf16[2560,1024]{1,0:T(8,128)(2,1)} fusion(bf16[1025,1024]{1,0:T(8,128)(2,1)S(1)} %concatenate.19, s32[3072]{0:T(1024)S(1)} %pad_clamp_fusion), kind=kCustom, calls=%fused_computation | custom fusion | bytes 10496000 | tf_op jit(solution)/shard_map/gather | solution.py:425
  189.7 5.7 slice_bitcast_fusion.3
  195.4 4.6 all-to-all-start.3
  200.0 25.3 %all-gather.15.cloned.1.call-done = bf16[1024,1024]{1,0:T(8,128)(2,1)} async-done(((bf16[256,1024]{1,0:T(8,128)(2,1)}), bf16[1024,1024]{1,0:T(8,128)(2,1)}) %all-gather.15.cloned.1.call-update) | async-done | bytes 2097168 | tf_op jit(solution)/shard_map/all_gather | solution.py:409
  227.0 8.8 %gather_fusion.3 = bf16[2560,1024]{1,0:T(8,128)(2,1)} fusion(bf16[1025,1024]{1,0:T(8,128)(2,1)S(1)} %concatenate.20, s32[3072]{0:T(1024)S(1)} %pad_clamp_fusion), kind=kCustom, calls=%fused_computation.3 | custom fusion | bytes 10496000 | tf_op jit(solution)/shard_map/gather | solution.py:427
  238.7 8.1 scatter_custom_fusion.1
  252.4 35.8 %all_to_all.50 = bf16[8,160,1024]{2,1,0:T(8,128)(2,1)} all-to-all(bf16[8,160,1024]{2,1,0:T(8,128)(2,1)S(1)} %get-tuple-element.99), channel_id=1, replica_groups=mesh['dp'=8,'tensor'=4] {'dp'}, dimensions={0} | all-to-all | bytes 5242880 | tf_op jit(solution)/shard_map/all_to_all | solution.py:414
  288.2 3.6 all-to-all-start.1
  291.8 6.0 fusion.31
  297.8 6.0 fusion.27
  303.9 20.1 %all-to-all-done.1 = bf16[8,160,1024]{2,1,0:T(8,128)(2,1)S(1)} async-done(((bf16[8,160,1024]{2,1,0:T(8,128)(2,1)}), bf16[8,160,1024]{2,1,0:T(8,128)(2,1)S(1)}, u32[]{:S(2)}, u32[]{:S(2)}) %all-to-all-start.1) | async-done | bytes 2621472 | tf_op jit(solution)/shard_map/all_to_all | solution.py:414
  325.5 4.9 all-to-all-start.5
  330.4 8.3 multiply_convert_fusion
  338.7 4.8 fusion.29
  343.6 5.4 fusion.41
  349.0 3.9 fusion.37
  352.9 3.7 add_convert_fusion
  356.6 6.1 all-to-all-done.5
  362.7 3.9 all-to-all-start.8
  366.6 9.3 %multiply_convert_fusion.1 = (bf16[1280,704]{0,1:T(8,128)(2,1)S(1)}, bf16[1280,704]{0,1:T(8,128)(2,1)S(1)}, bf16[1280,704]{0,1:T(8,128)(2,1)}) fusion(f32[1280,704]{0,1:T(8,128)} %fusion.41, f32[1280,704]{0,1:T(8,128)} %fusion.37, bf16[1280,1024]{1,0:T(8,128)(2,1)} %bitcast.35, bf16[2,704,1024]{2,1,0:T(8,128)(2,1)} %param.26), kind=kOutput, calls=%fused_computation.48 | convolution fusion | flops 1868922880 | bytes 16678912 | tf_op jit(solution)/shard_map/dot_general | solution.py:63
  375.8 4.6 fusion.39
  380.5 5.1 add_convert_fusion.1
  385.6 13.2 %all-to-all-done.8 = bf16[8,160,1024]{2,1,0:T(8,128)(2,1)S(1)} async-done(((bf16[8,160,1024]{2,1,0:T(8,128)(2,1)}), bf16[8,160,1024]{2,1,0:T(8,128)(2,1)S(1)}, u32[]{:S(2)}, u32[]{:S(2)}) %all-to-all-start.8) | async-done | bytes 2621472 | tf_op jit(solution)/shard_map/all_to_all | solution.py:420
  400.3 4.4 all-to-all-start.6
  404.7 5.6 convolution_convert_fusion
  410.3 26.6 %all-to-all-done.6 = bf16[8,160,1024]{2,1,0:T(8,128)(2,1)} async-done(((bf16[8,160,1024]{2,1,0:T(8,128)(2,1)}), bf16[8,160,1024]{2,1,0:T(8,128)(2,1)}, u32[]{:S(2)}, u32[]{:S(2)}) %all-to-all-start.6) | async-done | bytes 2621472 | tf_op jit(solution)/shard_map/all_to_all | solution.py:420
  436.9 3.6 all-to-all-start.4
  447.9 9.2 %gather_fusion.5 = bf16[1024,1024]{1,0:T(8,128)(2,1)} fusion(bf16[2560,1024]{1,0:T(8,128)(2,1)} %bitcast.185, s32[1024]{0:T(1024)S(1)} %get-tuple-element.120), kind=kCustom, calls=%fused_computation.5 | custom fusion | bytes 4198400 | tf_op jit(solution)/shard_map/gather | solution.py:467
  457.1 9.2 %gather_fusion.4 = bf16[1024,1024]{1,0:T(8,128)(2,1)} fusion(bf16[2560,1024]{1,0:T(8,128)(2,1)} %bitcast.186, s32[1024]{0:T(1024)S(1)} %get-tuple-element.121), kind=kCustom, calls=%fused_computation.4 | custom fusion | bytes 4198400 | tf_op jit(solution)/shard_map/gather | solution.py:467
  466.3 4.5 add_convert_fusion.2
  470.9 5.6 convolution_convert_fusion.1
  476.5 4.5 all-to-all-start.2
  482.5 30.9 %all-to-all-done.2 = bf16[8,160,1024]{2,1,0:T(8,128)(2,1)} async-done(((bf16[8,160,1024]{2,1,0:T(8,128)(2,1)}), bf16[8,160,1024]{2,1,0:T(8,128)(2,1)}, u32[]{:S(2)}, u32[]{:S(2)}) %all-to-all-start.2) | async-done | bytes 2621472 | tf_op jit(solution)/shard_map/all_to_all | solution.py:420
  518.9 8.1 gather_fusion.1
  527.0 9.2 %gather_fusion.2 = bf16[1024,1024]{1,0:T(8,128)(2,1)} fusion(bf16[2560,1024]{1,0:T(8,128)(2,1)} %bitcast.184, s32[1024]{0:T(1024)S(1)} %get-tuple-element.120), kind=kCustom, calls=%fused_computation.2 | custom fusion | bytes 4198400 | tf_op jit(solution)/shard_map/gather | solution.py:450
  536.2 5.3 fusion.3
  541.5 9.8 %psum.14 = f32[1024,2]{0,1:T(2,128)S(1)} all-reduce(f32[1024,2]{0,1:T(2,128)S(1)} %pad_maximum_fusion.5), channel_id=1, replica_groups=mesh['dp'=8,'tensor'=4] {'tensor'}, use_global_device_ids=true, to_apply=%region_16.17 | all-reduce | flops 2048 | bytes 16384 | tf_op jit(solution)/shard_map/psum | solution.py:473
  556.4 13.6 %all_to_all.51 = bf16[4,256,256]{2,1,0:T(8,128)(2,1)} all-to-all(bf16[4,256,256]{2,1,0:T(8,128)(2,1)S(1)} %bitcast.207), channel_id=1, replica_groups=mesh['dp'=8,'tensor'=4] {'tensor'}, dimensions={0} | all-to-all | bytes 1048576 | tf_op jit(solution)/shard_map/all_to_all | solution.py:491
  570.0 16.9 %attn_bwd.1 = (bf16[1024,768]{1,0:T(8,128)(2,1)}, f32[12,512]{1,0:T(8,128)}) custom-call(s32[4]{0:T(128)} %convert_reduce_fusion.1.lo_ref, bf16[1024,768]{1,0:T(8,128)(2,1)} %convolution_convert_fusion.3.qkv_ref, bf16[1024,256]{1,0:T(8,128)(2,1)} %get-tuple-element.26.out_ref, bf16[1024,256]{1,0:T(8,128)(2,1)} %bitcast.206, ...), custom_call_target="tpu_custom_call" | custom-call | tf_op jit(solution)/shard_map/attn_bwd/pallas_call | solution.py:258
  586.9 5.0 convolution_convert_fusion.2
  595.0 43.6 %reduce-scatter.12.cloned.1.call-done = bf16[256,1024]{1,0:T(8,128)(2,1)} async-done(((bf16[1024,1024]{1,0:T(8,128)(2,1)}), bf16[256,1024]{1,0:T(8,128)(2,1)}) %reduce-scatter.12.cloned.1.call-update) | async-done | bytes 524304 | tf_op jit(solution)/shard_map/reduce_scatter | solution.py:518
  640.9 45.2 %all-gather.17.cloned.1.call-done = bf16[1024,1024]{1,0:T(8,128)(2,1)} async-done(((bf16[256,1024]{1,0:T(8,128)(2,1)}), bf16[1024,1024]{1,0:T(8,128)(2,1)}) %all-gather.17.cloned.1.call-update) | async-done | bytes 2097168 | tf_op jit(solution)/shard_map/all_gather | solution.py:497
  689.7 4.4 convolution_bitcast_fusion.2
  694.1 3.8 convolution_bitcast_fusion.3
  701.3 3.5 fusion.94
  704.9 3.8 copy.108
  708.8 4.5 convolution_bitcast_fusion.4
  721.6 3.9 convolution_bitcast_fusion.1
  728.6 9.1 %pad_maximum_fusion = f32[2,2,704,1024]{3,2,1,0:T(8,128)} fusion(f32[1,2,704,1024]{3,2,1,0:T(8,128)S(1)} %bitcast.188, f32[1,2,704,1024]{3,2,1,0:T(8,128)} %maximum_bitcast_fusion), kind=kLoop, calls=%fused_computation.8 | loop fusion | flops 2883584 | bytes 23068672 | tf_op jit(solution)/shard_map/stack | solution.py:443
  739.5 13.6 %all-reduce.4 = f32[32,4]{0,1:T(4,128)S(1)} all-reduce(f32[32,4]{0,1:T(4,128)S(1)} %scatter-add.4), channel_id=7, replica_groups=mesh['dp'=8,'tensor'=4] {'dp'}, use_global_device_ids=true, to_apply=%region_30.31.clone | all-reduce | flops 128 | bytes 1024
  756.6 9.3 %reduce-scatter.18.cloned.1.call-done = f32[128,18]{0,1:T(8,128)} async-done(((f32[1024,18]{0,1:T(8,128)}), f32[128,18]{0,1:T(8,128)}) %reduce-scatter.18.cloned.1.call-update) | async-done | bytes 9232 | tf_op jit(solution)/shard_map/reduce_scatter | solution.py:533
  765.9 19.3 %psum.16 = f32[128,18]{0,1:T(8,128)S(1)} all-reduce(f32[128,18]{0,1:T(8,128)} %reduce-scatter.18.cloned.1.call-done), channel_id=1, replica_groups=mesh['dp'=8,'tensor'=4] {'tensor'}, use_global_device_ids=true, to_apply=%region_33.34 | all-reduce | flops 2304 | bytes 18432 | tf_op jit(solution)/shard_map/psum | solution.py:532
  786.4 19.7 %reduce-scatter.16.cloned.1.call-done = f32[256,128]{1,0:T(8,128)} async-done(((f32[256,1024]{1,0:T(8,128)}), f32[256,128]{1,0:T(8,128)}) %reduce-scatter.16.cloned.1.call-update) | async-done | bytes 131088 | tf_op jit(solution)/shard_map/reduce_scatter | solution.py:535
  806.1 50.4 %reduce-scatter.14.cloned.1.call-done = f32[128,3,256]{2,0,1:T(8,128)} async-done(((f32[1024,3,256]{2,0,1:T(8,128)}), f32[128,3,256]{2,0,1:T(8,128)}) %reduce-scatter.14.cloned.1.call-update) | async-done | bytes 393232 | tf_op jit(solution)/shard_map/reduce_scatter | solution.py:534
  (221 shorter events, 88.4 us)
Async XLA Ops:
  7.2 36.3 %copy-start.19 = (bf16[256,128]{1,0:T(8,128)(2,1)S(1)}, bf16[256,128]{1,0:T(8,128)(2,1)}, u32[]{:S(2)}) copy-start(bf16[256,128]{1,0:T(8,128)(2,1)} %param.20) | copy-start | bytes 196612
  7.2 52.0 %copy-start.23 = (s32[1,1024]{1,0:T(1,128)S(1)}, s32[1,1024]{1,0:T(1,128)}, u32[]{:S(2)}) copy-start(s32[1,1024]{1,0:T(1,128)} %seg_row_ref.3) | copy-start | bytes 12292
  7.2 33.3 %all-gather.7.cloned.1.call-start = ((), (), s32[]{:S(2)}) async-start(), calls=%async_computation.16 | async-start | bytes 2064384 | tf_op jit(solution)/shard_map/all_gather | solution.py:343
  8.0 53.3 %copy-start.15 = (f32[1024,32]{1,0:T(8,128)S(1)}, f32[1024,32]{1,0:T(8,128)}, u32[]{:S(2)}) copy-start(f32[1024,32]{1,0:T(8,128)} %constant.96.clone) | copy-start | bytes 393220
  10.6 80.6 %all-gather.9.cloned.1.call-start = ((), (), s32[]{:S(2)}) async-start(), calls=%async_computation.17 | async-start | bytes 2621440 | tf_op jit(solution)/shard_map/all_gather | solution.py:365
  11.9 49.3 %copy-start.27 = (f32[256]{0:T(256)}, f32[256]{0:T(256)S(1)}, u32[]{:S(2)}) copy-start(f32[256]{0:T(256)S(1)} %add_rsqrt_fusion.1) | copy-start | bytes 3076
  40.5 20.6 %copy-start.18 = (bf16[1024,896]{0,1:T(8,128)(2,1)S(1)}, bf16[1024,896]{0,1:T(8,128)(2,1)}, u32[]{:S(2)}) copy-start(bf16[1024,896]{0,1:T(8,128)(2,1)} %all-gather.7.cloned.1.call-done) | copy-start | bytes 5505028
  41.4 54.4 %copy-start.20 = (f32[1024,1]{0,1:T(1,128)}, f32[1024,1]{0,1:T(1,128)S(1)}, u32[]{:S(2)}) copy-start(f32[1024,1]{0,1:T(1,128)S(1)} %get-tuple-element.104) | copy-start | bytes 12292
  41.4 89.3 %copy-start.16 = (f32[1024,1]{0,1:T(1,128)}, f32[1024,1]{0,1:T(1,128)S(1)}, u32[]{:S(2)}) copy-start(f32[1024,1]{0,1:T(1,128)S(1)} %get-tuple-element.103) | copy-start | bytes 12292
  43.5 75.9 %all-gather.11.cloned.1.call-start = ((), (), s32[]{:S(2)}) async-start(), calls=%async_computation.18 | async-start | bytes 2359296 | tf_op jit(solution)/shard_map/all_gather | solution.py:360
  95.8 32.5 %copy-start.2 = (bf16[256,1024]{1,0:T(8,128)(2,1)S(1)}, bf16[256,1024]{1,0:T(8,128)(2,1)}, u32[]{:S(2)}) copy-start(bf16[256,1024]{1,0:T(8,128)(2,1)} %param.16) | copy-start | bytes 1572868
  110.0 18.3 %all-to-all-start = ((bf16[4,256,256]{1,2,0:T(8,128)(2,1)}), bf16[4,256,256]{1,2,0:T(8,128)(2,1)S(1)}, u32[]{:S(2)}, u32[]{:S(2)}) async-start(bf16[4,256,256]{1,2,0:T(8,128)(2,1)} %copy.99), calls=%async_computation | async-start | bytes 1048576 | tf_op jit(solution)/shard_map/all_to_all | solution.py:381
  113.5 65.7 %all-gather.13.cloned.1.call-start = ((), (), s32[]{:S(2)}) async-start(), calls=%async_computation.19 | async-start | bytes 2621440 | tf_op jit(solution)/shard_map/all_gather | solution.py:389
  128.3 5.1 copy-start.22
  130.7 1.1 copy-start
  130.7 1.1 copy-start.25
  132.7 92.5 %all-gather.15.cloned.1.call-start = ((), (), s32[]{:S(2)}) async-start(), calls=%async_computation.21 | async-start | bytes 2621440 | tf_op jit(solution)/shard_map/all_gather | solution.py:409
  195.4 57.0 %all-to-all-start.3 = ((bf16[8,160,1024]{2,1,0:T(8,128)(2,1)}), bf16[8,160,1024]{2,1,0:T(8,128)(2,1)}, u32[]{:S(2)}, u32[]{:S(2)}) async-start(bf16[8,160,1024]{2,1,0:T(8,128)(2,1)} %get-tuple-element.101), calls=%async_computation.3 | async-start | bytes 5242880 | tf_op jit(solution)/shard_map/all_to_all | solution.py:414
  288.2 35.8 %all-to-all-start.1 = ((bf16[8,160,1024]{2,1,0:T(8,128)(2,1)}), bf16[8,160,1024]{2,1,0:T(8,128)(2,1)S(1)}, u32[]{:S(2)}, u32[]{:S(2)}) async-start(bf16[8,160,1024]{2,1,0:T(8,128)(2,1)} %get-tuple-element.100), calls=%async_computation.1 | async-start | bytes 5242880 | tf_op jit(solution)/shard_map/all_to_all | solution.py:414
  324.0 1.5 copy-start.11
  325.5 4.9 copy-start.9
  325.5 37.2 %all-to-all-start.5 = ((bf16[8,160,1024]{2,1,0:T(8,128)(2,1)}), bf16[8,160,1024]{2,1,0:T(8,128)(2,1)}, u32[]{:S(2)}, u32[]{:S(2)}) async-start(bf16[8,160,1024]{2,1,0:T(8,128)(2,1)} %get-tuple-element.98), calls=%async_computation.6 | async-start | bytes 5242880 | tf_op jit(solution)/shard_map/all_to_all | solution.py:414
  338.7 4.9 copy-start.32
  338.7 14.2 %copy-start.38 = (bf16[1280,704]{0,1:T(8,128)(2,1)}, bf16[1280,704]{0,1:T(8,128)(2,1)S(1)}, u32[]{:S(2)}) copy-start(bf16[1280,704]{0,1:T(8,128)(2,1)S(1)} %get-tuple-element.95) | copy-start | bytes 5406724
  338.7 4.9 copy-start.12
  338.7 10.3 %slice-start.2 = ((s8[5767168]{0:T(1024)(128)(4,1)}), s8[4194304]{0:T(1024)(128)(4,1)S(1)}, s32[]{:S(2)}) async-start(s8[5767168]{0:T(1024)(128)(4,1)} %bitcast.236), calls=%async_computation.30 | async-start | bytes 8388608
  343.6 5.4 slice-start.3
  362.7 36.1 %all-to-all-start.8 = ((bf16[8,160,1024]{2,1,0:T(8,128)(2,1)}), bf16[8,160,1024]{2,1,0:T(8,128)(2,1)S(1)}, u32[]{:S(2)}, u32[]{:S(2)}) async-start(bf16[8,160,1024]{2,1,0:T(8,128)(2,1)} %bitcast.203), calls=%async_computation.9 | async-start | bytes 5242880 | tf_op jit(solution)/shard_map/all_to_all | solution.py:420
  375.8 4.7 copy-start.34
  375.8 4.7 copy-start.39
  398.8 1.5 copy-start.4
  400.3 36.7 %all-to-all-start.6 = ((bf16[8,160,1024]{2,1,0:T(8,128)(2,1)}), bf16[8,160,1024]{2,1,0:T(8,128)(2,1)}, u32[]{:S(2)}, u32[]{:S(2)}) async-start(bf16[8,160,1024]{2,1,0:T(8,128)(2,1)} %bitcast.204), calls=%async_computation.7 | async-start | bytes 5242880 | tf_op jit(solution)/shard_map/all_to_all | solution.py:420
  436.9 39.6 %all-to-all-start.4 = ((bf16[8,160,1024]{2,1,0:T(8,128)(2,1)}), bf16[8,160,1024]{2,1,0:T(8,128)(2,1)S(1)}, u32[]{:S(2)}, u32[]{:S(2)}) async-start(bf16[8,160,1024]{2,1,0:T(8,128)(2,1)} %bitcast.201), calls=%async_computation.4 | async-start | bytes 5242880 | tf_op jit(solution)/shard_map/all_to_all | solution.py:420
  440.6 110.9 %reduce-scatter.10.cloned.1.call-start = ((), (), s32[]{:S(2)}) async-start(), calls=%async_computation.22 | async-start | bytes 2621440 | tf_op jit(solution)/shard_map/reduce_scatter | solution.py:469
  476.5 4.8 copy-start.5
  476.5 36.8 %all-to-all-start.2 = ((bf16[8,160,1024]{2,1,0:T(8,128)(2,1)}), bf16[8,160,1024]{2,1,0:T(8,128)(2,1)}, u32[]{:S(2)}, u32[]{:S(2)}) async-start(bf16[8,160,1024]{2,1,0:T(8,128)(2,1)} %bitcast.202), calls=%async_computation.2 | async-start | bytes 5242880 | tf_op jit(solution)/shard_map/all_to_all | solution.py:420
  481.1 157.6 %reduce-scatter.12.cloned.1.call-start = ((), (), s32[]{:S(2)}) async-start(), calls=%async_computation.23 | async-start | bytes 2621440 | tf_op jit(solution)/shard_map/reduce_scatter | solution.py:518
  536.2 15.3 %copy-start.1 = (f32[256,1024]{1,0:T(8,128)S(1)}, f32[256,1024]{1,0:T(8,128)}, u32[]{:S(2)}) copy-start(f32[256,1024]{1,0:T(8,128)} %copy-done) | copy-start | bytes 3145732
  536.2 15.3 %copy-start.17 = (f32[1024,1]{0,1:T(1,128)S(1)}, f32[1024,1]{0,1:T(1,128)}, u32[]{:S(2)}) copy-start(f32[1024,1]{0,1:T(1,128)} %copy-done.16) | copy-start | bytes 12292
  536.2 15.3 %copy-start.26 = (f32[256]{0:T(256)S(1)}, f32[256]{0:T(256)}, u32[]{:S(2)}) copy-start(f32[256]{0:T(256)} %copy-done.25) | copy-start | bytes 3076
  541.5 12.0 %copy-start.7 = (bf16[256,1024]{1,0:T(8,128)(2,1)S(1)}, bf16[256,1024]{1,0:T(8,128)(2,1)}, u32[]{:S(2)}) copy-start(bf16[256,1024]{1,0:T(8,128)(2,1)} %param.27) | copy-start | bytes 1572868
  553.9 16.2 %copy-start.14 = (bf16[256,1024]{1,0:T(8,128)(2,1)}, bf16[256,1024]{1,0:T(8,128)(2,1)S(1)}, u32[]{:S(2)}) copy-start(bf16[256,1024]{1,0:T(8,128)(2,1)S(1)} %fusion.89) | copy-start | bytes 1572868
  591.9 1.6 copy-start.31
  591.9 2.8 copy-start.6
  591.9 46.8 %copy-start.3 = (bf16[256,1024]{1,0:T(8,128)(2,1)S(1)}, bf16[256,1024]{1,0:T(8,128)(2,1)}, u32[]{:S(2)}) copy-start(bf16[256,1024]{1,0:T(8,128)(2,1)} %param.16) | copy-start | bytes 1572868
  591.9 46.8 %copy-start.21 = (f32[1024,1]{0,1:T(1,128)S(1)}, f32[1024,1]{0,1:T(1,128)}, u32[]{:S(2)}) copy-start(f32[1024,1]{0,1:T(1,128)} %copy-done.20) | copy-start | bytes 12292
  591.9 46.8 %copy-start.28 = (f32[256]{0:T(256)S(1)}, f32[256]{0:T(256)}, u32[]{:S(2)}) copy-start(f32[256]{0:T(256)} %copy-done.27) | copy-start | bytes 3076
  591.9 94.2 %all-gather.17.cloned.1.call-start = ((), (), s32[]{:S(2)}) async-start(), calls=%async_computation.25 | async-start | bytes 2621440 | tf_op jit(solution)/shard_map/all_gather | solution.py:497
  592.7 161.2 %reduce-scatter.8.cloned.1.call-start = ((), (), s32[]{:S(2)}) async-start(), calls=%async_computation.20 | async-start | bytes 2621440 | tf_op jit(solution)/shard_map/reduce_scatter | solution.py:451
  593.4 172.5 %reduce-scatter.18.cloned.1.call-start = ((), (), s32[]{:S(2)}) async-start(), calls=%async_computation.27 | async-start | bytes 110592 | tf_op jit(solution)/shard_map/reduce_scatter | solution.py:533
  640.9 165.2 %reduce-scatter.16.cloned.1.call-start = ((), (), s32[]{:S(2)}) async-start(), calls=%async_computation.26 | async-start | bytes 1179648 | tf_op jit(solution)/shard_map/reduce_scatter | solution.py:535
  689.6 166.9 %reduce-scatter.14.cloned.1.call-start = ((), (), s32[]{:S(2)}) async-start(), calls=%async_computation.24 | async-start | bytes 3538944 | tf_op jit(solution)/shard_map/reduce_scatter | solution.py:534
  689.7 4.5 copy-start.33
  697.9 3.1 copy-start.29
  697.9 3.4 copy-start.30
  708.8 4.5 copy-start.13
  708.8 4.5 copy-start.35
  715.3 3.4 copy-start.10
  715.3 4.2 copy-start.36
  719.5 2.1 copy-start.37
  719.5 9.1 %slice-start = ((s8[5767168]{0:T(1024)(128)(4,1)}), s8[4194304]{0:T(1024)(128)(4,1)S(1)}, s32[]{:S(2)}) async-start(s8[5767168]{0:T(1024)(128)(4,1)} %bitcast.187), calls=%async_computation.28 | async-start | bytes 8388608
  721.6 7.0 slice-start.1
  728.6 9.1 %copy-start.24 = (f32[12,512]{1,0:T(8,128)S(1)}, f32[12,512]{1,0:T(8,128)}, u32[]{:S(2)}) copy-start(f32[12,512]{1,0:T(8,128)} %get-tuple-element.29) | copy-start | bytes 73732
  728.6 25.3 %copy-start.8 = (bf16[256,1024]{1,0:T(8,128)(2,1)S(1)}, bf16[256,1024]{1,0:T(8,128)(2,1)}, u32[]{:S(2)}) copy-start(bf16[256,1024]{1,0:T(8,128)(2,1)} %param.27) | copy-start | bytes 1572868
Sparse Core Ops, SparseCore 0:
  10.8 29.7 all-gather.6
  43.6 47.5 all-gather.8
  93.1 26.2 all-gather.10
  132.9 46.2 all-gather.12
  180.6 44.6 all-gather.14
  471.0 43.0 reduce-scatter.9
  592.1 46.5 reduce-scatter.11
  640.8 45.2 all-gather.16
  688.4 42.5 reduce-scatter.7
  734.2 31.7 reduce-scatter.17
  770.0 36.0 reduce-scatter.15
  810.3 46.2 reduce-scatter.13

commit v2 on v1

--- a/solution.py
+++ b/solution.py
@@ -274,6 +274,279 @@
     )(lo, projected, attended, grad, lse, seg_col, seg_row, patterns, far)
 
 
+MESH = pl.DeviceIdType.MESH
+SMALL = 32
+
+
+def remote(src, dst, send, recv, axis, peer):
+    return pltpu.make_async_remote_copy(
+        src_ref=src,
+        dst_ref=dst,
+        send_sem=send,
+        recv_sem=recv,
+        device_id={axis: peer},
+        device_id_type=MESH,
+    )
+
+
+def greet(groups):
+    barrier = pltpu.get_barrier_semaphore()
+    total = 0
+    for axis, n in groups:
+        me = lax.axis_index(axis)
+        for step in range(1, n):
+            pl.semaphore_signal(
+                barrier, inc=1, device_id={axis: lax.rem(me + step, n)}, device_id_type=MESH
+            )
+        total += n - 1
+    pl.semaphore_wait(barrier, total)
+
+
+class LineSum:
+    def __init__(self, n, partial, send, recv, send_sem, recv_sem, acc, total):
+        self.n, self.partial = n, partial
+        self.send, self.recv, self.send_sem, self.recv_sem = send, recv, send_sem, recv_sem
+        self.acc, self.total = acc, total
+        self.me = lax.axis_index("tensor")
+
+    def flow(self, first, k):
+        n, me = self.n, self.me
+        near = me * 2 < n
+        right = near if first else jnp.logical_not(near)
+        block = jnp.where(right, n - 1 - k, k)
+        comes = jnp.where(right, jnp.where(me > 0, me <= block, False), jnp.where(me < n - 1, me >= block, False))
+        goes = jnp.where(right, me < block, me > block)
+        peer = jnp.clip(jnp.where(right, me + 1, me - 1), 0, n - 1)
+        out_slot = jnp.clip(jnp.where(right, k, n - 1 - me + k), 0, n - 2)
+        in_slot = jnp.clip(jnp.where(right, k, n - me + k), 0, n)
+        peer_slot = jnp.clip(jnp.where(right, k, n - peer + k), 0, n)
+        return block, comes, goes, peer, out_slot, in_slot, peer_slot
+
+    def copy(self, peer, out_slot, slot):
+        return remote(
+            self.send.at[out_slot],
+            self.recv.at[slot],
+            self.send_sem.at[out_slot],
+            self.recv_sem.at[slot],
+            "tensor",
+            peer,
+        )
+
+    def start(self):
+        for k in range(self.n - 1):
+            for first in (True, False):
+                block, comes, goes, peer, out_slot, in_slot, peer_slot = self.flow(first, k)
+
+                @pl.when(goes & jnp.logical_not(comes))
+                def _():
+                    self.send[out_slot] = self.partial(block).astype(BF16)
+                    self.copy(peer, out_slot, peer_slot).start()
+
+        self.total[...] = self.partial(self.me)
+
+    def finish(self):
+        for k in range(self.n - 1):
+            for first in (True, False):
+                block, comes, goes, peer, out_slot, in_slot, peer_slot = self.flow(first, k)
+
+                @pl.when(goes & comes)
+                def _():
+                    self.acc[...] = self.partial(block)
+                    self.copy(peer, out_slot, in_slot).wait_recv()
+                    self.send[out_slot] = (
+                        self.acc[...] + self.recv[in_slot].astype(F32)
+                    ).astype(BF16)
+                    self.copy(peer, out_slot, peer_slot).start()
+
+                @pl.when(comes & jnp.logical_not(goes))
+                def _():
+                    self.copy(peer, 0, in_slot).wait_recv()
+                    self.total[...] += self.recv[in_slot].astype(F32)
+
+    def drain(self):
+        for k in range(self.n - 1):
+            for first in (True, False):
+                block, comes, goes, peer, out_slot, in_slot, peer_slot = self.flow(first, k)
+
+                @pl.when(goes)
+                def _():
+                    self.copy(peer, out_slot, in_slot).wait_send()
+
+
+def tail_kernel(
+    n_dp,
+    n_tensor,
+    experts,
+    table_rows,
+    hidden_ref,
+    grad_ref,
+    weight_ref,
+    attended_ref,
+    branch_ref,
+    small_ref,
+    weight_own_ref,
+    gain_own_ref,
+    grad_hidden_ref,
+    grad_qkv_ref,
+    grad_out_ref,
+    small_out_ref,
+    acc,
+    line_send,
+    line_recv,
+    qkv_send,
+    qkv_recv,
+    out_send,
+    out_recv,
+    small_recv,
+    small_sum,
+    gain_recv,
+    line_send_sem,
+    line_recv_sem,
+    qkv_send_sem,
+    qkv_recv_sem,
+    out_send_sem,
+    out_recv_sem,
+    small_send_sem,
+    small_recv_sem,
+    gain_send_sem,
+    gain_recv_sem,
+):
+    own_rows = grad_hidden_ref.shape[0]
+    depth = weight_own_ref.shape[0]
+    out_cols = grad_out_ref.shape[1]
+    me = lax.axis_index("dp")
+    me_t = lax.axis_index("tensor")
+    greet([("dp", n_dp), ("tensor", n_tensor)])
+
+    def partial(block):
+        rows = pl.ds(pl.multiple_of(block * own_rows, own_rows), own_rows)
+        return nt(grad_ref[rows, :], weight_ref[...])
+
+    line = LineSum(
+        n_tensor, partial, line_send, line_recv, line_send_sem, line_recv_sem, acc, grad_hidden_ref
+    )
+    line.start()
+    copies = []
+    for step in range(1, n_dp):
+        peer = lax.rem(me + step, n_dp)
+        copy = remote(
+            small_ref.at[peer],
+            small_recv.at[step - 1],
+            small_send_sem.at[step - 1],
+            small_recv_sem.at[step - 1],
+            "dp",
+            peer,
+        )
+        copy.start()
+        copies.append(copy)
+    for block in range(n_dp):
+        cols = slice(block * depth, (block + 1) * depth)
+        qkv_send[block] = tn(hidden_ref[:, cols], grad_ref[...]).astype(BF16)
+    for step in range(1, n_dp):
+        peer = lax.rem(me + step, n_dp)
+        copy = remote(
+            qkv_send.at[peer],
+            qkv_recv.at[step - 1],
+            qkv_send_sem.at[step - 1],
+            qkv_recv_sem.at[step - 1],
+            "dp",
+            peer,
+        )
+        copy.start()
+        copies.append(copy)
+    for block in range(n_dp):
+        cols = slice(block * out_cols, (block + 1) * out_cols)
+        out_send[block] = tn(attended_ref[...], branch_ref[:, cols]).astype(BF16)
+    for step in range(1, n_dp):
+        peer = lax.rem(me + step, n_dp)
+        copy = remote(
+            out_send.at[peer],
+            out_recv.at[step - 1],
+            out_send_sem.at[step - 1],
+            out_recv_sem.at[step - 1],
+            "dp",
+            peer,
+        )
+        copy.start()
+        copies.append(copy)
+    line.finish()
+    for copy in copies:
+        copy.wait()
+    small_sum[...] = small_ref[me]
+    grad_qkv_ref[...] = qkv_send[me].astype(F32)
+    grad_out_ref[...] = out_send[me].astype(F32)
+    for step in range(1, n_dp):
+        small_sum[...] += small_recv[step - 1]
+        grad_qkv_ref[...] += qkv_recv[step - 1].astype(F32)
+        grad_out_ref[...] += out_recv[step - 1].astype(F32)
+    column = jnp.sum(grad_qkv_ref[...] * weight_own_ref[...].astype(F32), axis=1, keepdims=True)
+    eye = lax.broadcasted_iota(jnp.int32, (depth, depth), 0) == lax.broadcasted_iota(
+        jnp.int32, (depth, depth), 1
+    )
+    row = jnp.sum(jnp.where(eye, column, 0.0), axis=0, keepdims=True)
+    small_sum[experts + 1 : experts + 2, :] = row / gain_own_ref[...]
+    gains = []
+    for step in range(1, n_tensor):
+        peer = lax.rem(me_t + step, n_tensor)
+        copy = remote(
+            small_sum,
+            gain_recv.at[step - 1],
+            gain_send_sem.at[step - 1],
+            gain_recv_sem.at[step - 1],
+            "tensor",
+            peer,
+        )
+        copy.start()
+        gains.append(copy)
+    line.drain()
+    for copy in gains:
+        copy.wait()
+    small_out_ref[...] = small_sum[...]
+    shared = slice(0, experts + 2)
+    for step in range(1, n_tensor):
+        small_out_ref[shared, :] += gain_recv[step - 1, shared, :]
+
+
+def tail(n_dp, n_tensor, experts, hidden, grad, weight, attended, branch, small, weight_own, gain_own):
+    seq_len, width = hidden.shape
+    own_rows = seq_len // n_tensor
+    depth, cols = weight_own.shape
+    heads_cols = attended.shape[1]
+    out_cols = width // n_dp
+    table_rows = NB // n_dp
+    return pl.pallas_call(
+        functools.partial(tail_kernel, n_dp, n_tensor, experts, table_rows),
+        out_shape=(
+            jax.ShapeDtypeStruct((own_rows, width), F32),
+            jax.ShapeDtypeStruct((depth, cols), F32),
+            jax.ShapeDtypeStruct((heads_cols, out_cols), F32),
+            jax.ShapeDtypeStruct((SMALL, depth), F32),
+        ),
+        in_specs=[vspec()] * 8,
+        out_specs=(vspec(),) * 4,
+        scratch_shapes=[
+            pltpu.VMEM((own_rows, width), F32),
+            pltpu.VMEM((n_tensor - 1, own_rows, width), BF16),
+            pltpu.VMEM((n_tensor + 1, own_rows, width), BF16),
+            pltpu.VMEM((n_dp, depth, cols), BF16),
+            pltpu.VMEM((n_dp - 1, depth, cols), BF16),
+            pltpu.VMEM((n_dp, heads_cols, out_cols), BF16),
+            pltpu.VMEM((n_dp - 1, heads_cols, out_cols), BF16),
+            pltpu.VMEM((n_dp - 1, SMALL, depth), F32),
+            pltpu.VMEM((SMALL, depth), F32),
+            pltpu.VMEM((n_tensor - 1, SMALL, depth), F32),
+            pltpu.SemaphoreType.DMA((n_tensor - 1,)),
+            pltpu.SemaphoreType.DMA((n_tensor + 1,)),
+        ]
+        + [pltpu.SemaphoreType.DMA((n_dp - 1,))] * 6
+        + [pltpu.SemaphoreType.DMA((n_tensor - 1,))] * 2,
+        compiler_params=pltpu.CompilerParams(
+            vmem_limit_bytes=VMEM_LIMIT, collective_id=0, has_side_effects=True
+        ),
+        name="tail",
+    )(hidden, grad, weight, attended, branch, small, weight_own, gain_own)
+
+
 def rms_scale(values):
     return lax.rsqrt(jnp.mean(values * values, axis=-1, keepdims=True) + EPS)
 
@@ -495,7 +768,6 @@
         0,
     ).reshape(seq_len, head_cols)
     grad_branch_all = lax.all_gather(grad_branch, "tensor", axis=0, tiled=True)
-    grad_w_attn_out = tn(attended, grad_branch_all)
     grad_projected, diag = attention_backward(
         projected,
         attended,
@@ -514,35 +786,42 @@
         jnp.asarray(skew_selectors()), near, (((0,), (0,)), ((), ())), precision=highest
     )
     grad_table = grad_table.at[NB - 1].add(jnp.sum(diag[:, 2], axis=1))
-    grad_w_qkv = tn(gathered_one, grad_projected).reshape(model_width, 3, head_cols)
-    grad_hidden_one = lax.psum_scatter(
-        nt(grad_projected, qkv_matrix).astype(BF16),
-        "tensor",
-        scatter_dimension=0,
-        tiled=True,
-    ).astype(F32)
-    grad_from_first, grad_gain_one = norm_backward(
-        grad_hidden_one, tokens_float, scale_one, gain_one
-    )
+    small = jnp.concatenate(
+        [
+            jnp.transpose(grad_router_part),
+            grad_gain_two[None],
+            jnp.zeros((SMALL - experts - 1, model_width), F32),
+        ],
+        axis=0,
+    )
+    small = jnp.transpose(small.reshape(SMALL, n_dp, depth), (1, 0, 2))
+    small = lax.dynamic_update_slice(
+        small, grad_table.reshape(n_dp, NB // n_dp, heads), (0, experts + 2, 0)
+    )
+    grad_hidden_one, reduced_qkv, reduced_attn_out, small_sum = tail(
+        n_dp,
+        n_tensor,
+        experts,
+        gathered_one,
+        grad_projected,
+        qkv_matrix,
+        attended,
+        grad_branch_all,
+        small,
+        w_qkv.reshape(depth, 3 * head_cols),
+        gain_attn[None].astype(F32),
+    )
+    grad_from_first, _ = norm_backward(grad_hidden_one, tokens_float, scale_one, gain_one)
     grad_tokens = (grad_residual + grad_from_first).astype(BF16)
-
-    small = jnp.concatenate(
-        [grad_router_part, grad_gain_one[:, None], grad_gain_two[:, None]], axis=1
-    )
-    small = lax.psum(small, "tensor")
-    small = lax.psum_scatter(small, "dp", scatter_dimension=0, tiled=True)
-    reduced_qkv = lax.psum_scatter(grad_w_qkv, "dp", scatter_dimension=0, tiled=True)
-    reduced_attn_out = lax.psum_scatter(grad_w_attn_out, "dp", scatter_dimension=1, tiled=True)
-    reduced_table = lax.psum_scatter(grad_table, "dp", scatter_dimension=0, tiled=True)
     return (
         layer_out,
         grad_tokens,
-        reduced_qkv,
+        reduced_qkv.reshape(depth, 3, head_cols),
         reduced_attn_out,
-        reduced_table,
-        small[:, experts],
-        small[:, experts + 1],
-        small[:, :experts],
+        small_sum[experts + 2 : experts + 2 + NB // n_dp, :heads],
+        small_sum[experts + 1],
+        small_sum[experts],
+        jnp.transpose(small_sum[:experts]),
         grad_w_in,
         grad_w_out,
     )

time: 874 us -> 724 us (0.83)
  waiting for transfers between devices: 394 us -> 222 us
  Pallas kernels: 29 us -> 89.4 us
  blocking collectives: 108 us -> 61.2 us
  matrix products: 118 us -> 107 us
  other arithmetic: 56.2 us -> 65.5 us
    reduce_scatter x4 -> x0, waiting for transfers between devices: 123 us -> none  [the longest x1 50.4 us: on_device(): lax.psum_scatter(grad_w_qkv, 'dp', scatter_dimension=0, tiled=True)]
    pallas_call x0 -> x1, Pallas kernels: none -> 55.1 us  [tail(): pl.pallas_call(functools.partial(tail_kernel, n_dp, n_tensor, experts, ta...]
    all_gather x1, waiting for transfers between devices: 45.2 us -> 0.02 us  [on_device(): grad_branch_all = lax.all_gather(grad_branch, 'tensor', axis=0, tiled=True)]
    psum x1 -> x0, blocking collectives: 19.3 us -> none  [on_device(): small = lax.psum(small, 'tensor')]
    unnamed x1 -> x0, blocking collectives: 13.6 us -> none
    all_to_all x1 -> x0, blocking collectives: 13.6 us -> none  [on_device(): lax.all_to_all(jnp.transpose(grad_attended_own.reshape(own_rows, n_tensor...]
    dot_general x8 -> x7, matrix products: 46.4 us -> 39.6 us  [nt(): lax.dot_general(a, b, (((1,), (1,)), ((), ())), preferred_element_type=F32)]
    dot_general x8 -> x6, matrix products: 27.7 us -> 24.2 us  [tn(): lax.dot_general(a, b, (((0,), (0,)), ((), ())), preferred_element_type=F32)]
  transfers between devices with their start and end apart: 20 -> 17, of which waited for: 16 -> 11; matrix products, arithmetic and copies ran while one was open for 30% -> 37% of each run, Pallas kernels for 1% -> 13%
where the time goes in v2:
time: 724 us; the launch traced here: 713 us
  waiting for transfers between devices  222 us (31%)
  local copies, waits for them, and re-layouts  114 us (16%)
  matrix products  107 us (15%)
  Pallas kernels  89.4 us (12%)
  other arithmetic  65.5 us (9%)
  blocking collectives  61.2 us (8%)
  starting transfers between devices  38.7 us (5%)
  between operations  15.2 us (2%)
    all_to_all x4, waiting for transfers between devices, give_back(): lax.all_to_all(part.reshape(n_dp, capacity, model_width), 'dp', 0, 0)  70.4 us
    pallas_call x1, Pallas kernels, tail(): pl.pallas_call(functools.partial(tail_kernel, n_dp, n_tensor, experts, ta...  55.1 us
    dot_general x7, matrix products, nt(): lax.dot_general(a, b, (((1,), (1,)), ((), ())), preferred_element_type=F32)  39.6 us
    all_to_all x1, blocking collectives, exchange(): lax.all_to_all(parts[:, i], 'dp', 0, 0)  35.8 us
    all_gather x1, waiting for transfers between devices, on_device(): gathered_two = lax.all_gather(hidden_two, 'tensor', axis=0, tiled=True)  30.5 us
    dot_general x6, matrix products, nn(): lax.dot_general(a, b, (((1,), (0,)), ((), ())), preferred_element_type=F32)  29.7 us
    all_gather x1, waiting for transfers between devices, on_device(): lax.all_gather(jnp.concatenate([w_qkv.reshape(depth, 3 * head_cols), extr...  28.3 us
    all_gather x1, waiting for transfers between devices, on_device(): gathered_one = lax.all_gather(hidden_one, 'tensor', axis=0, tiled=True)  28.2 us
  transfers between devices with their start and end apart: 17, of which 11 were waited for; matrix products, arithmetic and copies ran while one was open for 37% of the time, Pallas kernels for 13%

profile of v2, /device:TPU:0, one launch (start us, length us, event | category | flops | bytes accessed | tf_op | source)
XLA Modules:
  0.0 713.3 jit_solution(16080782301923907678)
XLA Ops:
  12.3 28.3 %all-gather.7.cloned.1.call-done = bf16[1024,896]{1,0:T(8,128)(2,1)} async-done(((bf16[128,896]{1,0:T(8,128)(2,1)}), bf16[1024,896]{1,0:T(8,128)(2,1)}) %all-gather.7.cloned.1.call-update) | async-done | bytes 1835024 | tf_op jit(solution)/shard_map/all_gather | solution.py:616
  43.3 15.6 %all_gather.23 = bf16[1024,128]{1,0:T(8,128)(2,1)} all-gather(bf16[256,128]{1,0:T(8,128)(2,1)S(1)} %copy-done.25), channel_id=1, replica_groups=mesh['dp'=8,'tensor'=4] {'tensor'}, dimensions={0}, use_global_device_ids=true | all-gather | bytes 327680 | tf_op jit(solution)/shard_map/all_gather | solution.py:632
  62.8 28.2 %all-gather.9.cloned.1.call-done.hidden_ref = bf16[1024,1024]{1,0:T(8,128)(2,1)} async-done(((bf16[256,1024]{1,0:T(8,128)(2,1)}), bf16[1024,1024]{1,0:T(8,128)(2,1)}) %all-gather.9.cloned.1.call-update) | async-done | bytes 2097168 | tf_op jit(solution)/shard_map/all_gather | solution.py:638
  91.0 4.5 convolution_convert_fusion.2.qkv_ref
  95.5 14.4 %attn_fwd.1 = (bf16[1024,256]{1,0:T(8,128)(2,1)}, f32[1024,4]{1,0:T(8,128)}) custom-call(s32[4]{0:T(128)} %convert_reduce_fusion.3.lo_ref, bf16[1024,768]{1,0:T(8,128)(2,1)} %convolution_convert_fusion.2.qkv_ref, s32[1024,1]{1,0:T(8,128)} %copy.125.seg_col_ref, s32[1,1024]{1,0:T(1,128)} %seg_row_ref.3, f32[8,512]{1,0:T(8,128)} %reshape.286.pattern_ref, ...), custom_call_target="tpu_custom_call" | custom-call | tf_op jit(solution)/shard_map/attn_fwd/pallas_call | solution.py:240
  112.0 3.5 all-to-all-start
  115.5 3.7 all-gather.11.cloned.1.call-done
  119.2 8.9 %all-to-all-done = bf16[4,256,256]{1,2,0:T(8,128)(2,1)S(1)} async-done(((bf16[4,256,256]{1,2,0:T(8,128)(2,1)}), bf16[4,256,256]{1,2,0:T(8,128)(2,1)S(1)}, u32[]{:S(2)}, u32[]{:S(2)}) %all-to-all-start) | async-done | bytes 524320 | tf_op jit(solution)/shard_map/all_to_all | solution.py:654
  133.9 4.6 reduce-window.6
  140.5 8.1 %scatter_custom_fusion = s32[2560]{0:T(1024)S(1)} fusion(s32[2048]{0:T(1024)S(1)} %bitcast.220, s32[2048]{0:T(1024)S(1)} %reshape.366, s32[]{:T(128)} %constant.84.clone.1), kind=kCustom, calls=%fused_computation.171 | custom fusion | bytes 10244 | tf_op jit(solution)/shard_map/scatter | solution.py:680
  148.6 30.5 %all-gather.13.cloned.1.call-done = bf16[1024,1024]{1,0:T(8,128)(2,1)} async-done(((bf16[256,1024]{1,0:T(8,128)(2,1)}), bf16[1024,1024]{1,0:T(8,128)(2,1)}) %all-gather.13.cloned.1.call-update) | async-done | bytes 2097168 | tf_op jit(solution)/shard_map/all_gather | solution.py:662
  180.8 8.8 %gather_fusion = bf16[2560,1024]{1,0:T(8,128)(2,1)} fusion(bf16[1025,1024]{1,0:T(8,128)(2,1)S(1)} %concatenate.24, s32[3072]{0:T(1024)S(1)} %pad_clamp_fusion), kind=kCustom, calls=%fused_computation | custom fusion | bytes 10496000 | tf_op jit(solution)/shard_map/gather | solution.py:698
  189.6 5.7 slice_bitcast_fusion.3
  195.3 4.6 all-to-all-start.3
  199.9 25.3 %all-gather.15.cloned.1.call-done = bf16[1024,1024]{1,0:T(8,128)(2,1)} async-done(((bf16[256,1024]{1,0:T(8,128)(2,1)}), bf16[1024,1024]{1,0:T(8,128)(2,1)}) %all-gather.15.cloned.1.call-update) | async-done | bytes 2097168 | tf_op jit(solution)/shard_map/all_gather | solution.py:682
  227.0 8.8 %gather_fusion.3 = bf16[2560,1024]{1,0:T(8,128)(2,1)} fusion(bf16[1025,1024]{1,0:T(8,128)(2,1)S(1)} %concatenate.25, s32[3072]{0:T(1024)S(1)} %pad_clamp_fusion), kind=kCustom, calls=%fused_computation.3 | custom fusion | bytes 10496000 | tf_op jit(solution)/shard_map/gather | solution.py:700
  238.7 8.1 %scatter_custom_fusion.1 = f32[2560]{0:T(1024)S(1)} fusion(s32[2048]{0:T(1024)S(1)} %bitcast.221, f32[2048]{0:T(1024)S(1)} %reshape.374, f32[]{:T(128)} %constant.79.clone.1), kind=kCustom, calls=%fused_computation.169 | custom fusion | bytes 10244 | tf_op jit(solution)/shard_map/scatter | solution.py:681
  246.8 3.4 fusion
  252.4 35.8 %all_to_all.50 = bf16[8,160,1024]{2,1,0:T(8,128)(2,1)} all-to-all(bf16[8,160,1024]{2,1,0:T(8,128)(2,1)S(1)} %get-tuple-element.107), channel_id=1, replica_groups=mesh['dp'=8,'tensor'=4] {'dp'}, dimensions={0} | all-to-all | bytes 5242880 | tf_op jit(solution)/shard_map/all_to_all | solution.py:687
  288.2 3.6 all-to-all-start.1
  291.8 6.0 fusion.30
  297.8 6.0 fusion.26
  303.9 20.1 %all-to-all-done.1 = bf16[8,160,1024]{2,1,0:T(8,128)(2,1)S(1)} async-done(((bf16[8,160,1024]{2,1,0:T(8,128)(2,1)}), bf16[8,160,1024]{2,1,0:T(8,128)(2,1)S(1)}, u32[]{:S(2)}, u32[]{:S(2)}) %all-to-all-start.1) | async-done | bytes 2621472 | tf_op jit(solution)/shard_map/all_to_all | solution.py:687
  325.5 5.1 all-to-all-start.5
  330.6 8.3 %multiply_convert_fusion = (bf16[1280,704]{0,1:T(8,128)(2,1)S(1)}, bf16[1280,704]{0,1:T(8,128)(2,1)S(1)}, bf16[1280,704]{0,1:T(8,128)(2,1)}) fusion(f32[1280,704]{0,1:T(8,128)} %fusion.30, f32[1280,704]{0,1:T(8,128)} %fusion.26, bf16[1280,1024]{1,0:T(8,128)(2,1)S(1)} %bitcast.190, bf16[2,704,1024]{2,1,0:T(8,128)(2,1)} %param.26), kind=kOutput, calls=%fused_computation.47 | convolution fusion | flops 1868922880 | bytes 16678912 | tf_op jit(solution)/shard_map/dot_general | solution.py:63
  338.9 4.8 fusion.28
  343.8 5.4 fusion.40
  349.2 3.9 fusion.36
  353.1 3.8 add_convert_fusion
  356.9 6.0 all-to-all-done.5
  362.9 3.8 all-to-all-start.8
  366.7 9.2 %multiply_convert_fusion.1 = (bf16[1280,704]{0,1:T(8,128)(2,1)S(1)}, bf16[1280,704]{0,1:T(8,128)(2,1)S(1)}, bf16[1280,704]{0,1:T(8,128)(2,1)}) fusion(f32[1280,704]{0,1:T(8,128)} %fusion.40, f32[1280,704]{0,1:T(8,128)} %fusion.36, bf16[1280,1024]{1,0:T(8,128)(2,1)} %bitcast.34, bf16[2,704,1024]{2,1,0:T(8,128)(2,1)} %param.26), kind=kOutput, calls=%fused_computation.48 | convolution fusion | flops 1868922880 | bytes 16678912 | tf_op jit(solution)/shard_map/dot_general | solution.py:63
  375.9 4.6 fusion.38
  380.5 5.1 add_convert_fusion.1
  385.7 13.2 %all-to-all-done.8 = bf16[8,160,1024]{2,1,0:T(8,128)(2,1)S(1)} async-done(((bf16[8,160,1024]{2,1,0:T(8,128)(2,1)}), bf16[8,160,1024]{2,1,0:T(8,128)(2,1)S(1)}, u32[]{:S(2)}, u32[]{:S(2)}) %all-to-all-start.8) | async-done | bytes 2621472 | tf_op jit(solution)/shard_map/all_to_all | solution.py:693
  400.4 4.4 all-to-all-start.6
  404.8 5.6 convolution_convert_fusion
  410.4 26.6 %all-to-all-done.6 = bf16[8,160,1024]{2,1,0:T(8,128)(2,1)} async-done(((bf16[8,160,1024]{2,1,0:T(8,128)(2,1)}), bf16[8,160,1024]{2,1,0:T(8,128)(2,1)}, u32[]{:S(2)}, u32[]{:S(2)}) %all-to-all-start.6) | async-done | bytes 2621472 | tf_op jit(solution)/shard_map/all_to_all | solution.py:693
  437.0 3.6 all-to-all-start.4
  444.5 3.3 copy.132
  447.8 9.2 %gather_fusion.5 = bf16[1024,1024]{1,0:T(8,128)(2,1)} fusion(bf16[2560,1024]{1,0:T(8,128)(2,1)} %bitcast.182, s32[1024]{0:T(1024)S(1)} %get-tuple-element.126), kind=kCustom, calls=%fused_computation.5 | custom fusion | bytes 4198400 | tf_op jit(solution)/shard_map/gather | solution.py:740
  457.0 9.2 %gather_fusion.4 = bf16[1024,1024]{1,0:T(8,128)(2,1)} fusion(bf16[2560,1024]{1,0:T(8,128)(2,1)} %bitcast.183, s32[1024]{0:T(1024)S(1)} %get-tuple-element.127), kind=kCustom, calls=%fused_computation.4 | custom fusion | bytes 4198400 | tf_op jit(solution)/shard_map/gather | solution.py:740
  466.2 4.5 add_convert_fusion.2
  470.7 5.6 convolution_convert_fusion.1
  476.4 4.5 all-to-all-start.2
  482.6 30.6 %all-to-all-done.2 = bf16[8,160,1024]{2,1,0:T(8,128)(2,1)} async-done(((bf16[8,160,1024]{2,1,0:T(8,128)(2,1)}), bf16[8,160,1024]{2,1,0:T(8,128)(2,1)}, u32[]{:S(2)}, u32[]{:S(2)}) %all-to-all-start.2) | async-done | bytes 2621472 | tf_op jit(solution)/shard_map/all_to_all | solution.py:693
  515.5 3.3 copy.130
  518.8 8.1 %gather_fusion.1 = bf16[1024,1024]{1,0:T(8,128)(2,1)S(1)} fusion(bf16[2560,1024]{1,0:T(8,128)(2,1)} %bitcast.180, s32[1024]{0:T(1024)S(1)} %get-tuple-element.127), kind=kCustom, calls=%fused_computation.1 | custom fusion | bytes 4198400 | tf_op jit(solution)/shard_map/gather | solution.py:722
  526.9 9.2 %gather_fusion.2 = bf16[1024,1024]{1,0:T(8,128)(2,1)} fusion(bf16[2560,1024]{1,0:T(8,128)(2,1)} %bitcast.181, s32[1024]{0:T(1024)S(1)} %get-tuple-element.126), kind=kCustom, calls=%fused_computation.2 | custom fusion | bytes 4198400 | tf_op jit(solution)/shard_map/gather | solution.py:723
  536.1 5.3 fusion.3
  541.4 9.8 %psum.7 = f32[1024,2]{0,1:T(2,128)S(1)} all-reduce(f32[1024,2]{0,1:T(2,128)S(1)} %pad_maximum_fusion.4), channel_id=1, replica_groups=mesh['dp'=8,'tensor'=4] {'tensor'}, use_global_device_ids=true, to_apply=%region_16.17 | all-reduce | flops 2048 | bytes 16384 | tf_op jit(solution)/shard_map/psum | solution.py:746
  558.4 4.0 convolution_bitcast_fusion.2
  562.5 3.8 convolution_bitcast_fusion.3
  566.3 3.4 maximum_bitcast_fusion.1
  570.5 3.6 convolution_bitcast_fusion.4
  574.1 3.6 convolution_bitcast_fusion.5
  577.8 6.4 maximum_bitcast_fusion
  584.2 3.6 convolution_bitcast_fusion
  587.8 5.6 convolution_bitcast_fusion.1
  595.1 4.3 all-to-all-start.9
  599.4 6.2 pad_maximum_fusion.1
  605.7 11.3 %pad_maximum_fusion = f32[2,2,704,1024]{3,2,1,0:T(8,128)} fusion(f32[1,2,704,1024]{3,2,1,0:T(8,128)} %maximum_bitcast_fusion.1, f32[1,2,704,1024]{3,2,1,0:T(8,128)} %maximum_bitcast_fusion), kind=kLoop, calls=%fused_computation.8 | loop fusion | flops 2883584 | bytes 23068672 | tf_op jit(solution)/shard_map/stack | solution.py:716
  617.4 19.9 %attn_bwd.1 = (bf16[1024,768]{1,0:T(8,128)(2,1)}, f32[12,512]{1,0:T(8,128)}) custom-call(s32[4]{0:T(128)} %convert_reduce_fusion.3.lo_ref, bf16[1024,768]{1,0:T(8,128)(2,1)} %convolution_convert_fusion.2.qkv_ref, bf16[1024,256]{1,0:T(8,128)(2,1)} %get-tuple-element.30.out_ref.attended_ref, bf16[1024,256]{1,0:T(8,128)(2,1)} %bitcast.45.grad_ref, ...), custom_call_target="tpu_custom_call" | custom-call | tf_op jit(solution)/shard_map/attn_bwd/pallas_call | solution.py:258
  640.1 55.1 %tail.1 = (f32[256,1024]{1,0:T(8,128)}, f32[128,768]{1,0:T(8,128)}, f32[256,128]{1,0:T(8,128)}, f32[32,128]{1,0:T(8,128)}) custom-call(bf16[1024,1024]{1,0:T(8,128)(2,1)} %all-gather.9.cloned.1.call-done.hidden_ref, bf16[1024,768]{1,0:T(8,128)(2,1)} %get-tuple-element.32.grad_ref, bf16[1024,768]{1,0:T(8,128)(2,1)} %slice.165.weight_ref, ...), custom_call_target="tpu_custom_call" | custom-call | tf_op jit(solution)/shard_map/tail/pallas_call | solution.py:517
  (219 shorter events, 64.4 us)
Async XLA Ops:
  7.2 35.1 %copy-start.2 = (bf16[256,1024]{1,0:T(8,128)(2,1)S(1)}, bf16[256,1024]{1,0:T(8,128)(2,1)}, u32[]{:S(2)}) copy-start(bf16[256,1024]{1,0:T(8,128)(2,1)} %param.16) | copy-start | bytes 1572868
  7.2 36.1 %copy-start.25 = (bf16[256,128]{1,0:T(8,128)(2,1)S(1)}, bf16[256,128]{1,0:T(8,128)(2,1)}, u32[]{:S(2)}) copy-start(bf16[256,128]{1,0:T(8,128)(2,1)} %param.20) | copy-start | bytes 196612
  7.2 51.8 %copy-start.27 = (s32[1,1024]{1,0:T(1,128)S(1)}, s32[1,1024]{1,0:T(1,128)}, u32[]{:S(2)}) copy-start(s32[1,1024]{1,0:T(1,128)} %seg_row_ref.3) | copy-start | bytes 12292
  7.2 33.4 %all-gather.7.cloned.1.call-start = ((), (), s32[]{:S(2)}) async-start(), calls=%async_computation.12 | async-start | bytes 2064384 | tf_op jit(solution)/shard_map/all_gather | solution.py:616
  10.0 51.0 %copy-start.19 = (f32[1024,32]{1,0:T(8,128)S(1)}, f32[1024,32]{1,0:T(8,128)}, u32[]{:S(2)}) copy-start(f32[1024,32]{1,0:T(8,128)} %constant.99.clone) | copy-start | bytes 393220
  10.2 2.1 copy-start.16
  11.0 80.0 %all-gather.9.cloned.1.call-start = ((), (), s32[]{:S(2)}) async-start(), calls=%async_computation.13 | async-start | bytes 2621440 | tf_op jit(solution)/shard_map/all_gather | solution.py:638
  12.3 83.3 %copy-start.30 = (f32[256]{0:T(256)}, f32[256]{0:T(256)S(1)}, u32[]{:S(2)}) copy-start(f32[256]{0:T(256)S(1)} %add_rsqrt_fusion.1) | copy-start | bytes 3076
  40.6 20.3 %slice-start = ((bf16[1024,896]{1,0:T(8,128)(2,1)}), bf16[1024,128]{1,0:T(8,128)(2,1)S(1)}, s32[]{:S(2)}) async-start(bf16[1024,896]{1,0:T(8,128)(2,1)} %all-gather.7.cloned.1.call-done), calls=%async_computation.20 | async-start | bytes 524288 | tf_op jit(solution)/shard_map/slice | solution.py:623
  40.6 50.4 %copy-start.7 = (bf16[1024,896]{1,0:T(8,128)(2,1)S(1)}, bf16[1024,896]{1,0:T(8,128)(2,1)}, u32[]{:S(2)}) copy-start(bf16[1024,896]{1,0:T(8,128)(2,1)} %all-gather.7.cloned.1.call-done) | copy-start | bytes 5505028
  42.2 53.3 %copy-start.23 = (f32[1024]{0:T(1024)}, f32[1024]{0:T(1024)S(1)}, u32[]{:S(2)}) copy-start(f32[1024]{0:T(1024)S(1)} %get-tuple-element.93) | copy-start | bytes 12292
  42.2 88.3 %copy-start.21 = (f32[1024]{0:T(1024)}, f32[1024]{0:T(1024)S(1)}, u32[]{:S(2)}) copy-start(f32[1024]{0:T(1024)S(1)} %get-tuple-element.92) | copy-start | bytes 12292
  43.2 75.9 %all-gather.11.cloned.1.call-start = ((), (), s32[]{:S(2)}) async-start(), calls=%async_computation.14 | async-start | bytes 2359296 | tf_op jit(solution)/shard_map/all_gather | solution.py:633
  112.0 16.1 %all-to-all-start = ((bf16[4,256,256]{1,2,0:T(8,128)(2,1)}), bf16[4,256,256]{1,2,0:T(8,128)(2,1)S(1)}, u32[]{:S(2)}, u32[]{:S(2)}) async-start(bf16[4,256,256]{1,2,0:T(8,128)(2,1)} %copy.126), calls=%async_computation | async-start | bytes 1048576 | tf_op jit(solution)/shard_map/all_to_all | solution.py:654
  115.5 63.6 %all-gather.13.cloned.1.call-start = ((), (), s32[]{:S(2)}) async-start(), calls=%async_computation.15 | async-start | bytes 2621440 | tf_op jit(solution)/shard_map/all_gather | solution.py:662
  128.1 5.0 copy-start.26
  130.5 1.0 copy-start
  130.5 8.7 %copy-start.28 = (f32[256]{0:T(256)}, f32[256]{0:T(256)S(1)}, u32[]{:S(2)}) copy-start(f32[256]{0:T(256)S(1)} %add_rsqrt_fusion) | copy-start | bytes 3076
  132.5 92.7 %all-gather.15.cloned.1.call-start = ((), (), s32[]{:S(2)}) async-start(), calls=%async_computation.17 | async-start | bytes 2621440 | tf_op jit(solution)/shard_map/all_gather | solution.py:682
  195.3 57.1 %all-to-all-start.3 = ((bf16[8,160,1024]{2,1,0:T(8,128)(2,1)}), bf16[8,160,1024]{2,1,0:T(8,128)(2,1)}, u32[]{:S(2)}, u32[]{:S(2)}) async-start(bf16[8,160,1024]{2,1,0:T(8,128)(2,1)} %get-tuple-element.109), calls=%async_computation.3 | async-start | bytes 5242880 | tf_op jit(solution)/shard_map/all_to_all | solution.py:687
  288.2 35.8 %all-to-all-start.1 = ((bf16[8,160,1024]{2,1,0:T(8,128)(2,1)}), bf16[8,160,1024]{2,1,0:T(8,128)(2,1)S(1)}, u32[]{:S(2)}, u32[]{:S(2)}) async-start(bf16[8,160,1024]{2,1,0:T(8,128)(2,1)} %get-tuple-element.108), calls=%async_computation.1 | async-start | bytes 5242880 | tf_op jit(solution)/shard_map/all_to_all | solution.py:687
  324.0 1.5 copy-start.11
  325.5 5.1 copy-start.9
  325.5 37.4 %all-to-all-start.5 = ((bf16[8,160,1024]{2,1,0:T(8,128)(2,1)}), bf16[8,160,1024]{2,1,0:T(8,128)(2,1)}, u32[]{:S(2)}, u32[]{:S(2)}) async-start(bf16[8,160,1024]{2,1,0:T(8,128)(2,1)} %get-tuple-element.106), calls=%async_computation.6 | async-start | bytes 5242880 | tf_op jit(solution)/shard_map/all_to_all | solution.py:687
  338.9 4.9 copy-start.34
  338.9 14.2 %copy-start.40 = (bf16[1280,704]{0,1:T(8,128)(2,1)}, bf16[1280,704]{0,1:T(8,128)(2,1)S(1)}, u32[]{:S(2)}) copy-start(bf16[1280,704]{0,1:T(8,128)(2,1)S(1)} %get-tuple-element.103) | copy-start | bytes 5406724
  338.9 4.9 copy-start.12
  338.9 10.3 %slice-start.1 = ((s8[5767168]{0:T(1024)(128)(4,1)}), s8[4194304]{0:T(1024)(128)(4,1)S(1)}, s32[]{:S(2)}) async-start(s8[5767168]{0:T(1024)(128)(4,1)} %bitcast.225), calls=%async_computation.21 | async-start | bytes 8388608
  343.8 5.4 slice-start.2
  362.9 36.0 %all-to-all-start.8 = ((bf16[8,160,1024]{2,1,0:T(8,128)(2,1)}), bf16[8,160,1024]{2,1,0:T(8,128)(2,1)S(1)}, u32[]{:S(2)}, u32[]{:S(2)}) async-start(bf16[8,160,1024]{2,1,0:T(8,128)(2,1)} %bitcast.198), calls=%async_computation.9 | async-start | bytes 5242880 | tf_op jit(solution)/shard_map/all_to_all | solution.py:693
  375.9 4.7 copy-start.36
  375.9 4.7 copy-start.42
  398.9 1.5 copy-start.4
  400.4 36.7 %all-to-all-start.6 = ((bf16[8,160,1024]{2,1,0:T(8,128)(2,1)}), bf16[8,160,1024]{2,1,0:T(8,128)(2,1)}, u32[]{:S(2)}, u32[]{:S(2)}) async-start(bf16[8,160,1024]{2,1,0:T(8,128)(2,1)} %bitcast.199), calls=%async_computation.7 | async-start | bytes 5242880 | tf_op jit(solution)/shard_map/all_to_all | solution.py:693
  437.0 39.3 %all-to-all-start.4 = ((bf16[8,160,1024]{2,1,0:T(8,128)(2,1)}), bf16[8,160,1024]{2,1,0:T(8,128)(2,1)S(1)}, u32[]{:S(2)}, u32[]{:S(2)}) async-start(bf16[8,160,1024]{2,1,0:T(8,128)(2,1)} %bitcast.196), calls=%async_computation.4 | async-start | bytes 5242880 | tf_op jit(solution)/shard_map/all_to_all | solution.py:693
  440.7 110.7 %reduce-scatter.5.cloned.1.call-start = ((), (), s32[]{:S(2)}) async-start(), calls=%async_computation.18 | async-start | bytes 2621440 | tf_op jit(solution)/shard_map/reduce_scatter | solution.py:742
  476.4 4.9 copy-start.5
  476.4 36.8 %all-to-all-start.2 = ((bf16[8,160,1024]{2,1,0:T(8,128)(2,1)}), bf16[8,160,1024]{2,1,0:T(8,128)(2,1)}, u32[]{:S(2)}, u32[]{:S(2)}) async-start(bf16[8,160,1024]{2,1,0:T(8,128)(2,1)} %bitcast.197), calls=%async_computation.2 | async-start | bytes 5242880 | tf_op jit(solution)/shard_map/all_to_all | solution.py:693
  481.0 158.5 %all-gather.17.cloned.1.call-start = ((), (), s32[]{:S(2)}) async-start(), calls=%async_computation.19 | async-start | bytes 2621440 | tf_op jit(solution)/shard_map/all_gather | solution.py:770
  536.1 15.3 %copy-start.1 = (f32[256,1024]{1,0:T(8,128)S(1)}, f32[256,1024]{1,0:T(8,128)}, u32[]{:S(2)}) copy-start(f32[256,1024]{1,0:T(8,128)} %copy-done) | copy-start | bytes 3145732
  536.1 15.3 %copy-start.22 = (f32[1024]{0:T(1024)S(1)}, f32[1024]{0:T(1024)}, u32[]{:S(2)}) copy-start(f32[1024]{0:T(1024)} %copy-done.21) | copy-start | bytes 12292
  536.1 15.3 %copy-start.29 = (f32[256]{0:T(256)S(1)}, f32[256]{0:T(256)}, u32[]{:S(2)}) copy-start(f32[256]{0:T(256)} %copy-done.28) | copy-start | bytes 3076
  541.4 12.1 %copy-start.8 = (bf16[256,1024]{1,0:T(8,128)(2,1)S(1)}, bf16[256,1024]{1,0:T(8,128)(2,1)}, u32[]{:S(2)}) copy-start(bf16[256,1024]{1,0:T(8,128)(2,1)} %param.27) | copy-start | bytes 1572868
  551.3 3.9 copy-start.33
  553.5 4.9 copy-start.32
  554.6 148.1 %reduce-scatter.3.cloned.1.call-start = ((), (), s32[]{:S(2)}) async-start(), calls=%async_computation.16 | async-start | bytes 2621440 | tf_op jit(solution)/shard_map/reduce_scatter | solution.py:724
  555.2 3.3 copy-start.41
  558.4 4.0 copy-start.35
  566.3 3.4 copy-start.13
  566.3 4.3 copy-start.43
  570.5 3.6 copy-start.37
  577.8 6.4 copy-start.10
  577.8 6.4 copy-start.38
  584.2 3.6 copy-start.39
  587.8 5.6 copy-start.14
  587.8 5.6 copy-start.15
  595.1 22.2 %all-to-all-start.9 = ((bf16[4,256,256]{2,1,0:T(8,128)(2,1)}), bf16[4,256,256]{2,1,0:T(8,128)(2,1)}, u32[]{:S(2)}, u32[]{:S(2)}) async-start(bf16[4,256,256]{2,1,0:T(8,128)(2,1)} %bitcast.177), calls=%async_computation.11 | async-start | bytes 1048576 | tf_op jit(solution)/shard_map/all_to_all | solution.py:764
  605.7 11.3 %copy-start.6 = (bf16[256,1024]{1,0:T(8,128)(2,1)S(1)}, bf16[256,1024]{1,0:T(8,128)(2,1)}, u32[]{:S(2)}) copy-start(bf16[256,1024]{1,0:T(8,128)(2,1)} %multiply_convert_fusion.4) | copy-start | bytes 1572868
  617.3 21.1 %copy-start.18 = (f32[1024,32]{1,0:T(8,128)S(1)}, f32[1024,32]{1,0:T(8,128)}, u32[]{:S(2)}) copy-start(f32[1024,32]{1,0:T(8,128)} %constant.100.clone) | copy-start | bytes 393220
  639.5 0.7 copy-start.17
  640.1 58.5 %copy-start.3 = (bf16[256,1024]{1,0:T(8,128)(2,1)S(1)}, bf16[256,1024]{1,0:T(8,128)(2,1)}, u32[]{:S(2)}) copy-start(bf16[256,1024]{1,0:T(8,128)(2,1)} %param.16) | copy-start | bytes 1572868
  640.1 58.5 %copy-start.24 = (f32[1024]{0:T(1024)S(1)}, f32[1024]{0:T(1024)}, u32[]{:S(2)}) copy-start(f32[1024]{0:T(1024)} %copy-done.23) | copy-start | bytes 12292
  640.1 58.5 %copy-start.31 = (f32[256]{0:T(256)S(1)}, f32[256]{0:T(256)}, u32[]{:S(2)}) copy-start(f32[256]{0:T(256)} %copy-done.30) | copy-start | bytes 3076
  702.7 2.9 copy-start.20
Sparse Core Ops, SparseCore 0:
  11.1 29.4 all-gather.6
  43.4 47.5 all-gather.8
  92.9 26.2 all-gather.10
  132.6 46.3 all-gather.12
  180.5 44.7 all-gather.14
  470.9 43.0 reduce-scatter.4
  554.8 42.5 all-gather.16
  599.7 43.4 reduce-scatter.2

commit v3 on v2

--- a/solution.py
+++ b/solution.py
@@ -547,6 +547,517 @@
     )(hidden, grad, weight, attended, branch, small, weight_own, gain_own)
 
 
+def line_gather(n, buf, send_sem, recv_sem, on_block):
+    me = lax.axis_index("tensor")
+
+    def copy(block, slot, k, peer):
+        return remote(
+            buf.at[block], buf.at[block], send_sem.at[slot, k], recv_sem.at[slot, k], "tensor", peer
+        )
+
+    def arrived(k, fn):
+        if k == 0:
+            fn(me, 0, 0)
+            return
+        for slot, sign in enumerate((1, -1)):
+            block = me - sign * k
+
+            @pl.when((block >= 0) & (block < n))
+            def _():
+                fn(block, slot, sign)
+
+    def outgoing(k, fn):
+        for slot, sign in enumerate((1, -1)):
+            block, peer = me - sign * k, me + sign
+
+            @pl.when((block >= 0) & (block < n) & (peer >= 0) & (peer < n))
+            def _():
+                fn(copy(block, slot, k, peer))
+
+    for k in range(n):
+        if k < n - 1:
+            outgoing(k, lambda c: c.start())
+        arrived(k, lambda block, slot, sign: on_block(block))
+        if k < n - 1:
+            arrived(
+                k + 1,
+                lambda block, slot, sign: copy(
+                    block, slot, k, jnp.clip(me - sign, 0, n - 1)
+                ).wait_recv(),
+            )
+    for k in range(n - 1):
+        outgoing(k, lambda c: c.wait_send())
+
+
+def diagonal(size):
+    return lax.broadcasted_iota(jnp.int32, (size, size), 0) == lax.broadcasted_iota(
+        jnp.int32, (size, size), 1
+    )
+
+
+def to_column(row):
+    return jnp.sum(jnp.where(diagonal(row.shape[1]), row, 0.0), axis=1, keepdims=True)
+
+
+def to_row(column):
+    return jnp.sum(jnp.where(diagonal(column.shape[0]), column, 0.0), axis=0, keepdims=True)
+
+
+def expert_kernel(
+    n_dp,
+    local,
+    capacity,
+    rows_ref,
+    grad_ref,
+    gates_ref,
+    in_ref,
+    out_ref,
+    back_ref,
+    gate_back_ref,
+    value_ref,
+    grad_in_ref,
+    grad_out_ref,
+    back_send,
+    gate_send,
+    zs,
+    ups,
+    gates_s,
+    stage,
+    value_stage,
+    back_send_sem,
+    back_recv_sem,
+    gate_send_sem,
+    gate_recv_sem,
+    own_sem,
+    stage_sem,
+    value_sem,
+):
+    me = lax.axis_index("dp")
+    pairs = n_dp // 2
+    hidden = in_ref.shape[2]
+    width = rows_ref.shape[2]
+    two = 2 * capacity
+    greet([("dp", n_dp)])
+
+    def back_copy(expert, target, sender):
+        part = slice(expert * capacity, (expert + 1) * capacity)
+        return remote(
+            back_send.at[target, part],
+            back_ref.at[sender, part],
+            back_send_sem.at[expert, target],
+            back_recv_sem.at[expert, sender],
+            "dp",
+            target,
+        )
+
+    def own_copy(expert):
+        part = slice(expert * capacity, (expert + 1) * capacity)
+        return pltpu.make_async_copy(
+            back_send.at[me, part], back_ref.at[me, part], own_sem.at[expert]
+        )
+
+    def stage_copy(slot, target):
+        return pltpu.make_async_copy(stage.at[slot], target, stage_sem.at[slot])
+
+    gate_send[...] = jnp.zeros_like(gate_send)
+    staged = []
+
+    def put(value, target):
+        slot = len(staged) % 2
+        if len(staged) >= 2:
+            staged[-2].wait()
+        stage[slot] = value
+        copy = stage_copy(slot, target)
+        copy.start()
+        staged.append(copy)
+
+    for expert in range(local):
+        part = slice(expert * capacity, (expert + 1) * capacity)
+
+        def group(index, _):
+            pair = (me // 2) ^ (pairs - 1 - index)
+            first = 2 * pair
+            rows = rows_ref[pl.ds(first, 2), part, :].reshape(two, width)
+            grads = grad_ref[pl.ds(first, 2), part, :].reshape(two, width)
+            column = jnp.concatenate(
+                [to_column(gates_ref[first + j, 0:1, part]) for j in range(2)], axis=0
+            )
+            gate = nt(rows, in_ref[expert, 0])
+            up = nt(rows, in_ref[expert, 1])
+            square = gate * gate
+            bent = jnp.tanh(0.7978845608028654 * gate * (1.0 + 0.044715 * square))
+            half = 0.5 * (1.0 + bent)
+            gelu = gate * half
+            slope = half + 0.5 * gate * (1.0 - bent * bent) * (
+                0.7978845608028654 * (1.0 + 3 * 0.044715 * square)
+            )
+            z = gelu * up
+            grad_z = nt(grads, out_ref[expert])
+            gate_grad = jnp.sum(z * grad_z, axis=1, keepdims=True)
+            grad_z = column * grad_z
+            zs[pl.ds(first, 2)] = (column * z).astype(BF16).reshape(2, capacity, hidden)
+            ups[0, pl.ds(first, 2)] = (grad_z * up * slope).astype(BF16).reshape(2, capacity, hidden)
+            ups[1, pl.ds(first, 2)] = (grad_z * gelu).astype(BF16).reshape(2, capacity, hidden)
+            for j in range(2):
+                gate_send[first + j, 0:1, part] = to_row(
+                    gate_grad[j * capacity : (j + 1) * capacity]
+                )
+            back = nn(ups[0, pl.ds(first, 2)].reshape(two, hidden), in_ref[expert, 0])
+            back += nn(ups[1, pl.ds(first, 2)].reshape(two, hidden), in_ref[expert, 1])
+            back_send[pl.ds(first, 2), part, :] = back.astype(BF16).reshape(2, capacity, width)
+            for j in range(2):
+                target = first + j
+
+                @pl.when(target != me)
+                def _():
+                    back_copy(expert, target, me).start()
+
+                @pl.when(target == me)
+                def _():
+                    own_copy(expert).start()
+
+            return 0
+
+        lax.fori_loop(0, pairs, group, 0)
+        if expert == local - 1:
+            gate_copies = []
+            for step in range(1, n_dp):
+                target = lax.rem(me + step, n_dp)
+                copy = remote(
+                    gate_send.at[target],
+                    gate_back_ref.at[me],
+                    gate_send_sem.at[step - 1],
+                    gate_recv_sem.at[step - 1],
+                    "dp",
+                    target,
+                )
+                copy.start()
+                gate_copies.append(copy)
+            gate_back_ref[me] = gate_send[me]
+        rows = rows_ref[:, part, :].reshape(n_dp * capacity, width)
+        for half in range(2):
+            put(tn(ups[half].reshape(n_dp * capacity, hidden), rows), grad_in_ref.at[expert, half])
+        grads = grad_ref[:, part, :].reshape(n_dp * capacity, width)
+        put(tn(zs[...].reshape(n_dp * capacity, hidden), grads), grad_out_ref.at[expert])
+        if expert > 0:
+            pltpu.make_async_copy(
+                value_stage, value_ref.at[:, slice((expert - 1) * capacity, expert * capacity)], value_sem
+            ).wait()
+
+        def value(pair, _):
+            out = nn(zs[pl.ds(2 * pair, 2)].reshape(two, hidden), out_ref[expert])
+            value_stage[pl.ds(2 * pair, 2)] = out.astype(BF16).reshape(2, capacity, width)
+            return 0
+
+        lax.fori_loop(0, pairs, value, 0)
+        pltpu.make_async_copy(value_stage, value_ref.at[:, part], value_sem).start()
+
+    last = slice((local - 1) * capacity, local * capacity)
+    pltpu.make_async_copy(value_stage, value_ref.at[:, last], value_sem).wait()
+    for copy in staged[-2:]:
+        copy.wait()
+    for copy in gate_copies:
+        copy.wait()
+    for expert in range(local):
+        own_copy(expert).wait()
+        for step in range(1, n_dp):
+            peer = lax.rem(me + step, n_dp)
+            back_copy(expert, peer, me).wait_send()
+            back_copy(expert, me, peer).wait_recv()
+
+
+def any_spec():
+    return pl.BlockSpec(memory_space=pl.ANY)
+
+
+def run_experts(n_dp, capacity, rows, grads, gates, w_in, w_out):
+    local, _, hidden, width = w_in.shape
+    slots = local * capacity
+    return pl.pallas_call(
+        functools.partial(expert_kernel, n_dp, local, capacity),
+        out_shape=(
+            jax.ShapeDtypeStruct((n_dp, slots, width), BF16),
+            jax.ShapeDtypeStruct((n_dp, 8, slots), F32),
+            jax.ShapeDtypeStruct((n_dp, slots, width), BF16),
+            jax.ShapeDtypeStruct(w_in.shape, F32),
+            jax.ShapeDtypeStruct(w_out.shape, F32),
+        ),
+        in_specs=[vspec()] * 5,
+        out_specs=(any_spec(), vspec(), any_spec(), any_spec(), any_spec()),
+        scratch_shapes=[
+            pltpu.VMEM((n_dp, slots, width), BF16),
+            pltpu.VMEM((n_dp, 8, slots), F32),
+            pltpu.VMEM((n_dp, capacity, hidden), BF16),
+            pltpu.VMEM((2, n_dp, capacity, hidden), BF16),
+            pltpu.VMEM((8, 128), F32),
+            pltpu.VMEM((2, hidden, width), F32),
+            pltpu.VMEM((n_dp, capacity, width), BF16),
+            pltpu.SemaphoreType.DMA((local, n_dp)),
+            pltpu.SemaphoreType.DMA((local, n_dp)),
+            pltpu.SemaphoreType.DMA((n_dp - 1,)),
+            pltpu.SemaphoreType.DMA((n_dp - 1,)),
+            pltpu.SemaphoreType.DMA((local,)),
+            pltpu.SemaphoreType.DMA((2,)),
+            pltpu.SemaphoreType.DMA,
+        ],
+        compiler_params=pltpu.CompilerParams(
+            vmem_limit_bytes=VMEM_LIMIT, collective_id=1, has_side_effects=True
+        ),
+        name="experts",
+    )(rows, grads, gates, w_in, w_out)
+
+
+def chosen_slots(columns, slots):
+    lane = lax.broadcasted_iota(jnp.int32, (1, slots), 1)
+    return columns[:, 0:1] == lane, columns[:, 1:2] == lane
+
+
+def combine_kernel(
+    n_dp,
+    n_tensor,
+    experts,
+    rows_ref,
+    gate_ref,
+    slots_ref,
+    routes_ref,
+    residual_ref,
+    hidden_ref,
+    cotangent_ref,
+    router_ref,
+    gain_ref,
+    weight_ref,
+    value_ref,
+    grad_residual_ref,
+    branch_ref,
+    grad_attended_ref,
+    small_ref,
+    value_back_ref,
+    acc,
+    total,
+    line_send,
+    line_recv,
+    gate_all,
+    gate_send,
+    gate_recv,
+    value_own,
+    line_send_sem,
+    line_recv_sem,
+    gate_send_sem,
+    gate_recv_sem,
+    value_send_sem,
+    value_recv_sem,
+    value_own_sem,
+    gather_send_sem,
+    gather_recv_sem,
+):
+    own_rows, width = residual_ref.shape
+    slots = rows_ref.shape[0]
+    per = slots // n_dp
+    me = lax.axis_index("dp")
+    me_t = lax.axis_index("tensor")
+    greet([("dp", n_dp), ("tensor", n_tensor)])
+    values = []
+    for step in range(1, n_dp):
+        peer = lax.rem(me + step, n_dp)
+        copy = remote(
+            value_ref.at[peer],
+            value_back_ref.at[me],
+            value_send_sem.at[step - 1],
+            value_recv_sem.at[step - 1],
+            "dp",
+            peer,
+        )
+        copy.start()
+        values.append(copy)
+    fetch = pltpu.make_async_copy(value_ref.at[me], value_own, value_own_sem.at[0])
+    fetch.start()
+
+    def partial(block):
+        one, two = chosen_slots(
+            slots_ref[pl.ds(pl.multiple_of(block * own_rows, own_rows), own_rows), :], slots
+        )
+        return nn(jnp.where(one | two, 1.0, 0.0).astype(BF16), rows_ref[...])
+
+    line = LineSum(
+        n_tensor, partial, line_send, line_recv, line_send_sem, line_recv_sem, acc, total
+    )
+    line.start()
+    for peer in range(n_dp):
+        gate_all[0:1, peer * per : (peer + 1) * per] = gate_ref[peer, 0:1, :]
+    gate_send[...] = jnp.zeros_like(gate_send)
+    gates = []
+    for step in range(n_tensor):
+        peer = lax.rem(me_t + step, n_tensor)
+        picks = chosen_slots(
+            slots_ref[pl.ds(pl.multiple_of(peer * own_rows, own_rows), own_rows), :], slots
+        )
+        for k in range(TOP):
+            column = jnp.sum(
+                jnp.where(picks[k], gate_all[0:1, :], 0.0), axis=1, keepdims=True
+            )
+            gate_send[step, k : k + 1, :] = to_row(column)
+        if step:
+            copy = remote(
+                gate_send.at[step],
+                gate_recv.at[step - 1],
+                gate_send_sem.at[step - 1],
+                gate_recv_sem.at[step - 1],
+                "tensor",
+                peer,
+            )
+            copy.start()
+            gates.append(copy)
+    fetch.wait()
+    put = pltpu.make_async_copy(value_own, value_back_ref.at[me], value_own_sem.at[1])
+    put.start()
+
+    hidden = hidden_ref[...]
+    router = router_ref[...]
+    logits = nt(router, hidden)
+    exps = jnp.exp(logits - jnp.max(logits, axis=0, keepdims=True))
+    probs = exps / jnp.sum(exps, axis=0, keepdims=True)
+    ids = lax.broadcasted_iota(jnp.int32, (experts, own_rows), 0)
+    first, second = ids == routes_ref[0:1, :], ids == routes_ref[1:2, :]
+    prob_one = jnp.sum(jnp.where(first, probs, 0.0), axis=0, keepdims=True)
+    prob_two = jnp.sum(jnp.where(second, probs, 0.0), axis=0, keepdims=True)
+    both = prob_one + prob_two
+    line.finish()
+    for copy in gates:
+        copy.wait()
+    gate_sum = gate_send[0]
+    for step in range(1, n_tensor):
+        gate_sum = gate_sum + gate_recv[step - 1]
+    grad_one, grad_two = gate_sum[0:1, :], gate_sum[1:2, :]
+    mean_grad = (prob_one * grad_one + prob_two * grad_two) / both
+    grad_probs = (
+        jnp.where(first, grad_one - mean_grad, 0.0) + jnp.where(second, grad_two - mean_grad, 0.0)
+    ) / both
+    grad_logits = probs * (grad_probs - jnp.sum(grad_probs * probs, axis=0, keepdims=True))
+    grad_hidden = total[...] + lax.dot_general(
+        grad_logits,
+        router.astype(F32),
+        (((0,), (0,)), ((), ())),
+        precision=lax.Precision.HIGHEST,
+        preferred_element_type=F32,
+    )
+    residual = residual_ref[...]
+    scale = lax.rsqrt(jnp.mean(residual * residual, axis=1, keepdims=True) + EPS)
+    unit = residual * scale
+    small_ref[...] = jnp.zeros_like(small_ref)
+    small_ref[experts : experts + 1, :] = jnp.sum(grad_hidden * unit, axis=0, keepdims=True)
+    grad_unit = grad_hidden * gain_ref[...]
+    grad_residual = cotangent_ref[...].astype(F32) + scale * (
+        grad_unit - unit * jnp.mean(grad_unit * unit, axis=1, keepdims=True)
+    )
+    grad_residual_ref[...] = grad_residual
+    branch_ref[me_t] = grad_residual.astype(BF16)
+
+    def on_block(block):
+        grad_attended_ref[pl.ds(pl.multiple_of(block * own_rows, own_rows), own_rows), :] = nt(
+            branch_ref[block], weight_ref[...]
+        ).astype(BF16)
+
+    line_gather(n_tensor, branch_ref, gather_send_sem, gather_recv_sem, on_block)
+    small_ref[0:experts, :] = jnp.dot(
+        grad_logits,
+        hidden.astype(F32),
+        precision=lax.Precision.HIGHEST,
+        preferred_element_type=F32,
+    )
+    line.drain()
+    put.wait()
+    for copy in values:
+        copy.wait()
+
+
+def combine(
+    n_dp,
+    n_tensor,
+    experts,
+    rows,
+    gates,
+    slot_columns,
+    routes_own,
+    residual,
+    hidden,
+    cotangent,
+    router_rows,
+    gain,
+    weight,
+    value,
+):
+    own_rows, width = residual.shape
+    slots = rows.shape[0]
+    return pl.pallas_call(
+        functools.partial(combine_kernel, n_dp, n_tensor, experts),
+        out_shape=(
+            jax.ShapeDtypeStruct((own_rows, width), F32),
+            jax.ShapeDtypeStruct((n_tensor, own_rows, width), BF16),
+            jax.ShapeDtypeStruct((n_tensor * own_rows, weight.shape[0]), BF16),
+            jax.ShapeDtypeStruct((SMALL, width), F32),
+            jax.ShapeDtypeStruct(value.shape, BF16),
+        ),
+        in_specs=[vspec()] * 10 + [any_spec()],
+        out_specs=(vspec(), vspec(), vspec(), vspec(), any_spec()),
+        scratch_shapes=[
+            pltpu.VMEM((own_rows, width), F32),
+            pltpu.VMEM((own_rows, width), F32),
+            pltpu.VMEM((n_tensor - 1, own_rows, width), BF16),
+            pltpu.VMEM((n_tensor + 1, own_rows, width), BF16),
+            pltpu.VMEM((8, slots), F32),
+            pltpu.VMEM((n_tensor, 8, own_rows), F32),
+            pltpu.VMEM((n_tensor - 1, 8, own_rows), F32),
+            pltpu.VMEM(value.shape[1:], BF16),
+            pltpu.SemaphoreType.DMA((n_tensor - 1,)),
+            pltpu.SemaphoreType.DMA((n_tensor + 1,)),
+            pltpu.SemaphoreType.DMA((n_tensor - 1,)),
+            pltpu.SemaphoreType.DMA((n_tensor - 1,)),
+            pltpu.SemaphoreType.DMA((n_dp - 1,)),
+            pltpu.SemaphoreType.DMA((n_dp - 1,)),
+            pltpu.SemaphoreType.DMA((2,)),
+            pltpu.SemaphoreType.DMA((2, n_tensor - 1)),
+            pltpu.SemaphoreType.DMA((2, n_tensor - 1)),
+        ],
+        compiler_params=pltpu.CompilerParams(
+            vmem_limit_bytes=VMEM_LIMIT, collective_id=2, has_side_effects=True
+        ),
+        name="combine",
+    )(
+        rows,
+        gates,
+        slot_columns,
+        routes_own,
+        residual,
+        hidden,
+        cotangent,
+        router_rows,
+        gain,
+        weight,
+        value,
+    )
+
+
+def merge_kernel(own_rows, slots_ref, value_ref, out_ref):
+    slots = value_ref.shape[0]
+    for block in range(out_ref.shape[0] // own_rows):
+        rows = slice(block * own_rows, (block + 1) * own_rows)
+        one, two = chosen_slots(slots_ref[rows, :], slots)
+        out_ref[rows, :] = nn(
+            jnp.where(one | two, 1.0, 0.0).astype(BF16), value_ref[...]
+        ).astype(BF16)
+
+
+def merge(own_rows, slot_columns, value):
+    return pl.pallas_call(
+        functools.partial(merge_kernel, own_rows),
+        out_shape=jax.ShapeDtypeStruct((slot_columns.shape[0], value.shape[1]), BF16),
+        in_specs=[vspec()] * 2,
+        out_specs=vspec(),
+        compiler_params=pltpu.CompilerParams(vmem_limit_bytes=VMEM_LIMIT),
+        name="merge",
+    )(slot_columns, value)
+
+
 def rms_scale(values):
     return lax.rsqrt(jnp.mean(values * values, axis=-1, keepdims=True) + EPS)
 
@@ -695,79 +1206,131 @@
         return jnp.stack(back, axis=1).reshape(slots, model_width)
 
     zero_row = jnp.zeros((1, model_width), BF16)
-    dispatched = exchange(jnp.concatenate([gathered_two, zero_row], axis=0)[sources])
-    padded_grad = jnp.concatenate([grad_gathered, zero_row], axis=0)
-    grad_expert = exchange((slot_gates[:, None] * padded_grad[sources]).astype(BF16))
-
-    outs, backs, grads_in, grads_out = [], [], [], []
-    for i in range(local_experts):
-        rows, grad_rows = dispatched[i], grad_expert[i]
-        gate_part = nt(rows, w_in[i, 0])
-        up_part = nt(rows, w_in[i, 1])
-        gelu_value, gelu_pull = jax.vjp(gelu_tanh, gate_part)
-        activated = (gelu_value * up_part).astype(BF16)
-        outs.append(nn(activated, w_out[i]).astype(BF16))
-        grad_act = nt(grad_rows, w_out[i])
-        grads_out.append(tn(activated, grad_rows))
-        grad_gate = gelu_pull(grad_act * up_part)[0].astype(BF16)
-        grad_up = (grad_act * gelu_value).astype(BF16)
-        backs.append((nn(grad_gate, w_in[i, 0]) + nn(grad_up, w_in[i, 1])).astype(BF16))
-        grads_in.append(jnp.stack([tn(grad_gate, rows), tn(grad_up, rows)]))
-    grad_w_in = jnp.stack(grads_in)
-    grad_w_out = jnp.stack(grads_out)
-    expert_out = give_back(outs)
-    grad_dispatched = give_back(backs)
-
-    first, second = slot_ids[:, 0], slot_ids[:, 1]
-    picked_first = expert_out[first].astype(F32)
-    picked_second = expert_out[second].astype(F32)
-    mixture = lax.psum_scatter(
-        (gates[:, 0:1] * picked_first + gates[:, 1:2] * picked_second).astype(BF16),
-        "tensor",
-        scatter_dimension=0,
-        tiled=True,
-    ).astype(F32)
-    layer_out = (residual + mixture).astype(BF16)
-    grad_float = grad_gathered.astype(F32)
-    grad_gate_part = jnp.stack(
-        [
-            jnp.sum(grad_float * picked_first, axis=1),
-            jnp.sum(grad_float * picked_second, axis=1),
-        ],
-        axis=1,
-    )
-    grad_hidden_part = (
-        grad_dispatched[first].astype(F32) + grad_dispatched[second].astype(F32)
-    ).astype(BF16)
-    grad_own = lax.psum_scatter(
-        grad_hidden_part, "tensor", scatter_dimension=0, tiled=True
-    ).astype(F32)
-    grad_gate_own = lax.dynamic_slice_in_dim(
-        lax.psum(grad_gate_part, "tensor"), own_start, own_rows, 0
-    )
-    own_routes = lax.dynamic_slice_in_dim(routes, own_start, own_rows, 0)
-    own_logits = jnp.dot(hidden_two, router_full, preferred_element_type=F32)
-
-    def own_gates(logit_values):
-        return gate_values(logit_values, own_routes)
-
-    _, gate_pull = jax.vjp(own_gates, own_logits)
-    grad_logits = gate_pull(grad_gate_own)[0]
-    router_float = router_full.astype(F32)
-    grad_hidden_two = grad_own + jnp.dot(grad_logits, router_float.T, precision=highest)
-    grad_router_part = jnp.dot(hidden_two.astype(F32).T, grad_logits, precision=highest)
-    grad_from_norm, grad_gain_two = norm_backward(grad_hidden_two, residual, scale_two, gain_two)
-    grad_residual = cotangent.astype(F32) + grad_from_norm
-
-    grad_branch = grad_residual.astype(BF16)
-    grad_attended_own = nt(grad_branch, out_matrix).astype(BF16)
-    grad_attended = lax.all_to_all(
-        jnp.transpose(grad_attended_own.reshape(own_rows, n_tensor, head_cols), (1, 0, 2)),
-        "tensor",
-        0,
-        0,
-    ).reshape(seq_len, head_cols)
-    grad_branch_all = lax.all_gather(grad_branch, "tensor", axis=0, tiled=True)
+    fast = n_dp % 2 == 0 and slots * model_width <= 4 * 1024 * 1024
+    if fast:
+        per = local_experts * capacity
+
+        def move(value):
+            return lax.all_to_all(value.reshape(n_dp, per, -1), "dp", 0, 0)
+
+        rows = move(jnp.concatenate([gathered_two, zero_row], axis=0)[sources])
+        grad_rows = move(jnp.concatenate([grad_gathered, zero_row], axis=0)[sources])
+        row_gates = lax.all_to_all(
+            jnp.broadcast_to(slot_gates.reshape(n_dp, 1, per), (n_dp, 8, per)), "dp", 0, 0
+        )
+        back, gate_back, value, grad_w_in, grad_w_out = run_experts(
+            n_dp, capacity, rows, grad_rows, row_gates, w_in, w_out
+        )
+        own_routes = lax.dynamic_slice_in_dim(routes, own_start, own_rows, 0)
+        weight_own = lax.dynamic_slice_in_dim(
+            out_matrix, lax.axis_index("tensor") * head_cols, head_cols, 0
+        )
+        grad_residual, grad_branch_all, grad_attended, small, value_back = combine(
+            n_dp,
+            n_tensor,
+            experts,
+            back.reshape(slots, model_width),
+            gate_back,
+            slot_ids,
+            jnp.pad(jnp.transpose(own_routes), ((0, 8 - TOP), (0, 0))),
+            residual,
+            hidden_two,
+            cotangent,
+            jnp.transpose(router_full),
+            gain_two[None],
+            weight_own,
+            value,
+        )
+        grad_branch_all = grad_branch_all.reshape(seq_len, model_width)
+        mixture = lax.psum_scatter(
+            merge(own_rows, slot_ids, value_back.reshape(slots, model_width)),
+            "tensor",
+            scatter_dimension=0,
+            tiled=True,
+        ).astype(F32)
+        layer_out = (residual + mixture).astype(BF16)
+    else:
+        dispatched = exchange(jnp.concatenate([gathered_two, zero_row], axis=0)[sources])
+        padded_grad = jnp.concatenate([grad_gathered, zero_row], axis=0)
+        grad_expert = exchange((slot_gates[:, None] * padded_grad[sources]).astype(BF16))
+
+        outs, backs, grads_in, grads_out = [], [], [], []
+        for i in range(local_experts):
+            rows, grad_rows = dispatched[i], grad_expert[i]
+            gate_part = nt(rows, w_in[i, 0])
+            up_part = nt(rows, w_in[i, 1])
+            gelu_value, gelu_pull = jax.vjp(gelu_tanh, gate_part)
+            activated = (gelu_value * up_part).astype(BF16)
+            outs.append(nn(activated, w_out[i]).astype(BF16))
+            grad_act = nt(grad_rows, w_out[i])
+            grads_out.append(tn(activated, grad_rows))
+            grad_gate = gelu_pull(grad_act * up_part)[0].astype(BF16)
+            grad_up = (grad_act * gelu_value).astype(BF16)
+            backs.append((nn(grad_gate, w_in[i, 0]) + nn(grad_up, w_in[i, 1])).astype(BF16))
+            grads_in.append(jnp.stack([tn(grad_gate, rows), tn(grad_up, rows)]))
+        grad_w_in = jnp.stack(grads_in)
+        grad_w_out = jnp.stack(grads_out)
+        expert_out = give_back(outs)
+        grad_dispatched = give_back(backs)
+
+        first, second = slot_ids[:, 0], slot_ids[:, 1]
+        picked_first = expert_out[first].astype(F32)
+        picked_second = expert_out[second].astype(F32)
+        mixture = lax.psum_scatter(
+            (gates[:, 0:1] * picked_first + gates[:, 1:2] * picked_second).astype(BF16),
+            "tensor",
+            scatter_dimension=0,
+            tiled=True,
+        ).astype(F32)
+        layer_out = (residual + mixture).astype(BF16)
+        grad_float = grad_gathered.astype(F32)
+        grad_gate_part = jnp.stack(
+            [
+                jnp.sum(grad_float * picked_first, axis=1),
+                jnp.sum(grad_float * picked_second, axis=1),
+            ],
+            axis=1,
+        )
+        grad_hidden_part = (
+            grad_dispatched[first].astype(F32) + grad_dispatched[second].astype(F32)
+        ).astype(BF16)
+        grad_own = lax.psum_scatter(
+            grad_hidden_part, "tensor", scatter_dimension=0, tiled=True
+        ).astype(F32)
+        grad_gate_own = lax.dynamic_slice_in_dim(
+            lax.psum(grad_gate_part, "tensor"), own_start, own_rows, 0
+        )
+        own_routes = lax.dynamic_slice_in_dim(routes, own_start, own_rows, 0)
+        own_logits = jnp.dot(hidden_two, router_full, preferred_element_type=F32)
+
+        def own_gates(logit_values):
+            return gate_values(logit_values, own_routes)
+
+        _, gate_pull = jax.vjp(own_gates, own_logits)
+        grad_logits = gate_pull(grad_gate_own)[0]
+        router_float = router_full.astype(F32)
+        grad_hidden_two = grad_own + jnp.dot(grad_logits, router_float.T, precision=highest)
+        grad_router_part = jnp.dot(hidden_two.astype(F32).T, grad_logits, precision=highest)
+        grad_from_norm, grad_gain_two = norm_backward(grad_hidden_two, residual, scale_two, gain_two)
+        grad_residual = cotangent.astype(F32) + grad_from_norm
+
+        grad_branch = grad_residual.astype(BF16)
+        grad_attended_own = nt(grad_branch, out_matrix).astype(BF16)
+        grad_attended = lax.all_to_all(
+            jnp.transpose(grad_attended_own.reshape(own_rows, n_tensor, head_cols), (1, 0, 2)),
+            "tensor",
+            0,
+            0,
+        ).reshape(seq_len, head_cols)
+        grad_branch_all = lax.all_gather(grad_branch, "tensor", axis=0, tiled=True)
+        small = jnp.concatenate(
+            [
+                jnp.transpose(grad_router_part),
+                grad_gain_two[None],
+                jnp.zeros((SMALL - experts - 1, model_width), F32),
+            ],
+            axis=0,
+        )
     grad_projected, diag = attention_backward(
         projected,
         attended,
@@ -786,14 +1349,6 @@
         jnp.asarray(skew_selectors()), near, (((0,), (0,)), ((), ())), precision=highest
     )
     grad_table = grad_table.at[NB - 1].add(jnp.sum(diag[:, 2], axis=1))
-    small = jnp.concatenate(
-        [
-            jnp.transpose(grad_router_part),
-            grad_gain_two[None],
-            jnp.zeros((SMALL - experts - 1, model_width), F32),
-        ],
-        axis=0,
-    )
     small = jnp.transpose(small.reshape(SMALL, n_dp, depth), (1, 0, 2))
     small = lax.dynamic_update_slice(
         small, grad_table.reshape(n_dp, NB // n_dp, heads), (0, experts + 2, 0)

time: 724 us -> 624 us (0.86)
  Pallas kernels: 89.4 us -> 261 us
  matrix products: 107 us -> 10.4 us
  other arithmetic: 65.5 us -> 18.8 us
  blocking collectives: 61.2 us -> 16.1 us
  local copies, waits for them, and re-layouts: 114 us -> 74.1 us
  starting transfers between devices: 38.7 us -> 17.1 us
  waiting for transfers between devices: 222 us -> 203 us
    pallas_call x0 -> x3, Pallas kernels: none -> 165 us  [the longest x1 83 us: combine(): pl.pallas_call(functools.partial(combine_kernel, n_dp, n_tensor, experts)...]
    dot_general x22 -> x0, matrix products: 97.2 us -> none  [the longest x7 39.6 us: nt(): lax.dot_general(a, b, (((1,), (1,)), ((), ())), preferred_element_type=F32)]
    all_to_all x8 -> x3, waiting for transfers between devices: 96.5 us -> 57.1 us  [the longest x2 57.1 us: move(): return lax.all_to_all(value.reshape(n_dp, per, -1), 'dp', 0, 0)]
    all_to_all x1 -> x0, blocking collectives: 35.8 us -> none  [exchange(): lax.all_to_all(parts[:, i], 'dp', 0, 0)]
    gather x6 -> x2, local copies, waits for them, and re-layouts: 53.3 us -> 17.6 us  [the longest x1 8.79 us: on_device(): jnp.concatenate([grad_gathered, zero_row], axis=0)[sources]]
    another operation x9 -> x2, other arithmetic: 37.3 us -> 4.71 us  [the longest x3 21.1 us: on_device(): grad_w_in = jnp.stack(grads_in)]
    all_gather x1, waiting for transfers between devices: 30.5 us -> 55.2 us  [on_device(): gathered_two = lax.all_gather(hidden_two, 'tensor', axis=0, tiled=True)]
    all_to_all x8 -> x3, starting transfers between devices: 34 us -> 13.1 us  [the longest x2 9.47 us: move(): return lax.all_to_all(value.reshape(n_dp, per, -1), 'dp', 0, 0)]
  transfers between devices with their start and end apart: 17 -> 10, of which waited for: 11 -> 6; matrix products, arithmetic and copies ran while one was open for 37% -> 13% of each run, Pallas kernels for 13% -> 16%
where the time goes in v3:
time: 624 us; the launch traced here: 616 us
  Pallas kernels  261 us (42%)
  waiting for transfers between devices  203 us (33%)
  local copies, waits for them, and re-layouts  74.1 us (12%)
  other arithmetic  18.8 us (3%)
  starting transfers between devices  17.1 us (3%)
  blocking collectives  16.1 us (3%)
  between operations  15 us (2%)
  matrix products  10.4 us (2%)
    pallas_call x1, Pallas kernels, combine(): pl.pallas_call(functools.partial(combine_kernel, n_dp, n_tensor, experts)...  83 us
    pallas_call x1, Pallas kernels, run_experts(): pl.pallas_call(functools.partial(expert_kernel, n_dp, local, capacity), o...  72.4 us
    pallas_call x1, Pallas kernels, tail(): pl.pallas_call(functools.partial(tail_kernel, n_dp, n_tensor, experts, ta...  61.8 us
    all_to_all x2, waiting for transfers between devices, move(): return lax.all_to_all(value.reshape(n_dp, per, -1), 'dp', 0, 0)  57.1 us
    all_gather x1, waiting for transfers between devices, on_device(): gathered_two = lax.all_gather(hidden_two, 'tensor', axis=0, tiled=True)  55.2 us
    all_gather x1, waiting for transfers between devices, on_device(): lax.all_gather(jnp.concatenate([w_qkv.reshape(depth, 3 * head_cols), extr...  28.4 us
    all_gather x1, waiting for transfers between devices, on_device(): grad_gathered = lax.all_gather(cotangent, 'tensor', axis=0, tiled=True)  22 us
    all_gather x1, waiting for transfers between devices, on_device(): gathered_one = lax.all_gather(hidden_one, 'tensor', axis=0, tiled=True)  20.8 us
  transfers between devices with their start and end apart: 10, of which 6 were waited for; matrix products, arithmetic and copies ran while one was open for 13% of the time, Pallas kernels for 16%

profile of v3, /device:TPU:0, one launch (start us, length us, event | category | flops | bytes accessed | tf_op | source)
XLA Modules:
  0.0 615.7 jit_solution(7031312125175418198)
XLA Ops:
  7.2 0.8 copy.81
  8.1 0.7 fusion.20
  8.9 1.1 copy.80
  10.2 0.7 fusion.13
  11.0 1.2 fusion.9
  12.2 28.4 %all-gather.6.cloned.1.call-done = bf16[1024,896]{1,0:T(8,128)(2,1)} async-done(((bf16[128,896]{1,0:T(8,128)(2,1)}), bf16[1024,896]{1,0:T(8,128)(2,1)}) %all-gather.6.cloned.1.call-update) | async-done | bytes 1835024 | tf_op jit(solution)/shard_map/all_gather | solution.py:1127
  40.6 1.4 convert_reduce_fusion
  42.0 1.0 fusion.3
  43.1 0.7 all-gather.14.cloned.1.call-update
  43.8 16.1 %all_gather.20 = bf16[1024,128]{1,0:T(8,128)(2,1)} all-gather(bf16[256,128]{1,0:T(8,128)(2,1)S(1)} %copy-done.15), channel_id=1, replica_groups=mesh['dp'=8,'tensor'=4] {'tensor'}, dimensions={0}, use_global_device_ids=true | all-gather | bytes 327680 | tf_op jit(solution)/shard_map/all_gather | solution.py:1143
  60.9 4.5 reduce-window.6
  66.1 1.0 copy.85.seg_col_ref
  67.3 0.5 reduce_sum.90
  67.8 0.7 convert_reduce_fusion.3.lo_ref
  69.1 0.6 reshape.229.pattern_ref
  69.7 0.6 convert_reduce_fusion.2.far_ref
  70.3 20.8 %all-gather.8.cloned.1.call-done.hidden_ref = bf16[1024,1024]{1,0:T(8,128)(2,1)} async-done(((bf16[256,1024]{1,0:T(8,128)(2,1)}), bf16[1024,1024]{1,0:T(8,128)(2,1)}) %all-gather.8.cloned.1.call-update) | async-done | bytes 2097168 | tf_op jit(solution)/shard_map/all_gather | solution.py:1149
  91.1 5.0 convolution_convert_fusion.qkv_ref
  96.1 14.5 %attn_fwd.1 = (bf16[1024,256]{1,0:T(8,128)(2,1)}, f32[1024,4]{1,0:T(8,128)}) custom-call(s32[4]{0:T(128)} %convert_reduce_fusion.3.lo_ref, bf16[1024,768]{1,0:T(8,128)(2,1)} %convolution_convert_fusion.qkv_ref, s32[1024,1]{1,0:T(8,128)} %copy.85.seg_col_ref, s32[1,1024]{1,0:T(1,128)} %seg_row_ref.3, f32[8,512]{1,0:T(8,128)} %reshape.229.pattern_ref, ...), custom_call_target="tpu_custom_call" | custom-call | tf_op jit(solution)/shard_map/attn_fwd/pallas_call | solution.py:240
  110.6 2.0 copy.86
  112.6 3.5 all-to-all-start
  116.1 0.9 broadcast_multiply_fusion
  117.6 8.1 %scatter_custom_fusion = s32[2560]{0:T(1024)S(1)} fusion(s32[2048]{0:T(1024)S(1)} %bitcast.99, s32[2048]{0:T(1024)S(1)} %reshape.270, s32[]{:T(128)} %constant.68.clone.1), kind=kCustom, calls=%fused_computation.56 | custom fusion | bytes 10244 | tf_op jit(solution)/shard_map/scatter | solution.py:1191
  125.7 22.0 %all-gather.14.cloned.1.call-done = bf16[1024,1024]{1,0:T(8,128)(2,1)} async-done(((bf16[256,1024]{1,0:T(8,128)(2,1)}), bf16[1024,1024]{1,0:T(8,128)(2,1)}) %all-gather.14.cloned.1.call-update) | async-done | bytes 2097168 | tf_op jit(solution)/shard_map/all_gather | solution.py:1193
  147.8 1.8 concatenate.17
  149.5 8.8 %gather_fusion.1 = bf16[2560,1024]{1,0:T(8,128)(2,1)} fusion(bf16[1025,1024]{1,0:T(8,128)(2,1)S(1)} %concatenate.17, s32[3072]{0:T(1024)S(1)} %pad_clamp_fusion), kind=kCustom, calls=%fused_computation.1 | custom fusion | bytes 10496000 | tf_op jit(solution)/shard_map/gather | solution.py:1217
  158.3 4.8 all-to-all-start.2
  163.4 18.7 %all-gather.10.cloned.1.call-done = bf16[1024,1024]{1,0:T(8,128)(2,1)} async-done(((bf16[1024,128]{1,0:T(8,128)(2,1)}), bf16[1024,1024]{1,0:T(8,128)(2,1)}) %all-gather.10.cloned.1.call-update) | async-done | bytes 2097168 | tf_op jit(solution)/shard_map/all_gather | solution.py:1144
  182.2 2.4 multiply_reduce_fusion
  184.7 1.0 multiply_convert_fusion.hidden_ref
  185.7 55.2 %all-gather.12.cloned.1.call-done = bf16[1024,1024]{1,0:T(8,128)(2,1)} async-done(((bf16[256,1024]{1,0:T(8,128)(2,1)}), bf16[1024,1024]{1,0:T(8,128)(2,1)}) %all-gather.12.cloned.1.call-update) | async-done | bytes 2097168 | tf_op jit(solution)/shard_map/all_gather | solution.py:1173
  240.9 2.3 fusion.27
  243.8 8.1 %scatter_custom_fusion.1 = f32[2560]{0:T(1024)S(1)} fusion(s32[2048]{0:T(1024)S(1)} %bitcast.100, f32[2048]{0:T(1024)S(1)} %reshape.278, f32[]{:T(128)} %constant.62.clone.1), kind=kCustom, calls=%fused_computation.54 | custom fusion | bytes 10244 | tf_op jit(solution)/shard_map/scatter | solution.py:1192
  252.0 0.6 broadcast_in_dim.65
  252.6 3.6 all-to-all-start.3
  256.2 1.8 concatenate.16
  258.0 8.8 %gather_fusion = bf16[2560,1024]{1,0:T(8,128)(2,1)} fusion(bf16[1025,1024]{1,0:T(8,128)(2,1)S(1)} %concatenate.16, s32[3072]{0:T(1024)S(1)} %pad_clamp_fusion), kind=kCustom, calls=%fused_computation | custom fusion | bytes 10496000 | tf_op jit(solution)/shard_map/gather | solution.py:1216
  266.8 0.6 copy-done.12
  267.4 4.7 all-to-all-start.1
  272.2 0.6 pad.18.routes_ref
  272.8 0.7 copy.91.router_ref
  273.5 1.9 constant_dynamic-slice_fusion.weight_ref
  275.4 57.1 %all-to-all-done.1.rows_ref = bf16[8,320,1024]{2,1,0:T(8,128)(2,1)} async-done(((bf16[8,320,1024]{2,1,0:T(8,128)(2,1)}), bf16[8,320,1024]{2,1,0:T(8,128)(2,1)}, u32[]{:S(2)}, u32[]{:S(2)}) %all-to-all-start.1) | async-done | bytes 5242912 | tf_op jit(solution)/shard_map/all_to_all | solution.py:1214
  332.5 72.4 %experts.1 = (bf16[8,320,1024]{2,1,0:T(8,128)(2,1)}, f32[8,8,320]{2,1,0:T(8,128)}, bf16[8,320,1024]{2,1,0:T(8,128)(2,1)}, f32[2,2,704,1024]{3,2,1,0:T(8,128)}, f32[2,704,1024]{2,1,0:T(8,128)}) custom-call(bf16[8,320,1024]{2,1,0:T(8,128)(2,1)} %all-to-all-done.1.rows_ref, bf16[8,320,1024]{2,1,0:T(8,128)(2,1)} %all-to-all-done.2.grad_ref, ...), custom_call_target="tpu_custom_call" | custom-call | tf_op jit(solution)/shard_map/experts/pallas_call | solution.py:776
  404.9 83.0 %combine.1 = (f32[256,1024]{1,0:T(8,128)}, bf16[4,256,1024]{2,1,0:T(8,128)(2,1)}, bf16[1024,256]{1,0:T(8,128)(2,1)}, f32[32,1024]{1,0:T(8,128)}, bf16[8,320,1024]{2,1,0:T(8,128)(2,1)}) custom-call(bf16[2560,1024]{1,0:T(8,128)(2,1)} %bitcast.80, f32[8,8,320]{2,1,0:T(8,128)} %get-tuple-element.42.gate_ref, s32[1024,2]{1,0:T(8,128)} %get-tuple-element.103.slots_ref, ...), custom_call_target="tpu_custom_call" | custom-call | tf_op jit(solution)/shard_map/combine/pallas_call | solution.py:991
  487.9 9.6 %merge.1 = bf16[1024,1024]{1,0:T(8,128)(2,1)} custom-call(s32[1024,2]{1,0:T(8,128)} %get-tuple-element.103.slots_ref, bf16[2560,1024]{1,0:T(8,128)(2,1)} %bitcast.81), custom_call_target="tpu_custom_call" | custom-call | tf_op jit(solution)/shard_map/merge/pallas_call | solution.py:1051
  497.6 0.6 copy-done.20
  498.2 0.5 bitcast_convert_fusion.gain_own_ref
  498.7 1.3 slice.95.weight_ref
  500.0 19.9 %attn_bwd.1 = (bf16[1024,768]{1,0:T(8,128)(2,1)}, f32[12,512]{1,0:T(8,128)}) custom-call(s32[4]{0:T(128)} %convert_reduce_fusion.3.lo_ref, bf16[1024,768]{1,0:T(8,128)(2,1)} %convolution_convert_fusion.qkv_ref, bf16[1024,256]{1,0:T(8,128)(2,1)} %get-tuple-element.40.out_ref.attended_ref, bf16[1024,256]{1,0:T(8,128)(2,1)} %get-tuple-element.46.grad_ref, ...), custom_call_target="tpu_custom_call" | custom-call | tf_op jit(solution)/shard_map/attn_bwd/pallas_call | solution.py:258
  519.9 0.8 reshape.240
  521.6 0.5 dynamic_update_slice.3.small_ref
  522.1 0.6 copy-done.9
  522.8 61.8 %tail.1 = (f32[256,1024]{1,0:T(8,128)}, f32[128,768]{1,0:T(8,128)}, f32[256,128]{1,0:T(8,128)}, f32[32,128]{1,0:T(8,128)}) custom-call(bf16[1024,1024]{1,0:T(8,128)(2,1)} %all-gather.8.cloned.1.call-done.hidden_ref, bf16[1024,768]{1,0:T(8,128)(2,1)} %get-tuple-element.48.grad_ref, bf16[1024,768]{1,0:T(8,128)(2,1)} %slice.95.weight_ref, ...), custom_call_target="tpu_custom_call" | custom-call | tf_op jit(solution)/shard_map/tail/pallas_call | solution.py:517
  584.6 1.2 copy.98
  585.8 0.9 copy.99
  586.8 1.2 slice.86
  588.3 0.5 slice_bitcast_fusion.3
  588.8 0.6 slice_bitcast_fusion.2
  589.4 2.4 fusion.8
  591.8 2.1 add_convert_fusion
  594.0 0.7 copy.114
  594.6 11.3 %copy.115 = f32[2,2,704,1024]{3,2,1,0:T(8,128)} copy(f32[2,2,704,1024]{3,2,1,0:T(8,128)} %get-tuple-element.128) | data formatting | bytes 23068672
  605.9 2.5 copy.116
  (106 shorter events, 5.8 us)
Async XLA Ops:
  7.2 34.9 %copy-start.2 = (bf16[256,1024]{1,0:T(8,128)(2,1)S(1)}, bf16[256,1024]{1,0:T(8,128)(2,1)}, u32[]{:S(2)}) copy-start(bf16[256,1024]{1,0:T(8,128)(2,1)} %param.16) | copy-start | bytes 1572868
  7.2 33.4 %all-gather.6.cloned.1.call-start = ((), (), s32[]{:S(2)}) async-start(), calls=%async_computation.5 | async-start | bytes 2064384 | tf_op jit(solution)/shard_map/all_gather | solution.py:1127
  10.0 33.8 %copy-start.15 = (bf16[256,128]{1,0:T(8,128)(2,1)S(1)}, bf16[256,128]{1,0:T(8,128)(2,1)}, u32[]{:S(2)}) copy-start(bf16[256,128]{1,0:T(8,128)(2,1)} %param.20) | copy-start | bytes 196612
  10.2 49.8 %copy-start.8 = (bf16[128,768]{1,0:T(8,128)(2,1)}, bf16[128,768]{1,0:T(8,128)(2,1)S(1)}, u32[]{:S(2)}) copy-start(bf16[128,768]{1,0:T(8,128)(2,1)S(1)} %copy.83.weight_own_ref) | copy-start | bytes 589828
  10.9 49.0 %copy-start.17 = (s32[1,1024]{1,0:T(1,128)S(1)}, s32[1,1024]{1,0:T(1,128)}, u32[]{:S(2)}) copy-start(s32[1,1024]{1,0:T(1,128)} %seg_row_ref.3) | copy-start | bytes 12292
  10.9 49.2 %copy-start.16 = (s32[1024,2]{0,1:T(2,128)S(1)}, s32[1024,2]{0,1:T(2,128)}, u32[]{:S(2)}) copy-start(s32[1024,2]{0,1:T(2,128)} %param.18) | copy-start | bytes 24580
  11.0 80.2 %all-gather.8.cloned.1.call-start = ((), (), s32[]{:S(2)}) async-start(), calls=%async_computation.6 | async-start | bytes 2621440 | tf_op jit(solution)/shard_map/all_gather | solution.py:1149
  42.0 142.6 %copy-start.18 = (f32[1024]{0:T(1024)}, f32[1024]{0:T(1024)S(1)}, u32[]{:S(2)}) copy-start(f32[1024]{0:T(1024)S(1)} %get-tuple-element.98) | copy-start | bytes 12292
  43.1 104.7 %all-gather.14.cloned.1.call-start = ((), (), s32[]{:S(2)}) async-start(), calls=%async_computation.9 | async-start | bytes 2621440 | tf_op jit(solution)/shard_map/all_gather | solution.py:1193
  43.8 138.4 %all-gather.10.cloned.1.call-start = ((), (), s32[]{:S(2)}) async-start(), calls=%async_computation.7 | async-start | bytes 2359296 | tf_op jit(solution)/shard_map/all_gather | solution.py:1144
  60.0 8.5 %slice-start.2 = ((bf16[1024,896]{1,0:T(8,128)(2,1)}), bf16[1024,128]{1,0:T(8,128)(2,1)S(1)}, s32[]{:S(2)}) async-start(bf16[1024,896]{1,0:T(8,128)(2,1)} %all-gather.6.cloned.1.call-done), calls=%async_computation.13 | async-start | bytes 524288 | tf_op jit(solution)/shard_map/slice | solution.py:1134
  60.2 8.5 %copy-start.11 = (f32[1024,32]{1,0:T(8,128)S(1)}, f32[1024,32]{1,0:T(8,128)}, u32[]{:S(2)}) copy-start(f32[1024,32]{1,0:T(8,128)} %constant.76.clone) | copy-start | bytes 393220
  112.6 45.7 %all-to-all-start = ((bf16[4,256,256]{1,2,0:T(8,128)(2,1)}), bf16[4,256,256]{1,2,0:T(8,128)(2,1)S(1)}, u32[]{:S(2)}, u32[]{:S(2)}) async-start(bf16[4,256,256]{1,2,0:T(8,128)(2,1)} %copy.86), calls=%async_computation | async-start | bytes 1048576 | tf_op jit(solution)/shard_map/all_to_all | solution.py:1165
  158.3 23.9 %copy-start.3 = (bf16[256,1024]{1,0:T(8,128)(2,1)S(1)}, bf16[256,1024]{1,0:T(8,128)(2,1)}, u32[]{:S(2)}) copy-start(bf16[256,1024]{1,0:T(8,128)(2,1)} %param.16) | copy-start | bytes 1572868
  158.3 93.6 %all-to-all-start.2 = ((bf16[8,320,1024]{2,1,0:T(8,128)(2,1)}), bf16[8,320,1024]{2,1,0:T(8,128)(2,1)}, u32[]{:S(2)}, u32[]{:S(2)}) async-start(bf16[8,320,1024]{2,1,0:T(8,128)(2,1)} %bitcast.76), calls=%async_computation.2 | async-start | bytes 10485760 | tf_op jit(solution)/shard_map/all_to_all | solution.py:1214
  163.1 77.7 %all-gather.12.cloned.1.call-start = ((), (), s32[]{:S(2)}) async-start(), calls=%async_computation.8 | async-start | bytes 2621440 | tf_op jit(solution)/shard_map/all_gather | solution.py:1173
  184.6 58.5 %copy-start = (f32[256,1024]{1,0:T(8,128)}, f32[256,1024]{1,0:T(8,128)S(1)}, u32[]{:S(2)}) copy-start(f32[256,1024]{1,0:T(8,128)S(1)} %get-tuple-element.107.residual_ref) | copy-start | bytes 3145732
  184.6 56.3 %copy-start.5 = (bf16[1024,896]{1,0:T(8,128)(2,1)S(1)}, bf16[1024,896]{1,0:T(8,128)(2,1)}, u32[]{:S(2)}) copy-start(bf16[1024,896]{1,0:T(8,128)(2,1)} %all-gather.6.cloned.1.call-done) | copy-start | bytes 5505028
  252.6 14.2 %all-to-all-start.3 = ((f32[8,8,320]{2,1,0:T(8,128)}), f32[8,8,320]{2,1,0:T(8,128)S(1)}, u32[]{:S(2)}, u32[]{:S(2)}) async-start(f32[8,8,320]{2,1,0:T(8,128)} %broadcast_in_dim.65), calls=%async_computation.3 | async-start | bytes 196608 | tf_op jit(solution)/shard_map/all_to_all | solution.py:1218
  266.8 0.6 copy-start.12
  266.8 6.0 copy-start.6
  267.4 65.0 %all-to-all-start.1 = ((bf16[8,320,1024]{2,1,0:T(8,128)(2,1)}), bf16[8,320,1024]{2,1,0:T(8,128)(2,1)}, u32[]{:S(2)}, u32[]{:S(2)}) async-start(bf16[8,320,1024]{2,1,0:T(8,128)(2,1)} %bitcast.77), calls=%async_computation.1 | async-start | bytes 10485760 | tf_op jit(solution)/shard_map/all_to_all | solution.py:1214
  272.1 319.7 %reduce-scatter.2.cloned.1.call-start = ((), (), s32[]{:S(2)}) async-start(), calls=%async_computation.10 | async-start | bytes 2621440 | tf_op jit(solution)/shard_map/reduce_scatter | solution.py:1245
  497.6 0.7 copy-start.20
  500.0 20.9 %copy-start.10 = (f32[1024,32]{1,0:T(8,128)S(1)}, f32[1024,32]{1,0:T(8,128)}, u32[]{:S(2)}) copy-start(f32[1024,32]{1,0:T(8,128)} %constant.77.clone) | copy-start | bytes 393220
  500.0 21.6 %copy-start.13 = (f32[32,1024]{1,0:T(8,128)S(1)}, f32[32,1024]{1,0:T(8,128)}, u32[]{:S(2)}) copy-start(f32[32,1024]{1,0:T(8,128)} %get-tuple-element.50) | copy-start | bytes 393220
  522.1 0.7 copy-start.9
  522.8 65.2 %copy-start.4 = (bf16[256,1024]{1,0:T(8,128)(2,1)S(1)}, bf16[256,1024]{1,0:T(8,128)(2,1)}, u32[]{:S(2)}) copy-start(bf16[256,1024]{1,0:T(8,128)(2,1)} %param.16) | copy-start | bytes 1572868
  584.6 3.4 copy-start.7
  584.6 3.7 copy-start.19
  588.0 3.8 copy-start.1
  589.4 4.5 copy-start.14
  591.8 14.1 %slice-start = ((s8[5767168]{0:T(1024)(128)(4,1)}), s8[4194304]{0:T(1024)(128)(4,1)S(1)}, s32[]{:S(2)}) async-start(s8[5767168]{0:T(1024)(128)(4,1)} %bitcast.78), calls=%async_computation.11 | async-start | bytes 8388608
  594.6 11.3 %slice-start.1 = ((s8[5767168]{0:T(1024)(128)(4,1)}), s8[1572864]{0:T(1024)(128)(4,1)S(1)}, s32[]{:S(2)}) async-start(s8[5767168]{0:T(1024)(128)(4,1)} %bitcast.78), calls=%async_computation.12 | async-start | bytes 3145728
Sparse Core Ops, SparseCore 0:
  11.1 29.4 all-gather.5
  43.2 47.9 all-gather.7
  92.7 55.0 all-gather.13
  149.5 32.6 all-gather.9
  185.8 55.0 all-gather.11
  497.7 52.4 reduce-scatter.1

commit v4 on v3

--- a/solution.py
+++ b/solution.py
@@ -1037,6 +1037,579 @@
     )
 
 
+class Streams:
+    def __init__(self, n, refs, send_sem, recv_sem):
+        self.n, self.refs, self.send_sem, self.recv_sem = n, refs, send_sem, recv_sem
+        self.me = lax.axis_index("tensor")
+
+    def copy(self, j, block, slot, k, peer):
+        ref = self.refs[j].at[block]
+        return remote(
+            ref, ref, self.send_sem.at[j, slot, k], self.recv_sem.at[j, slot, k], "tensor", peer
+        )
+
+    def outgoing(self, j, k, fn):
+        for slot, sign in enumerate((1, -1)):
+            block, peer = self.me - sign * k, self.me + sign
+
+            @pl.when((block >= 0) & (block < self.n) & (peer >= 0) & (peer < self.n))
+            def _():
+                fn(self.copy(j, block, slot, k, peer))
+
+    def incoming(self, j, k, fn):
+        for slot, sign in enumerate((1, -1)):
+            block = self.me - sign * (k + 1)
+
+            @pl.when((block >= 0) & (block < self.n))
+            def _():
+                fn(self.copy(j, block, slot, k, jnp.clip(self.me - sign, 0, self.n - 1)), block)
+
+    def turn(self, turn, used=None):
+        moved = []
+        for j in range(len(self.refs)):
+            k = turn - j
+            if k < 0 or k > self.n - 1:
+                continue
+            if k > 0:
+                self.incoming(j, k - 1, lambda c, block: c.wait_recv())
+            if k < self.n - 1:
+                self.outgoing(j, k, lambda c: c.start())
+            moved.append((j, k))
+        if used is not None:
+            for j, k in moved:
+                used(j, k)
+
+    def turns(self):
+        return range(self.n + len(self.refs) - 1)
+
+    def each_new(self, j, k, fn):
+        if k == 0:
+            fn(self.me)
+            return
+        for sign in (1, -1):
+            block = self.me - sign * k
+
+            @pl.when((block >= 0) & (block < self.n))
+            def _():
+                fn(block)
+
+    def drain(self):
+        for j in range(len(self.refs)):
+            for k in range(self.n - 1):
+                self.outgoing(j, k, lambda c: c.wait_send())
+
+
+class Spread:
+    def __init__(self, n, ref, far_send, far_recv, near_send, near_recv):
+        self.n, self.ref = n, ref
+        self.far_send, self.far_recv = far_send, far_recv
+        self.near_send, self.near_recv = near_send, near_recv
+        self.me = lax.axis_index("dp")
+        self.partner = self.me ^ 1
+
+    def far(self, step, block, peer):
+        ref = self.ref.at[block]
+        return remote(ref, ref, self.far_send.at[step], self.far_recv.at[step], "dp", peer)
+
+    def near(self, step, block):
+        ref = self.ref.at[block]
+        return remote(
+            ref, ref, self.near_send.at[step], self.near_recv.at[step], "dp", self.partner
+        )
+
+    def start(self):
+        for step in range(1, self.n // 2):
+            self.far(step - 1, self.me, lax.rem(self.me + 2 * step, self.n)).start()
+        self.near(0, self.me).start()
+
+    def source(self, me, step):
+        return lax.rem(me + self.n - 2 * step, self.n)
+
+    def relay(self):
+        for step in range(1, self.n // 2):
+            block = self.source(self.me, step)
+            self.far(step - 1, block, block).wait_recv()
+            self.near(step, block).start()
+
+    def finish(self):
+        for step in range(self.n // 2):
+            self.near(step, self.source(self.partner, step)).wait_recv()
+
+    def drain(self):
+        for step in range(1, self.n // 2):
+            self.far(step - 1, self.me, lax.rem(self.me + 2 * step, self.n)).wait_send()
+        for step in range(self.n // 2):
+            self.near(step, self.source(self.me, step)).wait_send()
+
+
+def peers_in_order(n):
+    order = (6, 2, 4, 7, 3, 5, 1) if n == 8 else tuple(range(n - 1, 0, -1))
+    return order + (0,)
+
+
+def one_hot(slot_rows, target, per):
+    lane_slots = lax.broadcasted_iota(jnp.int32, (per, 1), 0) + target * per
+    return jnp.where(
+        (lane_slots == slot_rows[0:1, :]) | (lane_slots == slot_rows[1:2, :]), 1.0, 0.0
+    ).astype(BF16)
+
+
+GRAD_PARTS = 2
+
+
+def front_kernel(n_dp, n_tensor, experts, capacity, fast, *refs):
+    (tokens_ref, cotangent_ref, weight_ref, extra_ref, out_ref, routes_ref) = refs[:6]
+    refs = refs[6:]
+    (hidden_ref, projected_ref, weights_ref, extras_ref, outs_ref) = refs[:5]
+    refs = refs[5:]
+    if fast:
+        (grad_rows_ref, slot_rows_ref, slot_columns_ref) = refs[:3]
+        refs = refs[3:]
+    (
+        gain,
+        extra_send,
+        extra_recv,
+        line_send,
+        line_recv,
+        weight_far_send,
+        weight_far_recv,
+        weight_near_send,
+        weight_near_recv,
+        out_far_send,
+        out_far_recv,
+        out_near_send,
+        out_near_recv,
+        stream_send,
+        stream_recv,
+    ) = refs[:15]
+    refs = refs[15:]
+    if fast:
+        grads, picks, grad_send, row_send, row_recv, row_own = refs
+    own_rows, width = tokens_ref.shape
+    seq_len = own_rows * n_tensor
+    depth = extra_ref.shape[1]
+    me = lax.axis_index("dp")
+    me_t = lax.axis_index("tensor")
+    per = experts // n_dp * capacity
+    greet([("dp", n_dp), ("tensor", n_tensor)])
+    extras_ref[me] = extra_ref[...]
+    copies = []
+    for step in range(1, n_dp):
+        peer = lax.rem(me + step, n_dp)
+        copy = remote(
+            extra_ref, extras_ref.at[me], extra_send.at[step - 1], extra_recv.at[step - 1], "dp", peer
+        )
+        copy.start()
+        copies.append(copy)
+    streams = []
+    part = width // GRAD_PARTS
+    if fast:
+        for j in range(GRAD_PARTS):
+            grads[j, me_t] = cotangent_ref[:, j * part : (j + 1) * part]
+            streams.append(grads.at[j])
+    streams.append(hidden_ref)
+    lines = Streams(n_tensor, streams, stream_send, stream_recv)
+    last = len(streams) - 1
+    if fast:
+        lines.turn(0)
+    weights_ref[me] = weight_ref[...]
+    weights = Spread(
+        n_dp, weights_ref, weight_far_send, weight_far_recv, weight_near_send, weight_near_recv
+    )
+    weights.start()
+    outs_ref[me, me_t] = out_ref[...]
+    line_copies = []
+    for step in range(1, n_tensor):
+        peer = lax.rem(me_t + step, n_tensor)
+        copy = remote(
+            out_ref,
+            outs_ref.at[me, me_t],
+            line_send.at[step - 1],
+            line_recv.at[step - 1],
+            "tensor",
+            peer,
+        )
+        copy.start()
+        line_copies.append(copy)
+    x = tokens_ref[...].astype(F32)
+    scaled = x * lax.rsqrt(jnp.mean(x * x, axis=1, keepdims=True) + EPS)
+    for copy in copies:
+        copy.wait()
+    for block in range(n_dp):
+        gain[:, block * depth : (block + 1) * depth] = extras_ref[
+            block, experts : experts + 1, :
+        ].astype(F32)
+    hidden_ref[me_t] = (scaled * gain[...]).astype(BF16)
+
+    if fast:
+        ids = lax.broadcasted_iota(jnp.int32, (experts, seq_len), 0)
+        hits = [ids == routes_ref[k : k + 1, :] for k in range(TOP)]
+        before = lax.broadcasted_iota(jnp.int32, (seq_len, seq_len), 0) < lax.broadcasted_iota(
+            jnp.int32, (seq_len, seq_len), 1
+        )
+        ranks = nn(
+            jnp.where(hits[0] | hits[1], 1.0, 0.0).astype(BF16),
+            jnp.where(before, 1.0, 0.0).astype(BF16),
+        )
+        places = ranks + (ids * capacity).astype(F32)
+        slot_rows_ref[...] = jnp.zeros_like(slot_rows_ref)
+        for k in range(TOP):
+            row = jnp.sum(jnp.where(hits[k], places, 0.0), axis=0, keepdims=True)
+            slot_rows_ref[k : k + 1, :] = row.astype(jnp.int32)
+            for block in range(n_tensor):
+                rows = slice(block * own_rows, (block + 1) * own_rows)
+                slot_columns_ref[rows, k : k + 1] = to_column(row[:, rows]).astype(jnp.int32)
+        for target in range(n_dp):
+            picks[target] = one_hot(slot_rows_ref, target, per)
+
+    def row_copy(j, target, sender):
+        cols = slice(j * part, (j + 1) * part)
+        return remote(
+            grad_send.at[j, target],
+            grad_rows_ref.at[sender, :, cols],
+            row_send.at[j, target],
+            row_recv.at[j, sender],
+            "dp",
+            target,
+        )
+
+    def own_row_copy(j):
+        cols = slice(j * part, (j + 1) * part)
+        return pltpu.make_async_copy(
+            grad_send.at[j, me], grad_rows_ref.at[me, :, cols], row_own.at[j]
+        )
+
+    def project(block):
+        rows = pl.ds(pl.multiple_of(block * own_rows, own_rows), own_rows)
+        projected_ref[rows, :] = nn(
+            hidden_ref[block], weights_ref[...].reshape(width, weights_ref.shape[2])
+        ).astype(BF16)
+
+    def used(j, k):
+        if j == last:
+            if k > 0:
+                if k == 1:
+                    weights.finish()
+                    lines.each_new(j, 0, project)
+                lines.each_new(j, k, project)
+        elif k == n_tensor - 1:
+            values = grads[j].reshape(seq_len, part)
+            for mask in peers_in_order(n_dp):
+                target = me ^ mask
+                grad_send[j, target] = nn(picks[target], values).astype(BF16)
+                if mask:
+                    row_copy(j, target, me).start()
+                else:
+                    own_row_copy(j).start()
+
+    if not fast:
+        weights.relay()
+    spread = Spread(n_dp, outs_ref, out_far_send, out_far_recv, out_near_send, out_near_recv)
+    for turn in lines.turns():
+        if turn == 0 and fast:
+            continue
+        lines.turn(turn, used)
+        if turn == 1:
+            if fast:
+                weights.relay()
+            for copy in line_copies:
+                copy.wait_recv()
+            spread.start()
+        if turn == 2:
+            spread.relay()
+    if n_tensor < 3:
+        spread.relay()
+    spread.finish()
+    lines.drain()
+    weights.drain()
+    spread.drain()
+    for copy in line_copies:
+        copy.wait_send()
+    if fast:
+        for j in range(GRAD_PARTS):
+            own_row_copy(j).wait()
+            for step in range(1, n_dp):
+                peer = lax.rem(me + step, n_dp)
+                row_copy(j, peer, me).wait_send()
+                row_copy(j, me, peer).wait_recv()
+
+
+def front(n_dp, n_tensor, experts, capacity, fast, tokens, cotangent, weight, extra, out, routes):
+    own_rows, width = tokens.shape
+    seq_len = own_rows * n_tensor
+    depth, cols = weight.shape
+    per = experts // n_dp * capacity
+    part = width // GRAD_PARTS
+    shapes = [
+        jax.ShapeDtypeStruct((n_tensor, own_rows, width), BF16),
+        jax.ShapeDtypeStruct((seq_len, cols), BF16),
+        jax.ShapeDtypeStruct((n_dp, depth, cols), BF16),
+        jax.ShapeDtypeStruct((n_dp,) + extra.shape, BF16),
+        jax.ShapeDtypeStruct((n_dp, n_tensor) + out.shape, BF16),
+    ]
+    specs = [vspec()] * 5
+    dma = pltpu.SemaphoreType.DMA
+    streams = 1 + (GRAD_PARTS if fast else 0)
+    half = n_dp // 2
+    scratch = (
+        [pltpu.VMEM((1, width), F32)]
+        + [dma((n_dp - 1,))] * 2
+        + [dma((n_tensor - 1,))] * 2
+        + ([dma((half,))] * 4) * 2
+        + [dma((streams, 2, n_tensor - 1))] * 2
+    )
+    if fast:
+        shapes += [
+            jax.ShapeDtypeStruct((n_dp, per, width), BF16),
+            jax.ShapeDtypeStruct((8, seq_len), jnp.int32),
+            jax.ShapeDtypeStruct((seq_len, TOP), jnp.int32),
+        ]
+        specs += [any_spec(), vspec(), vspec()]
+        scratch += [
+            pltpu.VMEM((GRAD_PARTS, n_tensor, own_rows, part), BF16),
+            pltpu.VMEM((n_dp, per, seq_len), BF16),
+            pltpu.VMEM((GRAD_PARTS, n_dp, per, part), BF16),
+            dma((GRAD_PARTS, n_dp)),
+            dma((GRAD_PARTS, n_dp)),
+            dma((GRAD_PARTS,)),
+        ]
+    return pl.pallas_call(
+        functools.partial(front_kernel, n_dp, n_tensor, experts, capacity, fast),
+        out_shape=tuple(shapes),
+        in_specs=[vspec()] * 6,
+        out_specs=tuple(specs),
+        scratch_shapes=scratch,
+        compiler_params=pltpu.CompilerParams(
+            vmem_limit_bytes=VMEM_LIMIT, collective_id=3, has_side_effects=True
+        ),
+        name="front",
+    )(tokens, cotangent, weight, extra, out, routes)
+
+
+PARTS = 4
+
+
+def middle_kernel(
+    n_dp,
+    n_tensor,
+    experts,
+    capacity,
+    attended_ref,
+    outs_ref,
+    tokens_ref,
+    gain_ref,
+    router_ref,
+    slots_ref,
+    routes_ref,
+    residual_ref,
+    hidden_ref,
+    weight_own_ref,
+    rows_ref,
+    gates_ref,
+    out_matrix,
+    attended_recv,
+    everyone,
+    picks,
+    row_stage,
+    logits,
+    gate_stage,
+    attended_send_sem,
+    attended_recv_sem,
+    stream_send,
+    stream_recv,
+    row_send,
+    row_recv,
+    row_own,
+    gate_send,
+    gate_recv,
+):
+    own_rows, width = tokens_ref.shape
+    seq_len = own_rows * n_tensor
+    head_cols = attended_ref.shape[1]
+    out_cols = outs_ref.shape[2]
+    local = experts // n_dp
+    per = local * capacity
+    part = width // PARTS
+    me = lax.axis_index("dp")
+    me_t = lax.axis_index("tensor")
+    greet([("dp", n_dp), ("tensor", n_tensor)])
+
+    def rows_of(block):
+        return pl.ds(pl.multiple_of(block * own_rows, own_rows), own_rows)
+
+    copies = []
+    for step in range(1, n_tensor):
+        peer = lax.rem(me_t + step, n_tensor)
+        copy = remote(
+            attended_ref.at[rows_of(peer)],
+            attended_recv.at[me_t],
+            attended_send_sem.at[step - 1],
+            attended_recv_sem.at[step - 1],
+            "tensor",
+            peer,
+        )
+        copy.start()
+        copies.append(copy)
+    attended_recv[me_t] = attended_ref[rows_of(me_t), :]
+    for block in range(n_dp):
+        out_matrix[:, block * out_cols : (block + 1) * out_cols] = outs_ref[block]
+    weight_own_ref[...] = out_matrix[
+        pl.ds(pl.multiple_of(me_t * head_cols, head_cols), head_cols), :
+    ]
+    for target in range(n_dp):
+        picks[target] = one_hot(slots_ref, target, per)
+    for copy in copies:
+        copy.wait_recv()
+    residual = tokens_ref[...].astype(F32)
+    for block in range(n_tensor):
+        residual += nn(
+            attended_recv[block], out_matrix[block * head_cols : (block + 1) * head_cols, :]
+        )
+    residual_ref[...] = residual
+    hidden = (
+        residual
+        * lax.rsqrt(jnp.mean(residual * residual, axis=1, keepdims=True) + EPS)
+        * gain_ref[...]
+    ).astype(BF16)
+    hidden_ref[...] = hidden
+    for j in range(PARTS):
+        everyone[j, me_t] = hidden[:, j * part : (j + 1) * part]
+    lines = Streams(n_tensor, [everyone.at[j] for j in range(PARTS)], stream_send, stream_recv)
+
+    def row_copy(j, target, sender):
+        cols = slice(j * part, (j + 1) * part)
+        return remote(
+            row_stage.at[j, target],
+            rows_ref.at[sender, :, cols],
+            row_send.at[j, target],
+            row_recv.at[j, sender],
+            "dp",
+            target,
+        )
+
+    def own_row_copy(j):
+        cols = slice(j * part, (j + 1) * part)
+        return pltpu.make_async_copy(row_stage.at[j, me], rows_ref.at[me, :, cols], row_own.at[j])
+
+    def used(j, k):
+        if k < n_tensor - 1:
+            return
+        values = everyone[j].reshape(seq_len, part)
+        for mask in peers_in_order(n_dp):
+            target = me ^ mask
+            row_stage[j, target] = nn(picks[target], values).astype(BF16)
+            if mask:
+                row_copy(j, target, me).start()
+            else:
+                own_row_copy(j).start()
+        term = nt(router_ref[:, j * part : (j + 1) * part], values)
+        if j == 0:
+            logits[...] = term
+        else:
+            logits[...] += term
+
+    for turn in lines.turns():
+        lines.turn(turn, used)
+    values = logits[...]
+    exps = jnp.exp(values - jnp.max(values, axis=0, keepdims=True))
+    probs = exps / jnp.sum(exps, axis=0, keepdims=True)
+    ids = lax.broadcasted_iota(jnp.int32, (experts, seq_len), 0)
+    named = (ids == routes_ref[0:1, :]) | (ids == routes_ref[1:2, :])
+    shares = probs / jnp.sum(jnp.where(named, probs, 0.0), axis=0, keepdims=True)
+    gate_copies = []
+    for mask in peers_in_order(n_dp):
+        target = me ^ mask
+        for expert in range(local):
+            row = jnp.sum(
+                jnp.where(ids == target * local + expert, shares, 0.0), axis=0, keepdims=True
+            )
+            high = row.astype(BF16)
+            rest = row - high.astype(F32)
+            mid = rest.astype(BF16)
+            low = (rest - mid.astype(F32)).astype(BF16)
+            lanes = slice(expert * capacity, (expert + 1) * capacity)
+            pieces = nt(
+                jnp.concatenate([high, mid, low, jnp.zeros((5, seq_len), BF16)], axis=0),
+                picks[target, lanes, :],
+            )
+            gate_stage[target, :, lanes] = jnp.broadcast_to(
+                jnp.sum(pieces, axis=0, keepdims=True), (8, capacity)
+            )
+        if mask:
+            copy = remote(
+                gate_stage.at[target],
+                gates_ref.at[me],
+                gate_send.at[target],
+                gate_recv.at[me],
+                "dp",
+                target,
+            )
+            copy.start()
+            gate_copies.append(copy)
+        else:
+            gates_ref[me] = gate_stage[me]
+    lines.drain()
+    for copy in copies:
+        copy.wait_send()
+    for copy in gate_copies:
+        copy.wait_send()
+    for step in range(1, n_dp):
+        peer = lax.rem(me + step, n_dp)
+        remote(
+            gate_stage.at[me], gates_ref.at[peer], gate_send.at[me], gate_recv.at[peer], "dp", peer
+        ).wait_recv()
+    for j in range(PARTS):
+        own_row_copy(j).wait()
+        for step in range(1, n_dp):
+            peer = lax.rem(me + step, n_dp)
+            row_copy(j, peer, me).wait_send()
+            row_copy(j, me, peer).wait_recv()
+
+
+def middle(
+    n_dp, n_tensor, experts, capacity, attended, outs, tokens, gain, router_rows, slot_rows, routes
+):
+    own_rows, width = tokens.shape
+    seq_len, head_cols = attended.shape
+    per = experts // n_dp * capacity
+    part = width // PARTS
+    dma = pltpu.SemaphoreType.DMA
+    return pl.pallas_call(
+        functools.partial(middle_kernel, n_dp, n_tensor, experts, capacity),
+        out_shape=(
+            jax.ShapeDtypeStruct((own_rows, width), F32),
+            jax.ShapeDtypeStruct((own_rows, width), BF16),
+            jax.ShapeDtypeStruct((head_cols, width), BF16),
+            jax.ShapeDtypeStruct((n_dp, per, width), BF16),
+            jax.ShapeDtypeStruct((n_dp, 8, per), F32),
+        ),
+        in_specs=[vspec()] * 7,
+        out_specs=(vspec(), vspec(), vspec(), any_spec(), vspec()),
+        scratch_shapes=[
+            pltpu.VMEM((width, width), BF16),
+            pltpu.VMEM((n_tensor, own_rows, head_cols), BF16),
+            pltpu.VMEM((PARTS, n_tensor, own_rows, part), BF16),
+            pltpu.VMEM((n_dp, per, seq_len), BF16),
+            pltpu.VMEM((PARTS, n_dp, per, part), BF16),
+            pltpu.VMEM((experts, seq_len), F32),
+            pltpu.VMEM((n_dp, 8, per), F32),
+            dma((n_tensor - 1,)),
+            dma((n_tensor - 1,)),
+            dma((PARTS, 2, n_tensor - 1)),
+            dma((PARTS, 2, n_tensor - 1)),
+            dma((PARTS, n_dp)),
+            dma((PARTS, n_dp)),
+            dma((PARTS,)),
+            dma((n_dp,)),
+            dma((n_dp,)),
+        ],
+        compiler_params=pltpu.CompilerParams(
+            vmem_limit_bytes=VMEM_LIMIT, collective_id=4, has_side_effects=True
+        ),
+        name="middle",
+    )(attended, outs, tokens, gain, router_rows, slot_rows, routes)
+
+
 def merge_kernel(own_rows, slots_ref, value_ref, out_ref):
     slots = value_ref.shape[0]
     for block in range(out_ref.shape[0] // own_rows):
@@ -1113,41 +1686,42 @@
     slots = experts * capacity
 
     depth = w_qkv.shape[0]
-    bias_rows = bias_table.shape[0]
+    bias_rows = NB // n_dp
+    lanes = depth
     extra = jnp.concatenate(
         [
-            router,
-            gain_attn[:, None],
-            gain_moe[:, None],
-            jnp.pad(bias_table, ((0, depth - bias_rows), (0, 0))),
+            jnp.transpose(router),
+            gain_attn[None],
+            gain_moe[None],
+            jnp.pad(bias_table, ((0, SMALL - experts - 2 - bias_rows), (0, lanes - heads))),
         ],
-        axis=1,
-    )
-    extra = jnp.pad(extra, ((0, 0), (0, 128 - extra.shape[1])))
-    packed = lax.all_gather(
-        jnp.concatenate([w_qkv.reshape(depth, 3 * head_cols), extra], axis=1),
-        "dp",
         axis=0,
-        tiled=True,
-    )
-    qkv_matrix = packed[:, : 3 * head_cols]
-    extras = packed[:, 3 * head_cols :]
-    router_full = extras[:, :experts]
-    gain_one = extras[:, experts].astype(F32)
-    gain_two = extras[:, experts + 1].astype(F32)
-    table = (
-        extras.reshape(n_dp, depth, 128)[:, :bias_rows, experts + 2 : experts + 2 + heads]
-        .reshape(NB, heads)
-        .astype(F32)
-    )
-    out_columns = lax.all_gather(w_attn_out, "tensor", axis=0, tiled=True)
-    out_matrix = lax.all_gather(out_columns, "dp", axis=1, tiled=True)
+    )
+    fast = n_dp == 8 and slots * model_width <= 4 * 1024 * 1024
+    route_rows = jnp.pad(jnp.transpose(routes), ((0, 8 - TOP), (0, 0)))
+    gathered, projected, weights_full, extras, outs_full, *routed = front(
+        n_dp,
+        n_tensor,
+        experts,
+        capacity,
+        fast,
+        tokens,
+        cotangent,
+        w_qkv.reshape(depth, 3 * head_cols),
+        extra,
+        w_attn_out,
+        route_rows,
+    )
+    gathered_one = gathered.reshape(seq_len, model_width)
+    qkv_matrix = weights_full.reshape(model_width, 3 * head_cols)
+    router_rows = jnp.transpose(extras[:, :experts], (1, 0, 2)).reshape(experts, model_width)
+    gain_one = extras[:, experts].reshape(model_width).astype(F32)
+    gain_two = extras[:, experts + 1].reshape(model_width).astype(F32)
+    table = extras[:, experts + 2 : experts + 2 + bias_rows, :heads].reshape(NB, heads).astype(F32)
+    outs_full = outs_full.reshape(n_dp, model_width, model_width // n_dp)
 
     tokens_float = tokens.astype(F32)
     scale_one = rms_scale(tokens_float)
-    hidden_one = (tokens_float * scale_one * gain_one).astype(BF16)
-    gathered_one = lax.all_gather(hidden_one, "tensor", axis=0, tiled=True)
-    projected = jnp.dot(gathered_one, qkv_matrix, preferred_element_type=F32).astype(BF16)
     selectors = jnp.asarray(distance_selectors())
     patterns = jnp.dot(selectors, table, precision=highest)
     patterns = jnp.transpose(patterns.reshape(2, 2 * BS, heads), (2, 0, 1)).reshape(
@@ -1162,94 +1736,96 @@
     attended, lse = attention_forward(
         projected, lowest, segment_col, segment_row, patterns, far, heads
     )
-    attended_own = lax.all_to_all(
-        attended.reshape(n_tensor, own_rows, head_cols), "tensor", 0, 0
-    )
-    attended_own = jnp.transpose(attended_own, (1, 0, 2)).reshape(own_rows, n_tensor * head_cols)
-    branch = jnp.dot(attended_own, out_matrix, preferred_element_type=F32)
-    residual = tokens_float + branch
-    scale_two = rms_scale(residual)
-    hidden_two = (residual * scale_two * gain_two).astype(BF16)
-    gathered_two = lax.all_gather(hidden_two, "tensor", axis=0, tiled=True)
-
-    expert_ids = jnp.arange(experts, dtype=jnp.int32)
-
-    def gate_values(logit_values, route_rows):
-        expert_probs = jax.nn.softmax(logit_values, axis=-1)
-        picked = jnp.sum(
-            jnp.where(
-                route_rows[:, :, None] == expert_ids[None, None, :], expert_probs[:, None, :], 0.0
-            ),
-            axis=-1,
-        )
-        return picked / jnp.sum(picked, axis=1, keepdims=True)
-
-    gates = gate_values(jnp.dot(gathered_two, router_full, preferred_element_type=F32), routes)
-    slot_ids = route_slots(routes, experts, capacity)
-    slot_flat = slot_ids.reshape(-1)
-    token_ids = jnp.repeat(jnp.arange(seq_len, dtype=jnp.int32), TOP)
-    sources = jnp.full((slots,), seq_len, jnp.int32).at[slot_flat].set(token_ids)
-    slot_gates = jnp.zeros((slots,), F32).at[slot_flat].set(gates.reshape(-1))
-    grad_gathered = lax.all_gather(cotangent, "tensor", axis=0, tiled=True)
-
-    def exchange(rows):
-        parts = rows.reshape(n_dp, local_experts, capacity, model_width)
-        return [
-            lax.all_to_all(parts[:, i], "dp", 0, 0).reshape(n_dp * capacity, model_width)
-            for i in range(local_experts)
-        ]
-
-    def give_back(parts):
-        back = [
-            lax.all_to_all(part.reshape(n_dp, capacity, model_width), "dp", 0, 0) for part in parts
-        ]
-        return jnp.stack(back, axis=1).reshape(slots, model_width)
-
-    zero_row = jnp.zeros((1, model_width), BF16)
-    fast = n_dp % 2 == 0 and slots * model_width <= 4 * 1024 * 1024
     if fast:
-        per = local_experts * capacity
-
-        def move(value):
-            return lax.all_to_all(value.reshape(n_dp, per, -1), "dp", 0, 0)
-
-        rows = move(jnp.concatenate([gathered_two, zero_row], axis=0)[sources])
-        grad_rows = move(jnp.concatenate([grad_gathered, zero_row], axis=0)[sources])
-        row_gates = lax.all_to_all(
-            jnp.broadcast_to(slot_gates.reshape(n_dp, 1, per), (n_dp, 8, per)), "dp", 0, 0
+        grad_rows, slot_rows, slot_columns = routed
+        residual, hidden_two, weight_own, rows, row_gates = middle(
+            n_dp,
+            n_tensor,
+            experts,
+            capacity,
+            attended,
+            outs_full,
+            tokens,
+            gain_two[None],
+            router_rows,
+            slot_rows,
+            route_rows,
         )
         back, gate_back, value, grad_w_in, grad_w_out = run_experts(
             n_dp, capacity, rows, grad_rows, row_gates, w_in, w_out
         )
-        own_routes = lax.dynamic_slice_in_dim(routes, own_start, own_rows, 0)
-        weight_own = lax.dynamic_slice_in_dim(
-            out_matrix, lax.axis_index("tensor") * head_cols, head_cols, 0
-        )
+        own_routes = lax.dynamic_slice_in_dim(route_rows, own_start, own_rows, 1)
         grad_residual, grad_branch_all, grad_attended, small, value_back = combine(
             n_dp,
             n_tensor,
             experts,
             back.reshape(slots, model_width),
             gate_back,
-            slot_ids,
-            jnp.pad(jnp.transpose(own_routes), ((0, 8 - TOP), (0, 0))),
+            slot_columns,
+            own_routes,
             residual,
             hidden_two,
             cotangent,
-            jnp.transpose(router_full),
+            router_rows,
             gain_two[None],
             weight_own,
             value,
         )
         grad_branch_all = grad_branch_all.reshape(seq_len, model_width)
         mixture = lax.psum_scatter(
-            merge(own_rows, slot_ids, value_back.reshape(slots, model_width)),
+            merge(own_rows, slot_columns, value_back.reshape(slots, model_width)),
             "tensor",
             scatter_dimension=0,
             tiled=True,
         ).astype(F32)
         layer_out = (residual + mixture).astype(BF16)
     else:
+        router_full = jnp.transpose(router_rows)
+        out_matrix = jnp.transpose(outs_full, (1, 0, 2)).reshape(model_width, model_width)
+        attended_own = lax.all_to_all(
+            attended.reshape(n_tensor, own_rows, head_cols), "tensor", 0, 0
+        )
+        attended_own = jnp.transpose(attended_own, (1, 0, 2)).reshape(own_rows, n_tensor * head_cols)
+        branch = jnp.dot(attended_own, out_matrix, preferred_element_type=F32)
+        residual = tokens_float + branch
+        scale_two = rms_scale(residual)
+        hidden_two = (residual * scale_two * gain_two).astype(BF16)
+        gathered_two = lax.all_gather(hidden_two, "tensor", axis=0, tiled=True)
+
+        expert_ids = jnp.arange(experts, dtype=jnp.int32)
+
+        def gate_values(logit_values, route_rows):
+            expert_probs = jax.nn.softmax(logit_values, axis=-1)
+            picked = jnp.sum(
+                jnp.where(
+                    route_rows[:, :, None] == expert_ids[None, None, :], expert_probs[:, None, :], 0.0
+                ),
+                axis=-1,
+            )
+            return picked / jnp.sum(picked, axis=1, keepdims=True)
+
+        gates = gate_values(jnp.dot(gathered_two, router_full, preferred_element_type=F32), routes)
+        slot_ids = route_slots(routes, experts, capacity)
+        slot_flat = slot_ids.reshape(-1)
+        token_ids = jnp.repeat(jnp.arange(seq_len, dtype=jnp.int32), TOP)
+        sources = jnp.full((slots,), seq_len, jnp.int32).at[slot_flat].set(token_ids)
+        slot_gates = jnp.zeros((slots,), F32).at[slot_flat].set(gates.reshape(-1))
+        grad_gathered = lax.all_gather(cotangent, "tensor", axis=0, tiled=True)
+
+        def exchange(rows):
+            parts = rows.reshape(n_dp, local_experts, capacity, model_width)
+            return [
+                lax.all_to_all(parts[:, i], "dp", 0, 0).reshape(n_dp * capacity, model_width)
+                for i in range(local_experts)
+            ]
+
+        def give_back(parts):
+            back = [
+                lax.all_to_all(part.reshape(n_dp, capacity, model_width), "dp", 0, 0) for part in parts
+            ]
+            return jnp.stack(back, axis=1).reshape(slots, model_width)
+
+        zero_row = jnp.zeros((1, model_width), BF16)
         dispatched = exchange(jnp.concatenate([gathered_two, zero_row], axis=0)[sources])
         padded_grad = jnp.concatenate([grad_gathered, zero_row], axis=0)
         grad_expert = exchange((slot_gates[:, None] * padded_grad[sources]).astype(BF16))

time: 624 us -> 542 us (0.87)
  Pallas kernels: 261 us -> 474 us
  waiting for transfers between devices: 203 us -> 0.02 us
  local copies, waits for them, and re-layouts: 74.1 us -> 32.9 us
  starting transfers between devices: 17.1 us -> 0.04 us
  blocking collectives: 16.1 us -> 0 us
  matrix products: 10.4 us -> 1.75 us
  other arithmetic: 18.8 us -> 11 us
    pallas_call x0 -> x2, Pallas kernels: none -> 211 us  [the longest x1 113 us: front(): pl.pallas_call(functools.partial(front_kernel, n_dp, n_tensor, experts, c...]
    all_gather x5 -> x0, waiting for transfers between devices: 145 us -> none  [the longest x1 55.2 us: on_device(): gathered_two = lax.all_gather(hidden_two, 'tensor', axis=0, tiled=True)]
    all_to_all x4 -> x0, waiting for transfers between devices: 57.1 us -> none  [the longest x2 57.1 us: move(): return lax.all_to_all(value.reshape(n_dp, per, -1), 'dp', 0, 0)]
    gather x2 -> x0, local copies, waits for them, and re-layouts: 17.6 us -> none  [the longest x1 8.79 us: on_device(): jnp.concatenate([grad_gathered, zero_row], axis=0)[sources]]
    all_to_all x4 -> x0, starting transfers between devices: 16.6 us -> none  [the longest x2 9.47 us: move(): return lax.all_to_all(value.reshape(n_dp, per, -1), 'dp', 0, 0)]
    scatter x2 -> x0, local copies, waits for them, and re-layouts: 16.1 us -> none  [the longest x1 8.06 us: on_device(): jnp.full((slots,), seq_len, jnp.int32).at[slot_flat].set(token_ids)]
    all_gather x1 -> x0, blocking collectives: 16.1 us -> none  [on_device(): out_columns = lax.all_gather(w_attn_out, 'tensor', axis=0, tiled=True)]
    dot_general x3 -> x0, matrix products: 9.65 us -> none  [the longest x1 4.98 us: on_device(): jnp.dot(gathered_one, qkv_matrix, preferred_element_type=F32).astype(BF16)]
  transfers between devices with their start and end apart: 10 -> 1, of which waited for: 6 -> 0; matrix products, arithmetic and copies ran while one was open for 13% -> 2% of each run, Pallas kernels for 16% -> 15%
where the time goes in v4:
time: 542 us; the launch traced here: 534 us
  Pallas kernels  474 us (87%)
  local copies, waits for them, and re-layouts  32.9 us (6%)
  between operations  14.6 us (3%)
  other arithmetic  11 us (2%)
    pallas_call x1, Pallas kernels, front(): pl.pallas_call(functools.partial(front_kernel, n_dp, n_tensor, experts, c...  113 us
    pallas_call x1, Pallas kernels, middle(): pl.pallas_call(functools.partial(middle_kernel, n_dp, n_tensor, experts,...  97.5 us
    pallas_call x1, Pallas kernels, combine(): pl.pallas_call(functools.partial(combine_kernel, n_dp, n_tensor, experts)...  86.6 us
    pallas_call x1, Pallas kernels, run_experts(): pl.pallas_call(functools.partial(expert_kernel, n_dp, local, capacity), o...  72.5 us
    pallas_call x1, Pallas kernels, tail(): pl.pallas_call(functools.partial(tail_kernel, n_dp, n_tensor, experts, ta...  59.9 us
    pallas_call x1, Pallas kernels, attention_backward(): pl.pallas_call(functools.partial(attn_bwd_kernel, heads, blocks), out_sha...  19.9 us
    unnamed x28, local copies, waits for them, and re-layouts  16.8 us
    pallas_call x1, Pallas kernels, attention_forward(): pl.pallas_call(functools.partial(attn_fwd_kernel, heads, blocks), out_sha...  14.4 us
  transfers between devices with their start and end apart: 1, of which 0 were waited for; matrix products, arithmetic and copies ran while one was open for 2% of the time, Pallas kernels for 15%

profile of v4, /device:TPU:0, one launch (start us, length us, event | category | flops | bytes accessed | tf_op | source)
XLA Modules:
  0.0 534.0 jit_solution(18407573965993159358)
XLA Ops:
  7.2 0.0 reduce-scatter.2.cloned.1.call-start
  7.2 0.8 slice.57
  8.0 0.8 slice.58
  8.8 1.1 copy.44
  9.9 0.8 copy.45.refs_2_.weight_own_ref
  10.7 1.3 pad.11.refs_5_.routes_ref
  12.0 1.3 fusion.9.refs_3_
  13.4 113.3 %front.1 = (bf16[4,256,1024]{2,1,0:T(8,128)(2,1)}, bf16[1024,768]{1,0:T(8,128)(2,1)}, bf16[8,128,768]{2,1,0:T(8,128)(2,1)}, bf16[8,32,128]{2,1,0:T(8,128)(2,1)},...) custom-call(bf16[256,1024]{1,0:T(8,128)(2,1)} %tokens_ref.1, ...), custom_call_target="tpu_custom_call" | custom-call | tf_op jit(solution)/shard_map/front/pallas_call | solution.py:1376
  126.7 0.7 slice.59
  127.4 1.4 slice_convert_fusion
  128.8 1.4 copy_bitcast_fusion.router_ref
  130.2 1.4 fusion.10
  131.6 0.6 reshape.150.pattern_ref
  132.2 0.1 copy.59
  132.4 0.6 convert_reduce_fusion.far_ref
  133.0 1.7 copy.47.seg_col_ref
  134.7 1.3 pad_dynamic-slice_fusion.routes_ref
  136.0 0.7 convert_reduce_fusion.1.lo_ref
  136.7 14.4 %attn_fwd.1 = (bf16[1024,256]{1,0:T(8,128)(2,1)}, f32[1024,4]{1,0:T(8,128)}) custom-call(s32[4]{0:T(128)} %convert_reduce_fusion.1.lo_ref, bf16[1024,768]{1,0:T(8,128)(2,1)} %get-tuple-element.53.qkv_ref, s32[1024,1]{1,0:T(8,128)} %copy.47.seg_col_ref, s32[1,1024]{1,0:T(1,128)} %seg_row_ref.3, f32[8,512]{1,0:T(8,128)} %reshape.150.pattern_ref, ...), custom_call_target="tpu_custom_call" | custom-call | tf_op jit(solution)/shard_map/attn_fwd/pallas_call | solution.py:240
  151.1 97.5 %middle.1 = (f32[256,1024]{1,0:T(8,128)}, bf16[256,1024]{1,0:T(8,128)(2,1)}, bf16[256,1024]{1,0:T(8,128)(2,1)}, bf16[8,320,1024]{2,1,0:T(8,128)(2,1)}, f32[8,8,320]{2,1,0:T(8,128)}) custom-call(bf16[1024,256]{1,0:T(8,128)(2,1)} %get-tuple-element.55.attended_ref.out_ref, bf16[8,1024,128]{2,1,0:T(8,128)(2,1)} %bitcast.59, bf16[256,1024]{1,0:T(8,128)(2,1)} %tokens_ref.1, ...), custom_call_target="tpu_custom_call" | custom-call | tf_op jit(solution)/shard_map/middle/pallas_call | solution.py:1577
  248.6 72.5 %experts.1 = (bf16[8,320,1024]{2,1,0:T(8,128)(2,1)}, f32[8,8,320]{2,1,0:T(8,128)}, bf16[8,320,1024]{2,1,0:T(8,128)(2,1)}, f32[2,2,704,1024]{3,2,1,0:T(8,128)}, f32[2,704,1024]{2,1,0:T(8,128)}) custom-call(bf16[8,320,1024]{2,1,0:T(8,128)(2,1)} %get-tuple-element.60.rows_ref, bf16[8,320,1024]{2,1,0:T(8,128)(2,1)} %get-tuple-element.61.grad_ref, ...), custom_call_target="tpu_custom_call" | custom-call | tf_op jit(solution)/shard_map/experts/pallas_call | solution.py:776
  321.0 86.6 %combine.1 = (f32[256,1024]{1,0:T(8,128)}, bf16[4,256,1024]{2,1,0:T(8,128)(2,1)}, bf16[1024,256]{1,0:T(8,128)(2,1)}, f32[32,1024]{1,0:T(8,128)}, bf16[8,320,1024]{2,1,0:T(8,128)(2,1)}) custom-call(bf16[2560,1024]{1,0:T(8,128)(2,1)} %bitcast.57, f32[8,8,320]{2,1,0:T(8,128)} %get-tuple-element.64.gate_ref, s32[1024,2]{1,0:T(8,128)} %get-tuple-element.59.slots_ref, ...), custom_call_target="tpu_custom_call" | custom-call | tf_op jit(solution)/shard_map/combine/pallas_call | solution.py:991
  407.6 0.0 copy-start.4
  407.6 0.0 copy-start.5
  407.7 9.7 %merge.1 = bf16[1024,1024]{1,0:T(8,128)(2,1)} custom-call(s32[1024,2]{1,0:T(8,128)} %get-tuple-element.59.slots_ref, bf16[2560,1024]{1,0:T(8,128)(2,1)} %bitcast.58), custom_call_target="tpu_custom_call" | custom-call | tf_op jit(solution)/shard_map/merge/pallas_call | solution.py:1624
  417.3 0.0 copy-start.7
  417.3 0.0 reduce-scatter.2.cloned.1.call-update
  417.3 19.9 %attn_bwd.1 = (bf16[1024,768]{1,0:T(8,128)(2,1)}, f32[12,512]{1,0:T(8,128)}) custom-call(s32[4]{0:T(128)} %convert_reduce_fusion.1.lo_ref, bf16[1024,768]{1,0:T(8,128)(2,1)} %get-tuple-element.53.qkv_ref, bf16[1024,256]{1,0:T(8,128)(2,1)} %get-tuple-element.55.attended_ref.out_ref, bf16[1024,256]{1,0:T(8,128)(2,1)} %get-tuple-element.71.grad_ref, ...), custom_call_target="tpu_custom_call" | custom-call | tf_op jit(solution)/shard_map/attn_bwd/pallas_call | solution.py:258
  437.2 0.8 reshape.159
  438.0 0.1 slice_reduce_fusion
  438.1 0.1 copy.52
  438.2 0.0 copy-done.4
  438.2 0.0 copy-start
  438.2 0.4 fusion.11
  438.6 0.1 bitcast_add_fusion
  438.7 0.1 scatter-add.4
  438.8 0.1 copy.58
  438.9 0.0 copy-done.5
  438.9 0.5 dynamic_update_slice.3.small_ref
  439.4 0.0 copy-done.7
  439.4 0.0 copy-start.3
  439.5 0.5 bitcast_convert_fusion.1.gain_own_ref
  440.0 0.1 copy-done.3
  440.1 59.9 %tail.1 = (f32[256,1024]{1,0:T(8,128)}, f32[128,768]{1,0:T(8,128)}, f32[256,128]{1,0:T(8,128)}, f32[32,128]{1,0:T(8,128)}) custom-call(bf16[1024,1024]{1,0:T(8,128)(2,1)} %bitcast.60, bf16[1024,768]{1,0:T(8,128)(2,1)} %get-tuple-element.73.grad_ref, bf16[1024,768]{1,0:T(8,128)(2,1)} %bitcast.62, bf16[1024,256]{1,0:T(8,128)(2,1)} %get-tuple-element.55.attended_ref.out_ref, ...), custom_call_target="tpu_custom_call" | custom-call | tf_op jit(solution)/shard_map/tail/pallas_call | solution.py:517
  500.0 0.0 copy-start.1
  500.0 0.0 copy-start.6
  500.0 1.2 copy.55
  501.3 0.9 copy.56
  502.2 1.3 slice.67
  503.5 0.0 copy-done
  503.5 0.2 fusion.7
  503.7 1.5 fusion.2
  505.2 1.3 slice_bitcast_fusion.3
  506.5 1.3 slice_bitcast_fusion.2
  507.8 0.0 copy-done.2
  507.8 2.3 fusion.6
  510.1 0.0 copy-done.1
  510.1 2.1 add_convert_fusion
  512.2 0.0 copy-done.6
  512.2 0.7 copy.70
  512.9 11.3 %copy.71 = f32[2,2,704,1024]{3,2,1,0:T(8,128)} copy(f32[2,2,704,1024]{3,2,1,0:T(8,128)} %get-tuple-element.136) | data formatting | bytes 23068672
  524.2 0.0 slice-done
  524.2 0.0 slice-done.1
  524.2 2.5 copy.72
  (12 shorter events, 0.1 us)
Async XLA Ops:
  7.2 502.9 %reduce-scatter.2.cloned.1.call-start = ((), (), s32[]{:S(2)}) async-start(), calls=%async_computation.1 | async-start | bytes 2621440 | tf_op jit(solution)/shard_map/reduce_scatter | solution.py:1775
  407.6 30.6 %copy-start.4 = (f32[1024,32]{1,0:T(8,128)S(1)}, f32[1024,32]{1,0:T(8,128)}, u32[]{:S(2)}) copy-start(f32[1024,32]{1,0:T(8,128)} %constant.55.clone) | copy-start | bytes 393220
  407.6 31.2 %copy-start.5 = (f32[32,1024]{1,0:T(8,128)S(1)}, f32[32,1024]{1,0:T(8,128)}, u32[]{:S(2)}) copy-start(f32[32,1024]{1,0:T(8,128)} %get-tuple-element.76) | copy-start | bytes 393220
  417.3 22.1 %copy-start.7 = (bf16[128]{0:T(256)(128)(2,1)S(1)}, bf16[128]{0:T(256)(128)(2,1)}, u32[]{:S(2)}) copy-start(bf16[128]{0:T(256)(128)(2,1)} %param.22) | copy-start | bytes 772
  438.2 65.2 %copy-start = (bf16[256,1024]{1,0:T(8,128)(2,1)S(1)}, bf16[256,1024]{1,0:T(8,128)(2,1)}, u32[]{:S(2)}) copy-start(bf16[256,1024]{1,0:T(8,128)(2,1)} %tokens_ref.1) | copy-start | bytes 1572868
  439.4 0.7 copy-start.3
  440.1 67.7 %copy-start.2 = (f32[256,1024]{1,0:T(8,128)S(1)}, f32[256,1024]{1,0:T(8,128)}, u32[]{:S(2)}) copy-start(f32[256,1024]{1,0:T(8,128)} %get-tuple-element.69) | copy-start | bytes 3145732
  500.0 10.1 %copy-start.1 = (f32[256,1024]{1,0:T(8,128)S(1)}, f32[256,1024]{1,0:T(8,128)}, u32[]{:S(2)}) copy-start(f32[256,1024]{1,0:T(8,128)} %get-tuple-element.58.residual_ref) | copy-start | bytes 3145732
  500.0 12.2 %copy-start.6 = (f32[256,128]{1,0:T(8,128)S(1)}, f32[256,128]{1,0:T(8,128)}, u32[]{:S(2)}) copy-start(f32[256,128]{1,0:T(8,128)} %get-tuple-element.131) | copy-start | bytes 393220
  510.1 14.1 %slice-start = ((s8[5767168]{0:T(1024)(128)(4,1)}), s8[4194304]{0:T(1024)(128)(4,1)S(1)}, s32[]{:S(2)}) async-start(s8[5767168]{0:T(1024)(128)(4,1)} %bitcast.55), calls=%async_computation.2 | async-start | bytes 8388608
  512.9 11.3 %slice-start.1 = ((s8[5767168]{0:T(1024)(128)(4,1)}), s8[1572864]{0:T(1024)(128)(4,1)S(1)}, s32[]{:S(2)}) async-start(s8[5767168]{0:T(1024)(128)(4,1)} %bitcast.55), calls=%async_computation.3 | async-start | bytes 3145728
Sparse Core Ops, SparseCore 0:
  417.5 52.9 reduce-scatter.1

commit v5 on v4

--- a/solution.py
+++ b/solution.py
@@ -88,58 +88,141 @@
     for h in range(heads):
         for t in range(2):
             bias[h, t] = toeplitz(pattern_ref[2 * h + t : 2 * h + t + 1, :])
-
-
-def block_mask(qb, kb, seg_col_ref, seg_row_ref):
-    q_seg = seg_col_ref[pl.ds(pl.multiple_of(qb * BS, BS), BS), :]
-    k_seg = seg_row_ref[:, pl.ds(pl.multiple_of(kb * BS, BS), BS)]
+        bias[h, 2] = jnp.broadcast_to(pattern_ref[2 * h + 1 : 2 * h + 2, 0:1], (BS, BS))
+
+
+def block_rows(block):
+    if isinstance(block, int):
+        return pl.ds(block * BS, BS)
+    return pl.ds(pl.multiple_of(block * BS, BS), BS)
+
+
+def segment_column(qb, segment_ref):
+    return to_column(segment_ref[:, block_rows(qb)].astype(F32))
+
+
+def block_mask(qb, kb, q_segments, segment_ref):
+    k_segments = segment_ref[:, block_rows(kb)].astype(F32)
     row = lax.broadcasted_iota(jnp.int32, (BS, BS), 0) + (qb - kb) * BS
     col = lax.broadcasted_iota(jnp.int32, (BS, BS), 1)
-    return (q_seg == k_seg) & (row >= col)
-
-
-def attn_fwd_kernel(heads, blocks, lo_ref, qkv_ref, seg_col_ref, seg_row_ref, pattern_ref, far_ref, out_ref, lse_ref, bias):
+    return (q_segments == k_segments) & (row >= col)
+
+
+def forward_rows(heads, qb, low, qkv_ref, segment_ref, bias, out_ref, lse_ref):
+    width = heads * HD
+    lanes = head_lanes(heads, width)
+    q_rows = block_rows(qb)
+    q_all = (qkv_ref[q_rows, 0:width] * HD**-0.5).astype(BF16)
+    q_heads = [own_head(q_all, lanes[h], heads) for h in range(heads)]
+    q_segments = segment_column(qb, segment_ref)
+
+    def k_step(kb, carry):
+        k = qkv_ref[block_rows(kb), width : 2 * width]
+        v = qkv_ref[block_rows(kb), 2 * width : 3 * width]
+        allowed = block_mask(qb, kb, q_segments, segment_ref)
+        place = jnp.minimum(qb - kb, 2)
+        new = []
+        for h in range(heads):
+            top, total, acc = carry[3 * h : 3 * h + 3]
+            s = jnp.where(allowed, nt(q_heads[h], k) + bias[h, place], NEG)
+            top_new = jnp.maximum(top, jnp.max(s, axis=1, keepdims=True))
+            alpha = jnp.exp(top - top_new)
+            p = jnp.exp(s - top_new)
+            total = alpha * total + jnp.sum(p, axis=1, keepdims=True)
+            acc = alpha * acc + nn(p.astype(BF16), v)
+            new += [top_new, total, acc]
+        return tuple(new)
+
+    init = []
+    for h in range(heads):
+        init += [jnp.full((BS, 1), NEG, F32), jnp.zeros((BS, 1), F32), jnp.zeros((BS, width), F32)]
+    res = lax.fori_loop(low, qb + 1, k_step, tuple(init))
+    out = jnp.zeros((BS, width), F32)
+    for h in range(heads):
+        top, total, acc = res[3 * h : 3 * h + 3]
+        value = acc / total
+        out = value if heads == 1 else jnp.where(lanes[h], value, out)
+        lse_ref[q_rows, h : h + 1] = top + jnp.log(total)
+    out_ref[q_rows, :] = out.astype(BF16)
+
+
+def backward_rows(
+    heads, qb, low, qkv_ref, out_ref, grad_ref, lse_ref, segment_ref, bias, grad_qkv_ref, dk, dv, sums
+):
     width = heads * HD
     lanes = head_lanes(heads, width)
     scale = HD**-0.5
+    q_rows = block_rows(qb)
+    q_all = (qkv_ref[q_rows, 0:width] * scale).astype(BF16)
+    g_all = grad_ref[q_rows, :]
+    both = g_all.astype(F32) * out_ref[q_rows, :].astype(F32)
+    q_heads = [own_head(q_all, lanes[h], heads) for h in range(heads)]
+    g_heads = [own_head(g_all, lanes[h], heads) for h in range(heads)]
+    deltas = [jnp.sum(own_head(both, lanes[h], heads), axis=1, keepdims=True) for h in range(heads)]
+    totals = [lse_ref[q_rows, h : h + 1] for h in range(heads)]
+    q_segments = segment_column(qb, segment_ref)
+
+    def k_step(kb, dq):
+        k_rows = block_rows(kb)
+        k = qkv_ref[k_rows, width : 2 * width]
+        v = qkv_ref[k_rows, 2 * width : 3 * width]
+        allowed = block_mask(qb, kb, q_segments, segment_ref)
+        place = jnp.minimum(qb - kb, 2)
+        dk_add = jnp.zeros((BS, width), F32)
+        dv_add = jnp.zeros((BS, width), F32)
+        for h in range(heads):
+            s = jnp.where(allowed, nt(q_heads[h], k) + bias[h, place], NEG)
+            p = jnp.exp(s - totals[h])
+            gp = nt(g_heads[h], v)
+            ds = (p * (gp - deltas[h])).astype(BF16)
+            dv_add += tn(p.astype(BF16), g_heads[h])
+            dk_add += tn(ds, q_heads[h])
+            dq = dq + own_head(nn(ds, k), lanes[h], heads)
+            sums[h, place] += ds.astype(F32)
+        dk[k_rows, :] += dk_add
+        dv[k_rows, :] += dv_add
+        return dq
+
+    dq = lax.fori_loop(low, qb + 1, k_step, jnp.zeros((BS, width), F32))
+    grad_qkv_ref[q_rows, 0:width] = (dq * scale).astype(BF16)
+
+
+def backward_start(dk, dv, sums):
+    dk[...] = jnp.zeros_like(dk)
+    dv[...] = jnp.zeros_like(dv)
+    sums[...] = jnp.zeros_like(sums)
+
+
+def backward_end(heads, grad_qkv_ref, dk, dv):
+    width = heads * HD
+    grad_qkv_ref[:, width : 2 * width] = dk[...].astype(BF16)
+    grad_qkv_ref[:, 2 * width : 3 * width] = dv[...].astype(BF16)
+
+
+def diagonal_sums(heads, sums, diag_ref):
+    row = lax.broadcasted_iota(jnp.int32, (BS, BS), 0)
+    col = lax.broadcasted_iota(jnp.int32, (BS, BS), 1)
+    upside_down = jnp.where(row + col == BS - 1, 1.0, 0.0).astype(F32)
+    for h in range(heads):
+        for t in range(2):
+            flipped = jnp.dot(
+                upside_down,
+                sums[h, t],
+                precision=lax.Precision.HIGHEST,
+                preferred_element_type=F32,
+            )
+            wide = jnp.concatenate([flipped, jnp.zeros((BS, BS), F32)], axis=1)
+            skewed = pltpu.roll(wide, 0, 1, stride=1, stride_axis=0)
+            diag_ref[t, h : h + 1, :] = jnp.sum(skewed, axis=0, keepdims=True)
+        rest = jnp.sum(sums[h, 2], axis=0, keepdims=True)
+        diag_ref[2, h : h + 1, :] = jnp.concatenate([rest, jnp.zeros((1, BS), F32)], axis=1)
+
+
+def attn_fwd_kernel(heads, blocks, lo_ref, qkv_ref, segment_ref, pattern_ref, out_ref, lse_ref, bias):
     build_bias(heads, pattern_ref, bias)
 
     def q_step(qb, _):
-        q_rows = pl.ds(pl.multiple_of(qb * BS, BS), BS)
-        q_all = (qkv_ref[q_rows, 0:width] * scale).astype(BF16)
-        q_heads = [own_head(q_all, lanes[h], heads) for h in range(heads)]
-
-        def k_step(kb, carry):
-            k_rows = pl.ds(pl.multiple_of(kb * BS, BS), BS)
-            k = qkv_ref[k_rows, width : 2 * width]
-            v = qkv_ref[k_rows, 2 * width : 3 * width]
-            allowed = block_mask(qb, kb, seg_col_ref, seg_row_ref)
-            near = jnp.minimum(qb - kb, 1)
-            is_far = qb - kb >= 2
-            new = []
-            for h in range(heads):
-                top, total, acc = carry[3 * h : 3 * h + 3]
-                b = jnp.where(is_far, far_ref[h], bias[h, near])
-                s = jnp.where(allowed, nt(q_heads[h], k) + b, NEG)
-                top_new = jnp.maximum(top, jnp.max(s, axis=1, keepdims=True))
-                alpha = jnp.exp(top - top_new)
-                p = jnp.exp(s - top_new)
-                total = alpha * total + jnp.sum(p, axis=1, keepdims=True)
-                acc = alpha * acc + nn(p.astype(BF16), v)
-                new += [top_new, total, acc]
-            return tuple(new)
-
-        init = []
-        for h in range(heads):
-            init += [jnp.full((BS, 1), NEG, F32), jnp.zeros((BS, 1), F32), jnp.zeros((BS, width), F32)]
-        res = lax.fori_loop(lo_ref[qb], qb + 1, k_step, tuple(init))
-        out = jnp.zeros((BS, width), F32)
-        for h in range(heads):
-            top, total, acc = res[3 * h : 3 * h + 3]
-            value = acc / total
-            out = value if heads == 1 else jnp.where(lanes[h], value, out)
-            lse_ref[q_rows, h : h + 1] = top + jnp.log(total)
-        out_ref[q_rows, :] = out.astype(BF16)
+        forward_rows(heads, qb, lo_ref[qb], qkv_ref, segment_ref, bias, out_ref, lse_ref)
         return 0
 
     lax.fori_loop(0, blocks, q_step, 0)
@@ -153,10 +236,8 @@
     out_ref,
     grad_ref,
     lse_ref,
-    seg_col_ref,
-    seg_row_ref,
+    segment_ref,
     pattern_ref,
-    far_ref,
     grad_qkv_ref,
     diag_ref,
     bias,
@@ -164,66 +245,30 @@
     dv,
     sums,
 ):
-    width = heads * HD
-    lanes = head_lanes(heads, width)
-    scale = HD**-0.5
     build_bias(heads, pattern_ref, bias)
-    dk[...] = jnp.zeros_like(dk)
-    dv[...] = jnp.zeros_like(dv)
-    sums[...] = jnp.zeros_like(sums)
+    backward_start(dk, dv, sums)
 
     def q_step(qb, _):
-        q_rows = pl.ds(pl.multiple_of(qb * BS, BS), BS)
-        q_all = (qkv_ref[q_rows, 0:width] * scale).astype(BF16)
-        g_all = grad_ref[q_rows, :]
-        both = g_all.astype(F32) * out_ref[q_rows, :].astype(F32)
-        q_heads = [own_head(q_all, lanes[h], heads) for h in range(heads)]
-        g_heads = [own_head(g_all, lanes[h], heads) for h in range(heads)]
-        deltas = [jnp.sum(own_head(both, lanes[h], heads), axis=1, keepdims=True) for h in range(heads)]
-        totals = [lse_ref[q_rows, h : h + 1] for h in range(heads)]
-
-        def k_step(kb, dq):
-            k_rows = pl.ds(pl.multiple_of(kb * BS, BS), BS)
-            k = qkv_ref[k_rows, width : 2 * width]
-            v = qkv_ref[k_rows, 2 * width : 3 * width]
-            allowed = block_mask(qb, kb, seg_col_ref, seg_row_ref)
-            near = jnp.minimum(qb - kb, 1)
-            place = jnp.minimum(qb - kb, 2)
-            is_far = qb - kb >= 2
-            dk_add = jnp.zeros((BS, width), F32)
-            dv_add = jnp.zeros((BS, width), F32)
-            for h in range(heads):
-                b = jnp.where(is_far, far_ref[h], bias[h, near])
-                s = jnp.where(allowed, nt(q_heads[h], k) + b, NEG)
-                p = jnp.exp(s - totals[h])
-                gp = nt(g_heads[h], v)
-                ds = (p * (gp - deltas[h])).astype(BF16)
-                dv_add += tn(p.astype(BF16), g_heads[h])
-                dk_add += tn(ds, q_heads[h])
-                dq = dq + own_head(nn(ds, k), lanes[h], heads)
-                sums[h, place] += ds.astype(F32)
-            dk[k_rows, :] += dk_add
-            dv[k_rows, :] += dv_add
-            return dq
-
-        dq = lax.fori_loop(lo_ref[qb], qb + 1, k_step, jnp.zeros((BS, width), F32))
-        grad_qkv_ref[q_rows, 0:width] = (dq * scale).astype(BF16)
+        backward_rows(
+            heads,
+            qb,
+            lo_ref[qb],
+            qkv_ref,
+            out_ref,
+            grad_ref,
+            lse_ref,
+            segment_ref,
+            bias,
+            grad_qkv_ref,
+            dk,
+            dv,
+            sums,
+        )
         return 0
 
     lax.fori_loop(0, blocks, q_step, 0)
-    grad_qkv_ref[:, width : 2 * width] = dk[...].astype(BF16)
-    grad_qkv_ref[:, 2 * width : 3 * width] = dv[...].astype(BF16)
-    row = lax.broadcasted_iota(jnp.int32, (BS, BS), 0)
-    col = lax.broadcasted_iota(jnp.int32, (BS, BS), 1)
-    upside_down = jnp.where(row + col == BS - 1, 1.0, 0.0).astype(F32)
-    for h in range(heads):
-        for t in range(2):
-            flipped = jnp.dot(upside_down, sums[h, t], precision=lax.Precision.HIGHEST, preferred_element_type=F32)
-            wide = jnp.concatenate([flipped, jnp.zeros((BS, BS), F32)], axis=1)
-            skewed = pltpu.roll(wide, 0, 1, stride=1, stride_axis=0)
-            diag_ref[3 * h + t : 3 * h + t + 1, :] = jnp.sum(skewed, axis=0, keepdims=True)
-        rest = jnp.sum(sums[h, 2], axis=0, keepdims=True)
-        diag_ref[3 * h + 2 : 3 * h + 3, :] = jnp.concatenate([rest, jnp.zeros((1, BS), F32)], axis=1)
+    backward_end(heads, grad_qkv_ref, dk, dv)
+    diagonal_sums(heads, sums, diag_ref)
 
 
 def vspec():
@@ -234,7 +279,7 @@
     return pl.BlockSpec(memory_space=pltpu.SMEM)
 
 
-def attention_forward(projected, lo, seg_col, seg_row, patterns, far, heads):
+def attention_forward(projected, lo, segments, patterns, heads):
     seq_len = projected.shape[0]
     blocks = seq_len // BS
     return pl.pallas_call(
@@ -243,15 +288,15 @@
             jax.ShapeDtypeStruct((seq_len, heads * HD), BF16),
             jax.ShapeDtypeStruct((seq_len, heads), F32),
         ),
-        in_specs=[sspec(), vspec(), vspec(), vspec(), vspec(), sspec()],
+        in_specs=[sspec(), vspec(), vspec(), vspec()],
         out_specs=(vspec(), vspec()),
-        scratch_shapes=[pltpu.VMEM((heads, 2, BS, BS), F32)],
+        scratch_shapes=[pltpu.VMEM((heads, 3, BS, BS), F32)],
         compiler_params=pltpu.CompilerParams(vmem_limit_bytes=VMEM_LIMIT),
         name="attn_fwd",
-    )(lo, projected, seg_col, seg_row, patterns, far)
-
-
-def attention_backward(projected, attended, grad, lse, lo, seg_col, seg_row, patterns, far, heads):
+    )(lo, projected, segments, patterns)
+
+
+def attention_backward(projected, attended, grad, lse, lo, segments, patterns, heads):
     seq_len = projected.shape[0]
     blocks = seq_len // BS
     width = heads * HD
@@ -259,19 +304,23 @@
         functools.partial(attn_bwd_kernel, heads, blocks),
         out_shape=(
             jax.ShapeDtypeStruct((seq_len, 3 * width), BF16),
-            jax.ShapeDtypeStruct((3 * heads, 2 * BS), F32),
+            jax.ShapeDtypeStruct((3, 8, 2 * BS), F32),
         ),
-        in_specs=[sspec(), vspec(), vspec(), vspec(), vspec(), vspec(), vspec(), vspec(), sspec()],
+        in_specs=[sspec()] + [vspec()] * 6,
         out_specs=(vspec(), vspec()),
-        scratch_shapes=[
-            pltpu.VMEM((heads, 2, BS, BS), F32),
-            pltpu.VMEM((seq_len, width), F32),
-            pltpu.VMEM((seq_len, width), F32),
-            pltpu.VMEM((heads, 3, BS, BS), F32),
-        ],
+        scratch_shapes=backward_scratch(heads, seq_len),
         compiler_params=pltpu.CompilerParams(vmem_limit_bytes=VMEM_LIMIT),
         name="attn_bwd",
-    )(lo, projected, attended, grad, lse, seg_col, seg_row, patterns, far)
+    )(lo, projected, attended, grad, lse, segments, patterns)
+
+
+def backward_scratch(heads, seq_len):
+    return [
+        pltpu.VMEM((heads, 3, BS, BS), F32),
+        pltpu.VMEM((seq_len, heads * HD), F32),
+        pltpu.VMEM((seq_len, heads * HD), F32),
+        pltpu.VMEM((heads, 3, BS, BS), F32),
+    ]
 
 
 MESH = pl.DeviceIdType.MESH
@@ -346,22 +395,23 @@
 
     def finish(self):
         for k in range(self.n - 1):
-            for first in (True, False):
-                block, comes, goes, peer, out_slot, in_slot, peer_slot = self.flow(first, k)
-
-                @pl.when(goes & comes)
-                def _():
-                    self.acc[...] = self.partial(block)
-                    self.copy(peer, out_slot, in_slot).wait_recv()
-                    self.send[out_slot] = (
-                        self.acc[...] + self.recv[in_slot].astype(F32)
-                    ).astype(BF16)
-                    self.copy(peer, out_slot, peer_slot).start()
-
-                @pl.when(comes & jnp.logical_not(goes))
-                def _():
-                    self.copy(peer, 0, in_slot).wait_recv()
-                    self.total[...] += self.recv[in_slot].astype(F32)
+            self.step(k)
+
+    def step(self, k):
+        for first in (True, False):
+            block, comes, goes, peer, out_slot, in_slot, peer_slot = self.flow(first, k)
+
+            @pl.when(goes & comes)
+            def _():
+                self.acc[...] = self.partial(block)
+                self.copy(peer, out_slot, in_slot).wait_recv()
+                self.send[out_slot] = (self.acc[...] + self.recv[in_slot].astype(F32)).astype(BF16)
+                self.copy(peer, out_slot, peer_slot).start()
+
+            @pl.when(comes & jnp.logical_not(goes))
+            def _():
+                self.copy(peer, 0, in_slot).wait_recv()
+                self.total[...] += self.recv[in_slot].astype(F32)
 
     def drain(self):
         for k in range(self.n - 1):
@@ -547,48 +597,6 @@
     )(hidden, grad, weight, attended, branch, small, weight_own, gain_own)
 
 
-def line_gather(n, buf, send_sem, recv_sem, on_block):
-    me = lax.axis_index("tensor")
-
-    def copy(block, slot, k, peer):
-        return remote(
-            buf.at[block], buf.at[block], send_sem.at[slot, k], recv_sem.at[slot, k], "tensor", peer
-        )
-
-    def arrived(k, fn):
-        if k == 0:
-            fn(me, 0, 0)
-            return
-        for slot, sign in enumerate((1, -1)):
-            block = me - sign * k
-
-            @pl.when((block >= 0) & (block < n))
-            def _():
-                fn(block, slot, sign)
-
-    def outgoing(k, fn):
-        for slot, sign in enumerate((1, -1)):
-            block, peer = me - sign * k, me + sign
-
-            @pl.when((block >= 0) & (block < n) & (peer >= 0) & (peer < n))
-            def _():
-                fn(copy(block, slot, k, peer))
-
-    for k in range(n):
-        if k < n - 1:
-            outgoing(k, lambda c: c.start())
-        arrived(k, lambda block, slot, sign: on_block(block))
-        if k < n - 1:
-            arrived(
-                k + 1,
-                lambda block, slot, sign: copy(
-                    block, slot, k, jnp.clip(me - sign, 0, n - 1)
-                ).wait_recv(),
-            )
-    for k in range(n - 1):
-        outgoing(k, lambda c: c.wait_send())
-
-
 def diagonal(size):
     return lax.broadcasted_iota(jnp.int32, (size, size), 0) == lax.broadcasted_iota(
         jnp.int32, (size, size), 1
@@ -608,7 +616,8 @@
     local,
     capacity,
     rows_ref,
-    grad_ref,
+    grad_one_ref,
+    grad_two_ref,
     gates_ref,
     in_ref,
     out_ref,
@@ -678,7 +687,13 @@
             pair = (me // 2) ^ (pairs - 1 - index)
             first = 2 * pair
             rows = rows_ref[pl.ds(first, 2), part, :].reshape(two, width)
-            grads = grad_ref[pl.ds(first, 2), part, :].reshape(two, width)
+            grads = jnp.concatenate(
+                [
+                    grad_one_ref[pl.ds(first, 2), part, :].reshape(two, width // 2),
+                    grad_two_ref[pl.ds(first, 2), part, :].reshape(two, width // 2),
+                ],
+                axis=1,
+            )
             column = jnp.concatenate(
                 [to_column(gates_ref[first + j, 0:1, part]) for j in range(2)], axis=0
             )
@@ -737,7 +752,13 @@
         rows = rows_ref[:, part, :].reshape(n_dp * capacity, width)
         for half in range(2):
             put(tn(ups[half].reshape(n_dp * capacity, hidden), rows), grad_in_ref.at[expert, half])
-        grads = grad_ref[:, part, :].reshape(n_dp * capacity, width)
+        grads = jnp.concatenate(
+            [
+                grad_one_ref[:, part, :].reshape(n_dp * capacity, width // 2),
+                grad_two_ref[:, part, :].reshape(n_dp * capacity, width // 2),
+            ],
+            axis=1,
+        )
         put(tn(zs[...].reshape(n_dp * capacity, hidden), grads), grad_out_ref.at[expert])
         if expert > 0:
             pltpu.make_async_copy(
@@ -770,7 +791,7 @@
     return pl.BlockSpec(memory_space=pl.ANY)
 
 
-def run_experts(n_dp, capacity, rows, grads, gates, w_in, w_out):
+def run_experts(n_dp, capacity, rows, grads_one, grads_two, gates, w_in, w_out):
     local, _, hidden, width = w_in.shape
     slots = local * capacity
     return pl.pallas_call(
@@ -782,7 +803,7 @@
             jax.ShapeDtypeStruct(w_in.shape, F32),
             jax.ShapeDtypeStruct(w_out.shape, F32),
         ),
-        in_specs=[vspec()] * 5,
+        in_specs=[vspec()] * 6,
         out_specs=(any_spec(), vspec(), any_spec(), any_spec(), any_spec()),
         scratch_shapes=[
             pltpu.VMEM((n_dp, slots, width), BF16),
@@ -804,7 +825,7 @@
             vmem_limit_bytes=VMEM_LIMIT, collective_id=1, has_side_effects=True
         ),
         name="experts",
-    )(rows, grads, gates, w_in, w_out)
+    )(rows, grads_one, grads_two, gates, w_in, w_out)
 
 
 def chosen_slots(columns, slots):
@@ -831,7 +852,7 @@
     branch_ref,
     grad_attended_ref,
     small_ref,
-    value_back_ref,
+    merged_ref,
     acc,
     total,
     line_send,
@@ -839,7 +860,7 @@
     gate_all,
     gate_send,
     gate_recv,
-    value_own,
+    value_back,
     line_send_sem,
     line_recv_sem,
     gate_send_sem,
@@ -861,7 +882,7 @@
         peer = lax.rem(me + step, n_dp)
         copy = remote(
             value_ref.at[peer],
-            value_back_ref.at[me],
+            value_back.at[me],
             value_send_sem.at[step - 1],
             value_recv_sem.at[step - 1],
             "dp",
@@ -869,7 +890,7 @@
         )
         copy.start()
         values.append(copy)
-    fetch = pltpu.make_async_copy(value_ref.at[me], value_own, value_own_sem.at[0])
+    fetch = pltpu.make_async_copy(value_ref.at[me], value_back.at[me], value_own_sem)
     fetch.start()
 
     def partial(block):
@@ -907,17 +928,14 @@
             )
             copy.start()
             gates.append(copy)
-    fetch.wait()
-    put = pltpu.make_async_copy(value_own, value_back_ref.at[me], value_own_sem.at[1])
-    put.start()
-
     hidden = hidden_ref[...]
     router = router_ref[...]
     logits = nt(router, hidden)
     exps = jnp.exp(logits - jnp.max(logits, axis=0, keepdims=True))
     probs = exps / jnp.sum(exps, axis=0, keepdims=True)
     ids = lax.broadcasted_iota(jnp.int32, (experts, own_rows), 0)
-    first, second = ids == routes_ref[0:1, :], ids == routes_ref[1:2, :]
+    own_lanes = pl.ds(pl.multiple_of(me_t * own_rows, own_rows), own_rows)
+    first, second = ids == routes_ref[0:1, own_lanes], ids == routes_ref[1:2, own_lanes]
     prob_one = jnp.sum(jnp.where(first, probs, 0.0), axis=0, keepdims=True)
     prob_two = jnp.sum(jnp.where(second, probs, 0.0), axis=0, keepdims=True)
     both = prob_one + prob_two
@@ -957,7 +975,20 @@
             branch_ref[block], weight_ref[...]
         ).astype(BF16)
 
-    line_gather(n_tensor, branch_ref, gather_send_sem, gather_recv_sem, on_block)
+    lines = Streams(n_tensor, [branch_ref], gather_send_sem, gather_recv_sem)
+    for turn in lines.turns():
+        lines.turn(turn, lambda j, k: lines.each_new(j, k, on_block))
+        if turn == n_tensor - 2:
+            fetch.wait()
+            for copy in values:
+                copy.wait_recv()
+            for block in range(n_tensor):
+                rows = slice(block * own_rows, (block + 1) * own_rows)
+                one, two = chosen_slots(slots_ref[rows, :], slots)
+                merged_ref[rows, :] = nn(
+                    jnp.where(one | two, 1.0, 0.0).astype(BF16), value_back[...].reshape(slots, width)
+                ).astype(BF16)
+    lines.drain()
     small_ref[0:experts, :] = jnp.dot(
         grad_logits,
         hidden.astype(F32),
@@ -965,9 +996,8 @@
         preferred_element_type=F32,
     )
     line.drain()
-    put.wait()
     for copy in values:
-        copy.wait()
+        copy.wait_send()
 
 
 def combine(
@@ -995,10 +1025,10 @@
             jax.ShapeDtypeStruct((n_tensor, own_rows, width), BF16),
             jax.ShapeDtypeStruct((n_tensor * own_rows, weight.shape[0]), BF16),
             jax.ShapeDtypeStruct((SMALL, width), F32),
-            jax.ShapeDtypeStruct(value.shape, BF16),
+            jax.ShapeDtypeStruct((n_tensor * own_rows, width), BF16),
         ),
         in_specs=[vspec()] * 10 + [any_spec()],
-        out_specs=(vspec(), vspec(), vspec(), vspec(), any_spec()),
+        out_specs=(vspec(),) * 5,
         scratch_shapes=[
             pltpu.VMEM((own_rows, width), F32),
             pltpu.VMEM((own_rows, width), F32),
@@ -1007,16 +1037,16 @@
             pltpu.VMEM((8, slots), F32),
             pltpu.VMEM((n_tensor, 8, own_rows), F32),
             pltpu.VMEM((n_tensor - 1, 8, own_rows), F32),
-            pltpu.VMEM(value.shape[1:], BF16),
+            pltpu.VMEM(value.shape, BF16),
             pltpu.SemaphoreType.DMA((n_tensor - 1,)),
             pltpu.SemaphoreType.DMA((n_tensor + 1,)),
             pltpu.SemaphoreType.DMA((n_tensor - 1,)),
             pltpu.SemaphoreType.DMA((n_tensor - 1,)),
             pltpu.SemaphoreType.DMA((n_dp - 1,)),
             pltpu.SemaphoreType.DMA((n_dp - 1,)),
-            pltpu.SemaphoreType.DMA((2,)),
-            pltpu.SemaphoreType.DMA((2, n_tensor - 1)),
-            pltpu.SemaphoreType.DMA((2, n_tensor - 1)),
+            pltpu.SemaphoreType.DMA,
+            pltpu.SemaphoreType.DMA((1, 2, n_tensor - 1)),
+            pltpu.SemaphoreType.DMA((1, 2, n_tensor - 1)),
         ],
         compiler_params=pltpu.CompilerParams(
             vmem_limit_bytes=VMEM_LIMIT, collective_id=2, has_side_effects=True
@@ -1154,19 +1184,28 @@
     ).astype(BF16)
 
 
-GRAD_PARTS = 2
+GRAD_PARTS = 4
+GRAD_EARLY = 2
+
+
+def band(seq_len):
+    return -(-(seq_len // 2 - 1) // BS)
 
 
 def front_kernel(n_dp, n_tensor, experts, capacity, fast, *refs):
     (tokens_ref, cotangent_ref, weight_ref, extra_ref, out_ref, routes_ref) = refs[:6]
-    refs = refs[6:]
-    (hidden_ref, projected_ref, weights_ref, extras_ref, outs_ref) = refs[:5]
-    refs = refs[5:]
+    (segment_ref, selector_ref) = refs[6:8]
+    refs = refs[8:]
+    (hidden_ref, projected_ref, weights_ref, outs_ref) = refs[:4]
+    (pattern_ref, router_ref, gains_ref) = refs[4:7]
+    refs = refs[7:]
     if fast:
         (grad_rows_ref, slot_rows_ref, slot_columns_ref) = refs[:3]
-        refs = refs[3:]
+        (attended_ref, lse_ref, late_ref) = refs[3:6]
+        refs = refs[6:]
+    (extras_ref, table) = refs[:2]
+    refs = refs[2:]
     (
-        gain,
         extra_send,
         extra_recv,
         line_send,
@@ -1181,10 +1220,10 @@
         out_near_recv,
         stream_send,
         stream_recv,
-    ) = refs[:15]
-    refs = refs[15:]
+    ) = refs[:14]
+    refs = refs[14:]
     if fast:
-        grads, picks, grad_send, row_send, row_recv, row_own = refs
+        grads, picks, grad_send, bias, row_send, row_recv, row_own = refs
     own_rows, width = tokens_ref.shape
     seq_len = own_rows * n_tensor
     depth = extra_ref.shape[1]
@@ -1201,17 +1240,14 @@
         )
         copy.start()
         copies.append(copy)
-    streams = []
+    streams = [hidden_ref]
     part = width // GRAD_PARTS
     if fast:
         for j in range(GRAD_PARTS):
-            grads[j, me_t] = cotangent_ref[:, j * part : (j + 1) * part]
-            streams.append(grads.at[j])
-    streams.append(hidden_ref)
+            whole = grads.at[j] if j < GRAD_EARLY else late_ref.at[j - GRAD_EARLY]
+            whole[me_t] = cotangent_ref[:, j * part : (j + 1) * part]
+            streams.append(whole)
     lines = Streams(n_tensor, streams, stream_send, stream_recv)
-    last = len(streams) - 1
-    if fast:
-        lines.turn(0)
     weights_ref[me] = weight_ref[...]
     weights = Spread(
         n_dp, weights_ref, weight_far_send, weight_far_recv, weight_near_send, weight_near_recv
@@ -1236,10 +1272,28 @@
     for copy in copies:
         copy.wait()
     for block in range(n_dp):
-        gain[:, block * depth : (block + 1) * depth] = extras_ref[
-            block, experts : experts + 1, :
+        gains_ref[0:2, block * depth : (block + 1) * depth] = extras_ref[
+            block, experts : experts + 2, :
         ].astype(F32)
-    hidden_ref[me_t] = (scaled * gain[...]).astype(BF16)
+    hidden_ref[me_t] = (scaled * gains_ref[0:1, :]).astype(BF16)
+    lines.turn(0)
+    rows_each = NB // n_dp
+    for block in range(n_dp):
+        router_ref[:, block * depth : (block + 1) * depth] = extras_ref[block, 0:experts, :]
+        table[block * rows_each : (block + 1) * rows_each, :] = extras_ref[
+            block, experts + 2 : experts + 2 + rows_each, :
+        ].astype(F32)
+    patterns = lax.dot_general(
+        table[...],
+        selector_ref[...],
+        (((0,), (0,)), ((), ())),
+        precision=lax.Precision.HIGHEST,
+        preferred_element_type=F32,
+    )
+    for row in range(pattern_ref.shape[0]):
+        pattern_ref[row : row + 1, :] = patterns[
+            row // 2 : row // 2 + 1, (row % 2) * 2 * BS : (row % 2 + 1) * 2 * BS
+        ]
 
     if fast:
         ids = lax.broadcasted_iota(jnp.int32, (experts, seq_len), 0)
@@ -1286,37 +1340,52 @@
         ).astype(BF16)
 
     def used(j, k):
-        if j == last:
+        if j == 0:
             if k > 0:
                 if k == 1:
                     weights.finish()
                     lines.each_new(j, 0, project)
                 lines.each_new(j, k, project)
-        elif k == n_tensor - 1:
-            values = grads[j].reshape(seq_len, part)
+        elif k == n_tensor - 1 and j - 1 < GRAD_EARLY:
+            values = grads[j - 1].reshape(seq_len, part)
             for mask in peers_in_order(n_dp):
                 target = me ^ mask
-                grad_send[j, target] = nn(picks[target], values).astype(BF16)
+                grad_send[j - 1, target] = nn(picks[target], values).astype(BF16)
                 if mask:
-                    row_copy(j, target, me).start()
+                    row_copy(j - 1, target, me).start()
                 else:
-                    own_row_copy(j).start()
-
-    if not fast:
-        weights.relay()
+                    own_row_copy(j - 1).start()
+
+    weights.relay()
+    for copy in line_copies:
+        copy.wait_recv()
     spread = Spread(n_dp, outs_ref, out_far_send, out_far_recv, out_near_send, out_near_recv)
+    spread.start()
+    if fast:
+        build_bias(pattern_ref.shape[0] // 2, pattern_ref, bias)
+    blocks = seq_len // BS
+    done = 0
     for turn in lines.turns():
-        if turn == 0 and fast:
+        if turn == 0:
             continue
         lines.turn(turn, used)
-        if turn == 1:
-            if fast:
-                weights.relay()
-            for copy in line_copies:
-                copy.wait_recv()
-            spread.start()
         if turn == 2:
             spread.relay()
+        if fast and turn >= n_tensor - 1:
+            while done < blocks and done <= turn - (n_tensor - 1):
+                forward_rows(
+                    pattern_ref.shape[0] // 2,
+                    done,
+                    max(0, done - band(seq_len)),
+                    projected_ref,
+                    segment_ref,
+                    bias,
+                    attended_ref,
+                    lse_ref,
+                )
+                done += 1
+    if fast:
+        assert done == blocks
     if n_tensor < 3:
         spread.relay()
     spread.finish()
@@ -1326,7 +1395,7 @@
     for copy in line_copies:
         copy.wait_send()
     if fast:
-        for j in range(GRAD_PARTS):
+        for j in range(GRAD_EARLY):
             own_row_copy(j).wait()
             for step in range(1, n_dp):
                 peer = lax.rem(me + step, n_dp)
@@ -1334,25 +1403,42 @@
                 row_copy(j, me, peer).wait_recv()
 
 
-def front(n_dp, n_tensor, experts, capacity, fast, tokens, cotangent, weight, extra, out, routes):
+def front(
+    n_dp,
+    n_tensor,
+    experts,
+    capacity,
+    fast,
+    tokens,
+    cotangent,
+    weight,
+    extra,
+    out,
+    routes,
+    segments,
+    selectors,
+):
     own_rows, width = tokens.shape
     seq_len = own_rows * n_tensor
     depth, cols = weight.shape
     per = experts // n_dp * capacity
     part = width // GRAD_PARTS
+    heads = cols // (3 * HD)
     shapes = [
         jax.ShapeDtypeStruct((n_tensor, own_rows, width), BF16),
         jax.ShapeDtypeStruct((seq_len, cols), BF16),
         jax.ShapeDtypeStruct((n_dp, depth, cols), BF16),
-        jax.ShapeDtypeStruct((n_dp,) + extra.shape, BF16),
         jax.ShapeDtypeStruct((n_dp, n_tensor) + out.shape, BF16),
+        jax.ShapeDtypeStruct((2 * heads, 2 * BS), F32),
+        jax.ShapeDtypeStruct((experts, width), BF16),
+        jax.ShapeDtypeStruct((2, width), F32),
     ]
-    specs = [vspec()] * 5
+    specs = [vspec()] * 7
     dma = pltpu.SemaphoreType.DMA
     streams = 1 + (GRAD_PARTS if fast else 0)
     half = n_dp // 2
     scratch = (
-        [pltpu.VMEM((1, width), F32)]
+        [pltpu.VMEM((n_dp,) + extra.shape, BF16), pltpu.VMEM((NB, depth), F32)]
         + [dma((n_dp - 1,))] * 2
         + [dma((n_tensor - 1,))] * 2
         + ([dma((half,))] * 4) * 2
@@ -1360,30 +1446,34 @@
     )
     if fast:
         shapes += [
-            jax.ShapeDtypeStruct((n_dp, per, width), BF16),
+            jax.ShapeDtypeStruct((n_dp, per, GRAD_EARLY * part), BF16),
             jax.ShapeDtypeStruct((8, seq_len), jnp.int32),
             jax.ShapeDtypeStruct((seq_len, TOP), jnp.int32),
+            jax.ShapeDtypeStruct((seq_len, heads * HD), BF16),
+            jax.ShapeDtypeStruct((seq_len, heads), F32),
+            jax.ShapeDtypeStruct((GRAD_PARTS - GRAD_EARLY, n_tensor, own_rows, part), BF16),
         ]
-        specs += [any_spec(), vspec(), vspec()]
+        specs += [any_spec()] + [vspec()] * 5
         scratch += [
-            pltpu.VMEM((GRAD_PARTS, n_tensor, own_rows, part), BF16),
+            pltpu.VMEM((GRAD_EARLY, n_tensor, own_rows, part), BF16),
             pltpu.VMEM((n_dp, per, seq_len), BF16),
-            pltpu.VMEM((GRAD_PARTS, n_dp, per, part), BF16),
-            dma((GRAD_PARTS, n_dp)),
-            dma((GRAD_PARTS, n_dp)),
-            dma((GRAD_PARTS,)),
+            pltpu.VMEM((GRAD_EARLY, n_dp, per, part), BF16),
+            pltpu.VMEM((heads, 3, BS, BS), F32),
+            dma((GRAD_EARLY, n_dp)),
+            dma((GRAD_EARLY, n_dp)),
+            dma((GRAD_EARLY,)),
         ]
     return pl.pallas_call(
         functools.partial(front_kernel, n_dp, n_tensor, experts, capacity, fast),
         out_shape=tuple(shapes),
-        in_specs=[vspec()] * 6,
+        in_specs=[vspec()] * 8,
         out_specs=tuple(specs),
         scratch_shapes=scratch,
         compiler_params=pltpu.CompilerParams(
             vmem_limit_bytes=VMEM_LIMIT, collective_id=3, has_side_effects=True
         ),
         name="front",
-    )(tokens, cotangent, weight, extra, out, routes)
+    )(tokens, cotangent, weight, extra, out, routes, segments, selectors)
 
 
 PARTS = 4
@@ -1401,16 +1491,19 @@
     router_ref,
     slots_ref,
     routes_ref,
+    late_ref,
     residual_ref,
     hidden_ref,
     weight_own_ref,
     rows_ref,
     gates_ref,
+    grad_rows_ref,
     out_matrix,
     attended_recv,
     everyone,
     picks,
     row_stage,
+    grad_stage,
     logits,
     gate_stage,
     attended_send_sem,
@@ -1420,6 +1513,9 @@
     row_send,
     row_recv,
     row_own,
+    grad_send,
+    grad_recv,
+    grad_own,
     gate_send,
     gate_recv,
 ):
@@ -1456,8 +1552,35 @@
     weight_own_ref[...] = out_matrix[
         pl.ds(pl.multiple_of(me_t * head_cols, head_cols), head_cols), :
     ]
-    for target in range(n_dp):
+    def grad_copy(j, target, sender):
+        cols = slice(j * part, (j + 1) * part)
+        return remote(
+            grad_stage.at[j, target],
+            grad_rows_ref.at[sender, :, cols],
+            grad_send.at[j, target],
+            grad_recv.at[j, sender],
+            "dp",
+            target,
+        )
+
+    def own_grad_copy(j):
+        cols = slice(j * part, (j + 1) * part)
+        return pltpu.make_async_copy(
+            grad_stage.at[j, me], grad_rows_ref.at[me, :, cols], grad_own.at[j]
+        )
+
+    late = late_ref.shape[0]
+    for mask in peers_in_order(n_dp):
+        target = me ^ mask
         picks[target] = one_hot(slots_ref, target, per)
+        for j in range(late):
+            grad_stage[j, target] = nn(
+                picks[target], late_ref[j].reshape(seq_len, part)
+            ).astype(BF16)
+            if mask:
+                grad_copy(j, target, me).start()
+            else:
+                own_grad_copy(j).start()
     for copy in copies:
         copy.wait_recv()
     residual = tokens_ref[...].astype(F32)
@@ -1558,6 +1681,12 @@
         remote(
             gate_stage.at[me], gates_ref.at[peer], gate_send.at[me], gate_recv.at[peer], "dp", peer
         ).wait_recv()
+    for j in range(late):
+        own_grad_copy(j).wait()
+        for step in range(1, n_dp):
+            peer = lax.rem(me + step, n_dp)
+            grad_copy(j, peer, me).wait_send()
+            grad_copy(j, me, peer).wait_recv()
     for j in range(PARTS):
         own_row_copy(j).wait()
         for step in range(1, n_dp):
@@ -1567,7 +1696,18 @@
 
 
 def middle(
-    n_dp, n_tensor, experts, capacity, attended, outs, tokens, gain, router_rows, slot_rows, routes
+    n_dp,
+    n_tensor,
+    experts,
+    capacity,
+    attended,
+    outs,
+    tokens,
+    gain,
+    router_rows,
+    slot_rows,
+    routes,
+    late,
 ):
     own_rows, width = tokens.shape
     seq_len, head_cols = attended.shape
@@ -1582,15 +1722,17 @@
             jax.ShapeDtypeStruct((head_cols, width), BF16),
             jax.ShapeDtypeStruct((n_dp, per, width), BF16),
             jax.ShapeDtypeStruct((n_dp, 8, per), F32),
+            jax.ShapeDtypeStruct((n_dp, per, late.shape[0] * part), BF16),
         ),
-        in_specs=[vspec()] * 7,
-        out_specs=(vspec(), vspec(), vspec(), any_spec(), vspec()),
+        in_specs=[vspec()] * 8,
+        out_specs=(vspec(), vspec(), vspec(), any_spec(), vspec(), any_spec()),
         scratch_shapes=[
             pltpu.VMEM((width, width), BF16),
             pltpu.VMEM((n_tensor, own_rows, head_cols), BF16),
             pltpu.VMEM((PARTS, n_tensor, own_rows, part), BF16),
             pltpu.VMEM((n_dp, per, seq_len), BF16),
             pltpu.VMEM((PARTS, n_dp, per, part), BF16),
+            pltpu.VMEM((late.shape[0], n_dp, per, part), BF16),
             pltpu.VMEM((experts, seq_len), F32),
             pltpu.VMEM((n_dp, 8, per), F32),
             dma((n_tensor - 1,)),
@@ -1600,6 +1742,9 @@
             dma((PARTS, n_dp)),
             dma((PARTS, n_dp)),
             dma((PARTS,)),
+            dma((late.shape[0], n_dp)),
+            dma((late.shape[0], n_dp)),
+            dma((late.shape[0],)),
             dma((n_dp,)),
             dma((n_dp,)),
         ],
@@ -1607,28 +1752,311 @@
             vmem_limit_bytes=VMEM_LIMIT, collective_id=4, has_side_effects=True
         ),
         name="middle",
-    )(attended, outs, tokens, gain, router_rows, slot_rows, routes)
-
-
-def merge_kernel(own_rows, slots_ref, value_ref, out_ref):
-    slots = value_ref.shape[0]
-    for block in range(out_ref.shape[0] // own_rows):
-        rows = slice(block * own_rows, (block + 1) * own_rows)
-        one, two = chosen_slots(slots_ref[rows, :], slots)
-        out_ref[rows, :] = nn(
-            jnp.where(one | two, 1.0, 0.0).astype(BF16), value_ref[...]
-        ).astype(BF16)
-
-
-def merge(own_rows, slot_columns, value):
+    )(attended, outs, tokens, gain, router_rows, slot_rows, routes, late)
+
+
+def last_kernel(
+    n_dp,
+    n_tensor,
+    experts,
+    heads,
+    qkv_ref,
+    attended_ref,
+    grad_attended_ref,
+    lse_ref,
+    segment_ref,
+    pattern_ref,
+    skew_ref,
+    hidden_ref,
+    weight_ref,
+    branch_ref,
+    small_ref,
+    weight_own_ref,
+    gain_own_ref,
+    merged_ref,
+    residual_ref,
+    grad_residual_ref,
+    tokens_ref,
+    gain_ref,
+    layer_ref,
+    grad_tokens_ref,
+    grad_weight_ref,
+    grad_out_ref,
+    small_out_ref,
+    bias,
+    dk,
+    dv,
+    sums,
+    grad_qkv,
+    diag,
+    acc,
+    mixture,
+    grad_hidden,
+    mix_send,
+    mix_recv,
+    line_send,
+    line_recv,
+    qkv_send,
+    qkv_recv,
+    out_send,
+    out_recv,
+    small_send,
+    small_recv,
+    small_sum,
+    gain_recv,
+    mix_send_sem,
+    mix_recv_sem,
+    line_send_sem,
+    line_recv_sem,
+    qkv_send_sem,
+    qkv_recv_sem,
+    out_send_sem,
+    out_recv_sem,
+    small_send_sem,
+    small_recv_sem,
+    gain_send_sem,
+    gain_recv_sem,
+):
+    own_rows, width = residual_ref.shape
+    seq_len = own_rows * n_tensor
+    depth = weight_own_ref.shape[0]
+    out_cols = grad_out_ref.shape[1]
+    me = lax.axis_index("dp")
+    me_t = lax.axis_index("tensor")
+    greet([("dp", n_dp), ("tensor", n_tensor)])
+
+    def rows_of(block):
+        return pl.ds(pl.multiple_of(block * own_rows, own_rows), own_rows)
+
+    mix = LineSum(
+        n_tensor,
+        lambda block: merged_ref[rows_of(block), :].astype(F32),
+        mix_send,
+        mix_recv,
+        mix_send_sem,
+        mix_recv_sem,
+        acc,
+        mixture,
+    )
+    line = LineSum(
+        n_tensor,
+        lambda block: nt(grad_qkv[rows_of(block), :], weight_ref[...]),
+        line_send,
+        line_recv,
+        line_send_sem,
+        line_recv_sem,
+        acc,
+        grad_hidden,
+    )
+    copies = []
+
+    def scatter(source, target, send_sem, recv_sem):
+        for step in range(1, n_dp):
+            peer = lax.rem(me + step, n_dp)
+            copy = remote(
+                source.at[peer],
+                target.at[step - 1],
+                send_sem.at[step - 1],
+                recv_sem.at[step - 1],
+                "dp",
+                peer,
+            )
+            copy.start()
+            copies.append(copy)
+
+    mix.start()
+    build_bias(heads, pattern_ref, bias)
+    backward_start(dk, dv, sums)
+    blocks = seq_len // BS
+    for qb in range(blocks):
+        backward_rows(
+            heads,
+            qb,
+            max(0, qb - band(seq_len)),
+            qkv_ref,
+            attended_ref,
+            grad_attended_ref,
+            lse_ref,
+            segment_ref,
+            bias,
+            grad_qkv,
+            dk,
+            dv,
+            sums,
+        )
+        if qb == 0:
+            for block in range(n_dp):
+                cols = slice(block * out_cols, (block + 1) * out_cols)
+                out_send[block] = tn(attended_ref[...], branch_ref[:, cols]).astype(BF16)
+            scatter(out_send, out_recv, out_send_sem, out_recv_sem)
+        if qb >= blocks - 2 and qb - (blocks - 2) < n_tensor - 1:
+            mix.step(qb - (blocks - 2))
+    backward_end(heads, grad_qkv, dk, dv)
+    line.start()
+    for k in range(2, n_tensor - 1):
+        mix.step(k)
+    for block in range(n_dp):
+        cols = slice(block * depth, (block + 1) * depth)
+        qkv_send[block] = tn(hidden_ref[:, cols], grad_qkv[...]).astype(BF16)
+    scatter(qkv_send, qkv_recv, qkv_send_sem, qkv_recv_sem)
+    diag[...] = jnp.zeros_like(diag)
+    diagonal_sums(heads, sums, diag)
+    tables = lax.dot_general(
+        skew_ref[...],
+        jnp.concatenate([diag[0], diag[1]], axis=1),
+        (((1,), (1,)), ((), ())),
+        precision=lax.Precision.HIGHEST,
+        preferred_element_type=F32,
+    )
+    far = jnp.sum(diag[2], axis=1, keepdims=True)
+    head = lax.broadcasted_iota(jnp.int32, (8, 8), 0)
+    lane = lax.broadcasted_iota(jnp.int32, (8, 8), 1)
+    far_row = jnp.sum(jnp.where(head == lane, far, 0.0), axis=0, keepdims=True)
+    bucket = lax.broadcasted_iota(jnp.int32, (NB, 8), 0)
+    tables += jnp.where(bucket == NB - 1, far_row, 0.0)
+    rows_each = NB // n_dp
+    for block in range(n_dp):
+        small_send[block] = small_ref[:, block * depth : (block + 1) * depth]
+        small_send[block, experts + 2 : experts + 2 + rows_each, 0:8] = tables[
+            block * rows_each : (block + 1) * rows_each, :
+        ]
+    scatter(small_send, small_recv, small_send_sem, small_recv_sem)
+    layer_ref[...] = (residual_ref[...] + mixture[...]).astype(BF16)
+    for k in range(n_tensor - 2):
+        line.step(k)
+    for copy in copies:
+        copy.wait_recv()
+    small_sum[...] = small_send[me]
+    grad_weight_ref[...] = qkv_send[me].astype(F32)
+    grad_out_ref[...] = out_send[me].astype(F32)
+    for step in range(1, n_dp):
+        small_sum[...] += small_recv[step - 1]
+        grad_weight_ref[...] += qkv_recv[step - 1].astype(F32)
+        grad_out_ref[...] += out_recv[step - 1].astype(F32)
+    column = jnp.sum(grad_weight_ref[...] * weight_own_ref[...].astype(F32), axis=1, keepdims=True)
+    small_sum[experts + 1 : experts + 2, :] = to_row(column) / gain_own_ref[...]
+    gains = []
+    for step in range(1, n_tensor):
+        peer = lax.rem(me_t + step, n_tensor)
+        copy = remote(
+            small_sum,
+            gain_recv.at[step - 1],
+            gain_send_sem.at[step - 1],
+            gain_recv_sem.at[step - 1],
+            "tensor",
+            peer,
+        )
+        copy.start()
+        gains.append(copy)
+    line.step(n_tensor - 2)
+    x = tokens_ref[...].astype(F32)
+    scale = lax.rsqrt(jnp.mean(x * x, axis=1, keepdims=True) + EPS)
+    unit = x * scale
+    grad_unit = grad_hidden[...] * gain_ref[...]
+    grad_tokens_ref[...] = (
+        grad_residual_ref[...]
+        + scale * (grad_unit - unit * jnp.mean(grad_unit * unit, axis=1, keepdims=True))
+    ).astype(BF16)
+    mix.drain()
+    line.drain()
+    for copy in copies:
+        copy.wait_send()
+    for copy in gains:
+        copy.wait()
+    small_out_ref[...] = small_sum[...]
+    shared = slice(0, experts + 2)
+    for step in range(1, n_tensor):
+        small_out_ref[shared, :] += gain_recv[step - 1, shared, :]
+
+
+def last(
+    n_dp,
+    n_tensor,
+    experts,
+    heads,
+    projected,
+    attended,
+    grad_attended,
+    lse,
+    segments,
+    patterns,
+    skew,
+    hidden,
+    weight,
+    branch,
+    small,
+    weight_own,
+    gain_own,
+    merged,
+    residual,
+    grad_residual,
+    tokens,
+    gain,
+):
+    seq_len, width = hidden.shape
+    own_rows = seq_len // n_tensor
+    depth, cols = weight_own.shape
+    out_cols = width // n_dp
+    dma = pltpu.SemaphoreType.DMA
+    line = [
+        pltpu.VMEM((n_tensor - 1, own_rows, width), BF16),
+        pltpu.VMEM((n_tensor + 1, own_rows, width), BF16),
+    ]
     return pl.pallas_call(
-        functools.partial(merge_kernel, own_rows),
-        out_shape=jax.ShapeDtypeStruct((slot_columns.shape[0], value.shape[1]), BF16),
-        in_specs=[vspec()] * 2,
-        out_specs=vspec(),
-        compiler_params=pltpu.CompilerParams(vmem_limit_bytes=VMEM_LIMIT),
-        name="merge",
-    )(slot_columns, value)
+        functools.partial(last_kernel, n_dp, n_tensor, experts, heads),
+        out_shape=(
+            jax.ShapeDtypeStruct((own_rows, width), BF16),
+            jax.ShapeDtypeStruct((own_rows, width), BF16),
+            jax.ShapeDtypeStruct((depth, cols), F32),
+            jax.ShapeDtypeStruct((heads * HD, out_cols), F32),
+            jax.ShapeDtypeStruct((SMALL, depth), F32),
+        ),
+        in_specs=[vspec()] * 18,
+        out_specs=(vspec(),) * 5,
+        scratch_shapes=backward_scratch(heads, seq_len)
+        + [
+            pltpu.VMEM((seq_len, cols), BF16),
+            pltpu.VMEM((3, 8, 2 * BS), F32),
+        ]
+        + [pltpu.VMEM((own_rows, width), F32)] * 3
+        + line * 2
+        + [
+            pltpu.VMEM((n_dp, depth, cols), BF16),
+            pltpu.VMEM((n_dp - 1, depth, cols), BF16),
+            pltpu.VMEM((n_dp, heads * HD, out_cols), BF16),
+            pltpu.VMEM((n_dp - 1, heads * HD, out_cols), BF16),
+            pltpu.VMEM((n_dp, SMALL, depth), F32),
+            pltpu.VMEM((n_dp - 1, SMALL, depth), F32),
+            pltpu.VMEM((SMALL, depth), F32),
+            pltpu.VMEM((n_tensor - 1, SMALL, depth), F32),
+        ]
+        + [dma((n_tensor - 1,)), dma((n_tensor + 1,))] * 2
+        + [dma((n_dp - 1,))] * 6
+        + [dma((n_tensor - 1,))] * 2,
+        compiler_params=pltpu.CompilerParams(
+            vmem_limit_bytes=VMEM_LIMIT, collective_id=5, has_side_effects=True
+        ),
+        name="last",
+    )(
+        projected,
+        attended,
+        grad_attended,
+        lse,
+        segments,
+        patterns,
+        skew,
+        hidden,
+        weight,
+        branch,
+        small,
+        weight_own,
+        gain_own,
+        merged,
+        residual,
+        grad_residual,
+        tokens,
+        gain,
+    )
 
 
 def rms_scale(values):
@@ -1699,7 +2127,7 @@
     )
     fast = n_dp == 8 and slots * model_width <= 4 * 1024 * 1024
     route_rows = jnp.pad(jnp.transpose(routes), ((0, 8 - TOP), (0, 0)))
-    gathered, projected, weights_full, extras, outs_full, *routed = front(
+    gathered, projected, weights_full, outs_full, patterns, router_rows, gains, *routed = front(
         n_dp,
         n_tensor,
         experts,
@@ -1711,34 +2139,33 @@
         extra,
         w_attn_out,
         route_rows,
+        segments,
+        jnp.asarray(distance_selectors().T),
     )
     gathered_one = gathered.reshape(seq_len, model_width)
     qkv_matrix = weights_full.reshape(model_width, 3 * head_cols)
-    router_rows = jnp.transpose(extras[:, :experts], (1, 0, 2)).reshape(experts, model_width)
-    gain_one = extras[:, experts].reshape(model_width).astype(F32)
-    gain_two = extras[:, experts + 1].reshape(model_width).astype(F32)
-    table = extras[:, experts + 2 : experts + 2 + bias_rows, :heads].reshape(NB, heads).astype(F32)
     outs_full = outs_full.reshape(n_dp, model_width, model_width // n_dp)
-
-    tokens_float = tokens.astype(F32)
-    scale_one = rms_scale(tokens_float)
-    selectors = jnp.asarray(distance_selectors())
-    patterns = jnp.dot(selectors, table, precision=highest)
-    patterns = jnp.transpose(patterns.reshape(2, 2 * BS, heads), (2, 0, 1)).reshape(
-        2 * heads, 2 * BS
-    )
-    far = table[NB - 1]
-    segment_row = segments
-    segment_col = segments.reshape(seq_len, 1)
-    starts = segments[0, ::BS]
-    ends = segments[0, BS - 1 :: BS]
-    lowest = jnp.sum((ends[None, :] < starts[:, None]).astype(jnp.int32), axis=1)
-    attended, lse = attention_forward(
-        projected, lowest, segment_col, segment_row, patterns, far, heads
-    )
+    weight_shard = w_qkv.reshape(depth, 3 * head_cols)
+    gain_shard = gain_attn[None].astype(F32)
+    skew = jnp.asarray(skew_selectors().T)
+
+    def finish(layer_out, grad_tokens, reduced_qkv, reduced_attn_out, small_sum, grad_w_in, grad_w_out):
+        return (
+            layer_out,
+            grad_tokens,
+            reduced_qkv.reshape(depth, 3, head_cols),
+            reduced_attn_out,
+            small_sum[experts + 2 : experts + 2 + NB // n_dp, :heads],
+            small_sum[experts + 1],
+            small_sum[experts],
+            jnp.transpose(small_sum[:experts]),
+            grad_w_in,
+            grad_w_out,
+        )
+
     if fast:
-        grad_rows, slot_rows, slot_columns = routed
-        residual, hidden_two, weight_own, rows, row_gates = middle(
+        grad_rows, slot_rows, slot_columns, attended, lse, late = routed
+        residual, hidden_two, weight_own, rows, row_gates, late_rows = middle(
             n_dp,
             n_tensor,
             experts,
@@ -1746,185 +2173,196 @@
             attended,
             outs_full,
             tokens,
-            gain_two[None],
+            gains[1:2],
             router_rows,
             slot_rows,
             route_rows,
+            late,
         )
         back, gate_back, value, grad_w_in, grad_w_out = run_experts(
-            n_dp, capacity, rows, grad_rows, row_gates, w_in, w_out
-        )
-        own_routes = lax.dynamic_slice_in_dim(route_rows, own_start, own_rows, 1)
-        grad_residual, grad_branch_all, grad_attended, small, value_back = combine(
+            n_dp, capacity, rows, grad_rows, late_rows, row_gates, w_in, w_out
+        )
+        grad_residual, grad_branch_all, grad_attended, small, merged = combine(
             n_dp,
             n_tensor,
             experts,
             back.reshape(slots, model_width),
             gate_back,
             slot_columns,
-            own_routes,
+            route_rows,
             residual,
             hidden_two,
             cotangent,
             router_rows,
-            gain_two[None],
+            gains[1:2],
             weight_own,
             value,
         )
-        grad_branch_all = grad_branch_all.reshape(seq_len, model_width)
-        mixture = lax.psum_scatter(
-            merge(own_rows, slot_columns, value_back.reshape(slots, model_width)),
-            "tensor",
-            scatter_dimension=0,
-            tiled=True,
-        ).astype(F32)
-        layer_out = (residual + mixture).astype(BF16)
-    else:
-        router_full = jnp.transpose(router_rows)
-        out_matrix = jnp.transpose(outs_full, (1, 0, 2)).reshape(model_width, model_width)
-        attended_own = lax.all_to_all(
-            attended.reshape(n_tensor, own_rows, head_cols), "tensor", 0, 0
-        )
-        attended_own = jnp.transpose(attended_own, (1, 0, 2)).reshape(own_rows, n_tensor * head_cols)
-        branch = jnp.dot(attended_own, out_matrix, preferred_element_type=F32)
-        residual = tokens_float + branch
-        scale_two = rms_scale(residual)
-        hidden_two = (residual * scale_two * gain_two).astype(BF16)
-        gathered_two = lax.all_gather(hidden_two, "tensor", axis=0, tiled=True)
-
-        expert_ids = jnp.arange(experts, dtype=jnp.int32)
-
-        def gate_values(logit_values, route_rows):
-            expert_probs = jax.nn.softmax(logit_values, axis=-1)
-            picked = jnp.sum(
-                jnp.where(
-                    route_rows[:, :, None] == expert_ids[None, None, :], expert_probs[:, None, :], 0.0
-                ),
-                axis=-1,
-            )
-            return picked / jnp.sum(picked, axis=1, keepdims=True)
-
-        gates = gate_values(jnp.dot(gathered_two, router_full, preferred_element_type=F32), routes)
-        slot_ids = route_slots(routes, experts, capacity)
-        slot_flat = slot_ids.reshape(-1)
-        token_ids = jnp.repeat(jnp.arange(seq_len, dtype=jnp.int32), TOP)
-        sources = jnp.full((slots,), seq_len, jnp.int32).at[slot_flat].set(token_ids)
-        slot_gates = jnp.zeros((slots,), F32).at[slot_flat].set(gates.reshape(-1))
-        grad_gathered = lax.all_gather(cotangent, "tensor", axis=0, tiled=True)
-
-        def exchange(rows):
-            parts = rows.reshape(n_dp, local_experts, capacity, model_width)
-            return [
-                lax.all_to_all(parts[:, i], "dp", 0, 0).reshape(n_dp * capacity, model_width)
-                for i in range(local_experts)
-            ]
-
-        def give_back(parts):
-            back = [
-                lax.all_to_all(part.reshape(n_dp, capacity, model_width), "dp", 0, 0) for part in parts
-            ]
-            return jnp.stack(back, axis=1).reshape(slots, model_width)
-
-        zero_row = jnp.zeros((1, model_width), BF16)
-        dispatched = exchange(jnp.concatenate([gathered_two, zero_row], axis=0)[sources])
-        padded_grad = jnp.concatenate([grad_gathered, zero_row], axis=0)
-        grad_expert = exchange((slot_gates[:, None] * padded_grad[sources]).astype(BF16))
-
-        outs, backs, grads_in, grads_out = [], [], [], []
-        for i in range(local_experts):
-            rows, grad_rows = dispatched[i], grad_expert[i]
-            gate_part = nt(rows, w_in[i, 0])
-            up_part = nt(rows, w_in[i, 1])
-            gelu_value, gelu_pull = jax.vjp(gelu_tanh, gate_part)
-            activated = (gelu_value * up_part).astype(BF16)
-            outs.append(nn(activated, w_out[i]).astype(BF16))
-            grad_act = nt(grad_rows, w_out[i])
-            grads_out.append(tn(activated, grad_rows))
-            grad_gate = gelu_pull(grad_act * up_part)[0].astype(BF16)
-            grad_up = (grad_act * gelu_value).astype(BF16)
-            backs.append((nn(grad_gate, w_in[i, 0]) + nn(grad_up, w_in[i, 1])).astype(BF16))
-            grads_in.append(jnp.stack([tn(grad_gate, rows), tn(grad_up, rows)]))
-        grad_w_in = jnp.stack(grads_in)
-        grad_w_out = jnp.stack(grads_out)
-        expert_out = give_back(outs)
-        grad_dispatched = give_back(backs)
-
-        first, second = slot_ids[:, 0], slot_ids[:, 1]
-        picked_first = expert_out[first].astype(F32)
-        picked_second = expert_out[second].astype(F32)
-        mixture = lax.psum_scatter(
-            (gates[:, 0:1] * picked_first + gates[:, 1:2] * picked_second).astype(BF16),
-            "tensor",
-            scatter_dimension=0,
-            tiled=True,
-        ).astype(F32)
-        layer_out = (residual + mixture).astype(BF16)
-        grad_float = grad_gathered.astype(F32)
-        grad_gate_part = jnp.stack(
-            [
-                jnp.sum(grad_float * picked_first, axis=1),
-                jnp.sum(grad_float * picked_second, axis=1),
-            ],
-            axis=1,
-        )
-        grad_hidden_part = (
-            grad_dispatched[first].astype(F32) + grad_dispatched[second].astype(F32)
-        ).astype(BF16)
-        grad_own = lax.psum_scatter(
-            grad_hidden_part, "tensor", scatter_dimension=0, tiled=True
-        ).astype(F32)
-        grad_gate_own = lax.dynamic_slice_in_dim(
-            lax.psum(grad_gate_part, "tensor"), own_start, own_rows, 0
-        )
-        own_routes = lax.dynamic_slice_in_dim(routes, own_start, own_rows, 0)
-        own_logits = jnp.dot(hidden_two, router_full, preferred_element_type=F32)
-
-        def own_gates(logit_values):
-            return gate_values(logit_values, own_routes)
-
-        _, gate_pull = jax.vjp(own_gates, own_logits)
-        grad_logits = gate_pull(grad_gate_own)[0]
-        router_float = router_full.astype(F32)
-        grad_hidden_two = grad_own + jnp.dot(grad_logits, router_float.T, precision=highest)
-        grad_router_part = jnp.dot(hidden_two.astype(F32).T, grad_logits, precision=highest)
-        grad_from_norm, grad_gain_two = norm_backward(grad_hidden_two, residual, scale_two, gain_two)
-        grad_residual = cotangent.astype(F32) + grad_from_norm
-
-        grad_branch = grad_residual.astype(BF16)
-        grad_attended_own = nt(grad_branch, out_matrix).astype(BF16)
-        grad_attended = lax.all_to_all(
-            jnp.transpose(grad_attended_own.reshape(own_rows, n_tensor, head_cols), (1, 0, 2)),
-            "tensor",
-            0,
-            0,
-        ).reshape(seq_len, head_cols)
-        grad_branch_all = lax.all_gather(grad_branch, "tensor", axis=0, tiled=True)
-        small = jnp.concatenate(
-            [
-                jnp.transpose(grad_router_part),
-                grad_gain_two[None],
-                jnp.zeros((SMALL - experts - 1, model_width), F32),
-            ],
-            axis=0,
-        )
+        results = last(
+            n_dp,
+            n_tensor,
+            experts,
+            heads,
+            projected,
+            attended,
+            grad_attended,
+            lse,
+            segments,
+            patterns,
+            skew,
+            gathered_one,
+            qkv_matrix,
+            grad_branch_all.reshape(seq_len, model_width),
+            small,
+            weight_shard,
+            gain_shard,
+            merged,
+            residual,
+            grad_residual,
+            tokens,
+            gains[0:1],
+        )
+        return finish(*results, grad_w_in, grad_w_out)
+    tokens_float = tokens.astype(F32)
+    scale_one = rms_scale(tokens_float)
+    gain_one, gain_two = gains[0], gains[1]
+    starts = segments[0, ::BS]
+    ends = segments[0, BS - 1 :: BS]
+    lowest = jnp.sum((ends[None, :] < starts[:, None]).astype(jnp.int32), axis=1)
+    attended, lse = attention_forward(projected, lowest, segments, patterns, heads)
+    router_full = jnp.transpose(router_rows)
+    out_matrix = jnp.transpose(outs_full, (1, 0, 2)).reshape(model_width, model_width)
+    attended_own = lax.all_to_all(
+        attended.reshape(n_tensor, own_rows, head_cols), "tensor", 0, 0
+    )
+    attended_own = jnp.transpose(attended_own, (1, 0, 2)).reshape(own_rows, n_tensor * head_cols)
+    branch = jnp.dot(attended_own, out_matrix, preferred_element_type=F32)
+    residual = tokens_float + branch
+    scale_two = rms_scale(residual)
+    hidden_two = (residual * scale_two * gain_two).astype(BF16)
+    gathered_two = lax.all_gather(hidden_two, "tensor", axis=0, tiled=True)
+
+    expert_ids = jnp.arange(experts, dtype=jnp.int32)
+
+    def gate_values(logit_values, route_rows):
+        expert_probs = jax.nn.softmax(logit_values, axis=-1)
+        picked = jnp.sum(
+            jnp.where(
+                route_rows[:, :, None] == expert_ids[None, None, :], expert_probs[:, None, :], 0.0
+            ),
+            axis=-1,
+        )
+        return picked / jnp.sum(picked, axis=1, keepdims=True)
+
+    gates = gate_values(jnp.dot(gathered_two, router_full, preferred_element_type=F32), routes)
+    slot_ids = route_slots(routes, experts, capacity)
+    slot_flat = slot_ids.reshape(-1)
+    token_ids = jnp.repeat(jnp.arange(seq_len, dtype=jnp.int32), TOP)
+    sources = jnp.full((slots,), seq_len, jnp.int32).at[slot_flat].set(token_ids)
+    slot_gates = jnp.zeros((slots,), F32).at[slot_flat].set(gates.reshape(-1))
+    grad_gathered = lax.all_gather(cotangent, "tensor", axis=0, tiled=True)
+
+    def exchange(rows):
+        parts = rows.reshape(n_dp, local_experts, capacity, model_width)
+        return [
+            lax.all_to_all(parts[:, i], "dp", 0, 0).reshape(n_dp * capacity, model_width)
+            for i in range(local_experts)
+        ]
+
+    def give_back(parts):
+        back = [
+            lax.all_to_all(part.reshape(n_dp, capacity, model_width), "dp", 0, 0) for part in parts
+        ]
+        return jnp.stack(back, axis=1).reshape(slots, model_width)
+
+    zero_row = jnp.zeros((1, model_width), BF16)
+    dispatched = exchange(jnp.concatenate([gathered_two, zero_row], axis=0)[sources])
+    padded_grad = jnp.concatenate([grad_gathered, zero_row], axis=0)
+    grad_expert = exchange((slot_gates[:, None] * padded_grad[sources]).astype(BF16))
+
+    outs, backs, grads_in, grads_out = [], [], [], []
+    for i in range(local_experts):
+        rows, grad_rows = dispatched[i], grad_expert[i]
+        gate_part = nt(rows, w_in[i, 0])
+        up_part = nt(rows, w_in[i, 1])
+        gelu_value, gelu_pull = jax.vjp(gelu_tanh, gate_part)
+        activated = (gelu_value * up_part).astype(BF16)
+        outs.append(nn(activated, w_out[i]).astype(BF16))
+        grad_act = nt(grad_rows, w_out[i])
+        grads_out.append(tn(activated, grad_rows))
+        grad_gate = gelu_pull(grad_act * up_part)[0].astype(BF16)
+        grad_up = (grad_act * gelu_value).astype(BF16)
+        backs.append((nn(grad_gate, w_in[i, 0]) + nn(grad_up, w_in[i, 1])).astype(BF16))
+        grads_in.append(jnp.stack([tn(grad_gate, rows), tn(grad_up, rows)]))
+    grad_w_in = jnp.stack(grads_in)
+    grad_w_out = jnp.stack(grads_out)
+    expert_out = give_back(outs)
+    grad_dispatched = give_back(backs)
+
+    first, second = slot_ids[:, 0], slot_ids[:, 1]
+    picked_first = expert_out[first].astype(F32)
+    picked_second = expert_out[second].astype(F32)
+    mixture = lax.psum_scatter(
+        (gates[:, 0:1] * picked_first + gates[:, 1:2] * picked_second).astype(BF16),
+        "tensor",
+        scatter_dimension=0,
+        tiled=True,
+    ).astype(F32)
+    layer_out = (residual + mixture).astype(BF16)
+    grad_float = grad_gathered.astype(F32)
+    grad_gate_part = jnp.stack(
+        [
+            jnp.sum(grad_float * picked_first, axis=1),
+            jnp.sum(grad_float * picked_second, axis=1),
+        ],
+        axis=1,
+    )
+    grad_hidden_part = (
+        grad_dispatched[first].astype(F32) + grad_dispatched[second].astype(F32)
+    ).astype(BF16)
+    grad_own = lax.psum_scatter(
+        grad_hidden_part, "tensor", scatter_dimension=0, tiled=True
+    ).astype(F32)
+    grad_gate_own = lax.dynamic_slice_in_dim(
+        lax.psum(grad_gate_part, "tensor"), own_start, own_rows, 0
+    )
+    own_routes = lax.dynamic_slice_in_dim(routes, own_start, own_rows, 0)
+    own_logits = jnp.dot(hidden_two, router_full, preferred_element_type=F32)
+
+    def own_gates(logit_values):
+        return gate_values(logit_values, own_routes)
+
+    _, gate_pull = jax.vjp(own_gates, own_logits)
+    grad_logits = gate_pull(grad_gate_own)[0]
+    router_float = router_full.astype(F32)
+    grad_hidden_two = grad_own + jnp.dot(grad_logits, router_float.T, precision=highest)
+    grad_router_part = jnp.dot(hidden_two.astype(F32).T, grad_logits, precision=highest)
+    grad_from_norm, grad_gain_two = norm_backward(grad_hidden_two, residual, scale_two, gain_two)
+    grad_residual = cotangent.astype(F32) + grad_from_norm
+
+    grad_branch = grad_residual.astype(BF16)
+    grad_attended_own = nt(grad_branch, out_matrix).astype(BF16)
+    grad_attended = lax.all_to_all(
+        jnp.transpose(grad_attended_own.reshape(own_rows, n_tensor, head_cols), (1, 0, 2)),
+        "tensor",
+        0,
+        0,
+    ).reshape(seq_len, head_cols)
+    grad_branch_all = lax.all_gather(grad_branch, "tensor", axis=0, tiled=True)
+    small = jnp.concatenate(
+        [
+            jnp.transpose(grad_router_part),
+            grad_gain_two[None],
+            jnp.zeros((SMALL - experts - 1, model_width), F32),
+        ],
+        axis=0,
+    )
     grad_projected, diag = attention_backward(
-        projected,
-        attended,
-        grad_attended,
-        lse,
-        lowest,
-        segment_col,
-        segment_row,
-        patterns,
-        far,
-        heads,
-    )
-    diag = diag.reshape(heads, 3, 2 * BS)
-    near = jnp.transpose(diag[:, :2].reshape(heads, 4 * BS))
-    grad_table = lax.dot_general(
-        jnp.asarray(skew_selectors()), near, (((0,), (0,)), ((), ())), precision=highest
-    )
-    grad_table = grad_table.at[NB - 1].add(jnp.sum(diag[:, 2], axis=1))
+        projected, attended, grad_attended, lse, lowest, segments, patterns, heads
+    )
+    near = jnp.concatenate([diag[0, :heads], diag[1, :heads]], axis=1)
+    grad_table = lax.dot_general(skew, near, (((1,), (1,)), ((), ())), precision=highest)
+    grad_table = grad_table.at[NB - 1].add(jnp.sum(diag[2, :heads], axis=1))
     small = jnp.transpose(small.reshape(SMALL, n_dp, depth), (1, 0, 2))
     small = lax.dynamic_update_slice(
         small, grad_table.reshape(n_dp, NB // n_dp, heads), (0, experts + 2, 0)
@@ -1939,22 +2377,13 @@
         attended,
         grad_branch_all,
         small,
-        w_qkv.reshape(depth, 3 * head_cols),
-        gain_attn[None].astype(F32),
+        weight_shard,
+        gain_shard,
     )
     grad_from_first, _ = norm_backward(grad_hidden_one, tokens_float, scale_one, gain_one)
     grad_tokens = (grad_residual + grad_from_first).astype(BF16)
-    return (
-        layer_out,
-        grad_tokens,
-        reduced_qkv.reshape(depth, 3, head_cols),
-        reduced_attn_out,
-        small_sum[experts + 2 : experts + 2 + NB // n_dp, :heads],
-        small_sum[experts + 1],
-        small_sum[experts],
-        jnp.transpose(small_sum[:experts]),
-        grad_w_in,
-        grad_w_out,
+    return finish(
+        layer_out, grad_tokens, reduced_qkv, reduced_attn_out, small_sum, grad_w_in, grad_w_out
     )
 
 

time: 542 us -> 484 us (0.89)
  Pallas kernels: 474 us -> 448 us
  between operations: 14.6 us -> 0.92 us
  other arithmetic: 11 us -> 1.86 us
    pallas_call x4 -> x1, Pallas kernels: 104 us -> 89.1 us  [last(): pl.pallas_call(functools.partial(last_kernel, n_dp, n_tensor, experts, he...]
    pallas_call x1, Pallas kernels: 113 us -> 99.5 us  [front(): pl.pallas_call(functools.partial(front_kernel, n_dp, n_tensor, experts, c...]
    convert_element_type x4 -> x1, other arithmetic: 6.39 us -> 0.51 us  [on_device(): gain_shard = gain_attn[None].astype(F32)]
    unnamed x28 -> x17, local copies, waits for them, and re-layouts: 16.8 us -> 19.2 us
  transfers between devices with their start and end apart: 1 -> 0, of which waited for: 0 -> 0; matrix products, arithmetic and copies ran while one was open for 2% -> 0% of each run, Pallas kernels for 15% -> 0%
where the time goes in v5:
time: 484 us; the launch traced here: 478 us
  Pallas kernels  448 us (93%)
  local copies, waits for them, and re-layouts  27.8 us (6%)
    pallas_call x1, Pallas kernels, front(): pl.pallas_call(functools.partial(front_kernel, n_dp, n_tensor, experts, c...  99.5 us
    pallas_call x1, Pallas kernels, middle(): pl.pallas_call(functools.partial(middle_kernel, n_dp, n_tensor, experts,...  99.2 us
    pallas_call x1, Pallas kernels, last(): pl.pallas_call(functools.partial(last_kernel, n_dp, n_tensor, experts, he...  89.1 us
    pallas_call x1, Pallas kernels, combine(): pl.pallas_call(functools.partial(combine_kernel, n_dp, n_tensor, experts)...  87.2 us
    pallas_call x1, Pallas kernels, run_experts(): pl.pallas_call(functools.partial(expert_kernel, n_dp, local, capacity), o...  72.4 us
    unnamed x17, local copies, waits for them, and re-layouts  19.2 us

profile of v5, /device:TPU:0, one launch (start us, length us, event | category | flops | bytes accessed | tf_op | source)
XLA Modules:
  0.0 478.0 jit_solution(16660517670568514276)
XLA Ops:
  0.6 1.1 copy.26
  1.7 0.8 copy.27.refs_2_.weight_own_ref
  2.6 1.3 fusion.1.refs_3_
  3.9 1.3 pad.9.refs_5_.routes_ref
  5.2 99.5 %front.1 = (bf16[4,256,1024]{2,1,0:T(8,128)(2,1)}, bf16[1024,768]{1,0:T(8,128)(2,1)}, bf16[8,128,768]{2,1,0:T(8,128)(2,1)}, bf16[8,4,256,128]{3,2,1,0:T(8,128)(2...) custom-call(bf16[256,1024]{1,0:T(8,128)(2,1)} %tokens_ref.3, ...), custom_call_target="tpu_custom_call" | custom-call | tf_op jit(solution)/shard_map/front/pallas_call | solution.py:1466
  104.8 1.4 fusion.2
  106.1 99.2 %middle.1 = (f32[256,1024]{1,0:T(8,128)}, bf16[256,1024]{1,0:T(8,128)(2,1)}, bf16[256,1024]{1,0:T(8,128)(2,1)}, bf16[8,320,1024]{2,1,0:T(8,128)(2,1)}, f32[8,8,3...) custom-call(bf16[1024,256]{1,0:T(8,128)(2,1)} %get-tuple-element.45.attended_ref, bf16[8,1024,128]{2,1,0:T(8,128)(2,1)} %bitcast.23, ...), custom_call_target="tpu_custom_call" | custom-call | tf_op jit(solution)/shard_map/middle/pallas_call | solution.py:1717
  205.3 72.4 %experts.1 = (bf16[8,320,1024]{2,1,0:T(8,128)(2,1)}, f32[8,8,320]{2,1,0:T(8,128)}, bf16[8,320,1024]{2,1,0:T(8,128)(2,1)}, f32[2,2,704,1024]{3,2,1,0:T(8,128)}, f32[2,704,1024]{2,1,0:T(8,128)}) custom-call(bf16[8,320,1024]{2,1,0:T(8,128)(2,1)} %get-tuple-element.51.rows_ref, bf16[8,320,512]{2,1,0:T(8,128)(2,1)} %get-tuple-element.52.grad_one_ref, ...), custom_call_target="tpu_custom_call" | custom-call | tf_op jit(solution)/shard_map/experts/pallas_call | solution.py:797
  277.7 0.0 copy-start.2
  277.8 87.2 %combine.1 = (f32[256,1024]{1,0:T(8,128)}, bf16[4,256,1024]{2,1,0:T(8,128)(2,1)}, bf16[1024,256]{1,0:T(8,128)(2,1)}, f32[32,1024]{1,0:T(8,128)}, bf16[1024,1024]{1,0:T(8,128)(2,1)}) custom-call(bf16[2560,1024]{1,0:T(8,128)(2,1)} %bitcast.20, f32[8,8,320]{2,1,0:T(8,128)} %get-tuple-element.56.gate_ref, s32[1024,2]{1,0:T(8,128)} %get-tuple-element.57.slots_ref, ...), custom_call_target="tpu_custom_call" | custom-call | tf_op jit(solution)/shard_map/combine/pallas_call | solution.py:1021
  365.0 0.0 copy-done.2
  365.0 0.5 bitcast_convert_fusion.gain_own_ref
  365.5 89.1 %last.1 = (bf16[256,1024]{1,0:T(8,128)(2,1)}, bf16[256,1024]{1,0:T(8,128)(2,1)}, f32[128,768]{1,0:T(8,128)}, f32[256,128]{1,0:T(8,128)}, f32[32,128]{1,0:T(8,128)}) custom-call(bf16[1024,768]{1,0:T(8,128)(2,1)} %get-tuple-element.44.qkv_ref, bf16[1024,256]{1,0:T(8,128)(2,1)} %get-tuple-element.45.attended_ref, ...), custom_call_target="tpu_custom_call" | custom-call | tf_op jit(solution)/shard_map/last/pallas_call | solution.py:2005
  454.7 0.0 copy-start
  454.7 0.0 copy-start.1
  454.7 1.2 copy.29
  455.9 0.9 copy.30
  456.8 1.3 slice.21
  458.1 1.3 slice_bitcast_fusion.1
  459.4 1.3 slice_bitcast_fusion
  460.7 1.9 copy.36
  462.6 0.0 copy-done
  462.6 0.0 slice-start
  462.6 0.8 copy.37
  463.3 0.0 copy-done.1
  463.4 0.7 copy.38
  464.0 0.0 slice-start.1
  464.0 11.3 %copy.39 = f32[2,2,704,1024]{3,2,1,0:T(8,128)} copy(f32[2,2,704,1024]{3,2,1,0:T(8,128)} %get-tuple-element.120) | data formatting | bytes 23068672
  475.3 0.0 slice-done
  475.3 0.0 slice-done.1
  475.3 2.5 copy.40
  (1 shorter events, 0.0 us)
Async XLA Ops:
  277.7 87.3 %copy-start.2 = (bf16[128]{0:T(256)(128)(2,1)S(1)}, bf16[128]{0:T(256)(128)(2,1)}, u32[]{:S(2)}) copy-start(bf16[128]{0:T(256)(128)(2,1)} %param.20) | copy-start | bytes 772
  454.7 7.9 %copy-start = (bf16[256,1024]{1,0:T(8,128)(2,1)S(1)}, bf16[256,1024]{1,0:T(8,128)(2,1)}, u32[]{:S(2)}) copy-start(bf16[256,1024]{1,0:T(8,128)(2,1)} %get-tuple-element.113) | copy-start | bytes 1572868
  454.7 8.7 %copy-start.1 = (f32[256,128]{1,0:T(8,128)S(1)}, f32[256,128]{1,0:T(8,128)}, u32[]{:S(2)}) copy-start(f32[256,128]{1,0:T(8,128)} %get-tuple-element.115) | copy-start | bytes 393220
  462.6 12.8 %slice-start = ((s8[5767168]{0:T(1024)(128)(4,1)}), s8[4194304]{0:T(1024)(128)(4,1)S(1)}, s32[]{:S(2)}) async-start(s8[5767168]{0:T(1024)(128)(4,1)} %bitcast.18), calls=%async_computation | async-start | bytes 8388608
  464.0 11.3 %slice-start.1 = ((s8[5767168]{0:T(1024)(128)(4,1)}), s8[1572864]{0:T(1024)(128)(4,1)S(1)}, s32[]{:S(2)}) async-start(s8[5767168]{0:T(1024)(128)(4,1)} %bitcast.18), calls=%async_computation.1 | async-start | bytes 3145728

commit v6 on v5

--- a/solution.py
+++ b/solution.py
@@ -352,10 +352,10 @@
 
 
 class LineSum:
-    def __init__(self, n, partial, send, recv, send_sem, recv_sem, acc, total):
-        self.n, self.partial = n, partial
+    def __init__(self, n, parts, send, recv, send_sem, recv_sem, total):
+        self.n, self.parts = n, parts
         self.send, self.recv, self.send_sem, self.recv_sem = send, recv, send_sem, recv_sem
-        self.acc, self.total = acc, total
+        self.total = total
         self.me = lax.axis_index("tensor")
 
     def flow(self, first, k):
@@ -381,17 +381,35 @@
             peer,
         )
 
-    def start(self):
-        for k in range(self.n - 1):
-            for first in (True, False):
-                block, comes, goes, peer, out_slot, in_slot, peer_slot = self.flow(first, k)
-
-                @pl.when(goes & jnp.logical_not(comes))
+    def start(self, partial=None):
+        n, me = self.n, self.me
+
+        def one(index, _):
+            block = jnp.where(me * 2 < n, n - 1 - index, index)
+            if partial is not None:
+                value = partial(block)
+                self.parts[block] = value.astype(BF16)
+
+                @pl.when(block == me)
                 def _():
-                    self.send[out_slot] = self.partial(block).astype(BF16)
-                    self.copy(peer, out_slot, peer_slot).start()
-
-        self.total[...] = self.partial(self.me)
+                    self.total[...] = value
+
+            @pl.when(jnp.logical_or(me == 0, me == n - 1) & (index < n - 1))
+            def _():
+                remote(
+                    self.parts.at[block],
+                    self.recv.at[jnp.where(me == 0, index, 2 + index)],
+                    self.send_sem.at[index],
+                    self.recv_sem.at[jnp.where(me == 0, index, 2 + index)],
+                    "tensor",
+                    jnp.where(me == 0, 1, n - 2),
+                ).start()
+
+            return 0
+
+        lax.fori_loop(0, n, one, 0)
+        if partial is None:
+            self.total[...] = self.parts[me].astype(F32)
 
     def finish(self):
         for k in range(self.n - 1):
@@ -403,9 +421,10 @@
 
             @pl.when(goes & comes)
             def _():
-                self.acc[...] = self.partial(block)
                 self.copy(peer, out_slot, in_slot).wait_recv()
-                self.send[out_slot] = (self.acc[...] + self.recv[in_slot].astype(F32)).astype(BF16)
+                self.send[out_slot] = (
+                    self.parts[block].astype(F32) + self.recv[in_slot].astype(F32)
+                ).astype(BF16)
                 self.copy(peer, out_slot, peer_slot).start()
 
             @pl.when(comes & jnp.logical_not(goes))
@@ -440,7 +459,7 @@
     grad_qkv_ref,
     grad_out_ref,
     small_out_ref,
-    acc,
+    parts,
     line_send,
     line_recv,
     qkv_send,
@@ -473,9 +492,9 @@
         return nt(grad_ref[rows, :], weight_ref[...])
 
     line = LineSum(
-        n_tensor, partial, line_send, line_recv, line_send_sem, line_recv_sem, acc, grad_hidden_ref
-    )
-    line.start()
+        n_tensor, parts, line_send, line_recv, line_send_sem, line_recv_sem, grad_hidden_ref
+    )
+    line.start(partial)
     copies = []
     for step in range(1, n_dp):
         peer = lax.rem(me + step, n_dp)
@@ -575,7 +594,7 @@
         in_specs=[vspec()] * 8,
         out_specs=(vspec(),) * 4,
         scratch_shapes=[
-            pltpu.VMEM((own_rows, width), F32),
+            pltpu.VMEM((n_tensor, own_rows, width), BF16),
             pltpu.VMEM((n_tensor - 1, own_rows, width), BF16),
             pltpu.VMEM((n_tensor + 1, own_rows, width), BF16),
             pltpu.VMEM((n_dp, depth, cols), BF16),
@@ -616,8 +635,7 @@
     local,
     capacity,
     rows_ref,
-    grad_one_ref,
-    grad_two_ref,
+    grad_ref,
     gates_ref,
     in_ref,
     out_ref,
@@ -687,13 +705,7 @@
             pair = (me // 2) ^ (pairs - 1 - index)
             first = 2 * pair
             rows = rows_ref[pl.ds(first, 2), part, :].reshape(two, width)
-            grads = jnp.concatenate(
-                [
-                    grad_one_ref[pl.ds(first, 2), part, :].reshape(two, width // 2),
-                    grad_two_ref[pl.ds(first, 2), part, :].reshape(two, width // 2),
-                ],
-                axis=1,
-            )
+            grads = grad_ref[pl.ds(first, 2), part, :].reshape(two, width)
             column = jnp.concatenate(
                 [to_column(gates_ref[first + j, 0:1, part]) for j in range(2)], axis=0
             )
@@ -752,13 +764,7 @@
         rows = rows_ref[:, part, :].reshape(n_dp * capacity, width)
         for half in range(2):
             put(tn(ups[half].reshape(n_dp * capacity, hidden), rows), grad_in_ref.at[expert, half])
-        grads = jnp.concatenate(
-            [
-                grad_one_ref[:, part, :].reshape(n_dp * capacity, width // 2),
-                grad_two_ref[:, part, :].reshape(n_dp * capacity, width // 2),
-            ],
-            axis=1,
-        )
+        grads = grad_ref[:, part, :].reshape(n_dp * capacity, width)
         put(tn(zs[...].reshape(n_dp * capacity, hidden), grads), grad_out_ref.at[expert])
         if expert > 0:
             pltpu.make_async_copy(
@@ -791,7 +797,7 @@
     return pl.BlockSpec(memory_space=pl.ANY)
 
 
-def run_experts(n_dp, capacity, rows, grads_one, grads_two, gates, w_in, w_out):
+def run_experts(n_dp, capacity, rows, grads, gates, w_in, w_out):
     local, _, hidden, width = w_in.shape
     slots = local * capacity
     return pl.pallas_call(
@@ -803,7 +809,7 @@
             jax.ShapeDtypeStruct(w_in.shape, F32),
             jax.ShapeDtypeStruct(w_out.shape, F32),
         ),
-        in_specs=[vspec()] * 6,
+        in_specs=[vspec()] * 5,
         out_specs=(any_spec(), vspec(), any_spec(), any_spec(), any_spec()),
         scratch_shapes=[
             pltpu.VMEM((n_dp, slots, width), BF16),
@@ -825,7 +831,7 @@
             vmem_limit_bytes=VMEM_LIMIT, collective_id=1, has_side_effects=True
         ),
         name="experts",
-    )(rows, grads_one, grads_two, gates, w_in, w_out)
+    )(rows, grads, gates, w_in, w_out)
 
 
 def chosen_slots(columns, slots):
@@ -853,7 +859,7 @@
     grad_attended_ref,
     small_ref,
     merged_ref,
-    acc,
+    parts,
     total,
     line_send,
     line_recv,
@@ -899,10 +905,8 @@
         )
         return nn(jnp.where(one | two, 1.0, 0.0).astype(BF16), rows_ref[...])
 
-    line = LineSum(
-        n_tensor, partial, line_send, line_recv, line_send_sem, line_recv_sem, acc, total
-    )
-    line.start()
+    line = LineSum(n_tensor, parts, line_send, line_recv, line_send_sem, line_recv_sem, total)
+    line.start(partial)
     for peer in range(n_dp):
         gate_all[0:1, peer * per : (peer + 1) * per] = gate_ref[peer, 0:1, :]
     gate_send[...] = jnp.zeros_like(gate_send)
@@ -982,12 +986,16 @@
             fetch.wait()
             for copy in values:
                 copy.wait_recv()
-            for block in range(n_tensor):
-                rows = slice(block * own_rows, (block + 1) * own_rows)
+
+            def merge(block, _):
+                rows = pl.ds(pl.multiple_of(block * own_rows, own_rows), own_rows)
                 one, two = chosen_slots(slots_ref[rows, :], slots)
-                merged_ref[rows, :] = nn(
+                merged_ref[block] = nn(
                     jnp.where(one | two, 1.0, 0.0).astype(BF16), value_back[...].reshape(slots, width)
                 ).astype(BF16)
+                return 0
+
+            lax.fori_loop(0, n_tensor, merge, 0)
     lines.drain()
     small_ref[0:experts, :] = jnp.dot(
         grad_logits,
@@ -1025,12 +1033,12 @@
             jax.ShapeDtypeStruct((n_tensor, own_rows, width), BF16),
             jax.ShapeDtypeStruct((n_tensor * own_rows, weight.shape[0]), BF16),
             jax.ShapeDtypeStruct((SMALL, width), F32),
-            jax.ShapeDtypeStruct((n_tensor * own_rows, width), BF16),
+            jax.ShapeDtypeStruct((n_tensor, own_rows, width), BF16),
         ),
         in_specs=[vspec()] * 10 + [any_spec()],
         out_specs=(vspec(),) * 5,
         scratch_shapes=[
-            pltpu.VMEM((own_rows, width), F32),
+            pltpu.VMEM((n_tensor, own_rows, width), BF16),
             pltpu.VMEM((own_rows, width), F32),
             pltpu.VMEM((n_tensor - 1, own_rows, width), BF16),
             pltpu.VMEM((n_tensor + 1, own_rows, width), BF16),
@@ -1100,10 +1108,7 @@
             k = turn - j
             if k < 0 or k > self.n - 1:
                 continue
-            if k > 0:
-                self.incoming(j, k - 1, lambda c, block: c.wait_recv())
-            if k < self.n - 1:
-                self.outgoing(j, k, lambda c: c.start())
+            self.advance(j, k)
             moved.append((j, k))
         if used is not None:
             for j, k in moved:
@@ -1111,6 +1116,12 @@
 
     def turns(self):
         return range(self.n + len(self.refs) - 1)
+
+    def advance(self, j, k):
+        if k > 0:
+            self.incoming(j, k - 1, lambda c, block: c.wait_recv())
+        if k < self.n - 1:
+            self.outgoing(j, k, lambda c: c.start())
 
     def each_new(self, j, k, fn):
         if k == 0:
@@ -1172,11 +1183,6 @@
             self.near(step, self.source(self.me, step)).wait_send()
 
 
-def peers_in_order(n):
-    order = (6, 2, 4, 7, 3, 5, 1) if n == 8 else tuple(range(n - 1, 0, -1))
-    return order + (0,)
-
-
 def one_hot(slot_rows, target, per):
     lane_slots = lax.broadcasted_iota(jnp.int32, (per, 1), 0) + target * per
     return jnp.where(
@@ -1184,77 +1190,28 @@
     ).astype(BF16)
 
 
-GRAD_PARTS = 4
-GRAD_EARLY = 2
-
-
 def band(seq_len):
     return -(-(seq_len // 2 - 1) // BS)
 
 
-def front_kernel(n_dp, n_tensor, experts, capacity, fast, *refs):
-    (tokens_ref, cotangent_ref, weight_ref, extra_ref, out_ref, routes_ref) = refs[:6]
-    (segment_ref, selector_ref) = refs[6:8]
-    refs = refs[8:]
-    (hidden_ref, projected_ref, weights_ref, outs_ref) = refs[:4]
-    (pattern_ref, router_ref, gains_ref) = refs[4:7]
-    refs = refs[7:]
-    if fast:
-        (grad_rows_ref, slot_rows_ref, slot_columns_ref) = refs[:3]
-        (attended_ref, lse_ref, late_ref) = refs[3:6]
-        refs = refs[6:]
-    (extras_ref, table) = refs[:2]
-    refs = refs[2:]
-    (
-        extra_send,
-        extra_recv,
-        line_send,
-        line_recv,
-        weight_far_send,
-        weight_far_recv,
-        weight_near_send,
-        weight_near_recv,
-        out_far_send,
-        out_far_recv,
-        out_near_send,
-        out_near_recv,
-        stream_send,
-        stream_recv,
-    ) = refs[:14]
-    refs = refs[14:]
-    if fast:
-        grads, picks, grad_send, bias, row_send, row_recv, row_own = refs
-    own_rows, width = tokens_ref.shape
-    seq_len = own_rows * n_tensor
-    depth = extra_ref.shape[1]
+def send_parameters(n_dp, n_tensor, weight_ref, extra_ref, out_ref, weights_ref, outs_ref, extras_ref, sems):
     me = lax.axis_index("dp")
     me_t = lax.axis_index("tensor")
-    per = experts // n_dp * capacity
-    greet([("dp", n_dp), ("tensor", n_tensor)])
+    (extra_send, extra_recv, line_send, line_recv) = sems[:4]
     extras_ref[me] = extra_ref[...]
-    copies = []
+    small = []
     for step in range(1, n_dp):
         peer = lax.rem(me + step, n_dp)
         copy = remote(
             extra_ref, extras_ref.at[me], extra_send.at[step - 1], extra_recv.at[step - 1], "dp", peer
         )
         copy.start()
-        copies.append(copy)
-    streams = [hidden_ref]
-    part = width // GRAD_PARTS
-    if fast:
-        for j in range(GRAD_PARTS):
-            whole = grads.at[j] if j < GRAD_EARLY else late_ref.at[j - GRAD_EARLY]
-            whole[me_t] = cotangent_ref[:, j * part : (j + 1) * part]
-            streams.append(whole)
-    lines = Streams(n_tensor, streams, stream_send, stream_recv)
+        small.append(copy)
     weights_ref[me] = weight_ref[...]
-    weights = Spread(
-        n_dp, weights_ref, weight_far_send, weight_far_recv, weight_near_send, weight_near_recv
-    )
+    weights = Spread(n_dp, weights_ref, *sems[4:8])
     weights.start()
     outs_ref[me, me_t] = out_ref[...]
-    line_copies = []
+    along = []
     for step in range(1, n_tensor):
         peer = lax.rem(me_t + step, n_tensor)
         copy = remote(
@@ -1266,17 +1223,12 @@
             peer,
         )
         copy.start()
-        line_copies.append(copy)
-    x = tokens_ref[...].astype(F32)
-    scaled = x * lax.rsqrt(jnp.mean(x * x, axis=1, keepdims=True) + EPS)
-    for copy in copies:
-        copy.wait()
-    for block in range(n_dp):
-        gains_ref[0:2, block * depth : (block + 1) * depth] = extras_ref[
-            block, experts : experts + 2, :
-        ].astype(F32)
-    hidden_ref[me_t] = (scaled * gains_ref[0:1, :]).astype(BF16)
-    lines.turn(0)
+        along.append(copy)
+    return small, weights, Spread(n_dp, outs_ref, *sems[8:12]), along
+
+
+def unpack_parameters(n_dp, experts, extras_ref, selector_ref, router_ref, table, pattern_ref):
+    depth = table.shape[1]
     rows_each = NB // n_dp
     for block in range(n_dp):
         router_ref[:, block * depth : (block + 1) * depth] = extras_ref[block, 0:experts, :]
@@ -1295,43 +1247,64 @@
             row // 2 : row // 2 + 1, (row % 2) * 2 * BS : (row % 2 + 1) * 2 * BS
         ]
 
-    if fast:
-        ids = lax.broadcasted_iota(jnp.int32, (experts, seq_len), 0)
-        hits = [ids == routes_ref[k : k + 1, :] for k in range(TOP)]
-        before = lax.broadcasted_iota(jnp.int32, (seq_len, seq_len), 0) < lax.broadcasted_iota(
-            jnp.int32, (seq_len, seq_len), 1
-        )
-        ranks = nn(
-            jnp.where(hits[0] | hits[1], 1.0, 0.0).astype(BF16),
-            jnp.where(before, 1.0, 0.0).astype(BF16),
-        )
-        places = ranks + (ids * capacity).astype(F32)
-        slot_rows_ref[...] = jnp.zeros_like(slot_rows_ref)
-        for k in range(TOP):
-            row = jnp.sum(jnp.where(hits[k], places, 0.0), axis=0, keepdims=True)
-            slot_rows_ref[k : k + 1, :] = row.astype(jnp.int32)
-            for block in range(n_tensor):
-                rows = slice(block * own_rows, (block + 1) * own_rows)
-                slot_columns_ref[rows, k : k + 1] = to_column(row[:, rows]).astype(jnp.int32)
-        for target in range(n_dp):
-            picks[target] = one_hot(slot_rows_ref, target, per)
-
-    def row_copy(j, target, sender):
-        cols = slice(j * part, (j + 1) * part)
-        return remote(
-            grad_send.at[j, target],
-            grad_rows_ref.at[sender, :, cols],
-            row_send.at[j, target],
-            row_recv.at[j, sender],
-            "dp",
-            target,
-        )
-
-    def own_row_copy(j):
-        cols = slice(j * part, (j + 1) * part)
-        return pltpu.make_async_copy(
-            grad_send.at[j, me], grad_rows_ref.at[me, :, cols], row_own.at[j]
-        )
+
+def first_hidden(n_dp, experts, tokens_ref, extras_ref, gains_ref, small):
+    depth = extras_ref.shape[2]
+    x = tokens_ref[...].astype(F32)
+    scaled = x * lax.rsqrt(jnp.mean(x * x, axis=1, keepdims=True) + EPS)
+    for copy in small:
+        copy.wait()
+    for block in range(n_dp):
+        gains_ref[0:2, block * depth : (block + 1) * depth] = extras_ref[
+            block, experts : experts + 2, :
+        ].astype(F32)
+    return (scaled * gains_ref[0:1, :]).astype(BF16)
+
+
+def parameter_sems(n_dp, n_tensor):
+    dma = pltpu.SemaphoreType.DMA
+    return (
+        [dma((n_dp - 1,))] * 2 + [dma((n_tensor - 1,))] * 2 + [dma((n_dp // 2,))] * 8
+    )
+
+
+def front_kernel(
+    n_dp,
+    n_tensor,
+    experts,
+    tokens_ref,
+    weight_ref,
+    extra_ref,
+    out_ref,
+    selector_ref,
+    hidden_ref,
+    projected_ref,
+    weights_ref,
+    outs_ref,
+    pattern_ref,
+    router_ref,
+    gains_ref,
+    extras_ref,
+    table,
+    *sems,
+):
+    own_rows, width = tokens_ref.shape
+    me_t = lax.axis_index("tensor")
+    greet([("dp", n_dp), ("tensor", n_tensor)])
+    small, weights, spread, along = send_parameters(
+        n_dp, n_tensor, weight_ref, extra_ref, out_ref, weights_ref, outs_ref, extras_ref, sems
+    )
+    hidden_ref[me_t] = first_hidden(n_dp, experts, tokens_ref, extras_ref, gains_ref, small)
+    lines = Streams(n_tensor, [hidden_ref], sems[12], sems[13])
+    lines.turn(0)
+    unpack_parameters(n_dp, experts, extras_ref, selector_ref, router_ref, table, pattern_ref)
+    weights.relay()
+    for copy in along:
+        copy.wait_recv()
+    spread.start()
+    weights.finish()
+    spread.relay()
+    spread.finish()
 
     def project(block):
         rows = pl.ds(pl.multiple_of(block * own_rows, own_rows), own_rows)
@@ -1339,76 +1312,392 @@
             hidden_ref[block], weights_ref[...].reshape(width, weights_ref.shape[2])
         ).astype(BF16)
 
-    def used(j, k):
-        if j == 0:
-            if k > 0:
-                if k == 1:
-                    weights.finish()
-                    lines.each_new(j, 0, project)
-                lines.each_new(j, k, project)
-        elif k == n_tensor - 1 and j - 1 < GRAD_EARLY:
-            values = grads[j - 1].reshape(seq_len, part)
-            for mask in peers_in_order(n_dp):
-                target = me ^ mask
-                grad_send[j - 1, target] = nn(picks[target], values).astype(BF16)
-                if mask:
-                    row_copy(j - 1, target, me).start()
-                else:
-                    own_row_copy(j - 1).start()
-
-    weights.relay()
-    for copy in line_copies:
-        copy.wait_recv()
-    spread = Spread(n_dp, outs_ref, out_far_send, out_far_recv, out_near_send, out_near_recv)
-    spread.start()
-    if fast:
-        build_bias(pattern_ref.shape[0] // 2, pattern_ref, bias)
-    blocks = seq_len // BS
-    done = 0
     for turn in lines.turns():
-        if turn == 0:
-            continue
-        lines.turn(turn, used)
-        if turn == 2:
-            spread.relay()
-        if fast and turn >= n_tensor - 1:
-            while done < blocks and done <= turn - (n_tensor - 1):
-                forward_rows(
-                    pattern_ref.shape[0] // 2,
-                    done,
-                    max(0, done - band(seq_len)),
-                    projected_ref,
-                    segment_ref,
-                    bias,
-                    attended_ref,
-                    lse_ref,
-                )
-                done += 1
-    if fast:
-        assert done == blocks
-    if n_tensor < 3:
-        spread.relay()
-    spread.finish()
+        if turn:
+            lines.turn(turn)
+
+    def every(block, _):
+        project(block)
+        return 0
+
+    lax.fori_loop(0, n_tensor, every, 0)
     lines.drain()
     weights.drain()
     spread.drain()
-    for copy in line_copies:
+    for copy in along:
         copy.wait_send()
-    if fast:
-        for j in range(GRAD_EARLY):
-            own_row_copy(j).wait()
-            for step in range(1, n_dp):
-                peer = lax.rem(me + step, n_dp)
-                row_copy(j, peer, me).wait_send()
-                row_copy(j, me, peer).wait_recv()
-
-
-def front(
+
+
+def front(n_dp, n_tensor, experts, tokens, weight, extra, out, selectors):
+    own_rows, width = tokens.shape
+    seq_len = own_rows * n_tensor
+    depth, cols = weight.shape
+    heads = cols // (3 * HD)
+    dma = pltpu.SemaphoreType.DMA
+    return pl.pallas_call(
+        functools.partial(front_kernel, n_dp, n_tensor, experts),
+        out_shape=(
+            jax.ShapeDtypeStruct((n_tensor, own_rows, width), BF16),
+            jax.ShapeDtypeStruct((seq_len, cols), BF16),
+            jax.ShapeDtypeStruct((n_dp, depth, cols), BF16),
+            jax.ShapeDtypeStruct((n_dp, n_tensor) + out.shape, BF16),
+            jax.ShapeDtypeStruct((2 * heads, 2 * BS), F32),
+            jax.ShapeDtypeStruct((experts, width), BF16),
+            jax.ShapeDtypeStruct((2, width), F32),
+        ),
+        in_specs=[vspec()] * 5,
+        out_specs=(vspec(),) * 7,
+        scratch_shapes=[pltpu.VMEM((n_dp,) + extra.shape, BF16), pltpu.VMEM((NB, depth), F32)]
+        + parameter_sems(n_dp, n_tensor)
+        + [dma((1, 2, n_tensor - 1))] * 2,
+        compiler_params=pltpu.CompilerParams(
+            vmem_limit_bytes=VMEM_LIMIT, collective_id=3, has_side_effects=True
+        ),
+        name="front",
+    )(tokens, weight, extra, out, selectors)
+
+
+PARTS = 4
+
+
+class Dispatch:
+    def __init__(self, n_dp, picks, stage, rows_ref, send_sem, recv_sem, own_sem):
+        self.n, self.picks, self.stage, self.rows = n_dp, picks, stage, rows_ref
+        self.send_sem, self.recv_sem, self.own_sem = send_sem, recv_sem, own_sem
+        self.me = lax.axis_index("dp")
+
+    def cols(self, j):
+        part = self.stage.shape[3]
+        return slice(j * part, (j + 1) * part)
+
+    def copy(self, j, target, sender):
+        return remote(
+            self.stage.at[j, target],
+            self.rows.at[sender, :, self.cols(j)],
+            self.send_sem.at[j, target],
+            self.recv_sem.at[j, sender],
+            "dp",
+            target,
+        )
+
+    def own(self, j):
+        return pltpu.make_async_copy(
+            self.stage.at[j, self.me], self.rows.at[self.me, :, self.cols(j)], self.own_sem.at[j]
+        )
+
+    def start(self, j, values_ref):
+        n_tensor, own_rows, part = values_ref.shape
+
+        def one(index, _):
+            mask = self.n - 1 - index
+            target = self.me ^ mask
+            self.stage[j, target] = nn(
+                self.picks[target], values_ref[...].reshape(n_tensor * own_rows, part)
+            ).astype(BF16)
+
+            @pl.when(mask != 0)
+            def _():
+                self.copy(j, target, self.me).start()
+
+            @pl.when(mask == 0)
+            def _():
+                self.own(j).start()
+
+            return 0
+
+        lax.fori_loop(0, self.n, one, 0)
+
+    def finish(self):
+        for j in range(self.stage.shape[0]):
+            self.own(j).wait()
+            for step in range(1, self.n):
+                peer = lax.rem(self.me + step, self.n)
+                self.copy(j, peer, self.me).wait_send()
+                self.copy(j, self.me, peer).wait_recv()
+
+
+def opening_kernel(
     n_dp,
     n_tensor,
     experts,
     capacity,
-    fast,
+    tokens_ref,
+    cotangent_ref,
+    weight_ref,
+    extra_ref,
+    out_ref,
+    routes_ref,
+    segment_ref,
+    selector_ref,
+    hidden_ref,
+    projected_ref,
+    weights_ref,
+    pattern_ref,
+    router_ref,
+    gains_ref,
+    slots_ref,
+    attended_ref,
+    lse_ref,
+    residual_ref,
+    hidden_two_ref,
+    weight_own_ref,
+    rows_ref,
+    grad_rows_ref,
+    gates_ref,
+    extras_ref,
+    table,
+    outs,
+    out_matrix,
+    grads,
+    everyone,
+    picks,
+    grad_stage,
+    row_stage,
+    bias,
+    slot_rows,
+    attended_recv,
+    logits,
+    gate_stage,
+    *sems,
+):
+    own_rows, width = tokens_ref.shape
+    seq_len = own_rows * n_tensor
+    heads = pattern_ref.shape[0] // 2
+    head_cols = heads * HD
+    out_cols = out_ref.shape[1]
+    local = experts // n_dp
+    per = local * capacity
+    part = width // PARTS
+    me = lax.axis_index("dp")
+    me_t = lax.axis_index("tensor")
+    (hop_send, hop_recv, late_send, late_recv) = sems[12:16]
+    (grad_send, grad_recv, grad_own, row_send, row_recv, row_own) = sems[16:22]
+    (gate_send, gate_recv, attended_send_sem, attended_recv_sem) = sems[22:26]
+    greet([("dp", n_dp), ("tensor", n_tensor)])
+
+    def rows_of(block):
+        return pl.ds(pl.multiple_of(block * own_rows, own_rows), own_rows)
+
+    for j in range(PARTS):
+        grads[j, me_t] = cotangent_ref[:, j * part : (j + 1) * part]
+    lines = Streams(
+        n_tensor, [hidden_ref] + [grads.at[j] for j in range(PARTS)], hop_send, hop_recv
+    )
+    lines.advance(1, 0)
+    small, weights, spread, along = send_parameters(
+        n_dp, n_tensor, weight_ref, extra_ref, out_ref, weights_ref, outs, extras_ref, sems
+    )
+    hidden_ref[me_t] = first_hidden(n_dp, experts, tokens_ref, extras_ref, gains_ref, small)
+    lines.advance(1, 1)
+    unpack_parameters(n_dp, experts, extras_ref, selector_ref, router_ref, table, pattern_ref)
+    lines.advance(1, 2)
+    lines.advance(0, 0)
+
+    ids = lax.broadcasted_iota(jnp.int32, (experts, seq_len), 0)
+    hits = [ids == routes_ref[k : k + 1, :] for k in range(TOP)]
+    before = lax.broadcasted_iota(jnp.int32, (seq_len, seq_len), 0) < lax.broadcasted_iota(
+        jnp.int32, (seq_len, seq_len), 1
+    )
+    ranks = nn(
+        jnp.where(hits[0] | hits[1], 1.0, 0.0).astype(BF16),
+        jnp.where(before, 1.0, 0.0).astype(BF16),
+    )
+    places = ranks + (ids * capacity).astype(F32)
+    for k in range(TOP):
+        row = jnp.sum(jnp.where(hits[k], places, 0.0), axis=0, keepdims=True)
+        slot_rows[k : k + 1, :] = row.astype(jnp.int32)
+        for block in range(n_tensor):
+            rows = slice(block * own_rows, (block + 1) * own_rows)
+            slots_ref[rows, k : k + 1] = to_column(row[:, rows]).astype(jnp.int32)
+
+
+    def pick(target, _):
+        picks[target] = one_hot(slot_rows, target, per)
+        return 0
+
+    lax.fori_loop(0, n_dp, pick, 0)
+    grad_moves = Dispatch(n_dp, picks, grad_stage, grad_rows_ref, grad_send, grad_recv, grad_own)
+    lines.advance(1, 3)
+    grad_moves.start(0, grads.at[0])
+    weights.relay()
+    for copy in along:
+        copy.wait_recv()
+    spread.start()
+    build_bias(heads, pattern_ref, bias)
+
+    def project(block):
+        projected_ref[rows_of(block), :] = nn(
+            hidden_ref[block], weights_ref[...].reshape(width, weights_ref.shape[2])
+        ).astype(BF16)
+
+    lines.advance(0, 1)
+    weights.finish()
+    project(me_t)
+    lines.advance(0, 2)
+    lines.advance(2, 0)
+    lines.advance(3, 0)
+    spread.relay()
+    lines.each_new(0, 1, project)
+    lines.advance(0, 3)
+    lines.advance(2, 1)
+    lines.advance(3, 1)
+    lines.each_new(0, 2, project)
+    lines.each_new(0, 3, project)
+
+    def attended_copy(target, sender):
+        return remote(
+            attended_ref.at[rows_of(target)],
+            attended_recv.at[sender],
+            attended_send_sem.at[target],
+            attended_recv_sem.at[sender],
+            "tensor",
+            target,
+        )
+
+    def attend(qb):
+        forward_rows(
+            heads,
+            qb,
+            max(0, qb - band(seq_len)),
+            projected_ref,
+            segment_ref,
+            bias,
+            attended_ref,
+            lse_ref,
+        )
+
+        @pl.when(me_t == qb)
+        def _():
+            attended_recv[me_t] = attended_ref[rows_of(me_t), :]
+
+        @pl.when(me_t != qb)
+        def _():
+            attended_copy(qb, me_t).start()
+
+    lines.advance(2, 2)
+    lines.advance(3, 2)
+    attend(3)
+    attend(0)
+    lines.advance(2, 3)
+    grad_moves.start(1, grads.at[1])
+    lines.advance(3, 3)
+    attend(2)
+    attend(1)
+    grad_moves.start(2, grads.at[2])
+    spread.finish()
+    for block in range(n_dp):
+        out_matrix[:, block * out_cols : (block + 1) * out_cols] = outs[block].reshape(
+            width, out_cols
+        )
+    weight_own_ref[...] = out_matrix[
+        pl.ds(pl.multiple_of(me_t * head_cols, head_cols), head_cols), :
+    ]
+    for step in range(1, n_tensor):
+        attended_copy(me_t, lax.rem(me_t + step, n_tensor)).wait_recv()
+    residual = tokens_ref[...].astype(F32)
+    for block in range(n_tensor):
+        residual += nn(
+            attended_recv[block], out_matrix[block * head_cols : (block + 1) * head_cols, :]
+        )
+    residual_ref[...] = residual
+    hidden = (
+        residual
+        * lax.rsqrt(jnp.mean(residual * residual, axis=1, keepdims=True) + EPS)
+        * gains_ref[1:2, :]
+    ).astype(BF16)
+    hidden_two_ref[...] = hidden
+    for j in range(PARTS):
+        everyone[j, me_t] = hidden[:, j * part : (j + 1) * part]
+    late = Streams(n_tensor, [everyone.at[j] for j in range(PARTS)], late_send, late_recv)
+    row_moves = Dispatch(n_dp, picks, row_stage, rows_ref, row_send, row_recv, row_own)
+
+    def used(j, k):
+        if k < n_tensor - 1:
+            return
+        row_moves.start(j, everyone.at[j])
+        term = nt(
+            router_ref[:, j * part : (j + 1) * part], everyone[j].reshape(seq_len, part)
+        )
+        if j == 0:
+            logits[...] = term
+        else:
+            logits[...] += term
+
+    for turn in late.turns():
+        late.turn(turn, used)
+        if turn >= n_tensor:
+            lines.advance(4, turn - n_tensor)
+    lines.advance(4, n_tensor - 1)
+    grad_moves.start(3, grads.at[3])
+    values = logits[...]
+    exps = jnp.exp(values - jnp.max(values, axis=0, keepdims=True))
+    probs = exps / jnp.sum(exps, axis=0, keepdims=True)
+    named = (ids == routes_ref[0:1, :]) | (ids == routes_ref[1:2, :])
+    shares = probs / jnp.sum(jnp.where(named, probs, 0.0), axis=0, keepdims=True)
+    logits[...] = shares
+
+    def gate_copy(target, sender):
+        return remote(
+            gate_stage.at[target],
+            gates_ref.at[sender],
+            gate_send.at[target],
+            gate_recv.at[sender],
+            "dp",
+            target,
+        )
+
+    def gate(index, _):
+        mask = n_dp - 1 - index
+        target = me ^ mask
+        for expert in range(local):
+            row = jnp.sum(
+                jnp.where(ids == target * local + expert, logits[...], 0.0), axis=0, keepdims=True
+            )
+            high = row.astype(BF16)
+            rest = row - high.astype(F32)
+            mid = rest.astype(BF16)
+            low = (rest - mid.astype(F32)).astype(BF16)
+            lanes = slice(expert * capacity, (expert + 1) * capacity)
+            pieces = nt(
+                jnp.concatenate([high, mid, low, jnp.zeros((5, seq_len), BF16)], axis=0),
+                picks[target, lanes, :],
+            )
+            gate_stage[target, :, lanes] = jnp.broadcast_to(
+                jnp.sum(pieces, axis=0, keepdims=True), (8, capacity)
+            )
+
+        @pl.when(mask != 0)
+        def _():
+            gate_copy(target, me).start()
+
+        @pl.when(mask == 0)
+        def _():
+            gates_ref[target] = gate_stage[target]
+
+        return 0
+
+    lax.fori_loop(0, n_dp, gate, 0)
+    lines.drain()
+    late.drain()
+    weights.drain()
+    spread.drain()
+    for copy in along:
+        copy.wait_send()
+    for step in range(1, n_tensor):
+        attended_copy(lax.rem(me_t + step, n_tensor), me_t).wait_send()
+    for step in range(1, n_dp):
+        peer = lax.rem(me + step, n_dp)
+        gate_copy(peer, me).wait_send()
+        gate_copy(me, peer).wait_recv()
+    grad_moves.finish()
+    row_moves.finish()
+
+
+def opening(
+    n_dp,
+    n_tensor,
+    experts,
+    capacity,
     tokens,
     cotangent,
     weight,
@@ -1422,337 +1711,58 @@
     seq_len = own_rows * n_tensor
     depth, cols = weight.shape
     per = experts // n_dp * capacity
-    part = width // GRAD_PARTS
+    part = width // PARTS
     heads = cols // (3 * HD)
-    shapes = [
-        jax.ShapeDtypeStruct((n_tensor, own_rows, width), BF16),
-        jax.ShapeDtypeStruct((seq_len, cols), BF16),
-        jax.ShapeDtypeStruct((n_dp, depth, cols), BF16),
-        jax.ShapeDtypeStruct((n_dp, n_tensor) + out.shape, BF16),
-        jax.ShapeDtypeStruct((2 * heads, 2 * BS), F32),
-        jax.ShapeDtypeStruct((experts, width), BF16),
-        jax.ShapeDtypeStruct((2, width), F32),
-    ]
-    specs = [vspec()] * 7
     dma = pltpu.SemaphoreType.DMA
-    streams = 1 + (GRAD_PARTS if fast else 0)
-    half = n_dp // 2
-    scratch = (
-        [pltpu.VMEM((n_dp,) + extra.shape, BF16), pltpu.VMEM((NB, depth), F32)]
-        + [dma((n_dp - 1,))] * 2
-        + [dma((n_tensor - 1,))] * 2
-        + ([dma((half,))] * 4) * 2
-        + [dma((streams, 2, n_tensor - 1))] * 2
-    )
-    if fast:
-        shapes += [
-            jax.ShapeDtypeStruct((n_dp, per, GRAD_EARLY * part), BF16),
-            jax.ShapeDtypeStruct((8, seq_len), jnp.int32),
+    rows = jax.ShapeDtypeStruct((n_dp, per, width), BF16)
+    return pl.pallas_call(
+        functools.partial(opening_kernel, n_dp, n_tensor, experts, capacity),
+        out_shape=(
+            jax.ShapeDtypeStruct((n_tensor, own_rows, width), BF16),
+            jax.ShapeDtypeStruct((seq_len, cols), BF16),
+            jax.ShapeDtypeStruct((n_dp, depth, cols), BF16),
+            jax.ShapeDtypeStruct((2 * heads, 2 * BS), F32),
+            jax.ShapeDtypeStruct((experts, width), BF16),
+            jax.ShapeDtypeStruct((2, width), F32),
             jax.ShapeDtypeStruct((seq_len, TOP), jnp.int32),
             jax.ShapeDtypeStruct((seq_len, heads * HD), BF16),
             jax.ShapeDtypeStruct((seq_len, heads), F32),
-            jax.ShapeDtypeStruct((GRAD_PARTS - GRAD_EARLY, n_tensor, own_rows, part), BF16),
-        ]
-        specs += [any_spec()] + [vspec()] * 5
-        scratch += [
-            pltpu.VMEM((GRAD_EARLY, n_tensor, own_rows, part), BF16),
-            pltpu.VMEM((n_dp, per, seq_len), BF16),
-            pltpu.VMEM((GRAD_EARLY, n_dp, per, part), BF16),
-            pltpu.VMEM((heads, 3, BS, BS), F32),
-            dma((GRAD_EARLY, n_dp)),
-            dma((GRAD_EARLY, n_dp)),
-            dma((GRAD_EARLY,)),
-        ]
-    return pl.pallas_call(
-        functools.partial(front_kernel, n_dp, n_tensor, experts, capacity, fast),
-        out_shape=tuple(shapes),
-        in_specs=[vspec()] * 8,
-        out_specs=tuple(specs),
-        scratch_shapes=scratch,
-        compiler_params=pltpu.CompilerParams(
-            vmem_limit_bytes=VMEM_LIMIT, collective_id=3, has_side_effects=True
-        ),
-        name="front",
-    )(tokens, cotangent, weight, extra, out, routes, segments, selectors)
-
-
-PARTS = 4
-
-
-def middle_kernel(
-    n_dp,
-    n_tensor,
-    experts,
-    capacity,
-    attended_ref,
-    outs_ref,
-    tokens_ref,
-    gain_ref,
-    router_ref,
-    slots_ref,
-    routes_ref,
-    late_ref,
-    residual_ref,
-    hidden_ref,
-    weight_own_ref,
-    rows_ref,
-    gates_ref,
-    grad_rows_ref,
-    out_matrix,
-    attended_recv,
-    everyone,
-    picks,
-    row_stage,
-    grad_stage,
-    logits,
-    gate_stage,
-    attended_send_sem,
-    attended_recv_sem,
-    stream_send,
-    stream_recv,
-    row_send,
-    row_recv,
-    row_own,
-    grad_send,
-    grad_recv,
-    grad_own,
-    gate_send,
-    gate_recv,
-):
-    own_rows, width = tokens_ref.shape
-    seq_len = own_rows * n_tensor
-    head_cols = attended_ref.shape[1]
-    out_cols = outs_ref.shape[2]
-    local = experts // n_dp
-    per = local * capacity
-    part = width // PARTS
-    me = lax.axis_index("dp")
-    me_t = lax.axis_index("tensor")
-    greet([("dp", n_dp), ("tensor", n_tensor)])
-
-    def rows_of(block):
-        return pl.ds(pl.multiple_of(block * own_rows, own_rows), own_rows)
-
-    copies = []
-    for step in range(1, n_tensor):
-        peer = lax.rem(me_t + step, n_tensor)
-        copy = remote(
-            attended_ref.at[rows_of(peer)],
-            attended_recv.at[me_t],
-            attended_send_sem.at[step - 1],
-            attended_recv_sem.at[step - 1],
-            "tensor",
-            peer,
-        )
-        copy.start()
-        copies.append(copy)
-    attended_recv[me_t] = attended_ref[rows_of(me_t), :]
-    for block in range(n_dp):
-        out_matrix[:, block * out_cols : (block + 1) * out_cols] = outs_ref[block]
-    weight_own_ref[...] = out_matrix[
-        pl.ds(pl.multiple_of(me_t * head_cols, head_cols), head_cols), :
-    ]
-    def grad_copy(j, target, sender):
-        cols = slice(j * part, (j + 1) * part)
-        return remote(
-            grad_stage.at[j, target],
-            grad_rows_ref.at[sender, :, cols],
-            grad_send.at[j, target],
-            grad_recv.at[j, sender],
-            "dp",
-            target,
-        )
-
-    def own_grad_copy(j):
-        cols = slice(j * part, (j + 1) * part)
-        return pltpu.make_async_copy(
-            grad_stage.at[j, me], grad_rows_ref.at[me, :, cols], grad_own.at[j]
-        )
-
-    late = late_ref.shape[0]
-    for mask in peers_in_order(n_dp):
-        target = me ^ mask
-        picks[target] = one_hot(slots_ref, target, per)
-        for j in range(late):
-            grad_stage[j, target] = nn(
-                picks[target], late_ref[j].reshape(seq_len, part)
-            ).astype(BF16)
-            if mask:
-                grad_copy(j, target, me).start()
-            else:
-                own_grad_copy(j).start()
-    for copy in copies:
-        copy.wait_recv()
-    residual = tokens_ref[...].astype(F32)
-    for block in range(n_tensor):
-        residual += nn(
-            attended_recv[block], out_matrix[block * head_cols : (block + 1) * head_cols, :]
-        )
-    residual_ref[...] = residual
-    hidden = (
-        residual
-        * lax.rsqrt(jnp.mean(residual * residual, axis=1, keepdims=True) + EPS)
-        * gain_ref[...]
-    ).astype(BF16)
-    hidden_ref[...] = hidden
-    for j in range(PARTS):
-        everyone[j, me_t] = hidden[:, j * part : (j + 1) * part]
-    lines = Streams(n_tensor, [everyone.at[j] for j in range(PARTS)], stream_send, stream_recv)
-
-    def row_copy(j, target, sender):
-        cols = slice(j * part, (j + 1) * part)
-        return remote(
-            row_stage.at[j, target],
-            rows_ref.at[sender, :, cols],
-            row_send.at[j, target],
-            row_recv.at[j, sender],
-            "dp",
-            target,
-        )
-
-    def own_row_copy(j):
-        cols = slice(j * part, (j + 1) * part)
-        return pltpu.make_async_copy(row_stage.at[j, me], rows_ref.at[me, :, cols], row_own.at[j])
-
-    def used(j, k):
-        if k < n_tensor - 1:
-            return
-        values = everyone[j].reshape(seq_len, part)
-        for mask in peers_in_order(n_dp):
-            target = me ^ mask
-            row_stage[j, target] = nn(picks[target], values).astype(BF16)
-            if mask:
-                row_copy(j, target, me).start()
-            else:
-                own_row_copy(j).start()
-        term = nt(router_ref[:, j * part : (j + 1) * part], values)
-        if j == 0:
-            logits[...] = term
-        else:
-            logits[...] += term
-
-    for turn in lines.turns():
-        lines.turn(turn, used)
-    values = logits[...]
-    exps = jnp.exp(values - jnp.max(values, axis=0, keepdims=True))
-    probs = exps / jnp.sum(exps, axis=0, keepdims=True)
-    ids = lax.broadcasted_iota(jnp.int32, (experts, seq_len), 0)
-    named = (ids == routes_ref[0:1, :]) | (ids == routes_ref[1:2, :])
-    shares = probs / jnp.sum(jnp.where(named, probs, 0.0), axis=0, keepdims=True)
-    gate_copies = []
-    for mask in peers_in_order(n_dp):
-        target = me ^ mask
-        for expert in range(local):
-            row = jnp.sum(
-                jnp.where(ids == target * local + expert, shares, 0.0), axis=0, keepdims=True
-            )
-            high = row.astype(BF16)
-            rest = row - high.astype(F32)
-            mid = rest.astype(BF16)
-            low = (rest - mid.astype(F32)).astype(BF16)
-            lanes = slice(expert * capacity, (expert + 1) * capacity)
-            pieces = nt(
-                jnp.concatenate([high, mid, low, jnp.zeros((5, seq_len), BF16)], axis=0),
-                picks[target, lanes, :],
-            )
-            gate_stage[target, :, lanes] = jnp.broadcast_to(
-                jnp.sum(pieces, axis=0, keepdims=True), (8, capacity)
-            )
-        if mask:
-            copy = remote(
-                gate_stage.at[target],
-                gates_ref.at[me],
-                gate_send.at[target],
-                gate_recv.at[me],
-                "dp",
-                target,
-            )
-            copy.start()
-            gate_copies.append(copy)
-        else:
-            gates_ref[me] = gate_stage[me]
-    lines.drain()
-    for copy in copies:
-        copy.wait_send()
-    for copy in gate_copies:
-        copy.wait_send()
-    for step in range(1, n_dp):
-        peer = lax.rem(me + step, n_dp)
-        remote(
-            gate_stage.at[me], gates_ref.at[peer], gate_send.at[me], gate_recv.at[peer], "dp", peer
-        ).wait_recv()
-    for j in range(late):
-        own_grad_copy(j).wait()
-        for step in range(1, n_dp):
-            peer = lax.rem(me + step, n_dp)
-            grad_copy(j, peer, me).wait_send()
-            grad_copy(j, me, peer).wait_recv()
-    for j in range(PARTS):
-        own_row_copy(j).wait()
-        for step in range(1, n_dp):
-            peer = lax.rem(me + step, n_dp)
-            row_copy(j, peer, me).wait_send()
-            row_copy(j, me, peer).wait_recv()
-
-
-def middle(
-    n_dp,
-    n_tensor,
-    experts,
-    capacity,
-    attended,
-    outs,
-    tokens,
-    gain,
-    router_rows,
-    slot_rows,
-    routes,
-    late,
-):
-    own_rows, width = tokens.shape
-    seq_len, head_cols = attended.shape
-    per = experts // n_dp * capacity
-    part = width // PARTS
-    dma = pltpu.SemaphoreType.DMA
-    return pl.pallas_call(
-        functools.partial(middle_kernel, n_dp, n_tensor, experts, capacity),
-        out_shape=(
             jax.ShapeDtypeStruct((own_rows, width), F32),
             jax.ShapeDtypeStruct((own_rows, width), BF16),
-            jax.ShapeDtypeStruct((head_cols, width), BF16),
-            jax.ShapeDtypeStruct((n_dp, per, width), BF16),
+            jax.ShapeDtypeStruct((heads * HD, width), BF16),
+            rows,
+            rows,
             jax.ShapeDtypeStruct((n_dp, 8, per), F32),
-            jax.ShapeDtypeStruct((n_dp, per, late.shape[0] * part), BF16),
         ),
         in_specs=[vspec()] * 8,
-        out_specs=(vspec(), vspec(), vspec(), any_spec(), vspec(), any_spec()),
+        out_specs=(vspec(),) * 12 + (any_spec(), any_spec(), vspec()),
         scratch_shapes=[
+            pltpu.VMEM((n_dp,) + extra.shape, BF16),
+            pltpu.VMEM((NB, depth), F32),
+            pltpu.VMEM((n_dp, n_tensor) + out.shape, BF16),
             pltpu.VMEM((width, width), BF16),
-            pltpu.VMEM((n_tensor, own_rows, head_cols), BF16),
+            pltpu.VMEM((PARTS, n_tensor, own_rows, part), BF16),
             pltpu.VMEM((PARTS, n_tensor, own_rows, part), BF16),
             pltpu.VMEM((n_dp, per, seq_len), BF16),
             pltpu.VMEM((PARTS, n_dp, per, part), BF16),
-            pltpu.VMEM((late.shape[0], n_dp, per, part), BF16),
+            pltpu.VMEM((PARTS, n_dp, per, part), BF16),
+            pltpu.VMEM((heads, 3, BS, BS), F32),
+            pltpu.VMEM((8, seq_len), jnp.int32),
+            pltpu.VMEM((n_tensor, own_rows, heads * HD), BF16),
             pltpu.VMEM((experts, seq_len), F32),
             pltpu.VMEM((n_dp, 8, per), F32),
-            dma((n_tensor - 1,)),
-            dma((n_tensor - 1,)),
-            dma((PARTS, 2, n_tensor - 1)),
-            dma((PARTS, 2, n_tensor - 1)),
-            dma((PARTS, n_dp)),
-            dma((PARTS, n_dp)),
-            dma((PARTS,)),
-            dma((late.shape[0], n_dp)),
-            dma((late.shape[0], n_dp)),
-            dma((late.shape[0],)),
-            dma((n_dp,)),
-            dma((n_dp,)),
-        ],
+        ]
+        + parameter_sems(n_dp, n_tensor)
+        + [dma((PARTS + 1, 2, n_tensor - 1))] * 2
+        + [dma((PARTS, 2, n_tensor - 1))] * 2
+        + [dma((PARTS, n_dp)), dma((PARTS, n_dp)), dma((PARTS,))] * 2
+        + [dma((n_dp,))] * 2
+        + [dma((n_tensor,))] * 2,
         compiler_params=pltpu.CompilerParams(
             vmem_limit_bytes=VMEM_LIMIT, collective_id=4, has_side_effects=True
         ),
-        name="middle",
-    )(attended, outs, tokens, gain, router_rows, slot_rows, routes, late)
+        name="opening",
+    )(tokens, cotangent, weight, extra, out, routes, segments, selectors)
 
 
 def last_kernel(
@@ -1789,7 +1799,7 @@
     sums,
     grad_qkv,
     diag,
-    acc,
+    parts,
     mixture,
     grad_hidden,
     mix_send,
@@ -1828,26 +1838,8 @@
     def rows_of(block):
         return pl.ds(pl.multiple_of(block * own_rows, own_rows), own_rows)
 
-    mix = LineSum(
-        n_tensor,
-        lambda block: merged_ref[rows_of(block), :].astype(F32),
-        mix_send,
-        mix_recv,
-        mix_send_sem,
-        mix_recv_sem,
-        acc,
-        mixture,
-    )
-    line = LineSum(
-        n_tensor,
-        lambda block: nt(grad_qkv[rows_of(block), :], weight_ref[...]),
-        line_send,
-        line_recv,
-        line_send_sem,
-        line_recv_sem,
-        acc,
-        grad_hidden,
-    )
+    mix = LineSum(n_tensor, merged_ref, mix_send, mix_recv, mix_send_sem, mix_recv_sem, mixture)
+    line = LineSum(n_tensor, parts, line_send, line_recv, line_send_sem, line_recv_sem, grad_hidden)
     copies = []
 
     def scatter(source, target, send_sem, recv_sem):
@@ -1892,7 +1884,7 @@
         if qb >= blocks - 2 and qb - (blocks - 2) < n_tensor - 1:
             mix.step(qb - (blocks - 2))
     backward_end(heads, grad_qkv, dk, dv)
-    line.start()
+    line.start(lambda block: nt(grad_qkv[rows_of(block), :], weight_ref[...]))
     for k in range(2, n_tensor - 1):
         mix.step(k)
     for block in range(n_dp):
@@ -2018,7 +2010,8 @@
             pltpu.VMEM((seq_len, cols), BF16),
             pltpu.VMEM((3, 8, 2 * BS), F32),
         ]
-        + [pltpu.VMEM((own_rows, width), F32)] * 3
+        + [pltpu.VMEM((n_tensor, own_rows, width), BF16)]
+        + [pltpu.VMEM((own_rows, width), F32)] * 2
         + line * 2
         + [
             pltpu.VMEM((n_dp, depth, cols), BF16),
@@ -2059,6 +2052,95 @@
     )
 
 
+def deliver_kernel(
+    grad_in_ref,
+    grad_out_ref,
+    layer_in_ref,
+    tokens_in_ref,
+    weight_in_ref,
+    out_in_ref,
+    small_ref,
+    layer_ref,
+    tokens_ref,
+    weight_ref,
+    out_ref,
+    table_ref,
+    gain_one_ref,
+    gain_two_ref,
+    router_ref,
+    in_ref,
+    down_ref,
+    stage_in,
+    stage_down,
+    in_sem,
+    down_sem,
+    out_sem,
+    last_sem,
+):
+    local, halves = grad_in_ref.shape[:2]
+    pieces = [
+        (grad_in_ref.at[e, g], stage_in.at[e, g], in_ref.at[e, g], in_sem.at[e, g], out_sem.at[e, g])
+        for e in range(local)
+        for g in range(halves)
+    ] + [
+        (grad_out_ref.at[e], stage_down.at[e], down_ref.at[e], down_sem.at[e], last_sem.at[e])
+        for e in range(local)
+    ]
+    for source, stage, _, sem, _ in pieces:
+        pltpu.make_async_copy(source, stage, sem).start()
+    layer_ref[...] = layer_in_ref[...]
+    tokens_ref[...] = tokens_in_ref[...]
+    cols = weight_ref.shape[2]
+    for part in range(3):
+        weight_ref[part] = weight_in_ref[:, part * cols : (part + 1) * cols]
+    out_ref[...] = out_in_ref[...]
+    experts = router_ref.shape[0]
+    router_ref[...] = small_ref[0:experts, :]
+    gain_two_ref[...] = small_ref[experts : experts + 1, :]
+    gain_one_ref[...] = small_ref[experts + 1 : experts + 2, :]
+    table_ref[...] = small_ref[
+        experts + 2 : experts + 2 + table_ref.shape[0], 0 : table_ref.shape[1]
+    ]
+    for source, stage, target, sem, done in pieces:
+        pltpu.make_async_copy(source, stage, sem).wait()
+        pltpu.make_async_copy(stage, target, done).start()
+    for _, stage, target, _, done in pieces:
+        pltpu.make_async_copy(stage, target, done).wait()
+
+
+def deliver(experts, heads, table_rows, grad_in, grad_out, layer, tokens, weight, out, small):
+    depth, cols = weight.shape
+    local, halves = grad_in.shape[:2]
+    dma = pltpu.SemaphoreType.DMA
+    return pl.pallas_call(
+        deliver_kernel,
+        out_shape=(
+            jax.ShapeDtypeStruct(layer.shape, BF16),
+            jax.ShapeDtypeStruct(tokens.shape, BF16),
+            jax.ShapeDtypeStruct((3, depth, cols // 3), F32),
+            jax.ShapeDtypeStruct(out.shape, F32),
+            jax.ShapeDtypeStruct((table_rows, heads), F32),
+            jax.ShapeDtypeStruct((1, depth), F32),
+            jax.ShapeDtypeStruct((1, depth), F32),
+            jax.ShapeDtypeStruct((experts, depth), F32),
+            jax.ShapeDtypeStruct(grad_in.shape, F32),
+            jax.ShapeDtypeStruct(grad_out.shape, F32),
+        ),
+        in_specs=[any_spec()] * 2 + [vspec()] * 5,
+        out_specs=(vspec(),) * 8 + (any_spec(),) * 2,
+        scratch_shapes=[
+            pltpu.VMEM(grad_in.shape, F32),
+            pltpu.VMEM(grad_out.shape, F32),
+            dma((local, halves)),
+            dma((local,)),
+            dma((local, halves)),
+            dma((local,)),
+        ],
+        compiler_params=pltpu.CompilerParams(vmem_limit_bytes=VMEM_LIMIT),
+        name="deliver",
+    )(grad_in, grad_out, layer, tokens, weight, out, small)
+
+
 def rms_scale(values):
     return lax.rsqrt(jnp.mean(values * values, axis=-1, keepdims=True) + EPS)
 
@@ -2125,62 +2207,83 @@
         ],
         axis=0,
     )
-    fast = n_dp == 8 and slots * model_width <= 4 * 1024 * 1024
+    fast = n_dp == 8 and n_tensor == 4 and seq_len == 4 * BS and slots * model_width <= 4 * 1024 * 1024
     route_rows = jnp.pad(jnp.transpose(routes), ((0, 8 - TOP), (0, 0)))
-    gathered, projected, weights_full, outs_full, patterns, router_rows, gains, *routed = front(
-        n_dp,
-        n_tensor,
-        experts,
-        capacity,
-        fast,
-        tokens,
-        cotangent,
-        w_qkv.reshape(depth, 3 * head_cols),
-        extra,
-        w_attn_out,
-        route_rows,
-        segments,
-        jnp.asarray(distance_selectors().T),
-    )
-    gathered_one = gathered.reshape(seq_len, model_width)
-    qkv_matrix = weights_full.reshape(model_width, 3 * head_cols)
-    outs_full = outs_full.reshape(n_dp, model_width, model_width // n_dp)
     weight_shard = w_qkv.reshape(depth, 3 * head_cols)
     gain_shard = gain_attn[None].astype(F32)
     skew = jnp.asarray(skew_selectors().T)
+    selectors = jnp.asarray(distance_selectors().T)
 
     def finish(layer_out, grad_tokens, reduced_qkv, reduced_attn_out, small_sum, grad_w_in, grad_w_out):
+        (
+            layer_out,
+            grad_tokens,
+            grad_w_qkv,
+            grad_w_attn_out,
+            grad_table,
+            grad_gain_one,
+            grad_gain_two,
+            grad_router,
+            grad_w_in,
+            grad_w_out,
+        ) = deliver(
+            experts,
+            heads,
+            NB // n_dp,
+            grad_w_in,
+            grad_w_out,
+            layer_out,
+            grad_tokens,
+            reduced_qkv,
+            reduced_attn_out,
+            small_sum,
+        )
         return (
             layer_out,
             grad_tokens,
-            reduced_qkv.reshape(depth, 3, head_cols),
-            reduced_attn_out,
-            small_sum[experts + 2 : experts + 2 + NB // n_dp, :heads],
-            small_sum[experts + 1],
-            small_sum[experts],
-            jnp.transpose(small_sum[:experts]),
+            jnp.transpose(grad_w_qkv, (1, 0, 2)),
+            grad_w_attn_out,
+            grad_table,
+            grad_gain_one[0],
+            grad_gain_two[0],
+            jnp.transpose(grad_router),
             grad_w_in,
             grad_w_out,
         )
 
     if fast:
-        grad_rows, slot_rows, slot_columns, attended, lse, late = routed
-        residual, hidden_two, weight_own, rows, row_gates, late_rows = middle(
+        (
+            gathered,
+            projected,
+            weights_full,
+            patterns,
+            router_rows,
+            gains,
+            slot_columns,
+            attended,
+            lse,
+            residual,
+            hidden_two,
+            weight_own,
+            rows,
+            grad_rows,
+            row_gates,
+        ) = opening(
             n_dp,
             n_tensor,
             experts,
             capacity,
-            attended,
-            outs_full,
             tokens,
-            gains[1:2],
-            router_rows,
-            slot_rows,
+            cotangent,
+            weight_shard,
+            extra,
+            w_attn_out,
             route_rows,
-            late,
+            segments,
+            selectors,
         )
         back, gate_back, value, grad_w_in, grad_w_out = run_experts(
-            n_dp, capacity, rows, grad_rows, late_rows, row_gates, w_in, w_out
+            n_dp, capacity, rows, grad_rows, row_gates, w_in, w_out
         )
         grad_residual, grad_branch_all, grad_attended, small, merged = combine(
             n_dp,
@@ -2210,8 +2313,8 @@
             segments,
             patterns,
             skew,
-            gathered_one,
-            qkv_matrix,
+            gathered.reshape(seq_len, model_width),
+            weights_full.reshape(model_width, 3 * head_cols),
             grad_branch_all.reshape(seq_len, model_width),
             small,
             weight_shard,
@@ -2223,6 +2326,12 @@
             gains[0:1],
         )
         return finish(*results, grad_w_in, grad_w_out)
+    gathered, projected, weights_full, outs_full, patterns, router_rows, gains = front(
+        n_dp, n_tensor, experts, tokens, weight_shard, extra, w_attn_out, selectors
+    )
+    gathered_one = gathered.reshape(seq_len, model_width)
+    qkv_matrix = weights_full.reshape(model_width, 3 * head_cols)
+    outs_full = outs_full.reshape(n_dp, model_width, model_width // n_dp)
     tokens_float = tokens.astype(F32)
     scale_one = rms_scale(tokens_float)
     gain_one, gain_two = gains[0], gains[1]

time: 484 us -> 462 us (0.955)
  local copies, waits for them, and re-layouts: 27.8 us -> 3.84 us
    unnamed x17 -> x5, local copies, waits for them, and re-layouts: 19.2 us -> 1.09 us
where the time goes in v6:
time: 462 us; the launch traced here: 454 us
  Pallas kernels  447 us (97%)
    pallas_call x1, Pallas kernels, opening(): pl.pallas_call(functools.partial(opening_kernel, n_dp, n_tensor, experts,...  186 us
    pallas_call x1, Pallas kernels, last(): pl.pallas_call(functools.partial(last_kernel, n_dp, n_tensor, experts, he...  90.3 us
    pallas_call x1, Pallas kernels, combine(): pl.pallas_call(functools.partial(combine_kernel, n_dp, n_tensor, experts)...  84.2 us
    pallas_call x1, Pallas kernels, run_experts(): pl.pallas_call(functools.partial(expert_kernel, n_dp, local, capacity), o...  72.9 us
    pallas_call x1, Pallas kernels, deliver(): pl.pallas_call(deliver_kernel, out_shape=(jax.ShapeDtypeStruct(layer.shap...  14 us

profile of v6, /device:TPU:0, one launch (start us, length us, event | category | flops | bytes accessed | tf_op | source)
XLA Modules:
  0.0 454.1 jit_solution(13880417810041574311)
XLA Ops:
  0.6 1.1 copy.25
  1.7 0.8 copy.26.weight_ref.weight_own_ref
  2.6 1.3 pad.9.routes_ref
  3.9 1.3 fusion.1.extra_ref
  5.2 185.8 %opening.1 = (bf16[4,256,1024]{2,1,0:T(8,128)(2,1)}, bf16[1024,768]{1,0:T(8,128)(2,1)}, bf16[8,128,768]{2,1,0:T(8,128)(2,1)}, f32[8,512]{1,0:T(8,128)}, bf16[16,...) custom-call(bf16[256,1024]{1,0:T(8,128)(2,1)} %tokens_ref.3, ...), custom_call_target="tpu_custom_call" | custom-call | tf_op jit(solution)/shard_map/opening/pallas_call | solution.py:1718
  191.1 0.0 copy-start
  191.1 72.9 %experts.1 = (bf16[8,320,1024]{2,1,0:T(8,128)(2,1)}, f32[8,8,320]{2,1,0:T(8,128)}, bf16[8,320,1024]{2,1,0:T(8,128)(2,1)}, f32[2,2,704,1024]{3,2,1,0:T(8,128)}, f32[2,704,1024]{2,1,0:T(8,128)}) custom-call(bf16[8,320,1024]{2,1,0:T(8,128)(2,1)} %get-tuple-element.50.rows_ref, bf16[8,320,1024]{2,1,0:T(8,128)(2,1)} %get-tuple-element.51.grad_ref, ...), custom_call_target="tpu_custom_call" | custom-call | tf_op jit(solution)/shard_map/experts/pallas_call | solution.py:803
  264.0 0.0 copy-done
  264.0 0.6 fusion.2
  264.6 0.0 copy-start.1
  264.6 84.2 %combine.1 = (f32[256,1024]{1,0:T(8,128)}, bf16[4,256,1024]{2,1,0:T(8,128)(2,1)}, bf16[1024,256]{1,0:T(8,128)(2,1)}, f32[32,1024]{1,0:T(8,128)}, bf16[4,256,1024]{2,1,0:T(8,128)(2,1)}) custom-call(bf16[2560,1024]{1,0:T(8,128)(2,1)} %bitcast.14, f32[8,8,320]{2,1,0:T(8,128)} %get-tuple-element.58.gate_ref, s32[1024,2]{1,0:T(8,128)} %get-tuple-element.59.slots_ref, ...), custom_call_target="tpu_custom_call" | custom-call | tf_op jit(solution)/shard_map/combine/pallas_call | solution.py:1029
  348.9 0.0 copy-done.1
  348.9 0.5 bitcast_convert_fusion.gain_own_ref
  349.4 90.3 %last.1 = (bf16[256,1024]{1,0:T(8,128)(2,1)}, bf16[256,1024]{1,0:T(8,128)(2,1)}, f32[128,768]{1,0:T(8,128)}, f32[256,128]{1,0:T(8,128)}, f32[32,128]{1,0:T(8,128)}) custom-call(bf16[1024,768]{1,0:T(8,128)(2,1)} %get-tuple-element.55.qkv_ref, bf16[1024,256]{1,0:T(8,128)(2,1)} %get-tuple-element.56.attended_ref, ...), custom_call_target="tpu_custom_call" | custom-call | tf_op jit(solution)/shard_map/last/pallas_call | solution.py:1997
  439.7 14.0 %deliver.1 = (bf16[256,1024]{1,0:T(8,128)(2,1)}, bf16[256,1024]{1,0:T(8,128)(2,1)}, f32[3,128,256]{2,1,0:T(8,128)}, f32[256,128]{1,0:T(8,128)}, f32[4,4]{1,0:T(4...) custom-call(f32[2,2,704,1024]{3,2,1,0:T(8,128)} %get-tuple-element.5, ...), custom_call_target="tpu_custom_call" | custom-call | tf_op jit(solution)/shard_map/deliver/pallas_call | solution.py:2115
Async XLA Ops:
  191.1 73.0 %copy-start = (f32[2,1024]{1,0:T(2,128)S(1)}, f32[2,1024]{1,0:T(2,128)}, u32[]{:S(2)}) copy-start(f32[2,1024]{1,0:T(2,128)} %get-tuple-element.63) | copy-start | bytes 24580
  264.6 84.2 %copy-start.1 = (bf16[128]{0:T(256)(128)(2,1)S(1)}, bf16[128]{0:T(256)(128)(2,1)}, u32[]{:S(2)}) copy-start(bf16[128]{0:T(256)(128)(2,1)} %param.20) | copy-start | bytes 772

commit v7 on v6

--- a/solution.py
+++ b/solution.py
@@ -338,7 +338,27 @@
     )
 
 
-def greet(groups):
+def staged(kernel, count, which):
+    def run(*refs):
+        inputs = list(refs[:count])
+        buffers, sems = refs[-len(which) - 1 : -1], refs[-1]
+        loads = []
+        for place, (index, buffer) in enumerate(zip(which, buffers)):
+            loads.append(pltpu.make_async_copy(inputs[index], buffer, sems.at[place]))
+            loads[-1].start()
+            inputs[index] = buffer
+        kernel(loads, *inputs, *refs[count : -len(which) - 1])
+
+    return run
+
+
+def staged_specs(args, which):
+    specs = [any_spec() if i in which else vspec() for i in range(len(args))]
+    scratch = [pltpu.VMEM(args[i].shape, args[i].dtype) for i in which]
+    return specs, scratch + [pltpu.SemaphoreType.DMA((len(which),))]
+
+
+def greet(groups, loads=()):
     barrier = pltpu.get_barrier_semaphore()
     total = 0
     for axis, n in groups:
@@ -349,6 +369,8 @@
             )
         total += n - 1
     pl.semaphore_wait(barrier, total)
+    for load in loads:
+        load.wait()
 
 
 class LineSum:
@@ -634,11 +656,11 @@
     n_dp,
     local,
     capacity,
-    rows_ref,
-    grad_ref,
+    rows_hbm,
+    grad_hbm,
     gates_ref,
-    in_ref,
-    out_ref,
+    in_hbm,
+    out_hbm,
     back_ref,
     gate_back_ref,
     value_ref,
@@ -658,12 +680,45 @@
     own_sem,
     stage_sem,
     value_sem,
+    rows_ref,
+    grad_ref,
+    in_ref,
+    out_ref,
+    rows_sem,
+    grad_sem,
+    in_sem,
+    out_sem,
 ):
     me = lax.axis_index("dp")
     pairs = n_dp // 2
     hidden = in_ref.shape[2]
     width = rows_ref.shape[2]
     two = 2 * capacity
+
+    def pair_at(index):
+        return (me // 2) ^ (pairs - 1 - index)
+
+    def load_pair(index):
+        where = pl.ds(2 * pair_at(index), 2)
+        return (
+            pltpu.make_async_copy(rows_hbm.at[where], rows_ref.at[where], rows_sem.at[index]),
+            pltpu.make_async_copy(grad_hbm.at[where], grad_ref.at[where], grad_sem.at[index]),
+        )
+
+    def load_expert(expert):
+        return (
+            pltpu.make_async_copy(in_hbm.at[expert], in_ref.at[expert], in_sem.at[expert]),
+            pltpu.make_async_copy(out_hbm.at[expert], out_ref.at[expert], out_sem.at[expert]),
+        )
+
+    for copy in load_expert(0) + load_pair(0):
+        copy.start()
+    for index in range(1, pairs):
+        for copy in load_pair(index):
+            copy.start()
+    for expert in range(1, local):
+        for copy in load_expert(expert):
+            copy.start()
     greet([("dp", n_dp)])
 
     def back_copy(expert, target, sender):
@@ -701,9 +756,14 @@
     for expert in range(local):
         part = slice(expert * capacity, (expert + 1) * capacity)
 
+        for copy in load_expert(expert):
+            copy.wait()
+
         def group(index, _):
-            pair = (me // 2) ^ (pairs - 1 - index)
-            first = 2 * pair
+            if expert == 0:
+                for copy in load_pair(index):
+                    copy.wait()
+            first = 2 * pair_at(index)
             rows = rows_ref[pl.ds(first, 2), part, :].reshape(two, width)
             grads = grad_ref[pl.ds(first, 2), part, :].reshape(two, width)
             column = jnp.concatenate(
@@ -809,7 +869,7 @@
             jax.ShapeDtypeStruct(w_in.shape, F32),
             jax.ShapeDtypeStruct(w_out.shape, F32),
         ),
-        in_specs=[vspec()] * 5,
+        in_specs=[any_spec(), any_spec(), vspec(), any_spec(), any_spec()],
         out_specs=(any_spec(), vspec(), any_spec(), any_spec(), any_spec()),
         scratch_shapes=[
             pltpu.VMEM((n_dp, slots, width), BF16),
@@ -826,6 +886,14 @@
             pltpu.SemaphoreType.DMA((local,)),
             pltpu.SemaphoreType.DMA((2,)),
             pltpu.SemaphoreType.DMA,
+            pltpu.VMEM(rows.shape, BF16),
+            pltpu.VMEM(grads.shape, BF16),
+            pltpu.VMEM(w_in.shape, BF16),
+            pltpu.VMEM(w_out.shape, BF16),
+            pltpu.SemaphoreType.DMA((n_dp // 2,)),
+            pltpu.SemaphoreType.DMA((n_dp // 2,)),
+            pltpu.SemaphoreType.DMA((local,)),
+            pltpu.SemaphoreType.DMA((local,)),
         ],
         compiler_params=pltpu.CompilerParams(
             vmem_limit_bytes=VMEM_LIMIT, collective_id=1, has_side_effects=True
@@ -843,6 +911,7 @@
     n_dp,
     n_tensor,
     experts,
+    loads,
     rows_ref,
     gate_ref,
     slots_ref,
@@ -882,7 +951,7 @@
     per = slots // n_dp
     me = lax.axis_index("dp")
     me_t = lax.axis_index("tensor")
-    greet([("dp", n_dp), ("tensor", n_tensor)])
+    greet([("dp", n_dp), ("tensor", n_tensor)], loads)
     values = []
     for step in range(1, n_dp):
         peer = lax.rem(me + step, n_dp)
@@ -1026,8 +1095,23 @@
 ):
     own_rows, width = residual.shape
     slots = rows.shape[0]
+    args = (
+        rows,
+        gates,
+        slot_columns,
+        routes_own,
+        residual,
+        hidden,
+        cotangent,
+        router_rows,
+        gain,
+        weight,
+        value,
+    )
+    which = (0, 4, 5, 6, 9)
+    specs, buffers = staged_specs(args[:10], which)
     return pl.pallas_call(
-        functools.partial(combine_kernel, n_dp, n_tensor, experts),
+        staged(functools.partial(combine_kernel, n_dp, n_tensor, experts), len(args), which),
         out_shape=(
             jax.ShapeDtypeStruct((own_rows, width), F32),
             jax.ShapeDtypeStruct((n_tensor, own_rows, width), BF16),
@@ -1035,7 +1119,7 @@
             jax.ShapeDtypeStruct((SMALL, width), F32),
             jax.ShapeDtypeStruct((n_tensor, own_rows, width), BF16),
         ),
-        in_specs=[vspec()] * 10 + [any_spec()],
+        in_specs=specs + [any_spec()],
         out_specs=(vspec(),) * 5,
         scratch_shapes=[
             pltpu.VMEM((n_tensor, own_rows, width), BF16),
@@ -1055,24 +1139,13 @@
             pltpu.SemaphoreType.DMA,
             pltpu.SemaphoreType.DMA((1, 2, n_tensor - 1)),
             pltpu.SemaphoreType.DMA((1, 2, n_tensor - 1)),
-        ],
+        ]
+        + buffers,
         compiler_params=pltpu.CompilerParams(
             vmem_limit_bytes=VMEM_LIMIT, collective_id=2, has_side_effects=True
         ),
         name="combine",
-    )(
-        rows,
-        gates,
-        slot_columns,
-        routes_own,
-        residual,
-        hidden,
-        cotangent,
-        router_rows,
-        gain,
-        weight,
-        value,
-    )
+    )(*args)
 
 
 class Streams:
@@ -1358,6 +1431,7 @@
 
 
 PARTS = 4
+ROW_PARTS = 8
 
 
 class Dispatch:
@@ -1421,6 +1495,7 @@
     n_tensor,
     experts,
     capacity,
+    loads,
     tokens_ref,
     cotangent_ref,
     weight_ref,
@@ -1468,12 +1543,13 @@
     local = experts // n_dp
     per = local * capacity
     part = width // PARTS
+    row_part = width // ROW_PARTS
     me = lax.axis_index("dp")
     me_t = lax.axis_index("tensor")
     (hop_send, hop_recv, late_send, late_recv) = sems[12:16]
     (grad_send, grad_recv, grad_own, row_send, row_recv, row_own) = sems[16:22]
     (gate_send, gate_recv, attended_send_sem, attended_recv_sem) = sems[22:26]
-    greet([("dp", n_dp), ("tensor", n_tensor)])
+    greet([("dp", n_dp), ("tensor", n_tensor)], loads)
 
     def rows_of(block):
         return pl.ds(pl.multiple_of(block * own_rows, own_rows), own_rows)
@@ -1484,13 +1560,16 @@
         n_tensor, [hidden_ref] + [grads.at[j] for j in range(PARTS)], hop_send, hop_recv
     )
     lines.advance(1, 0)
+    lines.advance(2, 0)
     small, weights, spread, along = send_parameters(
         n_dp, n_tensor, weight_ref, extra_ref, out_ref, weights_ref, outs, extras_ref, sems
     )
     hidden_ref[me_t] = first_hidden(n_dp, experts, tokens_ref, extras_ref, gains_ref, small)
     lines.advance(1, 1)
+    lines.advance(2, 1)
     unpack_parameters(n_dp, experts, extras_ref, selector_ref, router_ref, table, pattern_ref)
     lines.advance(1, 2)
+    lines.advance(2, 2)
     lines.advance(0, 0)
 
     ids = lax.broadcasted_iota(jnp.int32, (experts, seq_len), 0)
@@ -1519,6 +1598,8 @@
     grad_moves = Dispatch(n_dp, picks, grad_stage, grad_rows_ref, grad_send, grad_recv, grad_own)
     lines.advance(1, 3)
     grad_moves.start(0, grads.at[0])
+    lines.advance(2, 3)
+    grad_moves.start(1, grads.at[1])
     weights.relay()
     for copy in along:
         copy.wait_recv()
@@ -1534,13 +1615,13 @@
     weights.finish()
     project(me_t)
     lines.advance(0, 2)
-    lines.advance(2, 0)
     lines.advance(3, 0)
+    lines.advance(4, 0)
     spread.relay()
     lines.each_new(0, 1, project)
     lines.advance(0, 3)
-    lines.advance(2, 1)
     lines.advance(3, 1)
+    lines.advance(4, 1)
     lines.each_new(0, 2, project)
     lines.each_new(0, 3, project)
 
@@ -1574,16 +1655,16 @@
         def _():
             attended_copy(qb, me_t).start()
 
-    lines.advance(2, 2)
     lines.advance(3, 2)
+    lines.advance(4, 2)
     attend(3)
     attend(0)
-    lines.advance(2, 3)
-    grad_moves.start(1, grads.at[1])
     lines.advance(3, 3)
+    grad_moves.start(2, grads.at[2])
+    lines.advance(4, 3)
     attend(2)
     attend(1)
-    grad_moves.start(2, grads.at[2])
+    grad_moves.start(3, grads.at[3])
     spread.finish()
     for block in range(n_dp):
         out_matrix[:, block * out_cols : (block + 1) * out_cols] = outs[block].reshape(
@@ -1606,9 +1687,9 @@
         * gains_ref[1:2, :]
     ).astype(BF16)
     hidden_two_ref[...] = hidden
-    for j in range(PARTS):
-        everyone[j, me_t] = hidden[:, j * part : (j + 1) * part]
-    late = Streams(n_tensor, [everyone.at[j] for j in range(PARTS)], late_send, late_recv)
+    for j in range(ROW_PARTS):
+        everyone[j, me_t] = hidden[:, j * row_part : (j + 1) * row_part]
+    late = Streams(n_tensor, [everyone.at[j] for j in range(ROW_PARTS)], late_send, late_recv)
     row_moves = Dispatch(n_dp, picks, row_stage, rows_ref, row_send, row_recv, row_own)
 
     def used(j, k):
@@ -1616,7 +1697,7 @@
             return
         row_moves.start(j, everyone.at[j])
         term = nt(
-            router_ref[:, j * part : (j + 1) * part], everyone[j].reshape(seq_len, part)
+            router_ref[:, j * row_part : (j + 1) * row_part], everyone[j].reshape(seq_len, row_part)
         )
         if j == 0:
             logits[...] = term
@@ -1625,10 +1706,6 @@
 
     for turn in late.turns():
         late.turn(turn, used)
-        if turn >= n_tensor:
-            lines.advance(4, turn - n_tensor)
-    lines.advance(4, n_tensor - 1)
-    grad_moves.start(3, grads.at[3])
     values = logits[...]
     exps = jnp.exp(values - jnp.max(values, axis=0, keepdims=True))
     probs = exps / jnp.sum(exps, axis=0, keepdims=True)
@@ -1712,11 +1789,17 @@
     depth, cols = weight.shape
     per = experts // n_dp * capacity
     part = width // PARTS
+    row_part = width // ROW_PARTS
     heads = cols // (3 * HD)
     dma = pltpu.SemaphoreType.DMA
     rows = jax.ShapeDtypeStruct((n_dp, per, width), BF16)
+    args = (tokens, cotangent, weight, extra, out, routes, segments, selectors)
+    which = (0, 1, 2, 4)
+    specs, buffers = staged_specs(args, which)
     return pl.pallas_call(
-        functools.partial(opening_kernel, n_dp, n_tensor, experts, capacity),
+        staged(
+            functools.partial(opening_kernel, n_dp, n_tensor, experts, capacity), len(args), which
+        ),
         out_shape=(
             jax.ShapeDtypeStruct((n_tensor, own_rows, width), BF16),
             jax.ShapeDtypeStruct((seq_len, cols), BF16),
@@ -1734,7 +1817,7 @@
             rows,
             jax.ShapeDtypeStruct((n_dp, 8, per), F32),
         ),
-        in_specs=[vspec()] * 8,
+        in_specs=specs,
         out_specs=(vspec(),) * 12 + (any_spec(), any_spec(), vspec()),
         scratch_shapes=[
             pltpu.VMEM((n_dp,) + extra.shape, BF16),
@@ -1742,10 +1825,10 @@
             pltpu.VMEM((n_dp, n_tensor) + out.shape, BF16),
             pltpu.VMEM((width, width), BF16),
             pltpu.VMEM((PARTS, n_tensor, own_rows, part), BF16),
-            pltpu.VMEM((PARTS, n_tensor, own_rows, part), BF16),
+            pltpu.VMEM((ROW_PARTS, n_tensor, own_rows, row_part), BF16),
             pltpu.VMEM((n_dp, per, seq_len), BF16),
             pltpu.VMEM((PARTS, n_dp, per, part), BF16),
-            pltpu.VMEM((PARTS, n_dp, per, part), BF16),
+            pltpu.VMEM((ROW_PARTS, n_dp, per, row_part), BF16),
             pltpu.VMEM((heads, 3, BS, BS), F32),
             pltpu.VMEM((8, seq_len), jnp.int32),
             pltpu.VMEM((n_tensor, own_rows, heads * HD), BF16),
@@ -1754,15 +1837,17 @@
         ]
         + parameter_sems(n_dp, n_tensor)
         + [dma((PARTS + 1, 2, n_tensor - 1))] * 2
-        + [dma((PARTS, 2, n_tensor - 1))] * 2
-        + [dma((PARTS, n_dp)), dma((PARTS, n_dp)), dma((PARTS,))] * 2
+        + [dma((ROW_PARTS, 2, n_tensor - 1))] * 2
+        + [dma((PARTS, n_dp)), dma((PARTS, n_dp)), dma((PARTS,))]
+        + [dma((ROW_PARTS, n_dp)), dma((ROW_PARTS, n_dp)), dma((ROW_PARTS,))]
         + [dma((n_dp,))] * 2
-        + [dma((n_tensor,))] * 2,
+        + [dma((n_tensor,))] * 2
+        + buffers,
         compiler_params=pltpu.CompilerParams(
             vmem_limit_bytes=VMEM_LIMIT, collective_id=4, has_side_effects=True
         ),
         name="opening",
-    )(tokens, cotangent, weight, extra, out, routes, segments, selectors)
+    )(*args)
 
 
 def last_kernel(
@@ -1770,6 +1855,7 @@
     n_tensor,
     experts,
     heads,
+    loads,
     qkv_ref,
     attended_ref,
     grad_attended_ref,
@@ -1833,7 +1919,7 @@
     out_cols = grad_out_ref.shape[1]
     me = lax.axis_index("dp")
     me_t = lax.axis_index("tensor")
-    greet([("dp", n_dp), ("tensor", n_tensor)])
+    greet([("dp", n_dp), ("tensor", n_tensor)], loads)
 
     def rows_of(block):
         return pl.ds(pl.multiple_of(block * own_rows, own_rows), own_rows)
@@ -1994,8 +2080,30 @@
         pltpu.VMEM((n_tensor - 1, own_rows, width), BF16),
         pltpu.VMEM((n_tensor + 1, own_rows, width), BF16),
     ]
+    args = (
+        projected,
+        attended,
+        grad_attended,
+        lse,
+        segments,
+        patterns,
+        skew,
+        hidden,
+        weight,
+        branch,
+        small,
+        weight_own,
+        gain_own,
+        merged,
+        residual,
+        grad_residual,
+        tokens,
+        gain,
+    )
+    which = (0, 1, 2, 7, 8, 9, 11, 13, 14, 15, 16)
+    specs, buffers = staged_specs(args, which)
     return pl.pallas_call(
-        functools.partial(last_kernel, n_dp, n_tensor, experts, heads),
+        staged(functools.partial(last_kernel, n_dp, n_tensor, experts, heads), len(args), which),
         out_shape=(
             jax.ShapeDtypeStruct((own_rows, width), BF16),
             jax.ShapeDtypeStruct((own_rows, width), BF16),
@@ -2003,7 +2111,7 @@
             jax.ShapeDtypeStruct((heads * HD, out_cols), F32),
             jax.ShapeDtypeStruct((SMALL, depth), F32),
         ),
-        in_specs=[vspec()] * 18,
+        in_specs=specs,
         out_specs=(vspec(),) * 5,
         scratch_shapes=backward_scratch(heads, seq_len)
         + [
@@ -2025,31 +2133,13 @@
         ]
         + [dma((n_tensor - 1,)), dma((n_tensor + 1,))] * 2
         + [dma((n_dp - 1,))] * 6
-        + [dma((n_tensor - 1,))] * 2,
+        + [dma((n_tensor - 1,))] * 2
+        + buffers,
         compiler_params=pltpu.CompilerParams(
             vmem_limit_bytes=VMEM_LIMIT, collective_id=5, has_side_effects=True
         ),
         name="last",
-    )(
-        projected,
-        attended,
-        grad_attended,
-        lse,
-        segments,
-        patterns,
-        skew,
-        hidden,
-        weight,
-        branch,
-        small,
-        weight_own,
-        gain_own,
-        merged,
-        residual,
-        grad_residual,
-        tokens,
-        gain,
-    )
+    )(*args)
 
 
 def deliver_kernel(

time: 462 us -> 440 us (0.952)
  Pallas kernels: 447 us -> 425 us
    pallas_call x3, Pallas kernels: 360 us -> 341 us  [the longest x1 176 us: opening(): pl.pallas_call(staged(functools.partial(opening_kernel, n_dp, n_tensor, e...]
where the time goes in v7:
time: 440 us; the launch traced here: 431 us
  Pallas kernels  425 us (97%)
    pallas_call x1, Pallas kernels, opening(): pl.pallas_call(staged(functools.partial(opening_kernel, n_dp, n_tensor, e...  176 us
    pallas_call x1, Pallas kernels, last(): pl.pallas_call(staged(functools.partial(last_kernel, n_dp, n_tensor, expe...  83.8 us
    pallas_call x1, Pallas kernels, combine(): pl.pallas_call(staged(functools.partial(combine_kernel, n_dp, n_tensor, e...  81.8 us
    pallas_call x1, Pallas kernels, run_experts(): pl.pallas_call(functools.partial(expert_kernel, n_dp, local, capacity), o...  69.2 us
    pallas_call x1, Pallas kernels, deliver(): pl.pallas_call(deliver_kernel, out_shape=(jax.ShapeDtypeStruct(layer.shap...  14 us

profile of v7, /device:TPU:0, one launch (start us, length us, event | category | flops | bytes accessed | tf_op | source)
XLA Modules:
  0.0 431.5 jit_solution(14011412757570037230)
XLA Ops:
  0.6 1.1 copy.25
  1.7 0.8 copy.26.refs_2_.refs_11_
  2.6 1.3 pad.9.refs_5_.refs_3_
  3.9 1.3 fusion.1.refs_3_
  5.2 175.8 %opening.1 = (bf16[4,256,1024]{2,1,0:T(8,128)(2,1)}, bf16[1024,768]{1,0:T(8,128)(2,1)}, bf16[8,128,768]{2,1,0:T(8,128)(2,1)}, f32[8,512]{1,0:T(8,128)}, bf16[16,...) custom-call(bf16[256,1024]{1,0:T(8,128)(2,1)} %refs_16_.1, ...), custom_call_target="tpu_custom_call" | custom-call | tf_op jit(solution)/shard_map/opening/pallas_call | solution.py:1799
  181.0 0.0 copy-start
  181.1 69.2 %experts.1 = (bf16[8,320,1024]{2,1,0:T(8,128)(2,1)}, f32[8,8,320]{2,1,0:T(8,128)}, bf16[8,320,1024]{2,1,0:T(8,128)(2,1)}, f32[2,2,704,1024]{3,2,1,0:T(8,128)}, f32[2,704,1024]{2,1,0:T(8,128)}) custom-call(bf16[8,320,1024]{2,1,0:T(8,128)(2,1)} %get-tuple-element.50.rows_hbm, bf16[8,320,1024]{2,1,0:T(8,128)(2,1)} %get-tuple-element.51.grad_hbm, ...), custom_call_target="tpu_custom_call" | custom-call | tf_op jit(solution)/shard_map/experts/pallas_call | solution.py:863
  250.2 0.0 copy-done
  250.2 0.6 fusion.2
  250.9 0.0 copy-start.1
  250.9 81.8 %combine.1 = (f32[256,1024]{1,0:T(8,128)}, bf16[4,256,1024]{2,1,0:T(8,128)(2,1)}, bf16[1024,256]{1,0:T(8,128)(2,1)}, f32[32,1024]{1,0:T(8,128)}, bf16[4,256,1024]{2,1,0:T(8,128)(2,1)}) custom-call(bf16[2560,1024]{1,0:T(8,128)(2,1)} %bitcast.14, f32[8,8,320]{2,1,0:T(8,128)} %get-tuple-element.58.refs_1_, s32[1024,2]{1,0:T(8,128)} %get-tuple-element.59.refs_2_, ...), custom_call_target="tpu_custom_call" | custom-call | tf_op jit(solution)/shard_map/combine/pallas_call | solution.py:1113
  332.7 0.0 copy-done.1
  332.7 0.5 bitcast_convert_fusion.refs_12_
  333.2 83.8 %last.1 = (bf16[256,1024]{1,0:T(8,128)(2,1)}, bf16[256,1024]{1,0:T(8,128)(2,1)}, f32[128,768]{1,0:T(8,128)}, f32[256,128]{1,0:T(8,128)}, f32[32,128]{1,0:T(8,128)}) custom-call(bf16[1024,768]{1,0:T(8,128)(2,1)} %get-tuple-element.55.refs_0_, bf16[1024,256]{1,0:T(8,128)(2,1)} %get-tuple-element.56.refs_1_, bf16[1024,256]{1,0:T(8,128)(2,1)} %get-tuple-element.66.refs_2_, ...), custom_call_target="tpu_custom_call" | custom-call | tf_op jit(solution)/shard_map/last/pallas_call | solution.py:2105
  417.0 14.0 %deliver.1 = (bf16[256,1024]{1,0:T(8,128)(2,1)}, bf16[256,1024]{1,0:T(8,128)(2,1)}, f32[3,128,256]{2,1,0:T(8,128)}, f32[256,128]{1,0:T(8,128)}, f32[4,4]{1,0:T(4...) custom-call(f32[2,2,704,1024]{3,2,1,0:T(8,128)} %get-tuple-element.5, ...), custom_call_target="tpu_custom_call" | custom-call | tf_op jit(solution)/shard_map/deliver/pallas_call | solution.py:2205
Async XLA Ops:
  181.0 69.2 %copy-start = (f32[2,1024]{1,0:T(2,128)S(1)}, f32[2,1024]{1,0:T(2,128)}, u32[]{:S(2)}) copy-start(f32[2,1024]{1,0:T(2,128)} %get-tuple-element.63) | copy-start | bytes 24580
  250.9 81.8 %copy-start.1 = (bf16[128]{0:T(256)(128)(2,1)S(1)}, bf16[128]{0:T(256)(128)(2,1)}, u32[]{:S(2)}) copy-start(bf16[128]{0:T(256)(128)(2,1)} %param.20) | copy-start | bytes 772

commit v8 on v7

--- a/solution.py
+++ b/solution.py
@@ -338,27 +338,60 @@
     )
 
 
-def staged(kernel, count, which):
+class Staging:
+    def __init__(self):
+        self.loads, self.stores, self.flying = [], {}, []
+
+    def wait(self):
+        for load in self.loads:
+            load.wait()
+
+    def put(self, *indices):
+        for index in indices:
+            copy = self.stores.pop(index)
+            copy.start()
+            self.flying.append(copy)
+
+    def close(self):
+        self.put(*list(self.stores))
+        for copy in self.flying:
+            copy.wait()
+
+
+def staged(kernel, count, which, outs=0, which_out=()):
+    extra = len(which) + len(which_out) + 2
+
     def run(*refs):
-        inputs = list(refs[:count])
-        buffers, sems = refs[-len(which) - 1 : -1], refs[-1]
-        loads = []
-        for place, (index, buffer) in enumerate(zip(which, buffers)):
-            loads.append(pltpu.make_async_copy(inputs[index], buffer, sems.at[place]))
-            loads[-1].start()
-            inputs[index] = buffer
-        kernel(loads, *inputs, *refs[count : -len(which) - 1])
+        inputs, outputs = list(refs[:count]), list(refs[count : count + outs])
+        tail = refs[-extra:]
+        buffers, in_sems, out_sems = tail[:-2], tail[-2], tail[-1]
+        staging = Staging()
+        for place, index in enumerate(which):
+            copy = pltpu.make_async_copy(inputs[index], buffers[place], in_sems.at[place])
+            copy.start()
+            staging.loads.append(copy)
+            inputs[index] = buffers[place]
+        for place, index in enumerate(which_out):
+            buffer = buffers[len(which) + place]
+            staging.stores[index] = pltpu.make_async_copy(
+                buffer, outputs[index], out_sems.at[place]
+            )
+            outputs[index] = buffer
+        kernel(staging, *inputs, *outputs, *refs[count + outs : -extra])
+        staging.close()
 
     return run
 
 
-def staged_specs(args, which):
+def staged_specs(args, which, shapes=(), which_out=()):
     specs = [any_spec() if i in which else vspec() for i in range(len(args))]
     scratch = [pltpu.VMEM(args[i].shape, args[i].dtype) for i in which]
-    return specs, scratch + [pltpu.SemaphoreType.DMA((len(which),))]
-
-
-def greet(groups, loads=()):
+    scratch += [pltpu.VMEM(shapes[i].shape, shapes[i].dtype) for i in which_out]
+    dma = pltpu.SemaphoreType.DMA
+    return specs, scratch + [dma((len(which),)), dma((max(1, len(which_out)),))]
+
+
+def greet(groups, staging=None):
     barrier = pltpu.get_barrier_semaphore()
     total = 0
     for axis, n in groups:
@@ -369,8 +402,8 @@
             )
         total += n - 1
     pl.semaphore_wait(barrier, total)
-    for load in loads:
-        load.wait()
+    if staging is not None:
+        staging.wait()
 
 
 class LineSum:
@@ -748,7 +781,7 @@
         slot = len(staged) % 2
         if len(staged) >= 2:
             staged[-2].wait()
-        stage[slot] = value
+        stage[slot] = value.astype(BF16)
         copy = stage_copy(slot, target)
         copy.start()
         staged.append(copy)
@@ -866,8 +899,8 @@
             jax.ShapeDtypeStruct((n_dp, slots, width), BF16),
             jax.ShapeDtypeStruct((n_dp, 8, slots), F32),
             jax.ShapeDtypeStruct((n_dp, slots, width), BF16),
-            jax.ShapeDtypeStruct(w_in.shape, F32),
-            jax.ShapeDtypeStruct(w_out.shape, F32),
+            jax.ShapeDtypeStruct(w_in.shape, BF16),
+            jax.ShapeDtypeStruct(w_out.shape, BF16),
         ),
         in_specs=[any_spec(), any_spec(), vspec(), any_spec(), any_spec()],
         out_specs=(any_spec(), vspec(), any_spec(), any_spec(), any_spec()),
@@ -877,7 +910,7 @@
             pltpu.VMEM((n_dp, capacity, hidden), BF16),
             pltpu.VMEM((2, n_dp, capacity, hidden), BF16),
             pltpu.VMEM((8, 128), F32),
-            pltpu.VMEM((2, hidden, width), F32),
+            pltpu.VMEM((2, hidden, width), BF16),
             pltpu.VMEM((n_dp, capacity, width), BF16),
             pltpu.SemaphoreType.DMA((local, n_dp)),
             pltpu.SemaphoreType.DMA((local, n_dp)),
@@ -1041,6 +1074,7 @@
         grad_unit - unit * jnp.mean(grad_unit * unit, axis=1, keepdims=True)
     )
     grad_residual_ref[...] = grad_residual
+    loads.put(0)
     branch_ref[me_t] = grad_residual.astype(BF16)
 
     def on_block(block):
@@ -1065,6 +1099,8 @@
                 return 0
 
             lax.fori_loop(0, n_tensor, merge, 0)
+            loads.put(4)
+    loads.put(1, 2)
     lines.drain()
     small_ref[0:experts, :] = jnp.dot(
         grad_logits,
@@ -1108,19 +1144,26 @@
         weight,
         value,
     )
-    which = (0, 4, 5, 6, 9)
-    specs, buffers = staged_specs(args[:10], which)
+    which, which_out = (0, 4, 5, 6, 9), (0, 1, 2, 4)
+    shapes = (
+        jax.ShapeDtypeStruct((own_rows, width), F32),
+        jax.ShapeDtypeStruct((n_tensor, own_rows, width), BF16),
+        jax.ShapeDtypeStruct((n_tensor * own_rows, weight.shape[0]), BF16),
+        jax.ShapeDtypeStruct((SMALL, width), F32),
+        jax.ShapeDtypeStruct((n_tensor, own_rows, width), BF16),
+    )
+    specs, buffers = staged_specs(args[:10], which, shapes, which_out)
     return pl.pallas_call(
-        staged(functools.partial(combine_kernel, n_dp, n_tensor, experts), len(args), which),
-        out_shape=(
-            jax.ShapeDtypeStruct((own_rows, width), F32),
-            jax.ShapeDtypeStruct((n_tensor, own_rows, width), BF16),
-            jax.ShapeDtypeStruct((n_tensor * own_rows, weight.shape[0]), BF16),
-            jax.ShapeDtypeStruct((SMALL, width), F32),
-            jax.ShapeDtypeStruct((n_tensor, own_rows, width), BF16),
+        staged(
+            functools.partial(combine_kernel, n_dp, n_tensor, experts),
+            len(args),
+            which,
+            len(shapes),
+            which_out,
         ),
+        out_shape=shapes,
         in_specs=specs + [any_spec()],
-        out_specs=(vspec(),) * 5,
+        out_specs=(any_spec(), any_spec(), any_spec(), vspec(), any_spec()),
         scratch_shapes=[
             pltpu.VMEM((n_tensor, own_rows, width), BF16),
             pltpu.VMEM((own_rows, width), F32),
@@ -1665,6 +1708,7 @@
     attend(2)
     attend(1)
     grad_moves.start(3, grads.at[3])
+    loads.put(0, 1, 2, 7)
     spread.finish()
     for block in range(n_dp):
         out_matrix[:, block * out_cols : (block + 1) * out_cols] = outs[block].reshape(
@@ -1689,6 +1733,7 @@
     hidden_two_ref[...] = hidden
     for j in range(ROW_PARTS):
         everyone[j, me_t] = hidden[:, j * row_part : (j + 1) * row_part]
+    loads.put(9, 10, 11)
     late = Streams(n_tensor, [everyone.at[j] for j in range(ROW_PARTS)], late_send, late_recv)
     row_moves = Dispatch(n_dp, picks, row_stage, rows_ref, row_send, row_recv, row_own)
 
@@ -1794,13 +1839,8 @@
     dma = pltpu.SemaphoreType.DMA
     rows = jax.ShapeDtypeStruct((n_dp, per, width), BF16)
     args = (tokens, cotangent, weight, extra, out, routes, segments, selectors)
-    which = (0, 1, 2, 4)
-    specs, buffers = staged_specs(args, which)
-    return pl.pallas_call(
-        staged(
-            functools.partial(opening_kernel, n_dp, n_tensor, experts, capacity), len(args), which
-        ),
-        out_shape=(
+    which, which_out = (0, 1, 2, 4), (0, 1, 2, 7, 9, 10, 11)
+    shapes = (
             jax.ShapeDtypeStruct((n_tensor, own_rows, width), BF16),
             jax.ShapeDtypeStruct((seq_len, cols), BF16),
             jax.ShapeDtypeStruct((n_dp, depth, cols), BF16),
@@ -1816,9 +1856,21 @@
             rows,
             rows,
             jax.ShapeDtypeStruct((n_dp, 8, per), F32),
+    )
+    specs, buffers = staged_specs(args, which, shapes, which_out)
+    return pl.pallas_call(
+        staged(
+            functools.partial(opening_kernel, n_dp, n_tensor, experts, capacity),
+            len(args),
+            which,
+            len(shapes),
+            which_out,
         ),
+        out_shape=shapes,
         in_specs=specs,
-        out_specs=(vspec(),) * 12 + (any_spec(), any_spec(), vspec()),
+        out_specs=tuple(
+            any_spec() if i in which_out or i in (12, 13) else vspec() for i in range(len(shapes))
+        ),
         scratch_shapes=[
             pltpu.VMEM((n_dp,) + extra.shape, BF16),
             pltpu.VMEM((NB, depth), F32),
@@ -2162,6 +2214,8 @@
     down_ref,
     stage_in,
     stage_down,
+    wide_in,
+    wide_down,
     in_sem,
     down_sem,
     out_sem,
@@ -2169,14 +2223,28 @@
 ):
     local, halves = grad_in_ref.shape[:2]
     pieces = [
-        (grad_in_ref.at[e, g], stage_in.at[e, g], in_ref.at[e, g], in_sem.at[e, g], out_sem.at[e, g])
+        (
+            grad_in_ref.at[e, g],
+            stage_in.at[e, g],
+            wide_in.at[e, g],
+            in_ref.at[e, g],
+            in_sem.at[e, g],
+            out_sem.at[e, g],
+        )
         for e in range(local)
         for g in range(halves)
     ] + [
-        (grad_out_ref.at[e], stage_down.at[e], down_ref.at[e], down_sem.at[e], last_sem.at[e])
+        (
+            grad_out_ref.at[e],
+            stage_down.at[e],
+            wide_down.at[e],
+            down_ref.at[e],
+            down_sem.at[e],
+            last_sem.at[e],
+        )
         for e in range(local)
     ]
-    for source, stage, _, sem, _ in pieces:
+    for source, stage, _, _, sem, _ in pieces:
         pltpu.make_async_copy(source, stage, sem).start()
     layer_ref[...] = layer_in_ref[...]
     tokens_ref[...] = tokens_in_ref[...]
@@ -2191,11 +2259,12 @@
     table_ref[...] = small_ref[
         experts + 2 : experts + 2 + table_ref.shape[0], 0 : table_ref.shape[1]
     ]
-    for source, stage, target, sem, done in pieces:
+    for source, stage, wide, target, sem, done in pieces:
         pltpu.make_async_copy(source, stage, sem).wait()
-        pltpu.make_async_copy(stage, target, done).start()
-    for _, stage, target, _, done in pieces:
-        pltpu.make_async_copy(stage, target, done).wait()
+        wide[...] = stage[...].astype(F32)
+        pltpu.make_async_copy(wide, target, done).start()
+    for _, _, wide, target, _, done in pieces:
+        pltpu.make_async_copy(wide, target, done).wait()
 
 
 def deliver(experts, heads, table_rows, grad_in, grad_out, layer, tokens, weight, out, small):
@@ -2219,6 +2288,8 @@
         in_specs=[any_spec()] * 2 + [vspec()] * 5,
         out_specs=(vspec(),) * 8 + (any_spec(),) * 2,
         scratch_shapes=[
+            pltpu.VMEM(grad_in.shape, grad_in.dtype),
+            pltpu.VMEM(grad_out.shape, grad_out.dtype),
             pltpu.VMEM(grad_in.shape, F32),
             pltpu.VMEM(grad_out.shape, F32),
             dma((local, halves)),

time: 440 us -> 433 us (0.984)
  Pallas kernels: 425 us -> 418 us
where the time goes in v8:
time: 433 us; the launch traced here: 425 us
  Pallas kernels  418 us (97%)
    pallas_call x1, Pallas kernels, opening(): pl.pallas_call(staged(functools.partial(opening_kernel, n_dp, n_tensor, e...  173 us
    pallas_call x1, Pallas kernels, last(): pl.pallas_call(staged(functools.partial(last_kernel, n_dp, n_tensor, expe...  83.5 us
    pallas_call x1, Pallas kernels, combine(): pl.pallas_call(staged(functools.partial(combine_kernel, n_dp, n_tensor, e...  81 us
    pallas_call x1, Pallas kernels, run_experts(): pl.pallas_call(functools.partial(expert_kernel, n_dp, local, capacity), o...  69.3 us
    pallas_call x1, Pallas kernels, deliver(): pl.pallas_call(deliver_kernel, out_shape=(jax.ShapeDtypeStruct(layer.shap...  10.7 us

profile of v8, /device:TPU:0, one launch (start us, length us, event | category | flops | bytes accessed | tf_op | source)
XLA Modules:
  0.0 424.7 jit_solution(1753381708337648045)
XLA Ops:
  0.6 1.1 copy.25
  1.7 0.8 copy.26.refs_2_.refs_11_
  2.6 1.3 pad.9.refs_5_.refs_3_
  3.9 1.3 fusion.1.refs_3_
  5.2 173.3 %opening.1 = (bf16[4,256,1024]{2,1,0:T(8,128)(2,1)}, bf16[1024,768]{1,0:T(8,128)(2,1)}, bf16[8,128,768]{2,1,0:T(8,128)(2,1)}, f32[8,512]{1,0:T(8,128)}, bf16[16,...) custom-call(bf16[256,1024]{1,0:T(8,128)(2,1)} %refs_16_.1, ...), custom_call_target="tpu_custom_call" | custom-call | tf_op jit(solution)/shard_map/opening/pallas_call | solution.py:1861
  178.5 0.0 copy-start
  178.5 69.3 %experts.1 = (bf16[8,320,1024]{2,1,0:T(8,128)(2,1)}, f32[8,8,320]{2,1,0:T(8,128)}, bf16[8,320,1024]{2,1,0:T(8,128)(2,1)}, bf16[2,2,704,1024]{3,2,1,0:T(8,128)(2,1)}, bf16[2,704,1024]{2,1,0:T(8,128)(2,1)}) custom-call(bf16[8,320,1024]{2,1,0:T(8,128)(2,1)} %get-tuple-element.50.rows_hbm, bf16[8,320,1024]{2,1,0:T(8,128)(2,1)} %get-tuple-element.51.grad_hbm, ...), custom_call_target="tpu_custom_call" | custom-call | tf_op jit(solution)/shard_map/experts/pallas_call | solution.py:896
  247.8 0.0 copy-done
  247.9 0.6 fusion.2
  248.5 0.0 copy-start.1
  248.5 81.0 %combine.1 = (f32[256,1024]{1,0:T(8,128)}, bf16[4,256,1024]{2,1,0:T(8,128)(2,1)}, bf16[1024,256]{1,0:T(8,128)(2,1)}, f32[32,1024]{1,0:T(8,128)}, bf16[4,256,1024]{2,1,0:T(8,128)(2,1)}) custom-call(bf16[2560,1024]{1,0:T(8,128)(2,1)} %bitcast.14, f32[8,8,320]{2,1,0:T(8,128)} %get-tuple-element.58.refs_1_, s32[1024,2]{1,0:T(8,128)} %get-tuple-element.59.refs_2_, ...), custom_call_target="tpu_custom_call" | custom-call | tf_op jit(solution)/shard_map/combine/pallas_call | solution.py:1156
  329.5 0.0 copy-done.1
  329.5 0.5 bitcast_convert_fusion.refs_12_
  330.0 83.5 %last.1 = (bf16[256,1024]{1,0:T(8,128)(2,1)}, bf16[256,1024]{1,0:T(8,128)(2,1)}, f32[128,768]{1,0:T(8,128)}, f32[256,128]{1,0:T(8,128)}, f32[32,128]{1,0:T(8,128)}) custom-call(bf16[1024,768]{1,0:T(8,128)(2,1)} %get-tuple-element.55.refs_0_, bf16[1024,256]{1,0:T(8,128)(2,1)} %get-tuple-element.56.refs_1_, bf16[1024,256]{1,0:T(8,128)(2,1)} %get-tuple-element.66.refs_2_, ...), custom_call_target="tpu_custom_call" | custom-call | tf_op jit(solution)/shard_map/last/pallas_call | solution.py:2157
  413.6 10.7 %deliver.1 = (bf16[256,1024]{1,0:T(8,128)(2,1)}, bf16[256,1024]{1,0:T(8,128)(2,1)}, f32[3,128,256]{2,1,0:T(8,128)}, f32[256,128]{1,0:T(8,128)}, f32[4,4]{1,0:T(4...) custom-call(bf16[2,2,704,1024]{3,2,1,0:T(8,128)(2,1)} %get-tuple-ele, ...), custom_call_target="tpu_custom_call" | custom-call | tf_op jit(solution)/shard_map/deliver/pallas_call | solution.py:2274
Async XLA Ops:
  178.5 69.4 %copy-start = (f32[2,1024]{1,0:T(2,128)S(1)}, f32[2,1024]{1,0:T(2,128)}, u32[]{:S(2)}) copy-start(f32[2,1024]{1,0:T(2,128)} %get-tuple-element.63) | copy-start | bytes 24580
  248.5 81.1 %copy-start.1 = (bf16[128]{0:T(256)(128)(2,1)S(1)}, bf16[128]{0:T(256)(128)(2,1)}, u32[]{:S(2)}) copy-start(bf16[128]{0:T(256)(128)(2,1)} %param.20) | copy-start | bytes 772

commit v9 on v8

--- a/solution.py
+++ b/solution.py
@@ -1069,7 +1069,7 @@
     unit = residual * scale
     small_ref[...] = jnp.zeros_like(small_ref)
     small_ref[experts : experts + 1, :] = jnp.sum(grad_hidden * unit, axis=0, keepdims=True)
-    grad_unit = grad_hidden * gain_ref[...]
+    grad_unit = grad_hidden * gain_ref[1:2, :]
     grad_residual = cotangent_ref[...].astype(F32) + scale * (
         grad_unit - unit * jnp.mean(grad_unit * unit, axis=1, keepdims=True)
     )
@@ -1323,7 +1323,9 @@
         )
         copy.start()
         small.append(copy)
-    weights_ref[me] = weight_ref[...]
+    cols = weight_ref.shape[2]
+    for part in range(3):
+        weights_ref[me, :, part * cols : (part + 1) * cols] = weight_ref[part]
     weights = Spread(n_dp, weights_ref, *sems[4:8])
     weights.start()
     outs_ref[me, me_t] = out_ref[...]
@@ -1447,7 +1449,7 @@
 def front(n_dp, n_tensor, experts, tokens, weight, extra, out, selectors):
     own_rows, width = tokens.shape
     seq_len = own_rows * n_tensor
-    depth, cols = weight.shape
+    depth, cols = weight.shape[1], 3 * weight.shape[2]
     heads = cols // (3 * HD)
     dma = pltpu.SemaphoreType.DMA
     return pl.pallas_call(
@@ -1831,7 +1833,7 @@
 ):
     own_rows, width = tokens.shape
     seq_len = own_rows * n_tensor
-    depth, cols = weight.shape
+    depth, cols = weight.shape[1], 3 * weight.shape[2]
     per = experts // n_dp * capacity
     part = width // PARTS
     row_part = width // ROW_PARTS
@@ -1967,7 +1969,7 @@
 ):
     own_rows, width = residual_ref.shape
     seq_len = own_rows * n_tensor
-    depth = weight_own_ref.shape[0]
+    depth = weight_own_ref.shape[1]
     out_cols = grad_out_ref.shape[1]
     me = lax.axis_index("dp")
     me_t = lax.axis_index("tensor")
@@ -2063,8 +2065,15 @@
         small_sum[...] += small_recv[step - 1]
         grad_weight_ref[...] += qkv_recv[step - 1].astype(F32)
         grad_out_ref[...] += out_recv[step - 1].astype(F32)
-    column = jnp.sum(grad_weight_ref[...] * weight_own_ref[...].astype(F32), axis=1, keepdims=True)
-    small_sum[experts + 1 : experts + 2, :] = to_row(column) / gain_own_ref[...]
+    column = jnp.zeros((depth, 1), F32)
+    part = weight_own_ref.shape[2]
+    for k in range(3):
+        column += jnp.sum(
+            grad_weight_ref[:, k * part : (k + 1) * part] * weight_own_ref[k].astype(F32),
+            axis=1,
+            keepdims=True,
+        )
+    small_sum[experts + 1 : experts + 2, :] = to_row(column) / gain_own_ref[...].astype(F32)
     gains = []
     for step in range(1, n_tensor):
         peer = lax.rem(me_t + step, n_tensor)
@@ -2082,7 +2091,7 @@
     x = tokens_ref[...].astype(F32)
     scale = lax.rsqrt(jnp.mean(x * x, axis=1, keepdims=True) + EPS)
     unit = x * scale
-    grad_unit = grad_hidden[...] * gain_ref[...]
+    grad_unit = grad_hidden[...] * gain_ref[0:1, :]
     grad_tokens_ref[...] = (
         grad_residual_ref[...]
         + scale * (grad_unit - unit * jnp.mean(grad_unit * unit, axis=1, keepdims=True))
@@ -2125,7 +2134,7 @@
 ):
     seq_len, width = hidden.shape
     own_rows = seq_len // n_tensor
-    depth, cols = weight_own.shape
+    depth, cols = weight_own.shape[1], 3 * weight_own.shape[2]
     out_cols = width // n_dp
     dma = pltpu.SemaphoreType.DMA
     line = [
@@ -2369,9 +2378,8 @@
         axis=0,
     )
     fast = n_dp == 8 and n_tensor == 4 and seq_len == 4 * BS and slots * model_width <= 4 * 1024 * 1024
-    route_rows = jnp.pad(jnp.transpose(routes), ((0, 8 - TOP), (0, 0)))
-    weight_shard = w_qkv.reshape(depth, 3 * head_cols)
-    gain_shard = gain_attn[None].astype(F32)
+    route_rows = jnp.transpose(routes)
+    weight_parts = jnp.transpose(w_qkv, (1, 0, 2))
     skew = jnp.asarray(skew_selectors().T)
     selectors = jnp.asarray(distance_selectors().T)
 
@@ -2436,7 +2444,7 @@
             capacity,
             tokens,
             cotangent,
-            weight_shard,
+            weight_parts,
             extra,
             w_attn_out,
             route_rows,
@@ -2458,7 +2466,7 @@
             hidden_two,
             cotangent,
             router_rows,
-            gains[1:2],
+            gains,
             weight_own,
             value,
         )
@@ -2478,17 +2486,17 @@
             weights_full.reshape(model_width, 3 * head_cols),
             grad_branch_all.reshape(seq_len, model_width),
             small,
-            weight_shard,
-            gain_shard,
+            weight_parts,
+            gain_attn[None],
             merged,
             residual,
             grad_residual,
             tokens,
-            gains[0:1],
+            gains,
         )
         return finish(*results, grad_w_in, grad_w_out)
     gathered, projected, weights_full, outs_full, patterns, router_rows, gains = front(
-        n_dp, n_tensor, experts, tokens, weight_shard, extra, w_attn_out, selectors
+        n_dp, n_tensor, experts, tokens, weight_parts, extra, w_attn_out, selectors
     )
     gathered_one = gathered.reshape(seq_len, model_width)
     qkv_matrix = weights_full.reshape(model_width, 3 * head_cols)
@@ -2647,8 +2655,8 @@
         attended,
         grad_branch_all,
         small,
-        weight_shard,
-        gain_shard,
+        w_qkv.reshape(depth, 3 * head_cols),
+        gain_attn[None].astype(F32),
     )
     grad_from_first, _ = norm_backward(grad_hidden_one, tokens_float, scale_one, gain_one)
     grad_tokens = (grad_residual + grad_from_first).astype(BF16)

time: 433 us -> 429 us (level)
  no operation moved by 1% of the time
where the time goes in v9:
time: 429 us; the launch traced here: 421 us
  Pallas kernels  418 us (97%)
    pallas_call x1, Pallas kernels, opening(): pl.pallas_call(staged(functools.partial(opening_kernel, n_dp, n_tensor, e...  173 us
    pallas_call x1, Pallas kernels, last(): pl.pallas_call(staged(functools.partial(last_kernel, n_dp, n_tensor, expe...  83.8 us
    pallas_call x1, Pallas kernels, combine(): pl.pallas_call(staged(functools.partial(combine_kernel, n_dp, n_tensor, e...  81 us
    pallas_call x1, Pallas kernels, run_experts(): pl.pallas_call(functools.partial(expert_kernel, n_dp, local, capacity), o...  69.4 us
    pallas_call x1, Pallas kernels, deliver(): pl.pallas_call(deliver_kernel, out_shape=(jax.ShapeDtypeStruct(layer.shap...  10.7 us

profile of v9, /device:TPU:0, one launch (start us, length us, event | category | flops | bytes accessed | tf_op | source)
XLA Modules:
  0.0 420.5 jit_solution(9338319285385543275)
XLA Ops:
  0.6 1.3 fusion.1.refs_3_
  2.0 173.2 %opening.1 = (bf16[4,256,1024]{2,1,0:T(8,128)(2,1)}, bf16[1024,768]{1,0:T(8,128)(2,1)}, bf16[8,128,768]{2,1,0:T(8,128)(2,1)}, f32[8,512]{1,0:T(8,128)}, bf16[16,...) custom-call(bf16[256,1024]{1,0:T(8,128)(2,1)} %refs_16_.1, ...), custom_call_target="tpu_custom_call" | custom-call | tf_op jit(solution)/shard_map/opening/pallas_call | solution.py:1863
  175.2 69.4 %experts.1 = (bf16[8,320,1024]{2,1,0:T(8,128)(2,1)}, f32[8,8,320]{2,1,0:T(8,128)}, bf16[8,320,1024]{2,1,0:T(8,128)(2,1)}, bf16[2,2,704,1024]{3,2,1,0:T(8,128)(2,1)}, bf16[2,704,1024]{2,1,0:T(8,128)(2,1)}) custom-call(bf16[8,320,1024]{2,1,0:T(8,128)(2,1)} %get-tuple-element.50.rows_hbm, bf16[8,320,1024]{2,1,0:T(8,128)(2,1)} %get-tuple-element.51.grad_hbm, ...), custom_call_target="tpu_custom_call" | custom-call | tf_op jit(solution)/shard_map/experts/pallas_call | solution.py:896
  244.6 81.0 %combine.1 = (f32[256,1024]{1,0:T(8,128)}, bf16[4,256,1024]{2,1,0:T(8,128)(2,1)}, bf16[1024,256]{1,0:T(8,128)(2,1)}, f32[32,1024]{1,0:T(8,128)}, bf16[4,256,1024]{2,1,0:T(8,128)(2,1)}) custom-call(bf16[2560,1024]{1,0:T(8,128)(2,1)} %bitcast.13, f32[8,8,320]{2,1,0:T(8,128)} %get-tuple-element.58.refs_1_, s32[1024,2]{1,0:T(8,128)} %get-tuple-element.59.refs_2_, ...), custom_call_target="tpu_custom_call" | custom-call | tf_op jit(solution)/shard_map/combine/pallas_call | solution.py:1156
  325.6 83.8 %last.1 = (bf16[256,1024]{1,0:T(8,128)(2,1)}, bf16[256,1024]{1,0:T(8,128)(2,1)}, f32[128,768]{1,0:T(8,128)}, f32[256,128]{1,0:T(8,128)}, f32[32,128]{1,0:T(8,128)}) custom-call(bf16[1024,768]{1,0:T(8,128)(2,1)} %get-tuple-element.55.refs_0_, bf16[1024,256]{1,0:T(8,128)(2,1)} %get-tuple-element.56.refs_1_, bf16[1024,256]{1,0:T(8,128)(2,1)} %get-tuple-element.66.refs_2_, ...), custom_call_target="tpu_custom_call" | custom-call | tf_op jit(solution)/shard_map/last/pallas_call | solution.py:2166
  409.4 10.7 %deliver.1 = (bf16[256,1024]{1,0:T(8,128)(2,1)}, bf16[256,1024]{1,0:T(8,128)(2,1)}, f32[3,128,256]{2,1,0:T(8,128)}, f32[256,128]{1,0:T(8,128)}, f32[4,4]{1,0:T(4...) custom-call(bf16[2,2,704,1024]{3,2,1,0:T(8,128)(2,1)} %get-tuple-ele, ...), custom_call_target="tpu_custom_call" | custom-call | tf_op jit(solution)/shard_map/deliver/pallas_call | solution.py:2283

commit v10 on v9

--- a/solution.py
+++ b/solution.py
@@ -470,8 +470,8 @@
         for k in range(self.n - 1):
             self.step(k)
 
-    def step(self, k):
-        for first in (True, False):
+    def step(self, k, flows=(True, False)):
+        for first in flows:
             block, comes, goes, peer, out_slot, in_slot, peer_slot = self.flow(first, k)
 
             @pl.when(goes & comes)
@@ -2021,16 +2021,17 @@
                 cols = slice(block * out_cols, (block + 1) * out_cols)
                 out_send[block] = tn(attended_ref[...], branch_ref[:, cols]).astype(BF16)
             scatter(out_send, out_recv, out_send_sem, out_recv_sem)
-        if qb >= blocks - 2 and qb - (blocks - 2) < n_tensor - 1:
-            mix.step(qb - (blocks - 2))
+        if qb == blocks - 2:
+            mix.step(0, (True,))
+    mix.step(0, (False,))
+    mix.step(1, (True,))
     backward_end(heads, grad_qkv, dk, dv)
     line.start(lambda block: nt(grad_qkv[rows_of(block), :], weight_ref[...]))
-    for k in range(2, n_tensor - 1):
-        mix.step(k)
     for block in range(n_dp):
         cols = slice(block * depth, (block + 1) * depth)
         qkv_send[block] = tn(hidden_ref[:, cols], grad_qkv[...]).astype(BF16)
     scatter(qkv_send, qkv_recv, qkv_send_sem, qkv_recv_sem)
+    line.step(0, (True,))
     diag[...] = jnp.zeros_like(diag)
     diagonal_sums(heads, sums, diag)
     tables = lax.dot_general(
@@ -2053,8 +2054,12 @@
             block * rows_each : (block + 1) * rows_each, :
         ]
     scatter(small_send, small_recv, small_send_sem, small_recv_sem)
+    mix.step(1, (False,))
+    for k in range(2, n_tensor - 1):
+        mix.step(k)
     layer_ref[...] = (residual_ref[...] + mixture[...]).astype(BF16)
-    for k in range(n_tensor - 2):
+    line.step(0, (False,))
+    for k in range(1, n_tensor - 2):
         line.step(k)
     for copy in copies:
         copy.wait_recv()

time: 429 us -> 425 us (level)
  no operation moved by 1% of the time
where the time goes in v10:
time: 425 us; the launch traced here: 417 us
  Pallas kernels  414 us (97%)
    pallas_call x1, Pallas kernels, opening(): pl.pallas_call(staged(functools.partial(opening_kernel, n_dp, n_tensor, e...  173 us
    pallas_call x1, Pallas kernels, combine(): pl.pallas_call(staged(functools.partial(combine_kernel, n_dp, n_tensor, e...  81 us
    pallas_call x1, Pallas kernels, last(): pl.pallas_call(staged(functools.partial(last_kernel, n_dp, n_tensor, expe...  79.9 us
    pallas_call x1, Pallas kernels, run_experts(): pl.pallas_call(functools.partial(expert_kernel, n_dp, local, capacity), o...  69.4 us
    pallas_call x1, Pallas kernels, deliver(): pl.pallas_call(deliver_kernel, out_shape=(jax.ShapeDtypeStruct(layer.shap...  10.7 us

profile of v10, /device:TPU:0, one launch (start us, length us, event | category | flops | bytes accessed | tf_op | source)
XLA Modules:
  0.0 416.7 jit_solution(7261846183066367995)
XLA Ops:
  0.6 1.3 fusion.1.refs_3_
  2.0 173.2 %opening.1 = (bf16[4,256,1024]{2,1,0:T(8,128)(2,1)}, bf16[1024,768]{1,0:T(8,128)(2,1)}, bf16[8,128,768]{2,1,0:T(8,128)(2,1)}, f32[8,512]{1,0:T(8,128)}, bf16[16,...) custom-call(bf16[256,1024]{1,0:T(8,128)(2,1)} %refs_16_.1, ...), custom_call_target="tpu_custom_call" | custom-call | tf_op jit(solution)/shard_map/opening/pallas_call | solution.py:1863
  175.2 69.4 %experts.1 = (bf16[8,320,1024]{2,1,0:T(8,128)(2,1)}, f32[8,8,320]{2,1,0:T(8,128)}, bf16[8,320,1024]{2,1,0:T(8,128)(2,1)}, bf16[2,2,704,1024]{3,2,1,0:T(8,128)(2,1)}, bf16[2,704,1024]{2,1,0:T(8,128)(2,1)}) custom-call(bf16[8,320,1024]{2,1,0:T(8,128)(2,1)} %get-tuple-element.50.rows_hbm, bf16[8,320,1024]{2,1,0:T(8,128)(2,1)} %get-tuple-element.51.grad_hbm, ...), custom_call_target="tpu_custom_call" | custom-call | tf_op jit(solution)/shard_map/experts/pallas_call | solution.py:896
  244.6 81.0 %combine.1 = (f32[256,1024]{1,0:T(8,128)}, bf16[4,256,1024]{2,1,0:T(8,128)(2,1)}, bf16[1024,256]{1,0:T(8,128)(2,1)}, f32[32,1024]{1,0:T(8,128)}, bf16[4,256,1024]{2,1,0:T(8,128)(2,1)}) custom-call(bf16[2560,1024]{1,0:T(8,128)(2,1)} %bitcast.13, f32[8,8,320]{2,1,0:T(8,128)} %get-tuple-element.58.refs_1_, s32[1024,2]{1,0:T(8,128)} %get-tuple-element.59.refs_2_, ...), custom_call_target="tpu_custom_call" | custom-call | tf_op jit(solution)/shard_map/combine/pallas_call | solution.py:1156
  325.6 79.9 %last.1 = (bf16[256,1024]{1,0:T(8,128)(2,1)}, bf16[256,1024]{1,0:T(8,128)(2,1)}, f32[128,768]{1,0:T(8,128)}, f32[256,128]{1,0:T(8,128)}, f32[32,128]{1,0:T(8,128)}) custom-call(bf16[1024,768]{1,0:T(8,128)(2,1)} %get-tuple-element.55.refs_0_, bf16[1024,256]{1,0:T(8,128)(2,1)} %get-tuple-element.56.refs_1_, bf16[1024,256]{1,0:T(8,128)(2,1)} %get-tuple-element.66.refs_2_, ...), custom_call_target="tpu_custom_call" | custom-call | tf_op jit(solution)/shard_map/last/pallas_call | solution.py:2171
  405.5 10.7 %deliver.1 = (bf16[256,1024]{1,0:T(8,128)(2,1)}, bf16[256,1024]{1,0:T(8,128)(2,1)}, f32[3,128,256]{2,1,0:T(8,128)}, f32[256,128]{1,0:T(8,128)}, f32[4,4]{1,0:T(4...) custom-call(bf16[2,2,704,1024]{3,2,1,0:T(8,128)(2,1)} %get-tuple-ele, ...), custom_call_target="tpu_custom_call" | custom-call | tf_op jit(solution)/shard_map/deliver/pallas_call | solution.py:2288
